TPU v7x, 32 devices: a whole 2x2x4 slice. The times are simulated.
32 devices in a mesh: fsdp: 2 (over y), ctx: 16 (over z, x, core).
Axes of the slice: x: 2, y: 2, z: 4, core: 2. Of those that a mesh axis runs over, the one named last changes fastest.
Arguments:
- layer_input: bfloat16 [8, 1024, 1024], P('fsdp', 'ctx'), may hold values from -6 to 6
- output_grad: bfloat16 [8, 1024, 1024], P('fsdp', 'ctx'), may hold values from -6 to 6
- segments: int32 [8, 1024], P('fsdp'), may hold values from 0 to 3, never falling along the last dimension, each value on 1 to 512 neighbouring positions
- assignment: int32 [16], replicated, may hold values from 0 to 15, each once
- first_gain: bfloat16 [1024], P('fsdp'), may hold values from 0.5 to 1.5
- first_bias: bfloat16 [1024], P('fsdp'), may hold values from -1.5 to 1.5
- input_weight: bfloat16 [1024, 3072], P('fsdp'), may hold values from -0.25 to 0.25
- query_bias: bfloat16 [1024], P('fsdp'), may hold values from -2.5 to 2.5
- value_bias: bfloat16 [1024], P('fsdp'), may hold values from -2.5 to 2.5
- output_weight: bfloat16 [1024, 1024], P(None, 'fsdp'), may hold values from -1.5 to 1.5
- output_bias: bfloat16 [1024], P('fsdp'), may hold values from -1.5 to 1.5
- second_gain: bfloat16 [1024], P('fsdp'), may hold values from 0.5 to 1.5
- second_bias: bfloat16 [1024], P('fsdp'), may hold values from -1.5 to 1.5
- expand_weight: bfloat16 [1024, 4096], P('fsdp'), may hold values from -0.1875 to 0.1875
- expand_bias: bfloat16 [4096], P('fsdp'), may hold values from -2.5 to 2.5
- shrink_weight: bfloat16 [4096, 1024], P(None, 'fsdp'), may hold values from -0.09375 to 0.09375
- shrink_bias: bfloat16 [1024], P('fsdp'), may hold values from -1.5 to 1.5
Outputs:
- layer_output: bfloat16 [8, 1024, 1024], P('fsdp', 'ctx')
- input_grad: float32 [8, 1024, 1024], P('fsdp', 'ctx')
- first_gain_grad: float32 [1024], P('fsdp')
- first_bias_grad: float32 [1024], P('fsdp')
- input_weight_grad: float32 [1024, 3072], P('fsdp')
- query_bias_grad: float32 [1024], P('fsdp')
- value_bias_grad: float32 [1024], P('fsdp')
- output_weight_grad: float32 [1024, 1024], P(None, 'fsdp')
- output_bias_grad: float32 [1024], P('fsdp')
- second_gain_grad: float32 [1024], P('fsdp')
- second_bias_grad: float32 [1024], P('fsdp')
- expand_weight_grad: float32 [1024, 4096], P('fsdp')
- expand_bias_grad: float32 [4096], P('fsdp')
- shrink_weight_grad: float32 [4096, 1024], P(None, 'fsdp')
- shrink_bias_grad: float32 [1024], P('fsdp')
Inputs may be any that keep to these rules, and one draw needn't show every extreme that they name: `segments`: in each sequence, in the order of positions, the document numbers never fall; each document has 1 to 512 positions and one has exactly 512. A permutation: index i of ctx holds the blocks assignment[i] and 31 - assignment[i] of every sequence.
All inputs are finite; a program needn't handle non-finite values.
Results may differ from a plain program's by a relative error of at most 0.012.
The roundings to bfloat16 on the way count: a program that leaves them out, or rounds other values in their place, can miss the bound.
Values may be sent and summed in bfloat16 or wider, within the bound.
No kernel may reach another device: no remote copies, remote signals or barrier semaphores. Data moves between devices by JAX's collectives and lax.ppermute only.
A program may use at most 320 MiB of HBM per device.

v0:
```python
import math

import jax
import jax.numpy as jnp
from jax import lax
from jax.sharding import PartitionSpec as P

HEADS = 16
MICRO = 2


EPSILON = 1e-05
MASKED = -1000000000.0


def layer_norm(inputs, norm_gain, norm_bias):
    center = inputs - jnp.mean(inputs, axis=-1, keepdims=True)
    spread = jnp.mean(center * center, axis=-1, keepdims=True)
    return center * lax.rsqrt(spread + EPSILON) * norm_gain + norm_bias


def gelu_tanh(inputs):
    return jax.nn.gelu(inputs, approximate=True)


def key_places(assignment, row_count, length):
    pairs = assignment.shape[0]
    span_len = row_count // 2
    places = jnp.arange(length, dtype=jnp.int32)
    owner = places // row_count
    within = places % row_count
    match = owner[:, None] == jnp.arange(pairs, dtype=jnp.int32)[None, :]
    paired = jnp.sum(jnp.where(match, assignment[None, :], 0), axis=1)
    early = paired * span_len + within
    later = (2 * pairs - 1 - paired) * span_len + within - span_len
    return jnp.where(within < span_len, early, later)


def masked_scores(queries, key_rows, query_place, key_place, query_doc, key_doc, inv_root):
    scores = (
        jnp.einsum("sqhd,skhd->shqk", queries, key_rows, preferred_element_type=jnp.float32)
        * inv_root
    )
    allowed = (key_place[None, None, :] <= query_place[None, :, None]) & (
        key_doc[:, None, :] == query_doc[:, :, None]
    )
    return jnp.where(allowed[:, None], scores, MASKED)


def one_batch(weights, layer_input, output_grad, segments, places, own_places):
    (
        first_gain,
        first_bias,
        input_weight,
        query_bias,
        value_bias,
        output_weight,
        output_bias,
        second_gain,
        second_bias,
        expand_weight,
        expand_bias,
        shrink_weight,
        shrink_bias,
    ) = weights
    seq_count, row_count, features = layer_input.shape
    head_count = HEADS
    head_size = features // head_count
    inv_root = 1.0 / math.sqrt(head_size)
    length = places.shape[0]
    size_k = min(512, length)
    blocks = length // size_k
    key_docs = jnp.take(segments, places, axis=1)
    own_docs = jnp.take(segments, own_places, axis=1)
    inputs = layer_input.astype(jnp.float32)
    normed, first_pull = jax.vjp(
        layer_norm, inputs, first_gain.astype(jnp.float32), first_bias.astype(jnp.float32)
    )
    normed = normed.astype(jnp.bfloat16)
    joined = jnp.einsum("srd,de->sre", normed, input_weight, preferred_element_type=jnp.float32)
    queries = (joined[..., :features] + query_bias.astype(jnp.float32)).astype(jnp.bfloat16)
    key_value = jnp.concatenate(
        [
            joined[..., features : 2 * features],
            joined[..., 2 * features :] + value_bias.astype(jnp.float32),
        ],
        axis=-1,
    ).astype(jnp.bfloat16)
    gathered = lax.all_gather(key_value, "ctx", axis=1, tiled=True)
    query_heads = queries.reshape(seq_count, row_count, head_count, head_size)

    def key_block(number):
        offset = number * size_k
        pieces = lax.dynamic_slice_in_dim(gathered, offset, size_k, 1)
        key_rows = pieces[..., :features].reshape(seq_count, size_k, head_count, head_size)
        value_rows = pieces[..., features:].reshape(seq_count, size_k, head_count, head_size)
        block_places = lax.dynamic_slice_in_dim(places, offset, size_k, 0)
        block_docs = lax.dynamic_slice_in_dim(key_docs, offset, size_k, 1)
        scores = masked_scores(
            query_heads, key_rows, own_places, block_places, own_docs, block_docs, inv_root
        )
        return (key_rows, value_rows, scores)

    def max_sum(number, running):
        scores = key_block(number)[2]
        highest = jnp.maximum(running[0], jnp.max(scores, axis=-1))
        totals = running[1] * jnp.exp(running[0] - highest) + jnp.sum(
            jnp.exp(scores - highest[..., None]), axis=-1
        )
        return (highest, totals)

    stats_shape = (seq_count, head_count, row_count)
    highest, totals = lax.fori_loop(
        0,
        blocks,
        max_sum,
        (jnp.full(stats_shape, MASKED, jnp.float32), jnp.zeros(stats_shape, jnp.float32)),
    )
    log_total = highest + jnp.log(totals)

    def mix_values(number, running):
        pieces = key_block(number)
        probs_low = jnp.exp(pieces[2] - log_total[..., None]).astype(jnp.bfloat16)
        return running + jnp.einsum(
            "shqk,skhd->sqhd", probs_low, pieces[1], preferred_element_type=jnp.float32
        )

    mixed_heads = lax.fori_loop(
        0, blocks, mix_values, jnp.zeros((seq_count, row_count, head_count, head_size), jnp.float32)
    )
    mixed_low = mixed_heads.reshape(seq_count, row_count, features).astype(jnp.bfloat16)
    residual = (
        inputs
        + jnp.einsum("sre,ed->srd", mixed_low, output_weight, preferred_element_type=jnp.float32)
        + output_bias.astype(jnp.float32)
    )
    normed_two, second_pull = jax.vjp(
        layer_norm, residual, second_gain.astype(jnp.float32), second_bias.astype(jnp.float32)
    )
    normed_two = normed_two.astype(jnp.bfloat16)
    hidden = jnp.einsum(
        "srd,df->srf", normed_two, expand_weight, preferred_element_type=jnp.float32
    ) + expand_bias.astype(jnp.float32)
    active, gelu_pull = jax.vjp(gelu_tanh, hidden)
    active = active.astype(jnp.bfloat16)
    layer_output = (
        residual
        + jnp.einsum("srf,fd->srd", active, shrink_weight, preferred_element_type=jnp.float32)
        + shrink_bias.astype(jnp.float32)
    ).astype(jnp.bfloat16)
    cotangent = output_grad.astype(jnp.float32)
    shrink_weight_grad = jnp.einsum(
        "srf,srd->fd", active, output_grad, preferred_element_type=jnp.float32
    )
    shrink_bias_grad = jnp.sum(cotangent, axis=(0, 1))
    hidden_grad = gelu_pull(
        jnp.einsum("srd,fd->srf", output_grad, shrink_weight, preferred_element_type=jnp.float32)
    )[0].astype(jnp.bfloat16)
    expand_weight_grad = jnp.einsum(
        "srd,srf->df", normed_two, hidden_grad, preferred_element_type=jnp.float32
    )
    expand_bias_grad = jnp.sum(hidden_grad.astype(jnp.float32), axis=(0, 1))
    second_grads = second_pull(
        jnp.einsum("srf,df->srd", hidden_grad, expand_weight, preferred_element_type=jnp.float32)
    )
    residual_grad = cotangent + second_grads[0]
    branch_grad = residual_grad.astype(jnp.bfloat16)
    output_weight_grad = jnp.einsum(
        "sre,srd->ed", mixed_low, branch_grad, preferred_element_type=jnp.float32
    )
    output_bias_grad = jnp.sum(branch_grad.astype(jnp.float32), axis=(0, 1))
    mixed_flat = jnp.einsum(
        "srd,ed->sre", branch_grad, output_weight, preferred_element_type=jnp.float32
    ).astype(jnp.bfloat16)
    mixed_grad = mixed_flat.reshape(seq_count, row_count, head_count, head_size)

    def prob_grads(pieces):
        probs = jnp.exp(pieces[2] - log_total[..., None])
        prob_grad = jnp.einsum(
            "sqhd,skhd->shqk", mixed_grad, pieces[1], preferred_element_type=jnp.float32
        )
        return (probs, prob_grad)

    def delta_sum(number, running):
        probs, prob_grad = prob_grads(key_block(number))
        return running + jnp.sum(probs * prob_grad, axis=-1)

    deltas = lax.fori_loop(0, blocks, delta_sum, jnp.zeros(stats_shape, jnp.float32))
    query_zero = jnp.zeros((seq_count, row_count, head_count, head_size), jnp.float32)

    def key_grads(number, running):
        pieces = key_block(number)
        probs, prob_grad = prob_grads(pieces)
        score_grad = (probs * (prob_grad - deltas[..., None])).astype(jnp.bfloat16)
        query_grad = (
            running[0]
            + jnp.einsum(
                "shqk,skhd->sqhd", score_grad, pieces[0], preferred_element_type=jnp.float32
            )
            * inv_root
        )
        key_grad = (
            jnp.einsum(
                "shqk,sqhd->skhd", score_grad, query_heads, preferred_element_type=jnp.float32
            )
            * inv_root
        )
        value_grad = jnp.einsum(
            "shqk,sqhd->skhd",
            probs.astype(jnp.bfloat16),
            mixed_grad,
            preferred_element_type=jnp.float32,
        )
        joined_grad = jnp.concatenate(
            [
                key_grad.reshape(seq_count, size_k, features),
                value_grad.reshape(seq_count, size_k, features),
            ],
            axis=-1,
        )
        buffer = lax.dynamic_update_slice_in_dim(running[1], joined_grad, number * size_k, 1)
        return (query_grad, buffer)

    query_grad, buffer = lax.fori_loop(
        0,
        blocks,
        key_grads,
        (query_zero, jnp.zeros((seq_count, length, 2 * features), jnp.float32)),
    )
    key_value_grad = lax.psum_scatter(buffer, "ctx", scatter_dimension=1, tiled=True).astype(
        jnp.bfloat16
    )
    query_low = query_grad.reshape(seq_count, row_count, features).astype(jnp.bfloat16)
    joined_low = jnp.concatenate([query_low, key_value_grad], axis=-1)
    input_weight_grad = jnp.einsum(
        "srd,sre->de", normed, joined_low, preferred_element_type=jnp.float32
    )
    query_bias_grad = jnp.sum(query_low.astype(jnp.float32), axis=(0, 1))
    value_bias_grad = jnp.sum(key_value_grad[..., features:].astype(jnp.float32), axis=(0, 1))
    first_grads = first_pull(
        jnp.einsum("sre,de->srd", joined_low, input_weight, preferred_element_type=jnp.float32)
    )
    input_grad = residual_grad + first_grads[0]
    grads = (
        first_grads[1],
        first_grads[2],
        input_weight_grad,
        query_bias_grad,
        value_bias_grad,
        output_weight_grad,
        output_bias_grad,
        second_grads[1],
        second_grads[2],
        expand_weight_grad,
        expand_bias_grad,
        shrink_weight_grad,
        shrink_bias_grad,
    )
    return (layer_output, input_grad, grads)


def body(
    layer_input,
    output_grad,
    segments,
    assignment,
    first_gain,
    first_bias,
    input_weight,
    query_bias,
    value_bias,
    output_weight,
    output_bias,
    second_gain,
    second_bias,
    expand_weight,
    expand_bias,
    shrink_weight,
    shrink_bias,
):
    row_count = layer_input.shape[1]
    length = row_count * lax.axis_size("ctx")
    places = key_places(assignment, row_count, length)
    own_places = lax.dynamic_slice_in_dim(places, lax.axis_index("ctx") * row_count, row_count, 0)
    batch_seqs = layer_input.shape[0] // MICRO
    outputs = []
    input_grads = []
    summed = None
    for micro_turn in range(MICRO):
        weights = (
            lax.all_gather(first_gain, "fsdp", axis=0, tiled=True),
            lax.all_gather(first_bias, "fsdp", axis=0, tiled=True),
            lax.all_gather(input_weight, "fsdp", axis=0, tiled=True),
            lax.all_gather(query_bias, "fsdp", axis=0, tiled=True),
            lax.all_gather(value_bias, "fsdp", axis=0, tiled=True),
            lax.all_gather(output_weight, "fsdp", axis=1, tiled=True),
            lax.all_gather(output_bias, "fsdp", axis=0, tiled=True),
            lax.all_gather(second_gain, "fsdp", axis=0, tiled=True),
            lax.all_gather(second_bias, "fsdp", axis=0, tiled=True),
            lax.all_gather(expand_weight, "fsdp", axis=0, tiled=True),
            lax.all_gather(expand_bias, "fsdp", axis=0, tiled=True),
            lax.all_gather(shrink_weight, "fsdp", axis=1, tiled=True),
            lax.all_gather(shrink_bias, "fsdp", axis=0, tiled=True),
        )
        lower = micro_turn * batch_seqs
        upper = lower + batch_seqs
        result = one_batch(
            weights,
            layer_input[lower:upper],
            output_grad[lower:upper],
            segments[lower:upper],
            places,
            own_places,
        )
        outputs.append(result[0])
        input_grads.append(result[1])
        batch_grads = result[2]
        summed = (
            batch_grads
            if summed is None
            else tuple((first + second for first, second in zip(summed, batch_grads)))
        )
    summed = lax.psum(
        (
            lax.psum_scatter(summed[0], "fsdp", scatter_dimension=0, tiled=True),
            lax.psum_scatter(summed[1], "fsdp", scatter_dimension=0, tiled=True),
            lax.psum_scatter(summed[2], "fsdp", scatter_dimension=0, tiled=True),
            lax.psum_scatter(summed[3], "fsdp", scatter_dimension=0, tiled=True),
            lax.psum_scatter(summed[4], "fsdp", scatter_dimension=0, tiled=True),
            lax.psum_scatter(summed[5], "fsdp", scatter_dimension=1, tiled=True),
            lax.psum_scatter(summed[6], "fsdp", scatter_dimension=0, tiled=True),
            lax.psum_scatter(summed[7], "fsdp", scatter_dimension=0, tiled=True),
            lax.psum_scatter(summed[8], "fsdp", scatter_dimension=0, tiled=True),
            lax.psum_scatter(summed[9], "fsdp", scatter_dimension=0, tiled=True),
            lax.psum_scatter(summed[10], "fsdp", scatter_dimension=0, tiled=True),
            lax.psum_scatter(summed[11], "fsdp", scatter_dimension=1, tiled=True),
            lax.psum_scatter(summed[12], "fsdp", scatter_dimension=0, tiled=True),
        ),
        "ctx",
    )
    return (
        jnp.concatenate(outputs, axis=0),
        jnp.concatenate(input_grads, axis=0),
        summed[0],
        summed[1],
        summed[2],
        summed[3],
        summed[4],
        summed[5],
        summed[6],
        summed[7],
        summed[8],
        summed[9],
        summed[10],
        summed[11],
        summed[12],
    )


def solution(mesh):
    return jax.shard_map(
        body,
        mesh=mesh,
        in_specs=(
            P("fsdp", "ctx", None),
            P("fsdp", "ctx", None),
            P("fsdp", None),
            P(),
            P("fsdp"),
            P("fsdp"),
            P("fsdp", None),
            P("fsdp"),
            P("fsdp"),
            P(None, "fsdp"),
            P("fsdp"),
            P("fsdp"),
            P("fsdp"),
            P("fsdp", None),
            P("fsdp"),
            P(None, "fsdp"),
            P("fsdp"),
        ),
        out_specs=(
            P("fsdp", "ctx", None),
            P("fsdp", "ctx", None),
            P("fsdp"),
            P("fsdp"),
            P("fsdp", None),
            P("fsdp"),
            P("fsdp"),
            P(None, "fsdp"),
            P("fsdp"),
            P("fsdp"),
            P("fsdp"),
            P("fsdp", None),
            P("fsdp"),
            P(None, "fsdp"),
            P("fsdp"),
        ),
        check_vma=False,
    )
```

profile of v0, /device:TPU:0, one launch (start us, length us, event | category | flops | bytes accessed | tf_op | source)
XLA Modules:
  0.0 2027.4 jit_solution(2020608010366841230)
XLA Ops:
  8.0 5.3 all-gather.1
  27.5 65.3 %all-gather.15.cloned.1.call-done = bf16[1024,3072]{1,0:T(8,128)(2,1)} async-done(((bf16[512,3072]{1,0:T(8,128)(2,1)}), bf16[1024,3072]{1,0:T(8,128)(2,1)}) %all-gather.15.cloned.1.call-update) | async-done | bytes 6291472 | tf_op jit(solution)/shard_map/all_gather | solution.py:293
  123.6 4.5 all-gather.5
  130.7 44.0 %all-gather.25.cloned.1.call-done = bf16[2,1024,2048]{2,1,0:T(8,128)(2,1)} async-done(((bf16[2,64,2048]{2,1,0:T(8,128)(2,1)}), bf16[2,1024,2048]{2,1,0:T(8,128)(2,1)}) %all-gather.25.cloned.1.call-update) | async-done | bytes 8388624 | tf_op jit(solution)/shard_map/all_gather | solution.py:89
  174.7 12.0 copy.147
  186.6 16.3 while.122
  203.0 17.4 while.123
  215.8 4.5 fusion.337
  222.5 28.2 %all-gather.17.cloned.1.call-done = bf16[2,1024,2048]{2,1,0:T(8,128)(2,1)} async-done(((bf16[2,64,2048]{2,1,0:T(8,128)(2,1)}), bf16[2,1024,2048]{2,1,0:T(8,128)(2,1)}) %all-gather.17.cloned.1.call-update) | async-done | bytes 8388624 | tf_op jit(solution)/shard_map/all_gather | solution.py:89
  250.6 12.0 copy.137
  262.6 16.2 while.120
  278.9 18.0 while.121
  291.7 5.0 fusion.329
  303.5 85.4 %all-gather.21.cloned.1.call-done = bf16[1024,4096]{1,0:T(8,128)(2,1)} async-done(((bf16[512,4096]{1,0:T(8,128)(2,1)}), bf16[1024,4096]{1,0:T(8,128)(2,1)}) %all-gather.21.cloned.1.call-update) | async-done | bytes 8388624 | tf_op jit(solution)/shard_map/all_gather | solution.py:300
  388.9 6.3 fusion.81
  397.9 96.4 %all-gather.23.cloned.1.call-done = bf16[4096,1024]{1,0:T(8,128)(2,1)} async-done(((bf16[4096,512]{1,0:T(8,128)(2,1)}), bf16[4096,1024]{1,0:T(8,128)(2,1)}) %all-gather.23.cloned.1.call-update) | async-done | bytes 8388624 | tf_op jit(solution)/shard_map/all_gather | solution.py:302
  494.3 8.5 convert_reduce_fusion
  503.7 6.4 fusion.62
  510.2 4.4 convert_reduce_fusion.1
  523.0 10.5 while.126
  533.5 7.9 broadcast.727.clone2
  541.4 66.1 %while.127 = (s32[]{:T(128)}, f32[2,64,16,64]{1,3,2,0:T(8,128)}, f32[2,1024,2048]{2,1,0:T(8,128)}, bf16[2,1024,2048]{1,2,0:T(8,128)(2,1)}, s32[1024]{0:T(1024)S(...) while((s32[]{:T(128)}, f32[2,64,16,64]{1,3,2,0:T(8,128)}, ...), condition=%wide.region_37.40_spmd.clone, body=%wide.region_36.39_spmd.clone.sunk | while | flops 685277184 | bytes 136621136 | solution.py:224
  557.9 8.8 copy.231
  566.6 7.8 constant_dynamic-update-slice_fusion.5
  591.0 8.8 copy.231
  599.7 7.7 constant_dynamic-update-slice_fusion.5
  612.5 11.6 while.124
  624.1 10.6 broadcast.727.clone2.1
  634.7 66.7 %while.125 = (s32[]{:T(128)}, f32[2,64,16,64]{1,3,2,0:T(8,128)}, f32[2,1024,2048]{2,1,0:T(8,128)}, bf16[2,1024,2048]{1,2,0:T(8,128)(2,1)}, s32[1024]{0:T(1024)S(...) while((s32[]{:T(128)}, f32[2,64,16,64]{1,3,2,0:T(8,128)}, ...), condition=%wide.region_27.30_spmd.clone, body=%wide.region_26.29_spmd.clone.sunk | while | flops 685277184 | bytes 136621136 | solution.py:224
  651.4 8.9 copy.230
  660.2 7.8 constant_dynamic-update-slice_fusion.4
  684.9 8.8 copy.230
  693.7 7.8 constant_dynamic-update-slice_fusion.4
  710.0 8.3 bitcast_add_fusion.1
  723.4 9.8 bitcast_add_fusion
  737.1 49.1 %reduce-scatter.9.cloned.1.call-done = f32[2,64,2048]{2,1,0:T(8,128)} async-done(((f32[2,1024,2048]{2,1,0:T(8,128)}), f32[2,64,2048]{2,1,0:T(8,128)}) %reduce-scatter.9.cloned.1.call-update) | async-done | bytes 1048592 | tf_op jit(solution)/shard_map/reduce_scatter | solution.py:230
  787.5 180.4 %reduce-scatter.7.cloned.1.call-done = f32[2,64,2048]{2,1,0:T(8,128)} async-done(((f32[2,1024,2048]{2,1,0:T(8,128)}), f32[2,64,2048]{2,1,0:T(8,128)}) %reduce-scatter.7.cloned.1.call-update) | async-done | bytes 1048592 | tf_op jit(solution)/shard_map/reduce_scatter | solution.py:230
  971.2 6.8 bitcast_add_fusion.2
  978.1 46.0 %reduce-scatter.13.cloned.1.call-done = f32[1024,512]{1,0:T(8,128)} async-done(((f32[1024,1024]{1,0:T(8,128)}), f32[1024,512]{1,0:T(8,128)}) %reduce-scatter.13.cloned.1.call-update) | async-done | bytes 2097168 | tf_op jit(solution)/shard_map/reduce_scatter | solution.py:330
  1024.1 191.4 %reduce-scatter.15.cloned.1.call-done = f32[512,4096]{1,0:T(8,128)} async-done(((f32[1024,4096]{1,0:T(8,128)}), f32[512,4096]{1,0:T(8,128)}) %reduce-scatter.15.cloned.1.call-update) | async-done | bytes 8388624 | tf_op jit(solution)/shard_map/reduce_scatter | solution.py:334
  1215.5 191.5 %reduce-scatter.17.cloned.1.call-done = f32[4096,512]{1,0:T(8,128)} async-done(((f32[4096,1024]{1,0:T(8,128)}), f32[4096,512]{1,0:T(8,128)}) %reduce-scatter.17.cloned.1.call-update) | async-done | bytes 8388624 | tf_op jit(solution)/shard_map/reduce_scatter | solution.py:336
  1407.0 146.8 %reduce-scatter.11.cloned.1.call-done = f32[512,3072]{1,0:T(8,128)} async-done(((f32[1024,3072]{1,0:T(8,128)}), f32[512,3072]{1,0:T(8,128)}) %reduce-scatter.11.cloned.1.call-update) | async-done | bytes 6291472 | tf_op jit(solution)/shard_map/reduce_scatter | solution.py:327
  1560.9 5.9 fusion.134
  1566.8 5.1 fusion.137
  1579.1 7.4 all-reduce.11
  1587.2 63.6 %all-reduce.9 = (f32[512]{0:T(512)}, f32[512]{0:T(512)}, f32[512]{0:T(512)}, f32[512]{0:T(512)}, f32[512]{0:T(512)}, /*index=5*/f32[512]{0:T(512)}, f32[512]{0:T(512)}, f32[2048]{0:T(1024)}, f32[512]{0:T(512)}) all-reduce(f32[512]{0:T(512)S(1)} %dynamic-slice.1, ...), channel_id=1, replica_groups=mesh['fsdp'=2,'ctx'=16] {'ctx'}, use_global_device_ids=true, to_apply=%region_44.47 | all-reduce | flops 6144 | bytes 49152 | tf_op jit(solution)/shard_map/psum | solution.py:323
  1652.4 350.5 %all-reduce.14.cloned.1.call-done = (f32[512,3072]{1,0:T(8,128)}, f32[1024,512]{1,0:T(8,128)}, f32[512,4096]{1,0:T(8,128)}, f32[4096,512]{1,0:T(8,128)}) async-done(((f32[512,3072]{1,0:T(8,128)}, f32[1024,512]{1,0:T(8,128)}, f32[512,4096]{1,0:T(8,128)}, f32[4096,512]{1,0:T(8,128)}), (f32[512,3072]{1,0:T(8,128)}, f32[1024,512]{1,0:T(8,128)}, f32[512,4096]{1,0:T(8,128)}, ...) | async-done | bytes 25165840 | tf_op jit(solution)/shard_map/psum | solution.py:323
  2002.9 6.9 copy.298
  (558 shorter events, 266.3 us)
Async XLA Ops:
  7.2 14.8 copy-start.102
  7.2 19.2 copy-start.14
  7.2 85.5 %all-gather.15.cloned.1.call-start = ((), (), s32[]{:S(2)}) async-start(), calls=%async_computation.6 | async-start | bytes 9437184 | tf_op jit(solution)/shard_map/all_gather | solution.py:293
  8.0 166.7 %all-gather.25.cloned.1.call-start = ((), (), s32[]{:S(2)}) async-start(), calls=%async_computation.11 | async-start | bytes 8912896 | tf_op jit(solution)/shard_map/all_gather | solution.py:89
  13.3 83.5 %copy-start.53 = (f32[2,1,512]{2,1,0:T(1,128)}, f32[2,1,512]{2,1,0:T(1,128)S(1)}, u32[]{:S(2)}) copy-start(f32[2,1,512]{2,1,0:T(1,128)S(1)} %convert_element_type.246) | copy-start | bytes 12292
  17.7 79.2 %copy-start.48 = (f32[2,1,512]{2,1,0:T(1,128)}, f32[2,1,512]{2,1,0:T(1,128)S(1)}, u32[]{:S(2)}) copy-start(f32[2,1,512]{2,1,0:T(1,128)S(1)} %convert_element_type.245) | copy-start | bytes 12292
  26.6 70.2 %copy-start.67 = (f32[2,64]{1,0:T(2,128)}, f32[2,64]{1,0:T(2,128)S(1)}, u32[]{:S(2)}) copy-start(f32[2,64]{1,0:T(2,128)S(1)} %get-tuple-element.2158) | copy-start | bytes 1540
  26.6 70.3 %copy-start.69 = (f32[2,64]{1,0:T(2,128)}, f32[2,64]{1,0:T(2,128)S(1)}, u32[]{:S(2)}) copy-start(f32[2,64]{1,0:T(2,128)S(1)} %get-tuple-element.2159) | copy-start | bytes 1540
  26.9 69.9 %copy-start.96 = (f32[2,64]{1,0:T(2,128)}, f32[2,64]{1,0:T(2,128)S(1)}, u32[]{:S(2)}) copy-start(f32[2,64]{1,0:T(2,128)S(1)} %get-tuple-element.1907) | copy-start | bytes 1540
  27.5 69.3 %copy-start.73 = (f32[2,64]{1,0:T(2,128)}, f32[2,64]{1,0:T(2,128)S(1)}, u32[]{:S(2)}) copy-start(f32[2,64]{1,0:T(2,128)S(1)} %fusion.198) | copy-start | bytes 1540
  27.5 69.4 %copy-start.75 = (f32[2,64]{1,0:T(2,128)}, f32[2,64]{1,0:T(2,128)S(1)}, u32[]{:S(2)}) copy-start(f32[2,64]{1,0:T(2,128)S(1)} %fusion.196) | copy-start | bytes 1540
  99.6 151.1 %all-gather.17.cloned.1.call-start = ((), (), s32[]{:S(2)}) async-start(), calls=%async_computation.7 | async-start | bytes 8912896 | tf_op jit(solution)/shard_map/all_gather | solution.py:89
  100.5 198.9 %all-gather.19.cloned.1.call-start = ((), (), s32[]{:S(2)}) async-start(), calls=%async_computation.8 | async-start | bytes 3145728 | tf_op jit(solution)/shard_map/all_gather | solution.py:296
  101.1 287.8 %all-gather.21.cloned.1.call-start = ((), (), s32[]{:S(2)}) async-start(), calls=%async_computation.9 | async-start | bytes 12582912 | tf_op jit(solution)/shard_map/all_gather | solution.py:300
  101.7 392.6 %all-gather.23.cloned.1.call-start = ((), (), s32[]{:S(2)}) async-start(), calls=%async_computation.10 | async-start | bytes 12582912 | tf_op jit(solution)/shard_map/all_gather | solution.py:302
  102.3 12.6 copy-start.98
  102.3 683.9 %reduce-scatter.9.cloned.1.call-start = ((), (), s32[]{:S(2)}) async-start(), calls=%async_computation.13 | async-start | bytes 17825792 | tf_op jit(solution)/shard_map/reduce_scatter | solution.py:230
  102.5 16.8 copy-start.104
  102.5 21.1 %copy-start.105 = (bf16[512]{0:T(512)(128)(2,1)S(1)}, bf16[512]{0:T(512)(128)(2,1)}, u32[]{:S(2)}) copy-start(bf16[512]{0:T(512)(128)(2,1)} %param.48) | copy-start | bytes 3076
  123.6 271.6 %copy-start.55 = (f32[2,1,512]{2,1,0:T(1,128)}, f32[2,1,512]{2,1,0:T(1,128)S(1)}, u32[]{:S(2)}) copy-start(f32[2,1,512]{2,1,0:T(1,128)S(1)} %convert_element_type.251) | copy-start | bytes 12292
  128.2 390.1 %copy-start.50 = (f32[2,1,512]{2,1,0:T(1,128)}, f32[2,1,512]{2,1,0:T(1,128)S(1)}, u32[]{:S(2)}) copy-start(f32[2,1,512]{2,1,0:T(1,128)S(1)} %convert_element_type.250) | copy-start | bytes 12292
  130.5 56.1 %copy-start.39 = (bf16[2,64,16,64]{3,2,1,0:T(8,128)(2,1)}, bf16[2,64,16,64]{3,2,1,0:T(8,128)(2,1)S(1)}, u32[]{:S(2)}) copy-start(bf16[2,64,16,64]{3,2,1,0:T(8,128)(2,1)S(1)} %reshape.630) | copy-start | bytes 786436
  302.2 216.1 %copy-start.63 = (f32[2,64]{1,0:T(2,128)}, f32[2,64]{1,0:T(2,128)S(1)}, u32[]{:S(2)}) copy-start(f32[2,64]{1,0:T(2,128)S(1)} %broadcast_multiply_fusion) | copy-start | bytes 1540
  303.2 215.1 %copy-start.20 = (f32[2,64,1024]{2,1,0:T(8,128)}, f32[2,64,1024]{2,1,0:T(8,128)S(1)}, u32[]{:S(2)}) copy-start(f32[2,64,1024]{2,1,0:T(8,128)S(1)} %get-tuple-element.2151) | copy-start | bytes 1572868
  303.2 215.1 %copy-start.65 = (f32[2,64]{1,0:T(2,128)}, f32[2,64]{1,0:T(2,128)S(1)}, u32[]{:S(2)}) copy-start(f32[2,64]{1,0:T(2,128)S(1)} %broadcast_multiply_fusion.2) | copy-start | bytes 1540
  303.5 214.8 %copy-start.71 = (f32[2,64]{1,0:T(2,128)}, f32[2,64]{1,0:T(2,128)S(1)}, u32[]{:S(2)}) copy-start(f32[2,64]{1,0:T(2,128)S(1)} %fusion.199) | copy-start | bytes 1540
  303.5 214.8 %copy-start.77 = (f32[2,64]{1,0:T(2,128)}, f32[2,64]{1,0:T(2,128)S(1)}, u32[]{:S(2)}) copy-start(f32[2,64]{1,0:T(2,128)S(1)} %fusion.197) | copy-start | bytes 1540
  494.3 15.8 copy-start.108
  503.7 10.9 slice-start
  607.5 360.4 %reduce-scatter.7.cloned.1.call-start = ((), (), s32[]{:S(2)}) async-start(), calls=%async_computation.12 | async-start | bytes 17825792 | tf_op jit(solution)/shard_map/reduce_scatter | solution.py:230
  701.5 322.6 %reduce-scatter.13.cloned.1.call-start = ((), (), s32[]{:S(2)}) async-start(), calls=%async_computation.15 | async-start | bytes 6291456 | tf_op jit(solution)/shard_map/reduce_scatter | solution.py:330
  706.2 509.3 %reduce-scatter.15.cloned.1.call-start = ((), (), s32[]{:S(2)}) async-start(), calls=%async_computation.16 | async-start | bytes 25165824 | tf_op jit(solution)/shard_map/reduce_scatter | solution.py:334
  718.4 688.6 %reduce-scatter.17.cloned.1.call-start = ((), (), s32[]{:S(2)}) async-start(), calls=%async_computation.17 | async-start | bytes 25165824 | tf_op jit(solution)/shard_map/reduce_scatter | solution.py:336
  733.3 820.5 %reduce-scatter.11.cloned.1.call-start = ((), (), s32[]{:S(2)}) async-start(), calls=%async_computation.14 | async-start | bytes 18874368 | tf_op jit(solution)/shard_map/reduce_scatter | solution.py:327
  736.8 232.4 %copy-start.16 = (bf16[4,64,1024]{2,1,0:T(8,128)(2,1)S(1)}, bf16[4,64,1024]{2,1,0:T(8,128)(2,1)}, u32[]{:S(2)}) copy-start(bf16[4,64,1024]{2,1,0:T(8,128)(2,1)} %param.37) | copy-start | bytes 1572868
  736.8 232.4 %copy-start.49 = (f32[2,1,512]{2,1,0:T(1,128)S(1)}, f32[2,1,512]{2,1,0:T(1,128)}, u32[]{:S(2)}) copy-start(f32[2,1,512]{2,1,0:T(1,128)} %copy-done.48) | copy-start | bytes 12292
  736.8 232.4 %copy-start.54 = (f32[2,1,512]{2,1,0:T(1,128)S(1)}, f32[2,1,512]{2,1,0:T(1,128)}, u32[]{:S(2)}) copy-start(f32[2,1,512]{2,1,0:T(1,128)} %copy-done.53) | copy-start | bytes 12292
  736.8 232.4 %copy-start.70 = (f32[2,64]{1,0:T(2,128)S(1)}, f32[2,64]{1,0:T(2,128)}, u32[]{:S(2)}) copy-start(f32[2,64]{1,0:T(2,128)} %copy-done.69) | copy-start | bytes 1540
  736.9 232.4 %copy-start.76 = (f32[2,64]{1,0:T(2,128)S(1)}, f32[2,64]{1,0:T(2,128)}, u32[]{:S(2)}) copy-start(f32[2,64]{1,0:T(2,128)} %copy-done.75) | copy-start | bytes 1540
  787.5 785.4 %copy-start.41 = (bf16[2,64,2048]{2,1,0:T(8,128)(2,1)}, bf16[2,64,2048]{2,1,0:T(8,128)(2,1)S(1)}, u32[]{:S(2)}) copy-start(bf16[2,64,2048]{2,1,0:T(8,128)(2,1)S(1)} %convert_element_type.236) | copy-start | bytes 1572868
  969.2 605.8 %copy-start.43 = (bf16[2,64,2048]{2,1,0:T(8,128)(2,1)}, bf16[2,64,2048]{2,1,0:T(8,128)(2,1)S(1)}, u32[]{:S(2)}) copy-start(bf16[2,64,2048]{2,1,0:T(8,128)(2,1)S(1)} %convert_element_type.229) | copy-start | bytes 1572868
  978.0 1024.9 %all-reduce.14.cloned.1.call-start = ((), (), s32[]{:S(2)}) async-start(), calls=%async_computation.18 | async-start | bytes 50331648 | tf_op jit(solution)/shard_map/psum | solution.py:323
  1560.9 11.9 slice-start.2
  1577.4 73.4 %copy-start.31 = (bf16[4,64,1024]{2,1,0:T(8,128)(2,1)S(1)}, bf16[4,64,1024]{2,1,0:T(8,128)(2,1)}, u32[]{:S(2)}) copy-start(bf16[4,64,1024]{2,1,0:T(8,128)(2,1)} %param.38) | copy-start | bytes 1572868
  1577.4 73.4 %copy-start.36 = (f32[2,64,1024]{2,1,0:T(8,128)S(1)}, f32[2,64,1024]{2,1,0:T(8,128)}, u32[]{:S(2)}) copy-start(f32[2,64,1024]{2,1,0:T(8,128)} %copy-done.35) | copy-start | bytes 1572868
  1577.4 73.4 %copy-start.38 = (f32[2,64,1024]{2,1,0:T(8,128)S(1)}, f32[2,64,1024]{2,1,0:T(8,128)}, u32[]{:S(2)}) copy-start(f32[2,64,1024]{2,1,0:T(8,128)} %copy-done.37) | copy-start | bytes 1572868
  1577.4 73.4 %copy-start.91 = (f32[2,64]{1,0:T(2,128)S(1)}, f32[2,64]{1,0:T(2,128)}, u32[]{:S(2)}) copy-start(f32[2,64]{1,0:T(2,128)} %copy-done.90) | copy-start | bytes 1540
  1577.4 73.4 %copy-start.93 = (f32[2,64]{1,0:T(2,128)S(1)}, f32[2,64]{1,0:T(2,128)}, u32[]{:S(2)}) copy-start(f32[2,64]{1,0:T(2,128)} %copy-done.92) | copy-start | bytes 1540
  (87 other events, 326.7 us)
Sparse Core Ops, SparseCore 0:
  9.6 83.0 all-gather.14
  99.7 74.9 all-gather.24
  177.4 73.1 all-gather.16
  252.0 31.3 all-gather.18
  284.8 103.9 all-gather.20
  390.2 103.9 all-gather.22
  607.6 178.5 reduce-scatter.8
  790.3 177.5 reduce-scatter.6
  970.7 53.2 reduce-scatter.12
  1026.3 189.1 reduce-scatter.14
  1217.8 189.1 reduce-scatter.16
  1409.2 144.4 reduce-scatter.10
  1559.4 443.4 all-reduce.13
where the time goes:
time: 2030 us
  waiting for transfers between devices  1480 us (73%)
  local copies, waits for them, and re-layouts  198 us (10%)
  matrix products  171 us (8%)
  blocking collectives  111 us (5%)
  other arithmetic  51.2 us (3%)
    psum x1, waiting for transfers between devices, body(): lax.psum((lax.psum_scatter(summed[0], 'fsdp', scatter_dimension=0, tiled=...  351 us
    reduce_scatter x2, waiting for transfers between devices, one_batch(): lax.psum_scatter(buffer, 'ctx', scatter_dimension=1, tiled=True)  229 us
    reduce_scatter x1, waiting for transfers between devices, body(): lax.psum_scatter(summed[11], 'fsdp', scatter_dimension=1, tiled=True)  191 us
    reduce_scatter x1, waiting for transfers between devices, body(): lax.psum_scatter(summed[9], 'fsdp', scatter_dimension=0, tiled=True)  191 us
    reduce_scatter x1, waiting for transfers between devices, body(): lax.psum_scatter(summed[2], 'fsdp', scatter_dimension=0, tiled=True)  147 us
    all_gather x1, waiting for transfers between devices, body(): lax.all_gather(shrink_weight, 'fsdp', axis=1, tiled=True)  96.4 us
    all_gather x1, waiting for transfers between devices, body(): lax.all_gather(expand_weight, 'fsdp', axis=0, tiled=True)  85.4 us
    all_gather x2, waiting for transfers between devices, one_batch(): gathered = lax.all_gather(key_value, 'ctx', axis=1, tiled=True)  72.1 us
  transfers between devices with their start and end apart: 13, of which 12 were waited for; matrix products, arithmetic and copies ran while one was open for 14% of the time, Pallas kernels for 0%

commit v1 on v0

v1 whole, which is shorter than its diff:
```python
import functools
import math

import jax
import jax.numpy as jnp
from jax import lax
from jax.experimental import pallas as pl
from jax.experimental.pallas import tpu as pltpu
from jax.sharding import PartitionSpec as P

HEADS = 16
EPSILON = 1e-05
MASKED = -1000000000.0
LANES = 128
MIB = 1024 * 1024
F32 = jnp.float32
BF16 = jnp.bfloat16

V_G1, V_B1, V_BQ, V_BV, V_BO, V_G2, V_B2, V_BS = range(8)


def bits_of(number):
    return number.bit_length() - 1


def dot(left, right):
    return jnp.dot(left, right, preferred_element_type=F32)


def dot_nt(left, right):
    return lax.dot_general(left, right, (((1,), (1,)), ((), ())), preferred_element_type=F32)


def dot_tn(left, right):
    return lax.dot_general(left, right, (((0,), (0,)), ((), ())), preferred_element_type=F32)


def swap_bit(value, axis, size, bit):
    return lax.ppermute(value, axis, [(i, i ^ (1 << bit)) for i in range(size)])


def reverse_bits(value, count):
    out = jnp.zeros_like(value)
    for bit in range(count):
        out = out | (((value >> bit) & 1) << (count - 1 - bit))
    return out


def params(limit_mib=48):
    return pltpu.CompilerParams(vmem_limit_bytes=limit_mib * MIB)


def whole(shape):
    rank = len(shape)
    return pl.BlockSpec(tuple(shape), lambda *_: (0,) * rank)


def cost(flops, moved):
    return pl.CostEstimate(flops=int(flops), bytes_accessed=int(moved), transcendentals=0)


def gather_parts(weight, dim, fsdp_size, ctx_size, y_index, c_index, bits):
    extent = weight.shape[dim]
    if fsdp_size != 2:
        full = lax.all_gather(weight, "fsdp", axis=dim, tiled=True)
        return [(full, jnp.int32(0))]
    pieces = 1 << len(bits)
    size = extent // pieces
    mine = jnp.int32(0)
    for place, bit in enumerate(bits):
        mine = mine | (((c_index >> bit) & 1) << place)
    first = lax.dynamic_slice_in_dim(weight, mine * size, size, dim)
    held = [(swap_bit(first, "fsdp", 2, 0), mine)]
    for place, bit in enumerate(bits):
        held = held + [
            (swap_bit(array, "ctx", ctx_size, bit), number ^ (1 << place)) for array, number in held
        ]
    base = (1 - y_index) * extent
    parts = [(weight, y_index * extent)]
    return parts + [(array, base + number * size) for array, number in held]


def split_parts(parts):
    arrays = [part[0] for part in parts]
    offsets = jnp.stack([part[1] for part in parts]).astype(jnp.int32)
    return arrays, offsets


def place_rows(target, offsets, part_refs):
    for number, ref in enumerate(part_refs):
        rows = ref.shape[0]
        target[pl.ds(pl.multiple_of(offsets[number], 32), rows), :] = ref[...]


def place_columns(target, offsets, part_refs):
    for number, ref in enumerate(part_refs):
        columns = ref.shape[1]
        target[:, pl.ds(pl.multiple_of(offsets[number], LANES), columns)] = ref[...]


def norm_stats(values):
    center = values - jnp.mean(values, axis=-1, keepdims=True)
    spread = jnp.mean(center * center, axis=-1, keepdims=True)
    rate = lax.rsqrt(spread + EPSILON)
    return center * rate, rate


def norm_kernel(x_ref, v_ref, h_ref):
    hat, _ = norm_stats(x_ref[...].astype(F32))
    h_ref[...] = (hat * v_ref[V_G1 : V_G1 + 1, :] + v_ref[V_B1 : V_B1 + 1, :]).astype(BF16)


def first_norm(x, vectors):
    return pl.pallas_call(
        norm_kernel,
        out_shape=jax.ShapeDtypeStruct(x.shape, BF16),
        compiler_params=params(),
        name="first_norm",
    )(x, vectors)


def qkv_kernel(part_count, seqs, rows, off_ref, h_ref, v_ref, *refs):
    parts = refs[: 3 * part_count]
    out_ref, weight = refs[3 * part_count :]
    group = pl.program_id(0)
    width = weight.shape[-1]
    per = width // LANES
    for kind in range(3):
        place_rows(
            weight.at[kind], off_ref, parts[kind * part_count : (kind + 1) * part_count]
        )
        value = dot(h_ref[...], weight[kind])
        if kind != 1:
            row = V_BQ if kind == 0 else V_BV
            start = pl.multiple_of(group * width, LANES)
            value = value + v_ref[row : row + 1, pl.ds(start, width)]
        value = value.astype(BF16)
        for pair in range(per):
            out_ref[pair, :, :, kind * LANES : (kind + 1) * LANES] = value[
                :, pair * LANES : (pair + 1) * LANES
            ].reshape(seqs, rows, LANES)


def project(h1, vectors, parts, seqs, rows):
    arrays, offsets = split_parts(parts)
    tokens, features = h1.shape
    width = 2 * LANES
    groups = features // width
    pairs = features // LANES
    specs = []
    operands = []
    for kind in range(3):
        for array in arrays:
            specs.append(
                pl.BlockSpec((array.shape[0], width), lambda g, o, k=kind: (0, k * groups + g))
            )
            operands.append(array)
    return pl.pallas_call(
        functools.partial(qkv_kernel, len(arrays), seqs, rows),
        grid_spec=pltpu.PrefetchScalarGridSpec(
            num_scalar_prefetch=1,
            grid=(groups,),
            in_specs=[whole(h1.shape), whole(vectors.shape)] + specs,
            out_specs=pl.BlockSpec((2, seqs, rows, 3 * LANES), lambda g, o: (g, 0, 0, 0)),
            scratch_shapes=[pltpu.VMEM((3, features, width), BF16)],
        ),
        out_shape=jax.ShapeDtypeStruct((pairs, seqs, rows, 3 * LANES), BF16),
        compiler_params=params(),
        cost_estimate=cost(6 * tokens * features * features, 6 * features * features),
        name="project",
    )(offsets, h1, vectors, *operands)


def to_places(table, ctx_size, half, source, target):
    for device in range(ctx_size):
        pair = table[device]
        early = pl.multiple_of(pair * half, half)
        later = pl.multiple_of((2 * ctx_size - 1 - pair) * half, half)
        target[pl.ds(early, half), :] = source[device, 0, 0:half, :]
        target[pl.ds(later, half), :] = source[device, 0, half : 2 * half, :]


def both_heads(block):
    first = lax.broadcasted_iota(jnp.int32, block.shape, 0) < LANES // 2
    zero = jnp.zeros_like(block)
    return jnp.concatenate([jnp.where(first, block, zero), jnp.where(first, zero, block)], axis=1)


def stacked_heads(block):
    first = lax.broadcasted_iota(jnp.int32, block.shape, 1) < LANES // 2
    zero = jnp.zeros_like(block)
    return jnp.concatenate([jnp.where(first, block, zero), jnp.where(first, zero, block)], axis=0)


def flipped(block):
    return block.astype(F32).T.astype(BF16)


def band_mask(low, high, start_row, size):
    count = high - low
    key = lax.broadcasted_iota(jnp.int32, (count, 2 * size), 0) + low
    query = lax.broadcasted_iota(jnp.int32, (count, 2 * size), 1) % size + (high - size)
    return (key >= start_row) & (key <= query)


def attend_kernel(
    ctx_size, table, seq_ref, qkv_ref, start_ref, out_ref, lse_ref, held, query_t, value_t, mixed
):
    length = held.shape[0]
    half = length // (2 * ctx_size)
    size = LANES
    blocks = length // size
    reach = blocks // 2
    to_places(table, ctx_size, half, qkv_ref, held)
    for block in range(blocks):
        span = slice(block * size, (block + 1) * size)
        query_t[:, span] = (held[span, 0:LANES].astype(F32) * 0.125).T.astype(BF16)
        value_t[:, span] = flipped(held[span, 2 * LANES :])
    for block in range(blocks):
        low = max(0, block - reach) * size
        high = (block + 1) * size
        span = slice(block * size, high)
        scores = dot(held[low:high, LANES : 2 * LANES], both_heads(query_t[:, span]))
        start_row = start_ref[0, :, span]
        start_row = jnp.concatenate([start_row, start_row], axis=1)
        scores = jnp.where(band_mask(low, high, start_row, size), scores, MASKED)
        top = jnp.max(scores, axis=0, keepdims=True)
        weights = jnp.exp(scores - top)
        total = jnp.sum(weights, axis=0, keepdims=True)
        lse = top + jnp.log(total)
        probs = (weights * (1.0 / total)).astype(BF16)
        lse_ref[0, 0:1, span] = lse[:, :size]
        lse_ref[0, 1:2, span] = lse[:, size:]
        mixed_t = dot(value_t[:, low:high], probs)
        both = jnp.concatenate(
            [mixed_t[0 : LANES // 2, :size], mixed_t[LANES // 2 :, size:]], axis=0
        )
        mixed[span, :] = both.T.astype(BF16)
    for device in range(ctx_size):
        pair = table[device]
        early = pl.multiple_of(pair * half, half)
        later = pl.multiple_of((2 * ctx_size - 1 - pair) * half, half)
        out_ref[device, 0, 0:half, :] = mixed[pl.ds(early, half), :]
        out_ref[device, 0, half : 2 * half, :] = mixed[pl.ds(later, half), :]


def attend(table, unit_seqs, qkv, starts):
    ctx_size, units, rows, width = qkv.shape
    length = ctx_size * rows
    return pl.pallas_call(
        functools.partial(attend_kernel, ctx_size),
        grid_spec=pltpu.PrefetchScalarGridSpec(
            num_scalar_prefetch=2,
            grid=(units,),
            in_specs=[
                pl.BlockSpec((ctx_size, 1, rows, width), lambda u, t, s: (0, u, 0, 0)),
                pl.BlockSpec((1, 1, length), lambda u, t, s: (s[u], 0, 0)),
            ],
            out_specs=[
                pl.BlockSpec((ctx_size, 1, rows, LANES), lambda u, t, s: (0, u, 0, 0)),
                pl.BlockSpec((1, 2, length), lambda u, t, s: (u, 0, 0)),
            ],
            scratch_shapes=[
                pltpu.VMEM((length, width), BF16),
                pltpu.VMEM((LANES, length), BF16),
                pltpu.VMEM((LANES, length), BF16),
                pltpu.VMEM((length, LANES), BF16),
            ],
        ),
        out_shape=[
            jax.ShapeDtypeStruct((ctx_size, units, rows, LANES), BF16),
            jax.ShapeDtypeStruct((units, 2, length), F32),
        ],
        compiler_params=params(),
        cost_estimate=cost(units * length * length * 256, qkv.size * 4),
        name="attend",
    )(table, unit_seqs, qkv, starts)


def attend_back_kernel(
    ctx_size,
    table,
    seq_ref,
    qkv_ref,
    grad_ref,
    start_ref,
    lse_ref,
    out_ref,
    held,
    grad,
    query_t,
    key_t,
    grad_t,
    query_grad,
    key_grad,
    value_grad,
):
    length = held.shape[0]
    half = length // (2 * ctx_size)
    size = LANES
    blocks = length // size
    reach = blocks // 2
    to_places(table, ctx_size, half, qkv_ref, held)
    to_places(table, ctx_size, half, grad_ref, grad)
    for block in range(blocks):
        span = slice(block * size, (block + 1) * size)
        scaled = (held[span, 0:LANES].astype(F32) * 0.125).astype(BF16)
        held[span, 0:LANES] = scaled
        query_t[:, span] = flipped(scaled)
        key_t[:, span] = flipped(held[span, LANES : 2 * LANES])
        grad_t[:, span] = flipped(grad[span, :])
    for block in range(blocks):
        low = max(0, block - reach) * size
        high = (block + 1) * size
        span = slice(block * size, high)
        scores = dot(held[low:high, LANES : 2 * LANES], both_heads(query_t[:, span]))
        start_row = start_ref[0, :, span]
        start_row = jnp.concatenate([start_row, start_row], axis=1)
        scores = jnp.where(band_mask(low, high, start_row, size), scores, MASKED)
        lse = jnp.concatenate([lse_ref[0, 0:1, span], lse_ref[0, 1:2, span]], axis=1)
        probs = jnp.exp(scores - lse)
        prob_grad = dot(held[low:high, 2 * LANES :], both_heads(grad_t[:, span]))
        delta = jnp.sum(probs * prob_grad, axis=0, keepdims=True)
        score_grad = (probs * (prob_grad - delta)).astype(BF16)
        probs = probs.astype(BF16)
        new_value = dot(probs, stacked_heads(grad[span, :]))
        new_key = dot(score_grad, stacked_heads(held[span, 0:LANES]))
        if low < high - size:
            value_grad[low : high - size, :] += new_value[: high - size - low]
            key_grad[low : high - size, :] += new_key[: high - size - low]
        value_grad[span, :] = new_value[high - size - low :]
        key_grad[span, :] = new_key[high - size - low :]
        query_t_grad = dot(key_t[:, low:high], score_grad)
        both = jnp.concatenate(
            [query_t_grad[0 : LANES // 2, :size], query_t_grad[LANES // 2 :, size:]], axis=0
        )
        query_grad[span, :] = (both.T * 0.125).astype(BF16)
    for device in range(ctx_size):
        pair = table[device]
        early = pl.multiple_of(pair * half, half)
        later = pl.multiple_of((2 * ctx_size - 1 - pair) * half, half)
        for place, source in ((0, early), (half, later)):
            rows = pl.ds(source, half)
            out_ref[device, 0, place : place + half, 0:LANES] = query_grad[rows, :]
            out_ref[device, 0, place : place + half, LANES : 2 * LANES] = key_grad[
                rows, :
            ].astype(BF16)
            out_ref[device, 0, place : place + half, 2 * LANES :] = value_grad[rows, :].astype(
                BF16
            )


def attend_back(table, unit_seqs, qkv, grad, starts, lse):
    ctx_size, units, rows, width = qkv.shape
    length = ctx_size * rows
    return pl.pallas_call(
        functools.partial(attend_back_kernel, ctx_size),
        grid_spec=pltpu.PrefetchScalarGridSpec(
            num_scalar_prefetch=2,
            grid=(units,),
            in_specs=[
                pl.BlockSpec((ctx_size, 1, rows, width), lambda u, t, s: (0, u, 0, 0)),
                pl.BlockSpec((ctx_size, 1, rows, LANES), lambda u, t, s: (0, u, 0, 0)),
                pl.BlockSpec((1, 1, length), lambda u, t, s: (s[u], 0, 0)),
                pl.BlockSpec((1, 2, length), lambda u, t, s: (u, 0, 0)),
            ],
            out_specs=pl.BlockSpec((ctx_size, 1, rows, width), lambda u, t, s: (0, u, 0, 0)),
            scratch_shapes=[
                pltpu.VMEM((length, width), BF16),
                pltpu.VMEM((length, LANES), BF16),
                pltpu.VMEM((LANES, length), BF16),
                pltpu.VMEM((LANES, length), BF16),
                pltpu.VMEM((LANES, length), BF16),
                pltpu.VMEM((length, LANES), BF16),
                pltpu.VMEM((length, LANES), F32),
                pltpu.VMEM((length, LANES), F32),
            ],
        ),
        out_shape=jax.ShapeDtypeStruct(qkv.shape, BF16),
        compiler_params=params(),
        cost_estimate=cost(units * length * length * 640, qkv.size * 6),
        name="attend_back",
    )(table, unit_seqs, qkv, grad, starts, lse)


def branch_kernel(off_ref, att_ref, x_ref, v_ref, *refs):
    residual_ref, h2_ref, mixed_ref, weight = refs[-4:]
    pairs = att_ref.shape[0]
    tokens = x_ref.shape[0]
    for pair in range(pairs):
        mixed_ref[:, pair * LANES : (pair + 1) * LANES] = att_ref[pair].reshape(tokens, LANES)
    place_columns(weight, off_ref, refs[:-4])
    residual = (
        x_ref[...].astype(F32) + dot(mixed_ref[...], weight[...]) + v_ref[V_BO : V_BO + 1, :]
    )
    residual_ref[...] = residual
    hat, _ = norm_stats(residual)
    h2_ref[...] = (hat * v_ref[V_G2 : V_G2 + 1, :] + v_ref[V_B2 : V_B2 + 1, :]).astype(BF16)


def branch(att, x, vectors, parts):
    arrays, offsets = split_parts(parts)
    tokens, features = x.shape
    return pl.pallas_call(
        branch_kernel,
        grid_spec=pltpu.PrefetchScalarGridSpec(
            num_scalar_prefetch=1,
            grid=(1,),
            in_specs=[whole(att.shape), whole(x.shape), whole(vectors.shape)]
            + [whole(array.shape) for array in arrays],
            out_specs=[whole(x.shape)] * 3,
            scratch_shapes=[pltpu.VMEM((features, features), BF16)],
        ),
        out_shape=[
            jax.ShapeDtypeStruct(x.shape, F32),
            jax.ShapeDtypeStruct(x.shape, BF16),
            jax.ShapeDtypeStruct(x.shape, BF16),
        ],
        compiler_params=params(),
        cost_estimate=cost(2 * tokens * features * features, 2 * features * features),
        name="branch",
    )(offsets, att, x, vectors, *arrays)


def ffn_kernel(
    expand_count,
    shrink_count,
    steps,
    sc_ref,
    residual_ref,
    h2_ref,
    og_ref,
    v_ref,
    eb_ref,
    *refs,
):
    expand_parts = refs[:expand_count]
    shrink_parts = refs[expand_count : expand_count + shrink_count]
    (
        out_ref,
        dh2_ref,
        send_s,
        keep_s,
        send_e,
        keep_e,
        eb_grad_ref,
        sb_grad_ref,
        expand,
        shrink,
        total,
        back,
        h2_t,
    ) = refs[expand_count + shrink_count :]
    step = pl.program_id(0)
    y_index = sc_ref[0]
    low_label = sc_ref[2]
    expand_offsets = [sc_ref[3 + i] for i in range(expand_count)]
    shrink_offsets = [sc_ref[3 + expand_count + i] for i in range(shrink_count)]

    @pl.when(step == 0)
    def _():
        total[...] = residual_ref[...] + v_ref[V_BS : V_BS + 1, :]
        back[...] = jnp.zeros_like(back)
        h2_t[...] = h2_ref[...].astype(F32).T.astype(BF16)
        sb_grad_ref[...] = jnp.sum(og_ref[...].astype(F32), axis=0, keepdims=True)

    place_rows(expand, expand_offsets, expand_parts)
    place_columns(shrink, shrink_offsets, shrink_parts)
    width = expand.shape[1]
    pre = dot(h2_ref[...], expand[...]) + eb_ref[...]
    root = math.sqrt(2.0 / math.pi)
    square = pre * pre
    curve = jnp.tanh(root * (pre + 0.044715 * (square * pre)))
    slope = 0.5 * (1.0 + curve)
    active = (pre * slope).astype(BF16)
    slope = slope + (0.5 * root) * pre * (1.0 - curve * curve) * (1.0 + 0.134145 * square)
    total[...] += dot(active, shrink[...])
    dpre = (dot_nt(og_ref[...], shrink[...]) * slope).astype(BF16)
    eb_grad_ref[...] = jnp.sum(dpre.astype(F32), axis=0, keepdims=True)
    back[...] += dot_nt(dpre, expand[...])
    shrink_grad = dot_tn(active, og_ref[...]).astype(BF16)
    expand_grad = dot(h2_t[...], dpre).astype(BF16)

    def store(target_s, target_e):
        fsdp_size, _, subs, rows, columns = target_s.shape
        for part in range(fsdp_size):
            for sub in range(subs):
                here = slice(sub * rows, (sub + 1) * rows)
                there = slice(part * columns, (part + 1) * columns)
                target_s[part ^ y_index, 0, sub ^ low_label] = shrink_grad[here, there]
                target_e[part ^ y_index, 0, sub ^ low_label] = expand_grad[there, here]

    @pl.when(step < steps // 2)
    def _():
        store(send_s, send_e)

    @pl.when(step >= steps // 2)
    def _():
        store(keep_s, keep_e)

    @pl.when(step == steps - 1)
    def _():
        out_ref[...] = total[...].astype(BF16)
        dh2_ref[...] = back[...]


def feed_forward(
    residual, h2, og, vectors, expand_bias, expand_parts, shrink_parts, sizes, y_index, label
):
    fsdp_size, ctx_size = sizes
    expand_arrays, expand_offsets = split_parts(expand_parts)
    shrink_arrays, shrink_offsets = split_parts(shrink_parts)
    tokens, features = h2.shape
    hidden = expand_arrays[0].shape[1]
    rows = hidden // ctx_size
    columns = features // fsdp_size
    width = 512
    subs = width // rows
    steps = hidden // width
    high_label = label // subs
    low_label = label % subs
    scalars = jnp.concatenate(
        [
            jnp.stack([y_index, high_label, low_label]).astype(jnp.int32),
            expand_offsets,
            shrink_offsets,
        ]
    )
    middle = steps // 2

    def chunk(step, sc):
        return (step ^ middle) ^ sc[1]

    grad_s = (fsdp_size, middle, subs, rows, columns)
    grad_e = (fsdp_size, middle, subs, columns, rows)

    def send_map(step, sc):
        return (0, jnp.minimum(step, middle - 1), 0, 0, 0)

    def keep_map(step, sc):
        return (0, jnp.maximum(step - middle, 0), 0, 0, 0)

    def block(shape, index):
        return pl.BlockSpec((shape[0], 1) + shape[2:], index)

    return pl.pallas_call(
        functools.partial(ffn_kernel, len(expand_arrays), len(shrink_arrays), steps),
        grid_spec=pltpu.PrefetchScalarGridSpec(
            num_scalar_prefetch=1,
            grid=(steps,),
            in_specs=[
                whole(residual.shape),
                whole(h2.shape),
                whole(og.shape),
                whole(vectors.shape),
                pl.BlockSpec((1, width), lambda s, sc: (0, chunk(s, sc))),
            ]
            + [
                pl.BlockSpec((array.shape[0], width), lambda s, sc: (0, chunk(s, sc)))
                for array in expand_arrays
            ]
            + [
                pl.BlockSpec((width, array.shape[1]), lambda s, sc: (chunk(s, sc), 0))
                for array in shrink_arrays
            ],
            out_specs=[
                whole(h2.shape),
                whole(h2.shape),
                block(grad_s, send_map),
                block(grad_s, keep_map),
                block(grad_e, send_map),
                block(grad_e, keep_map),
                pl.BlockSpec((1, width), lambda s, sc: (0, chunk(s, sc))),
                whole((1, features)),
            ],
            scratch_shapes=[
                pltpu.VMEM((features, width), BF16),
                pltpu.VMEM((width, features), BF16),
                pltpu.VMEM((tokens, features), F32),
                pltpu.VMEM((tokens, features), F32),
                pltpu.VMEM((features, tokens), BF16),
            ],
        ),
        out_shape=[
            jax.ShapeDtypeStruct(h2.shape, BF16),
            jax.ShapeDtypeStruct(h2.shape, F32),
            jax.ShapeDtypeStruct(grad_s, BF16),
            jax.ShapeDtypeStruct(grad_s, BF16),
            jax.ShapeDtypeStruct(grad_e, BF16),
            jax.ShapeDtypeStruct(grad_e, BF16),
            jax.ShapeDtypeStruct((1, hidden), F32),
            jax.ShapeDtypeStruct((1, features), F32),
        ],
        compiler_params=params(),
        cost_estimate=cost(12 * tokens * features * hidden, 8 * features * hidden),
        name="feed_forward",
    )(scalars, residual, h2, og, vectors, expand_bias, *expand_arrays, *shrink_arrays)


def branch_back_kernel(
    part_count, seqs, rows, sc_ref, dh2_ref, residual_ref, og_ref, mixed_ref, v_ref, *refs
):
    parts = refs[:part_count]
    dres_ref, dmixed_ref, grad_ref, vec_ref, weight, rounded = refs[part_count:]
    y_index = sc_ref[0]
    label = sc_ref[1]
    place_columns(weight, [sc_ref[2 + i] for i in range(part_count)], parts)
    hat, rate = norm_stats(residual_ref[...])
    dh2 = dh2_ref[...]
    scaled = dh2 * v_ref[V_G2 : V_G2 + 1, :]
    first = jnp.mean(scaled, axis=-1, keepdims=True)
    second = jnp.mean(scaled * hat, axis=-1, keepdims=True)
    dres = og_ref[...].astype(F32) + rate * (scaled - first - hat * second)
    dres_ref[...] = dres
    rounded[...] = dres.astype(BF16)
    vec_ref[0:1, :] = jnp.sum(dh2 * hat, axis=0, keepdims=True)
    vec_ref[1:2, :] = jnp.sum(dh2, axis=0, keepdims=True)
    vec_ref[2:3, :] = jnp.sum(rounded[...].astype(F32), axis=0, keepdims=True)
    vec_ref[3:, :] = jnp.zeros((vec_ref.shape[0] - 3, vec_ref.shape[1]), F32)
    dmixed = dot_nt(rounded[...], weight[...]).astype(BF16)
    for pair in range(dmixed_ref.shape[0]):
        dmixed_ref[pair] = dmixed[:, pair * LANES : (pair + 1) * LANES].reshape(seqs, rows, LANES)
    _, fsdp_size, count, size, columns = grad_ref.shape
    grad = dot_tn(mixed_ref[...], rounded[...]).astype(BF16)
    for number in range(2 * count):
        place = number ^ label
        for part in range(fsdp_size):
            grad_ref[place // count, part ^ y_index, place % count] = grad[
                number * size : (number + 1) * size, part * columns : (part + 1) * columns
            ]


def branch_back(dh2, residual, og, mixed, vectors, parts, sizes, y_index, label, seqs, rows):
    fsdp_size, ctx_size = sizes
    arrays, offsets = split_parts(parts)
    tokens, features = dh2.shape
    pairs = features // LANES
    grad = (2, fsdp_size, ctx_size // 2, features // ctx_size, features // fsdp_size)
    scalars = jnp.concatenate([jnp.stack([y_index, label]).astype(jnp.int32), offsets])
    full = whole(dh2.shape)
    return pl.pallas_call(
        functools.partial(branch_back_kernel, len(arrays), seqs, rows),
        grid_spec=pltpu.PrefetchScalarGridSpec(
            num_scalar_prefetch=1,
            grid=(1,),
            in_specs=[full, full, full, full, whole(vectors.shape)]
            + [whole(array.shape) for array in arrays],
            out_specs=[
                full,
                whole((pairs, seqs, rows, LANES)),
                whole(grad),
                whole((8, features)),
            ],
            scratch_shapes=[
                pltpu.VMEM((features, features), BF16),
                pltpu.VMEM((tokens, features), BF16),
            ],
        ),
        out_shape=[
            jax.ShapeDtypeStruct(dh2.shape, F32),
            jax.ShapeDtypeStruct((pairs, seqs, rows, LANES), BF16),
            jax.ShapeDtypeStruct(grad, BF16),
            jax.ShapeDtypeStruct((8, features), F32),
        ],
        compiler_params=params(),
        cost_estimate=cost(4 * tokens * features * features, 8 * features * features),
        name="branch_back",
    )(scalars, dh2, residual, og, mixed, vectors, *arrays)


def input_grad_kernel(group_ref, h_ref, d_ref, out_ref):
    left = h_ref[...].reshape(-1, h_ref.shape[-1])
    right = d_ref[...].reshape(-1, d_ref.shape[-1])
    out_ref[...] = dot_tn(left, right).astype(BF16)


def input_weight_terms(gathered, dqkv, group):
    ctx_size, units, rows, width = dqkv.shape
    features = gathered.shape[-1]
    block = 2 * LANES
    return pl.pallas_call(
        input_grad_kernel,
        grid_spec=pltpu.PrefetchScalarGridSpec(
            num_scalar_prefetch=1,
            grid=(features // block,),
            in_specs=[
                pl.BlockSpec((ctx_size, units, rows, block), lambda g, s: (0, s[0], 0, g)),
                whole(dqkv.shape),
            ],
            out_specs=pl.BlockSpec((block, width), lambda g, s: (g, 0)),
        ),
        out_shape=jax.ShapeDtypeStruct((features, width), BF16),
        compiler_params=params(),
        cost_estimate=cost(2 * dqkv.size * features, 2 * dqkv.size + dqkv.size * features // 192),
        name="input_weight_terms",
    )(group, gathered, dqkv)


def entry_back_kernel(part_count, groups, off_ref, d_ref, x_ref, dres_ref, v_ref, *refs):
    parts = refs[: 3 * part_count]
    out_ref, vec_ref, weight, back = refs[3 * part_count :]
    group = pl.program_id(0)
    tokens = x_ref.shape[0]
    width = weight.shape[-1]

    @pl.when(group == 0)
    def _():
        back[...] = jnp.zeros_like(back)

    for kind in range(3):
        place_rows(
            weight.at[kind], off_ref, parts[kind * part_count : (kind + 1) * part_count]
        )
        lanes = slice(kind * LANES, (kind + 1) * LANES)
        value = jnp.concatenate(
            [d_ref[pair, :, :, lanes].reshape(tokens, LANES) for pair in range(d_ref.shape[0])],
            axis=1,
        )
        back[...] += dot_nt(value, weight[kind])
        if kind != 1:
            row = 2 if kind == 0 else 3
            start = pl.multiple_of(group * width, LANES)
            vec_ref[row : row + 1, pl.ds(start, width)] = jnp.sum(
                value.astype(F32), axis=0, keepdims=True
            )

    @pl.when(group == groups - 1)
    def _():
        hat, rate = norm_stats(x_ref[...].astype(F32))
        dh1 = back[...]
        scaled = dh1 * v_ref[V_G1 : V_G1 + 1, :]
        first = jnp.mean(scaled, axis=-1, keepdims=True)
        second = jnp.mean(scaled * hat, axis=-1, keepdims=True)
        out_ref[...] = dres_ref[...] + rate * (scaled - first - hat * second)
        vec_ref[0:1, :] = jnp.sum(dh1 * hat, axis=0, keepdims=True)
        vec_ref[1:2, :] = jnp.sum(dh1, axis=0, keepdims=True)


def entry_back(dqkv, x, dres, vectors, parts):
    arrays, offsets = split_parts(parts)
    tokens, features = x.shape
    pairs, seqs, rows, _ = dqkv.shape
    width = 2 * LANES
    groups = features // width
    specs = []
    operands = []
    for kind in range(3):
        for array in arrays:
            specs.append(
                pl.BlockSpec((array.shape[0], width), lambda g, o, k=kind: (0, k * groups + g))
            )
            operands.append(array)
    return pl.pallas_call(
        functools.partial(entry_back_kernel, len(arrays), groups),
        grid_spec=pltpu.PrefetchScalarGridSpec(
            num_scalar_prefetch=1,
            grid=(groups,),
            in_specs=[
                pl.BlockSpec((2, seqs, rows, 3 * LANES), lambda g, o: (g, 0, 0, 0)),
                whole(x.shape),
                whole(x.shape),
                whole(vectors.shape),
            ]
            + specs,
            out_specs=[whole(x.shape), whole((4, features))],
            scratch_shapes=[
                pltpu.VMEM((3, features, width), BF16),
                pltpu.VMEM((tokens, features), F32),
            ],
        ),
        out_shape=[
            jax.ShapeDtypeStruct(x.shape, F32),
            jax.ShapeDtypeStruct((4, features), F32),
        ],
        compiler_params=params(),
        cost_estimate=cost(6 * tokens * features * features, 6 * features * features),
        name="entry_back",
    )(offsets, dqkv, x, dres, vectors, *operands)


def scatter_sum(send, keep, sizes):
    fsdp_size, ctx_size = sizes
    term = keep + swap_bit(send, "ctx", ctx_size, 0)
    term = term.reshape((fsdp_size, ctx_size // 2) + term.shape[-2:])
    for bit in reversed(range(bits_of(fsdp_size))):
        middle = term.shape[0] // 2
        term = term[:middle] + swap_bit(term[middle:], "fsdp", fsdp_size, bit)
    term = term[0]
    for bit in range(1, bits_of(ctx_size)):
        middle = term.shape[0] // 2
        term = term[:middle] + swap_bit(term[middle:], "ctx", ctx_size, bit)
    return term


def spread(term, ctx_size):
    for bit in reversed(range(1, bits_of(ctx_size))):
        term = jnp.concatenate([term, swap_bit(term, "ctx", ctx_size, bit)], axis=0)
    return term, swap_bit(term, "ctx", ctx_size, 0)


def finish_rows_kernel(half, label_ref, near_ref, far_ref, out_ref):
    number = pl.program_id(0)

    @pl.when(number < half)
    def _():
        out_ref[...] = near_ref[0].astype(F32)

    @pl.when(number >= half)
    def _():
        out_ref[...] = far_ref[0].astype(F32)


def finish(near, far, label, dim):
    half, rows, columns = near.shape
    count = 2 * half
    if dim == 0:
        shape = (count * rows, columns)
        out_spec = pl.BlockSpec((rows, columns), lambda n, k: (n ^ k[0], 0))
    else:
        shape = (rows, count * columns)
        out_spec = pl.BlockSpec((rows, columns), lambda n, k: (0, n ^ k[0]))
    return pl.pallas_call(
        functools.partial(finish_rows_kernel, half),
        grid_spec=pltpu.PrefetchScalarGridSpec(
            num_scalar_prefetch=1,
            grid=(count,),
            in_specs=[
                pl.BlockSpec((1, rows, columns), lambda n, k: (jnp.minimum(n, half - 1), 0, 0)),
                pl.BlockSpec((1, rows, columns), lambda n, k: (jnp.maximum(n - half, 0), 0, 0)),
            ],
            out_specs=out_spec,
        ),
        out_shape=jax.ShapeDtypeStruct(shape, F32),
        compiler_params=params(),
        cost_estimate=cost(0, near.size * 12),
        name="finish",
    )(label.reshape(1), near, far)


def finish_input_kernel(low_bits, table, near_ref, far_ref, out_ref):
    half, rows, _ = near_ref.shape
    for number in range(2 * half):
        owner = table[number]
        place = owner & ((1 << low_bits) - 1)
        pair = owner >> low_bits
        source = near_ref[number] if number < half else far_ref[number - half]
        out_ref[
            pl.ds(pl.multiple_of(place * rows, rows), rows),
            pl.ds(pl.multiple_of(pair * LANES, LANES), LANES),
        ] = source.astype(F32)


def finish_input(near, far, table, low_bits, features):
    half, rows, _ = near.shape
    block = pl.BlockSpec((half, rows, LANES), lambda j, t: (0, 0, j))
    height = rows << low_bits
    return pl.pallas_call(
        functools.partial(finish_input_kernel, low_bits),
        grid_spec=pltpu.PrefetchScalarGridSpec(
            num_scalar_prefetch=1,
            grid=(3,),
            in_specs=[block, block],
            out_specs=pl.BlockSpec((height, features), lambda j, t: (0, j)),
        ),
        out_shape=jax.ShapeDtypeStruct((height, 3 * features), F32),
        compiler_params=params(),
        cost_estimate=cost(0, near.size * 12),
        name="finish_input",
    )(table, near, far)


def input_scatter_sum(term, low_bits, sizes, y_index, c_index):
    fsdp_size, ctx_size = sizes
    rows = term.shape[0] // (fsdp_size << low_bits)
    width = term.shape[1]
    term = term.reshape(fsdp_size, 1 << low_bits, rows, width)
    for bit in reversed(range(low_bits)):
        mine = (c_index >> bit) & 1
        term = term.reshape(fsdp_size, 2, 1 << bit, rows, width)
        send = lax.dynamic_index_in_dim(term, 1 - mine, 1, keepdims=False)
        keep = lax.dynamic_index_in_dim(term, mine, 1, keepdims=False)
        term = keep + swap_bit(send, "ctx", ctx_size, bit)
    term = term.reshape(fsdp_size, rows, width)
    for bit in reversed(range(bits_of(fsdp_size))):
        mine = (y_index >> bit) & 1
        term = term.reshape(2, 1 << bit, rows, width)
        send = lax.dynamic_index_in_dim(term, 1 - mine, 0, keepdims=False)
        keep = lax.dynamic_index_in_dim(term, mine, 0, keepdims=False)
        term = keep + swap_bit(send, "fsdp", fsdp_size, bit)
    return term.reshape(1, rows, width)


def sum_everywhere(value, sizes):
    fsdp_size, ctx_size = sizes
    for bit in range(bits_of(ctx_size)):
        value = value + swap_bit(value, "ctx", ctx_size, bit)
    for bit in range(bits_of(fsdp_size)):
        value = value + swap_bit(value, "fsdp", fsdp_size, bit)
    return value


def body(
    sizes,
    layer_input,
    output_grad,
    segments,
    assignment,
    first_gain,
    first_bias,
    input_weight,
    query_bias,
    value_bias,
    output_weight,
    output_bias,
    second_gain,
    second_bias,
    expand_weight,
    expand_bias,
    shrink_weight,
    shrink_bias,
):
    fsdp_size, ctx_size = sizes
    seqs, rows, features = layer_input.shape
    tokens = seqs * rows
    hidden = expand_weight.shape[1]
    pairs = features // LANES
    units = seqs * pairs // ctx_size
    y_index = lax.axis_index("fsdp").astype(jnp.int32)
    c_index = lax.axis_index("ctx").astype(jnp.int32)
    label = reverse_bits(c_index, bits_of(ctx_size))

    small = jnp.concatenate(
        [
            first_gain,
            first_bias,
            query_bias,
            value_bias,
            output_bias,
            second_gain,
            second_bias,
            shrink_bias,
            expand_bias,
        ]
    )
    small = lax.all_gather(small, "fsdp", axis=0).astype(F32)
    vectors = (
        small[:, : 8 * (features // fsdp_size)]
        .reshape(fsdp_size, 8, features // fsdp_size)
        .transpose(1, 0, 2)
        .reshape(8, features)
    )
    expand_vector = small[:, 8 * (features // fsdp_size) :].reshape(1, hidden)

    def parts_of(weight, dim, bits):
        return gather_parts(weight, dim, fsdp_size, ctx_size, y_index, c_index, bits)

    input_parts = parts_of(input_weight, 0, (0,))
    output_parts = parts_of(output_weight, 1, (0,))
    expand_parts = parts_of(expand_weight, 0, (0,))
    shrink_parts = parts_of(shrink_weight, 1, (0,))

    starts = jnp.sum(
        (segments[:, None, :] < segments[:, :, None]).astype(jnp.int32), axis=-1
    )[:, None, :]
    unit_seqs = (c_index * units + jnp.arange(units, dtype=jnp.int32)) % seqs

    x = layer_input.reshape(tokens, features)
    og = output_grad.reshape(tokens, features)
    h1 = first_norm(x, vectors)
    qkv = project(h1, vectors, input_parts, seqs, rows)
    qkv = qkv.reshape(ctx_size, units, rows, 3 * LANES)
    qkv = lax.all_to_all(qkv, "ctx", 0, 0, tiled=True)
    h1_late, qkv = lax.optimization_barrier((h1, qkv))
    gathered = lax.all_gather(h1_late.reshape(seqs, rows, features), "ctx", axis=0)
    att, lse = attend(assignment, unit_seqs, qkv, starts)
    att = lax.all_to_all(att, "ctx", 0, 0, tiled=True).reshape(pairs, seqs, rows, LANES)
    residual, h2, mixed = branch(att, x, vectors, output_parts)
    out, dh2, send_s, keep_s, send_e, keep_e, eb_grad, sb_grad = feed_forward(
        residual, h2, og, vectors, expand_vector, expand_parts, shrink_parts, sizes, y_index, label
    )
    dres, dmixed, output_terms, vec_two = branch_back(
        dh2, residual, og, mixed, vectors, output_parts, sizes, y_index, label, seqs, rows
    )
    dmixed = dmixed.reshape(ctx_size, units, rows, LANES)
    dmixed = lax.all_to_all(dmixed, "ctx", 0, 0, tiled=True)
    dqkv = attend_back(assignment, unit_seqs, qkv, dmixed, starts, lse)
    group = ((c_index * units) % seqs) // units
    input_terms = input_weight_terms(gathered, dqkv, group.reshape(1))
    dqkv = lax.all_to_all(dqkv, "ctx", 0, 0, tiled=True).reshape(pairs, seqs, rows, 3 * LANES)
    input_grad, vec_one = entry_back(dqkv, x, dres, vectors, input_parts)

    shrink_near, shrink_far = spread(scatter_sum(send_s, keep_s, sizes), ctx_size)
    expand_near, expand_far = spread(scatter_sum(send_e, keep_e, sizes), ctx_size)
    output_near, output_far = spread(
        scatter_sum(output_terms[1], output_terms[0], sizes), ctx_size
    )
    low_bits = bits_of(ctx_size // pairs)
    input_near, input_far = spread(
        input_scatter_sum(input_terms, low_bits, sizes, y_index, c_index), ctx_size
    )
    owners = reverse_bits(
        jnp.arange(ctx_size, dtype=jnp.int32) ^ label, bits_of(ctx_size)
    )
    shrink_grad = finish(shrink_near, shrink_far, label, 0)
    expand_grad = finish(expand_near, expand_far, label, 1)
    output_grad_w = finish(output_near, output_far, label, 0)
    input_grad_w = finish_input(input_near, input_far, owners, low_bits, features)

    early = jnp.concatenate([vec_two[:3], sb_grad, eb_grad.reshape(-1, features)], axis=0)
    early = sum_everywhere(early, sizes)
    late = sum_everywhere(vec_one, sizes)
    part = features // fsdp_size

    def own(vector):
        return lax.dynamic_slice_in_dim(vector, y_index * (vector.shape[0] // fsdp_size), vector.shape[0] // fsdp_size, 0)

    return (
        out.reshape(seqs, rows, features),
        input_grad.reshape(seqs, rows, features),
        own(late[0]),
        own(late[1]),
        input_grad_w,
        own(late[2]),
        own(late[3]),
        output_grad_w,
        own(early[2]),
        own(early[0]),
        own(early[1]),
        expand_grad,
        own(early[4:].reshape(-1)),
        shrink_grad,
        own(early[3]),
    )


def solution(mesh):
    sizes = (mesh.shape["fsdp"], mesh.shape["ctx"])
    return jax.shard_map(
        functools.partial(body, sizes),
        mesh=mesh,
        in_specs=(
            P("fsdp", "ctx", None),
            P("fsdp", "ctx", None),
            P("fsdp", None),
            P(),
            P("fsdp"),
            P("fsdp"),
            P("fsdp", None),
            P("fsdp"),
            P("fsdp"),
            P(None, "fsdp"),
            P("fsdp"),
            P("fsdp"),
            P("fsdp"),
            P("fsdp", None),
            P("fsdp"),
            P(None, "fsdp"),
            P("fsdp"),
        ),
        out_specs=(
            P("fsdp", "ctx", None),
            P("fsdp", "ctx", None),
            P("fsdp"),
            P("fsdp"),
            P("fsdp", None),
            P("fsdp"),
            P("fsdp"),
            P(None, "fsdp"),
            P("fsdp"),
            P("fsdp"),
            P("fsdp"),
            P("fsdp", None),
            P("fsdp"),
            P(None, "fsdp"),
            P("fsdp"),
        ),
        check_vma=False,
    )
```

time: 2030 us -> 605 us (0.30)
  waiting for transfers between devices: 1480 us -> 348 us
  matrix products: 171 us -> 0 us
  local copies, waits for them, and re-layouts: 198 us -> 36.3 us
  blocking collectives: 111 us -> 4.39 us
  Pallas kernels: 0 us -> 105 us
  starting transfers between devices: 1.1 us -> 63 us
    reduce_scatter x6 -> x0, waiting for transfers between devices: 805 us -> none  [the longest x2 229 us: one_batch(): lax.psum_scatter(buffer, 'ctx', scatter_dimension=1, tiled=True)]
    psum x1 -> x0, waiting for transfers between devices: 351 us -> none  [body(): lax.psum((lax.psum_scatter(summed[0], 'fsdp', scatter_dimension=0, tiled=...]
    all_gather x6 -> x1, waiting for transfers between devices: 319 us -> 0.02 us  [body(): lax.all_gather(h1_late.reshape(seqs, rows, features), 'ctx', axis=0)]
    ppermute x0 -> x51, waiting for transfers between devices: none -> 308 us  [swap_bit(): return lax.ppermute(value, axis, [(i, i ^ 1 << bit) for i in range(size)])]
    dot_general x60 -> x0, matrix products: 171 us -> none  [the longest x4 18 us: mix_values(): jnp.einsum('shqk,skhd->sqhd', probs_low, pieces[1], preferred_element_typ...]
    pallas_call x0 -> x13, Pallas kernels: none -> 105 us  [the longest x3 27.4 us: finish(): pl.pallas_call(functools.partial(finish_rows_kernel, half), grid_spec=plt...]
    dynamic_update_slice x8 -> x0, local copies, waits for them, and re-layouts: 66.3 us -> none  [key_grads(): lax.dynamic_update_slice_in_dim(running[1], joined_grad, number * size_k, 1)]
    psum x1 -> x0, blocking collectives: 63.6 us -> none  [body(): lax.psum((lax.psum_scatter(summed[0], 'fsdp', scatter_dimension=0, tiled=...]
  transfers between devices with their start and end apart: 13 -> 56, of which waited for: 12 -> 25; matrix products, arithmetic and copies ran while one was open for 14% -> 8% of each run, Pallas kernels for 0% -> 16%
where the time goes in v1:
time: 605 us; the launch traced here: 603 us
  waiting for transfers between devices  348 us (58%)
  Pallas kernels  105 us (17%)
  starting transfers between devices  63 us (10%)
  local copies, waits for them, and re-layouts  36.3 us (6%)
  other arithmetic  31.7 us (5%)
  between operations  15 us (2%)
    ppermute x51, waiting for transfers between devices, swap_bit(): return lax.ppermute(value, axis, [(i, i ^ 1 << bit) for i in range(size)])  308 us
    ppermute x51, starting transfers between devices, swap_bit(): return lax.ppermute(value, axis, [(i, i ^ 1 << bit) for i in range(size)])  42.5 us
    pallas_call x3, Pallas kernels, finish(): pl.pallas_call(functools.partial(finish_rows_kernel, half), grid_spec=plt...  27.4 us
    all_to_all x1, waiting for transfers between devices, body(): qkv = lax.all_to_all(qkv, 'ctx', 0, 0, tiled=True)  27.3 us
    pallas_call x1, Pallas kernels, feed_forward(): pl.pallas_call(functools.partial(ffn_kernel, len(expand_arrays), len(shri...  25.3 us
    unnamed x95, local copies, waits for them, and re-layouts  17.1 us
    concatenate x12, other arithmetic, spread(): term = jnp.concatenate([term, swap_bit(term, 'ctx', ctx_size, bit)], axis=0)  12.6 us
    all_to_all x1, waiting for transfers between devices, body(): lax.all_to_all(att, 'ctx', 0, 0, tiled=True)  12.2 us
  transfers between devices with their start and end apart: 56, of which 25 were waited for; matrix products, arithmetic and copies ran while one was open for 8% of the time, Pallas kernels for 16%

profile of v1, /device:TPU:0, one launch (start us, length us, event | category | flops | bytes accessed | tf_op | source)
XLA Modules:
  0.0 602.8 jit_solution(12828586112095619631)
XLA Ops:
  8.8 3.0 collective-permute-start
  11.9 34.4 %collective-permute-done.refs_1_.refs_4_.refs_7_ = bf16[256,3072]{1,0:T(8,128)(2,1)S(1)} collective-permute-done((bf16[256,3072]{1,0:T(8,128)(2,1)S(1)}, bf16[256,3072]{1,0:T(8,128)(2,1)S(1)}, u32[]{:S(2)}, u32[]{:S(2)}) %collective-permute-start) | collective-permute-done | bytes 1572896 | tf_op jit(solution)/shard_map/ppermute | solution.py:39
  48.1 4.4 all-gather
  54.8 5.2 project.1
  61.2 6.1 %all-to-all-start = ((bf16[16,2,64,384]{3,2,1,0:T(8,128)(2,1)}), bf16[16,2,64,384]{3,2,1,0:T(8,128)(2,1)S(1)}, u32[]{:S(2)}, u32[]{:S(2)}) async-start(bf16[16,2,64,384]{3,2,1,0:T(8,128)(2,1)} %bitcast.77), calls=%async_computation | async-start | bytes 3145728 | tf_op jit(solution)/shard_map/all_to_all | solution.py:972
  67.4 3.1 constant_dynamic-slice_fusion.9
  72.1 27.3 %all-to-all-done.qkv_ref = bf16[16,2,64,384]{3,2,1,0:T(8,128)(2,1)S(1)} async-done(((bf16[16,2,64,384]{3,2,1,0:T(8,128)(2,1)}), bf16[16,2,64,384]{3,2,1,0:T(8,128)(2,1)S(1)}, u32[]{:S(2)}, u32[]{:S(2)}) %all-to-all-start) | async-done | bytes 1572896 | tf_op jit(solution)/shard_map/all_to_all | solution.py:972
  104.0 15.2 %collective-permute-done.4.refs_1_ = bf16[256,4096]{1,0:T(8,128)(2,1)} collective-permute-done((bf16[256,4096]{1,0:T(8,128)(2,1)}, bf16[256,4096]{1,0:T(8,128)(2,1)}, u32[]{:S(2)}, u32[]{:S(2)}) %collective-permute-start.4) | collective-permute-done | bytes 2097184 | tf_op jit(solution)/shard_map/ppermute | solution.py:39
  119.3 44.5 %collective-permute-done.6.refs_4_ = bf16[4096,256]{1,0:T(8,128)(2,1)} collective-permute-done((bf16[4096,256]{1,0:T(8,128)(2,1)S(1)}, bf16[4096,256]{1,0:T(8,128)(2,1)}, u32[]{:S(2)}, u32[]{:S(2)}) %collective-permute-start.6) | collective-permute-done | bytes 2097184 | tf_op jit(solution)/shard_map/ppermute | solution.py:39
  169.8 9.0 %attend.1 = (bf16[16,2,64,128]{3,2,1,0:T(8,128)(2,1)S(1)}, f32[2,2,1024]{2,1,0:T(2,128)S(1)}) custom-call(s32[16]{0:T(128)S(1)} %copy-done.22, s32[2]{0:T(128)S(1)} %and_select_fusion.seq_ref, bf16[16,2,64,384]{3,2,1,0:T(8,128)(2,1)S(1)} %copy-done.9, s32[4,1,1024]{2,1,0:T(1,128)S(1)} %broadcast_in_dim.2.start_ref), custom_call_target="tpu_custom_call" | custom-call | flops 536870912 | bytes 3145728 | tf_op jit(solution)/shard_map/attend/pallas_call | solution.py:250
  179.6 5.8 all-to-all-start.1
  187.8 12.2 %all-to-all-done.1 = bf16[16,2,64,128]{3,2,1,0:T(8,128)(2,1)} async-done(((bf16[16,2,64,128]{3,2,1,0:T(8,128)(2,1)}), bf16[16,2,64,128]{3,2,1,0:T(8,128)(2,1)}, u32[]{:S(2)}, u32[]{:S(2)}) %all-to-all-start.1) | async-done | bytes 524320 | tf_op jit(solution)/shard_map/all_to_all | solution.py:976
  199.9 3.2 branch.1
  203.9 25.3 %feed_forward.1 = (bf16[256,1024]{1,0:T(8,128)(2,1)}, f32[256,1024]{1,0:T(8,128)S(1)}, bf16[2,4,2,256,512]{4,3,2,1,0:T(8,128)(2,1)}, bf16[2,4,2,256,512]{4,3,2,1...) custom-call(s32[9]{0:T(128)S(1)} %concatenate.56.sc_ref, ...), custom_call_target="tpu_custom_call" | custom-call | flops 12884901888 | bytes 33554432 | tf_op jit(solution)/shard_map/feed_forward/pallas_call | solution.py:546
  229.8 6.9 %collective-permute-done.42 = bf16[2,4,2,256,512]{4,3,2,1,0:T(8,128)(2,1)S(1)} collective-permute-done((bf16[2,4,2,256,512]{4,3,2,1,0:T(8,128)(2,1)}, bf16[2,4,2,256,512]{4,3,2,1,0:T(8,128)(2,1)S(1)}, u32[]{:S(2)}, u32[]{:S(2)}) %collective-permute-start.42) | collective-permute-done | bytes 4194336 | tf_op jit(solution)/shard_map/ppermute | solution.py:39
  236.7 3.2 add.185
  239.9 2.4 fusion.4
  250.3 5.6 branch_back.1
  256.9 4.5 all-to-all-start.2
  261.4 29.7 %collective-permute-done.43 = bf16[1,8,256,512]{3,2,1,0:T(8,128)(2,1)} collective-permute-done((bf16[1,8,256,512]{3,2,1,0:T(8,128)(2,1)}, bf16[1,8,256,512]{3,2,1,0:T(8,128)(2,1)}, u32[]{:S(2)}, u32[]{:S(2)}) %collective-permute-start.43) | collective-permute-done | bytes 2097184 | tf_op jit(solution)/shard_map/ppermute | solution.py:39
  291.1 2.9 add.186
  295.9 39.4 %collective-permute-done.34 = bf16[1,8,512,256]{3,2,1,0:T(8,128)(2,1)} collective-permute-done((bf16[1,8,512,256]{3,2,1,0:T(8,128)(2,1)}, bf16[1,8,512,256]{3,2,1,0:T(8,128)(2,1)}, u32[]{:S(2)}, u32[]{:S(2)}) %collective-permute-start.34) | collective-permute-done | bytes 2097184 | tf_op jit(solution)/shard_map/ppermute | solution.py:39
  342.5 10.2 %attend_back.1.d_ref = bf16[16,2,64,384]{3,2,1,0:T(8,128)(2,1)S(1)} custom-call(s32[16]{0:T(128)S(1)} %copy-done.22, s32[2]{0:T(128)S(1)} %and_select_fusion.seq_ref, bf16[16,2,64,384]{3,2,1,0:T(8,128)(2,1)S(1)} %copy-done.10, bf16[16,2,64,128]{3,2,1,0:T(8,128)(2,1)} %all-to-all-done.2.grad_ref, s32[4,1,1024]{2,1,0:T(1,128)S(1)} %broadcast_in_dim.2.start_ref, ...), custom_call_target="tpu_custom_call" | custom-call | flops 1342177280 | bytes 4718592 | tf_op jit(solution)/shard_map/attend_back/pallas_call | solution.py:356
  353.9 4.1 all-to-all-start.3
  361.8 6.3 %collective-permute-done.35 = bf16[4,512,256]{2,1,0:T(8,128)(2,1)} collective-permute-done((bf16[4,512,256]{2,1,0:T(8,128)(2,1)}, bf16[4,512,256]{2,1,0:T(8,128)(2,1)}, u32[]{:S(2)}, u32[]{:S(2)}) %collective-permute-start.35) | collective-permute-done | bytes 1048608 | tf_op jit(solution)/shard_map/ppermute | solution.py:39
  371.6 26.5 %collective-permute-done.45 = bf16[2,256,512]{2,1,0:T(8,128)(2,1)S(1)} collective-permute-done((bf16[2,256,512]{2,1,0:T(8,128)(2,1)S(1)}, bf16[2,256,512]{2,1,0:T(8,128)(2,1)S(1)}, u32[]{:S(2)}, u32[]{:S(2)}) %collective-permute-start.45) | collective-permute-done | bytes 524320 | tf_op jit(solution)/shard_map/ppermute | solution.py:39
  398.2 2.6 collective-permute-start.46
  400.7 13.7 %collective-permute-done.36 = bf16[2,512,256]{2,1,0:T(8,128)(2,1)S(1)} collective-permute-done((bf16[2,512,256]{2,1,0:T(8,128)(2,1)S(1)}, bf16[2,512,256]{2,1,0:T(8,128)(2,1)S(1)}, u32[]{:S(2)}, u32[]{:S(2)}) %collective-permute-start.36) | collective-permute-done | bytes 524320 | tf_op jit(solution)/shard_map/ppermute | solution.py:39
  419.1 15.4 %collective-permute-done.37 = bf16[1,512,256]{2,1,0:T(8,128)(2,1)S(1)} collective-permute-done((bf16[1,512,256]{2,1,0:T(8,128)(2,1)S(1)}, bf16[1,512,256]{2,1,0:T(8,128)(2,1)S(1)}, u32[]{:S(2)}, u32[]{:S(2)}) %collective-permute-start.37) | collective-permute-done | bytes 262176 | tf_op jit(solution)/shard_map/ppermute | solution.py:39
  436.0 4.9 input_weight_terms.1
  441.1 4.7 collective-permute-done.47
  447.0 4.5 collective-permute-done.38
  454.7 7.9 %collective-permute-done.48 = bf16[2,256,512]{2,1,0:T(8,128)(2,1)S(1)} collective-permute-done((bf16[2,256,512]{2,1,0:T(8,128)(2,1)S(1)}, bf16[2,256,512]{2,1,0:T(8,128)(2,1)S(1)}, u32[]{:S(2)}, u32[]{:S(2)}) %collective-permute-start.48) | collective-permute-done | bytes 524320 | tf_op jit(solution)/shard_map/ppermute | solution.py:39
  465.2 8.6 %collective-permute-done.39 = bf16[2,512,256]{2,1,0:T(8,128)(2,1)S(1)} collective-permute-done((bf16[2,512,256]{2,1,0:T(8,128)(2,1)S(1)}, bf16[2,512,256]{2,1,0:T(8,128)(2,1)S(1)}, u32[]{:S(2)}, u32[]{:S(2)}) %collective-permute-start.39) | collective-permute-done | bytes 524320 | tf_op jit(solution)/shard_map/ppermute | solution.py:39
  478.6 8.3 %collective-permute-done.15 = bf16[1,256,384]{2,1,0:T(8,128)(2,1)S(1)} collective-permute-done((bf16[1,256,384]{2,1,0:T(8,128)(2,1)S(1)}, bf16[1,256,384]{2,1,0:T(8,128)(2,1)S(1)}, u32[]{:S(2)}, u32[]{:S(2)}) %collective-permute-start.15) | collective-permute-done | bytes 196640 | tf_op jit(solution)/shard_map/ppermute | solution.py:39
  487.8 24.1 %collective-permute-done.29 = f32[8,1024]{1,0:T(8,128)S(1)} collective-permute-done((f32[8,1024]{1,0:T(8,128)S(1)}, f32[8,1024]{1,0:T(8,128)S(1)}, u32[]{:S(2)}, u32[]{:S(2)}) %collective-permute-start.29) | collective-permute-done | bytes 32800 | tf_op jit(solution)/shard_map/ppermute | solution.py:39
  515.8 2.6 pad_maximum_fusion.1.near_ref
  518.4 2.5 pad_maximum_fusion.near_ref
  524.4 4.3 collective-permute-done.31
  529.8 2.6 collective-permute-done.17
  538.2 7.2 %entry_back.1 = (f32[256,1024]{1,0:T(8,128)}, f32[4,1024]{1,0:T(4,128)S(1)}) custom-call(s32[3]{0:T(128)S(1)} %pad_add_fusion.off_ref, bf16[8,4,64,384]{3,2,1,0:T(8,128)(2,1)S(1)} %bitcast.76, bf16[256,1024]{1,0:T(8,128)(2,1)S(1)} %bitcast.80, f32[256,1024]{1,0:T(8,128)S(1)} %copy-done.12, f32[8,1024]{1,0:T(8,128)S(1)} %bitcast.88, ...), custom_call_target="tpu_custom_call" | custom-call | flops 1610612736 | bytes 6291456 | tf_op jit(solution)/shard_map/entry_back/pallas_call | solution.py:753
  548.2 2.6 collective-permute-done.9
  551.1 3.4 collective-permute-done.10
  556.1 3.0 collective-permute-done.11
  561.8 5.4 finish.3
  568.3 11.0 %finish.5 = f32[4096,512]{1,0:T(8,128)} custom-call(s32[1]{0:T(128)} %bitcast.14.label_ref, bf16[8,256,512]{2,1,0:T(8,128)(2,1)} %pad_maximum_fusion.1.near_ref, bf16[8,256,512]{2,1,0:T(8,128)(2,1)} %collective-permute-done.50.far_ref), custom_call_target="tpu_custom_call" | custom-call | bytes 12582912 | tf_op jit(solution)/shard_map/finish/pallas_call | solution.py:822
  579.3 11.0 %finish.4 = f32[512,4096]{1,0:T(8,128)} custom-call(s32[1]{0:T(128)} %bitcast.14.label_ref, bf16[8,512,256]{2,1,0:T(8,128)(2,1)} %pad_maximum_fusion.near_ref, bf16[8,512,256]{2,1,0:T(8,128)(2,1)} %collective-permute-done.41.far_ref), custom_call_target="tpu_custom_call" | custom-call | bytes 12582912 | tf_op jit(solution)/shard_map/finish/pallas_call | solution.py:822
  590.3 5.6 finish_input.1
  (255 shorter events, 91.9 us)
Async XLA Ops:
  8.8 37.4 %collective-permute-start = (bf16[256,3072]{1,0:T(8,128)(2,1)S(1)}, bf16[256,3072]{1,0:T(8,128)(2,1)S(1)}, u32[]{:S(2)}, u32[]{:S(2)}) collective-permute-start(bf16[256,3072]{1,0:T(8,128)(2,1)S(1)} %constant_dynamic-slice_fusion.11), channel_id=1, source_target_pairs={{0,16},{16,0},{1,17},{17,1},{2,18},{18,2},{3,19},{19,3},{4,20},{20... | collective-permute-start | bytes 4718600 | tf_op jit(solution)/shard_map/ppermute | solution.py:39
  46.3 8.6 %collective-permute-start.1 = (bf16[256,3072]{1,0:T(8,128)(2,1)S(1)}, bf16[256,3072]{1,0:T(8,128)(2,1)S(1)}, u32[]{:S(2)}, u32[]{:S(2)}) collective-permute-start(bf16[256,3072]{1,0:T(8,128)(2,1)S(1)} %collective-permute-done.refs_1_.refs_4_.refs_7_), channel_id=1, source_target_pairs={{0,1},{1,0},{2,3},{3,2},{4,5},{5,4},{6,7},{7,6},{8,9},{9,8},{10,11... | collective-permute-start | bytes 4718600 | tf_op jit(solution)/shard_map/ppermute | solution.py:39
  61.2 38.1 %all-to-all-start = ((bf16[16,2,64,384]{3,2,1,0:T(8,128)(2,1)}), bf16[16,2,64,384]{3,2,1,0:T(8,128)(2,1)S(1)}, u32[]{:S(2)}, u32[]{:S(2)}) async-start(bf16[16,2,64,384]{3,2,1,0:T(8,128)(2,1)} %bitcast.77), calls=%async_computation | async-start | bytes 3145728 | tf_op jit(solution)/shard_map/all_to_all | solution.py:972
  67.4 367.3 %all-gather.3.cloned.1.call-start = ((), (), s32[]{:S(2)}) async-start(), calls=%async_computation.4 | async-start | bytes 8912896 | tf_op jit(solution)/shard_map/all_gather | solution.py:974
  70.5 48.8 %collective-permute-start.4 = (bf16[256,4096]{1,0:T(8,128)(2,1)}, bf16[256,4096]{1,0:T(8,128)(2,1)}, u32[]{:S(2)}, u32[]{:S(2)}) collective-permute-start(bf16[256,4096]{1,0:T(8,128)(2,1)} %constant_dynamic-slice_fusion.9), channel_id=1, source_target_pairs={{0,16},{16,0},{1,17},{17,1},{2,18},{18,2},{3,19},{19,3},{4,20},{20... | collective-permute-start | bytes 6291464 | tf_op jit(solution)/shard_map/ppermute | solution.py:39
  102.5 61.3 %collective-permute-start.6 = (bf16[4096,256]{1,0:T(8,128)(2,1)S(1)}, bf16[4096,256]{1,0:T(8,128)(2,1)}, u32[]{:S(2)}, u32[]{:S(2)}) collective-permute-start(bf16[4096,256]{1,0:T(8,128)(2,1)S(1)} %constant_dynamic-slice_fusion.8), channel_id=1, source_target_pairs={{0,16},{16,0},{1,17},{17,1},{2,18},{18,2},{3,19},{19,3},{4,20},{20... | collective-permute-start | bytes 6291464 | tf_op jit(solution)/shard_map/ppermute | solution.py:39
  119.3 84.6 %collective-permute-start.5 = (bf16[256,4096]{1,0:T(8,128)(2,1)}, bf16[256,4096]{1,0:T(8,128)(2,1)}, u32[]{:S(2)}, u32[]{:S(2)}) collective-permute-start(bf16[256,4096]{1,0:T(8,128)(2,1)} %collective-permute-done.4.refs_1_), channel_id=1, source_target_pairs={{0,1},{1,0},{2,3},{3,2},{4,5},{5,4},{6,7},{7,6},{8,9},{9,8},{10,11... | collective-permute-start | bytes 6291464 | tf_op jit(solution)/shard_map/ppermute | solution.py:39
  163.8 40.2 %collective-permute-start.7 = (bf16[4096,256]{1,0:T(8,128)(2,1)}, bf16[4096,256]{1,0:T(8,128)(2,1)}, u32[]{:S(2)}, u32[]{:S(2)}) collective-permute-start(bf16[4096,256]{1,0:T(8,128)(2,1)} %collective-permute-done.6.refs_4_), channel_id=1, source_target_pairs={{0,1},{1,0},{2,3},{3,2},{4,5},{5,4},{6,7},{7,6},{8,9},{9,8},{10,11... | collective-permute-start | bytes 6291464 | tf_op jit(solution)/shard_map/ppermute | solution.py:39
  164.6 20.8 %collective-permute-start.2 = (bf16[1024,256]{1,0:T(8,128)(2,1)}, bf16[1024,256]{1,0:T(8,128)(2,1)}, u32[]{:S(2)}, u32[]{:S(2)}) collective-permute-start(bf16[1024,256]{1,0:T(8,128)(2,1)} %constant_dynamic-slice_fusion.10), channel_id=1, source_target_pairs={{0,16},{16,0},{1,17},{17,1},{2,18},{18,2},{3,19},{19,3},{4,20},{20... | collective-permute-start | bytes 1572872 | tf_op jit(solution)/shard_map/ppermute | solution.py:39
  179.6 20.3 %all-to-all-start.1 = ((bf16[16,2,64,128]{3,2,1,0:T(8,128)(2,1)}), bf16[16,2,64,128]{3,2,1,0:T(8,128)(2,1)}, u32[]{:S(2)}, u32[]{:S(2)}) async-start(bf16[16,2,64,128]{3,2,1,0:T(8,128)(2,1)} %copy-done.17), calls=%async_computation.1 | async-start | bytes 1048576 | tf_op jit(solution)/shard_map/all_to_all | solution.py:976
  229.3 7.4 %collective-permute-start.42 = (bf16[2,4,2,256,512]{4,3,2,1,0:T(8,128)(2,1)}, bf16[2,4,2,256,512]{4,3,2,1,0:T(8,128)(2,1)S(1)}, u32[]{:S(2)}, u32[]{:S(2)}) collective-permute-start(bf16[2,4,2,256,512]{4,3,2,1,0:T(8,128)(2,1)} %get-tuple-element.56), channel_id=1, source_target_pairs={{0,1},{1,0},{2,3},{3,2},{4,5},{5,4},{6,7},{7,6},{8,9},{9,8},{10,11... | collective-permute-start | bytes 12582920 | tf_op jit(solution)/shard_map/ppermute | solution.py:39
  229.3 13.5 %collective-permute-start.33 = (bf16[2,4,2,512,256]{4,3,2,1,0:T(8,128)(2,1)}, bf16[2,4,2,512,256]{4,3,2,1,0:T(8,128)(2,1)S(1)}, u32[]{:S(2)}, u32[]{:S(2)}) collective-permute-start(bf16[2,4,2,512,256]{4,3,2,1,0:T(8,128)(2,1)} %get-tuple-element.54), channel_id=1, source_target_pairs={{0,1},{1,0},{2,3},{3,2},{4,5},{5,4},{6,7},{7,6},{8,9},{9,8},{10,11... | collective-permute-start | bytes 12582920 | tf_op jit(solution)/shard_map/ppermute | solution.py:39
  242.3 48.8 %collective-permute-start.43 = (bf16[1,8,256,512]{3,2,1,0:T(8,128)(2,1)}, bf16[1,8,256,512]{3,2,1,0:T(8,128)(2,1)}, u32[]{:S(2)}, u32[]{:S(2)}) collective-permute-start(bf16[1,8,256,512]{3,2,1,0:T(8,128)(2,1)} %bitcast.41), channel_id=1, source_target_pairs={{0,16},{16,0},{1,17},{17,1},{2,18},{18,2},{3,19},{19,3},{4,20},{20... | collective-permute-start | bytes 6291464 | tf_op jit(solution)/shard_map/ppermute | solution.py:39
  247.2 88.0 %collective-permute-start.34 = (bf16[1,8,512,256]{3,2,1,0:T(8,128)(2,1)}, bf16[1,8,512,256]{3,2,1,0:T(8,128)(2,1)}, u32[]{:S(2)}, u32[]{:S(2)}) collective-permute-start(bf16[1,8,512,256]{3,2,1,0:T(8,128)(2,1)} %bitcast.37), channel_id=1, source_target_pairs={{0,16},{16,0},{1,17},{17,1},{2,18},{18,2},{3,19},{19,3},{4,20},{20... | collective-permute-start | bytes 6291464 | tf_op jit(solution)/shard_map/ppermute | solution.py:39
  256.9 85.6 %all-to-all-start.2 = ((bf16[16,2,64,128]{3,2,1,0:T(8,128)(2,1)}), bf16[16,2,64,128]{3,2,1,0:T(8,128)(2,1)}, u32[]{:S(2)}, u32[]{:S(2)}) async-start(bf16[16,2,64,128]{3,2,1,0:T(8,128)(2,1)} %bitcast.15), calls=%async_computation.2 | async-start | bytes 1048576 | tf_op jit(solution)/shard_map/all_to_all | solution.py:985
  295.1 62.9 %collective-permute-start.44 = (bf16[4,256,512]{2,1,0:T(8,128)(2,1)}, bf16[4,256,512]{2,1,0:T(8,128)(2,1)}, u32[]{:S(2)}, u32[]{:S(2)}) collective-permute-start(bf16[4,256,512]{2,1,0:T(8,128)(2,1)} %slice_bitcast_fusion), channel_id=1, source_target_pairs={{0,2},{1,3},{2,0},{3,1},{4,6},{5,7},{6,4},{7,5},{8,10},{9,11},{10,... | collective-permute-start | bytes 3145736 | tf_op jit(solution)/shard_map/ppermute | solution.py:39
  338.6 29.6 %collective-permute-start.35 = (bf16[4,512,256]{2,1,0:T(8,128)(2,1)}, bf16[4,512,256]{2,1,0:T(8,128)(2,1)}, u32[]{:S(2)}, u32[]{:S(2)}) collective-permute-start(bf16[4,512,256]{2,1,0:T(8,128)(2,1)} %slice_bitcast_fusion.2), channel_id=1, source_target_pairs={{0,2},{1,3},{2,0},{3,1},{4,6},{5,7},{6,4},{7,5},{8,10},{9,11},{10,... | collective-permute-start | bytes 3145736 | tf_op jit(solution)/shard_map/ppermute | solution.py:39
  340.7 28.9 %collective-permute-start.19 = (bf16[2,8,64,512]{3,2,1,0:T(8,128)(2,1)}, bf16[2,8,64,512]{3,2,1,0:T(8,128)(2,1)}, u32[]{:S(2)}, u32[]{:S(2)}) collective-permute-start(bf16[2,8,64,512]{3,2,1,0:T(8,128)(2,1)} %slice_bitcast_fusion.4), channel_id=1, source_target_pairs={{0,1},{1,0},{2,3},{3,2},{4,5},{5,4},{6,7},{7,6},{8,9},{9,8},{10,11... | collective-permute-start | bytes 3145736 | tf_op jit(solution)/shard_map/ppermute | solution.py:39
  341.9 145.2 %collective-permute-start.28 = (f32[8,1024]{1,0:T(8,128)S(1)}, f32[8,1024]{1,0:T(8,128)S(1)}, u32[]{:S(2)}, u32[]{:S(2)}) collective-permute-start(f32[8,1024]{1,0:T(8,128)S(1)} %pad_maximum_fusion.12), channel_id=1, source_target_pairs={{0,1},{1,0},{2,3},{3,2},{4,5},{5,4},{6,7},{7,6},{8,9},{9,8},{10,11... | collective-permute-start | bytes 98312 | tf_op jit(solution)/shard_map/ppermute | solution.py:39
  353.9 182.0 %all-to-all-start.3 = ((bf16[16,2,64,384]{3,2,1,0:T(8,128)(2,1)}), bf16[16,2,64,384]{3,2,1,0:T(8,128)(2,1)S(1)}, u32[]{:S(2)}, u32[]{:S(2)}) async-start(bf16[16,2,64,384]{3,2,1,0:T(8,128)(2,1)} %copy-done.3), calls=%async_computation.3 | async-start | bytes 3145728 | tf_op jit(solution)/shard_map/all_to_all | solution.py:989
  359.8 38.2 %collective-permute-start.45 = (bf16[2,256,512]{2,1,0:T(8,128)(2,1)S(1)}, bf16[2,256,512]{2,1,0:T(8,128)(2,1)S(1)}, u32[]{:S(2)}, u32[]{:S(2)}) collective-permute-start(bf16[2,256,512]{2,1,0:T(8,128)(2,1)S(1)} %slice.223), channel_id=1, source_target_pairs={{0,4},{1,5},{2,6},{3,7},{4,0},{5,1},{6,2},{7,3},{8,12},{9,13},{10,... | collective-permute-start | bytes 1572872 | tf_op jit(solution)/shard_map/ppermute | solution.py:39
  369.5 44.9 %collective-permute-start.36 = (bf16[2,512,256]{2,1,0:T(8,128)(2,1)S(1)}, bf16[2,512,256]{2,1,0:T(8,128)(2,1)S(1)}, u32[]{:S(2)}, u32[]{:S(2)}) collective-permute-start(bf16[2,512,256]{2,1,0:T(8,128)(2,1)S(1)} %slice.214), channel_id=1, source_target_pairs={{0,4},{1,5},{2,6},{3,7},{4,0},{5,1},{6,2},{7,3},{8,12},{9,13},{10,... | collective-permute-start | bytes 1572872 | tf_op jit(solution)/shard_map/ppermute | solution.py:39
  371.0 44.1 %collective-permute-start.20 = (bf16[1,8,64,512]{3,2,1,0:T(8,128)(2,1)S(1)}, bf16[1,8,64,512]{3,2,1,0:T(8,128)(2,1)S(1)}, u32[]{:S(2)}, u32[]{:S(2)}) collective-permute-start(bf16[1,8,64,512]{3,2,1,0:T(8,128)(2,1)S(1)} %slice.199), channel_id=1, source_target_pairs={{0,16},{16,0},{1,17},{17,1},{2,18},{18,2},{3,19},{19,3},{4,20},{20... | collective-permute-start | bytes 1572872 | tf_op jit(solution)/shard_map/ppermute | solution.py:39
  398.2 17.8 %collective-permute-start.46 = (bf16[1,256,512]{2,1,0:T(8,128)(2,1)S(1)}, bf16[1,256,512]{2,1,0:T(8,128)(2,1)S(1)}, u32[]{:S(2)}, u32[]{:S(2)}) collective-permute-start(bf16[1,256,512]{2,1,0:T(8,128)(2,1)S(1)} %slice.225), channel_id=1, source_target_pairs={{0,8},{1,9},{2,10},{3,11},{4,12},{5,13},{6,14},{7,15},{8,0},{9,1},... | collective-permute-start | bytes 786440 | tf_op jit(solution)/shard_map/ppermute | solution.py:39
  414.5 19.9 %collective-permute-start.37 = (bf16[1,512,256]{2,1,0:T(8,128)(2,1)S(1)}, bf16[1,512,256]{2,1,0:T(8,128)(2,1)S(1)}, u32[]{:S(2)}, u32[]{:S(2)}) collective-permute-start(bf16[1,512,256]{2,1,0:T(8,128)(2,1)S(1)} %slice.216), channel_id=1, source_target_pairs={{0,8},{1,9},{2,10},{3,11},{4,12},{5,13},{6,14},{7,15},{8,0},{9,1},... | collective-permute-start | bytes 786440 | tf_op jit(solution)/shard_map/ppermute | solution.py:39
  416.7 29.1 %collective-permute-start.47 = (bf16[1,256,512]{2,1,0:T(8,128)(2,1)}, bf16[1,256,512]{2,1,0:T(8,128)(2,1)}, u32[]{:S(2)}, u32[]{:S(2)}) collective-permute-start(bf16[1,256,512]{2,1,0:T(8,128)(2,1)} %slice_add_fusion.3), channel_id=1, source_target_pairs={{0,8},{1,9},{2,10},{3,11},{4,12},{5,13},{6,14},{7,15},{8,0},{9,1},... | collective-permute-start | bytes 786440 | tf_op jit(solution)/shard_map/ppermute | solution.py:39
  434.5 16.9 %collective-permute-start.38 = (bf16[1,512,256]{2,1,0:T(8,128)(2,1)S(1)}, bf16[1,512,256]{2,1,0:T(8,128)(2,1)}, u32[]{:S(2)}, u32[]{:S(2)}) collective-permute-start(bf16[1,512,256]{2,1,0:T(8,128)(2,1)S(1)} %slice_add_fusion.4), channel_id=1, source_target_pairs={{0,8},{1,9},{2,10},{3,11},{4,12},{5,13},{6,14},{7,15},{8,0},{9,1},... | collective-permute-start | bytes 786440 | tf_op jit(solution)/shard_map/ppermute | solution.py:39
  441.0 13.0 %collective-permute-start.13 = (bf16[2,1,256,384]{3,2,1,0:T(8,128)(2,1)S(1)}, bf16[2,1,256,384]{3,2,1,0:T(8,128)(2,1)S(1)}, u32[]{:S(2)}, u32[]{:S(2)}) collective-permute-start(bf16[2,1,256,384]{3,2,1,0:T(8,128)(2,1)S(1)} %dynamic-slice_bitcast_fusion), channel_id=1, source_target_pairs={{0,1},{1,0},{2,3},{3,2},{4,5},{5,4},{6,7},{7,6},{8,9},{9,8},{10,11... | collective-permute-start | bytes 1179656 | tf_op jit(solution)/shard_map/ppermute | solution.py:39
  446.9 15.7 %collective-permute-start.48 = (bf16[2,256,512]{2,1,0:T(8,128)(2,1)S(1)}, bf16[2,256,512]{2,1,0:T(8,128)(2,1)S(1)}, u32[]{:S(2)}, u32[]{:S(2)}) collective-permute-start(bf16[2,256,512]{2,1,0:T(8,128)(2,1)S(1)} %pad_maximum_fusion.8), channel_id=1, source_target_pairs={{0,4},{1,5},{2,6},{3,7},{4,0},{5,1},{6,2},{7,3},{8,12},{9,13},{10,... | collective-permute-start | bytes 1572872 | tf_op jit(solution)/shard_map/ppermute | solution.py:39
  452.5 21.3 %collective-permute-start.39 = (bf16[2,512,256]{2,1,0:T(8,128)(2,1)S(1)}, bf16[2,512,256]{2,1,0:T(8,128)(2,1)S(1)}, u32[]{:S(2)}, u32[]{:S(2)}) collective-permute-start(bf16[2,512,256]{2,1,0:T(8,128)(2,1)S(1)} %pad_maximum_fusion.7), channel_id=1, source_target_pairs={{0,4},{1,5},{2,6},{3,7},{4,0},{5,1},{6,2},{7,3},{8,12},{9,13},{10,... | collective-permute-start | bytes 1572872 | tf_op jit(solution)/shard_map/ppermute | solution.py:39
  452.6 23.8 %collective-permute-start.21 = (bf16[4,64,512]{2,1,0:T(8,128)(2,1)S(1)}, bf16[4,64,512]{2,1,0:T(8,128)(2,1)S(1)}, u32[]{:S(2)}, u32[]{:S(2)}) collective-permute-start(bf16[4,64,512]{2,1,0:T(8,128)(2,1)S(1)} %slice_bitcast_fusion.5), channel_id=1, source_target_pairs={{0,2},{1,3},{2,0},{3,1},{4,6},{5,7},{6,4},{7,5},{8,10},{9,11},{10,... | collective-permute-start | bytes 786440 | tf_op jit(solution)/shard_map/ppermute | solution.py:39
  454.1 22.1 %collective-permute-start.14 = (bf16[1,256,384]{2,1,0:T(8,128)(2,1)S(1)}, bf16[1,256,384]{2,1,0:T(8,128)(2,1)S(1)}, u32[]{:S(2)}, u32[]{:S(2)}) collective-permute-start(bf16[1,256,384]{2,1,0:T(8,128)(2,1)S(1)} %dynamic-slice_bitcast_fusion.1), channel_id=1, source_target_pairs={{0,16},{16,0},{1,17},{17,1},{2,18},{18,2},{3,19},{19,3},{4,20},{20... | collective-permute-start | bytes 589832 | tf_op jit(solution)/shard_map/ppermute | solution.py:39
  463.7 52.1 %collective-permute-start.49 = (bf16[4,256,512]{2,1,0:T(8,128)(2,1)S(1)}, bf16[4,256,512]{2,1,0:T(8,128)(2,1)S(1)}, u32[]{:S(2)}, u32[]{:S(2)}) collective-permute-start(bf16[4,256,512]{2,1,0:T(8,128)(2,1)S(1)} %pad_maximum_fusion.4), channel_id=1, source_target_pairs={{0,2},{1,3},{2,0},{3,1},{4,6},{5,7},{6,4},{7,5},{8,10},{9,11},{10,... | collective-permute-start | bytes 3145736 | tf_op jit(solution)/shard_map/ppermute | solution.py:39
  474.8 43.6 %collective-permute-start.40 = (bf16[4,512,256]{2,1,0:T(8,128)(2,1)S(1)}, bf16[4,512,256]{2,1,0:T(8,128)(2,1)S(1)}, u32[]{:S(2)}, u32[]{:S(2)}) collective-permute-start(bf16[4,512,256]{2,1,0:T(8,128)(2,1)S(1)} %pad_maximum_fusion.3), channel_id=1, source_target_pairs={{0,2},{1,3},{2,0},{3,1},{4,6},{5,7},{6,4},{7,5},{8,10},{9,11},{10,... | collective-permute-start | bytes 3145736 | tf_op jit(solution)/shard_map/ppermute | solution.py:39
  476.3 10.7 %collective-permute-start.15 = (bf16[1,256,384]{2,1,0:T(8,128)(2,1)S(1)}, bf16[1,256,384]{2,1,0:T(8,128)(2,1)S(1)}, u32[]{:S(2)}, u32[]{:S(2)}) collective-permute-start(bf16[1,256,384]{2,1,0:T(8,128)(2,1)S(1)} %bitcast_add_fusion.2), channel_id=1, source_target_pairs={{0,8},{1,9},{2,10},{3,11},{4,12},{5,13},{6,14},{7,15},{8,0},{9,1},... | collective-permute-start | bytes 589832 | tf_op jit(solution)/shard_map/ppermute | solution.py:39
  476.4 35.6 %collective-permute-start.22 = (bf16[2,64,512]{2,1,0:T(8,128)(2,1)S(1)}, bf16[2,64,512]{2,1,0:T(8,128)(2,1)S(1)}, u32[]{:S(2)}, u32[]{:S(2)}) collective-permute-start(bf16[2,64,512]{2,1,0:T(8,128)(2,1)S(1)} %slice.203), channel_id=1, source_target_pairs={{0,4},{1,5},{2,6},{3,7},{4,0},{5,1},{6,2},{7,3},{8,12},{9,13},{10,... | collective-permute-start | bytes 393224 | tf_op jit(solution)/shard_map/ppermute | solution.py:39
  487.0 27.2 %collective-permute-start.16 = (bf16[2,256,384]{2,1,0:T(8,128)(2,1)S(1)}, bf16[2,256,384]{2,1,0:T(8,128)(2,1)S(1)}, u32[]{:S(2)}, u32[]{:S(2)}) collective-permute-start(bf16[2,256,384]{2,1,0:T(8,128)(2,1)S(1)} %pad_maximum_fusion.9), channel_id=1, source_target_pairs={{0,4},{1,5},{2,6},{3,7},{4,0},{5,1},{6,2},{7,3},{8,12},{9,13},{10,... | collective-permute-start | bytes 1179656 | tf_op jit(solution)/shard_map/ppermute | solution.py:39
  487.1 24.8 %collective-permute-start.29 = (f32[8,1024]{1,0:T(8,128)S(1)}, f32[8,1024]{1,0:T(8,128)S(1)}, u32[]{:S(2)}, u32[]{:S(2)}) collective-permute-start(f32[8,1024]{1,0:T(8,128)S(1)} %fusion.8), channel_id=1, source_target_pairs={{0,2},{1,3},{2,0},{3,1},{4,6},{5,7},{6,4},{7,5},{8,10},{9,11},{10,... | collective-permute-start | bytes 98312 | tf_op jit(solution)/shard_map/ppermute | solution.py:39
  511.9 10.2 %collective-permute-start.30 = (f32[8,1024]{1,0:T(8,128)S(1)}, f32[8,1024]{1,0:T(8,128)S(1)}, u32[]{:S(2)}, u32[]{:S(2)}) collective-permute-start(f32[8,1024]{1,0:T(8,128)S(1)} %add.175), channel_id=1, source_target_pairs={{0,4},{1,5},{2,6},{3,7},{4,0},{5,1},{6,2},{7,3},{8,12},{9,13},{10,... | collective-permute-start | bytes 98312 | tf_op jit(solution)/shard_map/ppermute | solution.py:39
  512.0 9.3 %collective-permute-start.23 = (bf16[1,64,512]{2,1,0:T(8,128)(2,1)S(1)}, bf16[1,64,512]{2,1,0:T(8,128)(2,1)S(1)}, u32[]{:S(2)}, u32[]{:S(2)}) collective-permute-start(bf16[1,64,512]{2,1,0:T(8,128)(2,1)S(1)} %slice.205), channel_id=1, source_target_pairs={{0,8},{1,9},{2,10},{3,11},{4,12},{5,13},{6,14},{7,15},{8,0},{9,1},... | collective-permute-start | bytes 196616 | tf_op jit(solution)/shard_map/ppermute | solution.py:39
  514.3 18.0 %collective-permute-start.17 = (bf16[4,256,384]{2,1,0:T(8,128)(2,1)S(1)}, bf16[4,256,384]{2,1,0:T(8,128)(2,1)S(1)}, u32[]{:S(2)}, u32[]{:S(2)}) collective-permute-start(bf16[4,256,384]{2,1,0:T(8,128)(2,1)S(1)} %pad_maximum_fusion.5), channel_id=1, source_target_pairs={{0,2},{1,3},{2,0},{3,1},{4,6},{5,7},{6,4},{7,5},{8,10},{9,11},{10,... | collective-permute-start | bytes 2359304 | tf_op jit(solution)/shard_map/ppermute | solution.py:39
  518.3 50.0 %collective-permute-start.50 = (bf16[8,256,512]{2,1,0:T(8,128)(2,1)}, bf16[8,256,512]{2,1,0:T(8,128)(2,1)}, u32[]{:S(2)}, u32[]{:S(2)}) collective-permute-start(bf16[8,256,512]{2,1,0:T(8,128)(2,1)} %pad_maximum_fusion.1.near_ref), channel_id=1, source_target_pairs={{0,1},{1,0},{2,3},{3,2},{4,5},{5,4},{6,7},{7,6},{8,9},{9,8},{10,11... | collective-permute-start | bytes 6291464 | tf_op jit(solution)/shard_map/ppermute | solution.py:39
  520.8 58.5 %collective-permute-start.41 = (bf16[8,512,256]{2,1,0:T(8,128)(2,1)}, bf16[8,512,256]{2,1,0:T(8,128)(2,1)}, u32[]{:S(2)}, u32[]{:S(2)}) collective-permute-start(bf16[8,512,256]{2,1,0:T(8,128)(2,1)} %pad_maximum_fusion.near_ref), channel_id=1, source_target_pairs={{0,1},{1,0},{2,3},{3,2},{4,5},{5,4},{6,7},{7,6},{8,9},{9,8},{10,11... | collective-permute-start | bytes 6291464 | tf_op jit(solution)/shard_map/ppermute | solution.py:39
  521.3 7.9 %collective-permute-start.24 = (bf16[1,64,512]{2,1,0:T(8,128)(2,1)S(1)}, bf16[1,64,512]{2,1,0:T(8,128)(2,1)S(1)}, u32[]{:S(2)}, u32[]{:S(2)}) collective-permute-start(bf16[1,64,512]{2,1,0:T(8,128)(2,1)S(1)} %slice_add_fusion.6), channel_id=1, source_target_pairs={{0,8},{1,9},{2,10},{3,11},{4,12},{5,13},{6,14},{7,15},{8,0},{9,1},... | collective-permute-start | bytes 196616 | tf_op jit(solution)/shard_map/ppermute | solution.py:39
  533.7 56.6 %collective-permute-start.18 = (bf16[8,256,384]{2,1,0:T(8,128)(2,1)}, bf16[8,256,384]{2,1,0:T(8,128)(2,1)}, u32[]{:S(2)}, u32[]{:S(2)}) collective-permute-start(bf16[8,256,384]{2,1,0:T(8,128)(2,1)} %pad_maximum_fusion.2.near_ref), channel_id=1, source_target_pairs={{0,1},{1,0},{2,3},{3,2},{4,5},{5,4},{6,7},{7,6},{8,9},{9,8},{10,11... | collective-permute-start | bytes 4718600 | tf_op jit(solution)/shard_map/ppermute | solution.py:39
  535.0 10.6 %collective-permute-start.26 = (bf16[4,64,512]{2,1,0:T(8,128)(2,1)}, bf16[4,64,512]{2,1,0:T(8,128)(2,1)}, u32[]{:S(2)}, u32[]{:S(2)}) collective-permute-start(bf16[4,64,512]{2,1,0:T(8,128)(2,1)} %pad_maximum_fusion.10), channel_id=1, source_target_pairs={{0,2},{1,3},{2,0},{3,1},{4,6},{5,7},{6,4},{7,5},{8,10},{9,11},{10,... | collective-permute-start | bytes 786440 | tf_op jit(solution)/shard_map/ppermute | solution.py:39
  546.6 15.2 %collective-permute-start.27 = (bf16[8,64,512]{2,1,0:T(8,128)(2,1)S(1)}, bf16[8,64,512]{2,1,0:T(8,128)(2,1)S(1)}, u32[]{:S(2)}, u32[]{:S(2)}) collective-permute-start(bf16[8,64,512]{2,1,0:T(8,128)(2,1)S(1)} %pad_maximum_fusion.6.near_ref), channel_id=1, source_target_pairs={{0,1},{1,0},{2,3},{3,2},{4,5},{5,4},{6,7},{7,6},{8,9},{9,8},{10,11... | collective-permute-start | bytes 1572872 | tf_op jit(solution)/shard_map/ppermute | solution.py:39
  559.2 8.0 %collective-permute-start.12 = (f32[4,1024]{1,0:T(4,128)S(1)}, f32[4,1024]{1,0:T(4,128)S(1)}, u32[]{:S(2)}, u32[]{:S(2)}) collective-permute-start(f32[4,1024]{1,0:T(4,128)S(1)} %add.159), channel_id=1, source_target_pairs={{0,16},{16,0},{1,17},{17,1},{2,18},{18,2},{3,19},{19,3},{4,20},{20... | collective-permute-start | bytes 49160 | tf_op jit(solution)/shard_map/ppermute | solution.py:39
  (49 other events, 886.7 us)
Sparse Core Ops, SparseCore 0:
  100.7 79.3 all-gather.2

commit v2 on v1

v2 whole, which is shorter than its diff:
```python
import functools
import math

import jax
import jax.numpy as jnp
from jax import lax
from jax.experimental import pallas as pl
from jax.experimental.pallas import tpu as pltpu
from jax.sharding import PartitionSpec as P

HEADS = 16
EPSILON = 1e-05
MASKED = -1000000000.0
LANES = 128
WIDTH = 512
MIB = 1024 * 1024
F32 = jnp.float32
BF16 = jnp.bfloat16
TOKEN = jax.ShapeDtypeStruct((8, LANES), F32)

V_G1, V_B1, V_BQ, V_BV, V_BO, V_G2, V_B2, V_BS = range(8)


def bits_of(number):
    return number.bit_length() - 1


def dot(left, right):
    return jnp.dot(left, right, preferred_element_type=F32)


def dot_nt(left, right):
    return lax.dot_general(left, right, (((1,), (1,)), ((), ())), preferred_element_type=F32)


def dot_tn(left, right):
    return lax.dot_general(left, right, (((0,), (0,)), ((), ())), preferred_element_type=F32)


def swap_bit(value, axis, size, bit):
    return lax.ppermute(value, axis, [(i, i ^ (1 << bit)) for i in range(size)])


class Event:
    def __init__(self, keep):
        self.keep = keep


def after(value, event):
    value, event.keep = lax.optimization_barrier((value, event.keep))
    return value


def params(limit_mib=48):
    return pltpu.CompilerParams(vmem_limit_bytes=limit_mib * MIB)


def whole(shape):
    rank = len(shape)
    return pl.BlockSpec(tuple(shape), lambda *_: (0,) * rank)


def cost(flops, moved):
    return pl.CostEstimate(flops=0, bytes_accessed=0, transcendentals=0)


class Gather:
    def __init__(self, weight, dim, place, bits, core=None):
        (fsdp_size, self.ctx_size), y_index, c_index = place
        extent = weight.shape[dim]
        self.bits = bits
        self.stage = 0
        self.two = fsdp_size == 2
        if not self.two:
            self.bits = ()
            self.parts = []
            self.first = lax.all_gather(weight, "fsdp", axis=dim, tiled=True)
            self.offsets = jnp.zeros((1,), jnp.int32)
            self.held = [self.first]
            return
        size = extent >> len(bits)
        mine = jnp.int32(0)
        for number, bit in enumerate(bits):
            mine = mine | (((c_index >> bit) & 1) << number)
        if core is None:
            self.first = lax.dynamic_slice_in_dim(weight, mine * size, size, dim)
        else:
            half = weight.shape[1 - dim] // 2
            begins = (mine * size, core * half) if dim == 0 else (core * half, mine * size)
            self.first = lax.dynamic_slice(
                weight, begins, (size, half) if dim == 0 else (half, size)
            )
        order = y_index * extent + jnp.zeros((1,), jnp.int32)
        numbers = mine ^ jnp.arange(1 << len(bits), dtype=jnp.int32)
        self.offsets = jnp.concatenate([order, (1 - y_index) * extent + numbers * size])
        self.parts = [weight]

    def fetch(self, event=None):
        if not self.two:
            return
        first = self.first if event is None else after(self.first, event)
        self.held = [swap_bit(first, "fsdp", 2, 0)]

    @property
    def keep(self):
        return self.held[-1]

    @keep.setter
    def keep(self, value):
        self.held[-1] = value

    def exchange(self, event=None):
        if self.stage == len(self.bits):
            return
        bit = self.bits[self.stage]
        if event is not None:
            self.keep = after(self.keep, event)
        self.held = self.held + [swap_bit(array, "ctx", self.ctx_size, bit) for array in self.held]
        self.stage += 1

    def result(self):
        return self.parts + self.held, self.offsets


def place_rows(target, offsets, part_refs):
    for number, ref in enumerate(part_refs):
        rows = ref.shape[0]
        target[pl.ds(pl.multiple_of(offsets[number], 32), rows), :] = ref[...]


def place_columns(target, offsets, part_refs):
    for number, ref in enumerate(part_refs):
        columns = ref.shape[1]
        target[:, pl.ds(pl.multiple_of(offsets[number], LANES), columns)] = ref[...]


def norm_stats(values):
    center = values - jnp.mean(values, axis=-1, keepdims=True)
    spread = jnp.mean(center * center, axis=-1, keepdims=True)
    rate = lax.rsqrt(spread + EPSILON)
    return center * rate, rate


def norm_kernel(sc_ref, x_ref, *refs):
    shards = refs[:-3]
    h_ref, v_ref, e_ref = refs[-3:]
    part = v_ref.shape[1] // len(shards)
    hidden = e_ref.shape[1] // len(shards)
    for number, ref in enumerate(shards):
        where = sc_ref[number]
        for row in range(8):
            v_ref[row : row + 1, pl.ds(pl.multiple_of(where * part, LANES), part)] = ref[
                :, row * part : (row + 1) * part
            ].astype(F32)
        e_ref[:, pl.ds(pl.multiple_of(where * hidden, LANES), hidden)] = ref[:, 8 * part :].astype(
            F32
        )
    hat, _ = norm_stats(x_ref[...].astype(F32))
    h_ref[...] = (hat * v_ref[V_G1 : V_G1 + 1, :] + v_ref[V_B1 : V_B1 + 1, :]).astype(BF16)


def first_norm(x, shards, owners, hidden):
    shapes = [
        jax.ShapeDtypeStruct(x.shape, BF16),
        jax.ShapeDtypeStruct((8, x.shape[1]), F32),
        jax.ShapeDtypeStruct((1, hidden), F32),
    ]
    return pl.pallas_call(
        norm_kernel,
        grid_spec=pltpu.PrefetchScalarGridSpec(
            num_scalar_prefetch=1,
            grid=(1,),
            in_specs=[whole(x.shape)] + [whole(shard.shape) for shard in shards],
            out_specs=[whole(shape.shape) for shape in shapes],
        ),
        out_shape=shapes,
        compiler_params=params(),
        cost_estimate=cost(0, 0),
        name="first_norm",
    )(owners, x, *shards)


def qkv_kernel(part_count, seqs, rows, off_ref, h_ref, v_ref, *refs):
    parts = refs[: 3 * part_count]
    out_ref, token_ref, weight = refs[3 * part_count :]
    token_ref[...] = jnp.zeros_like(token_ref)
    group = pl.program_id(0)
    width = weight.shape[-1]
    per = width // LANES
    for kind in range(3):
        place_rows(
            weight.at[kind], off_ref, parts[kind * part_count : (kind + 1) * part_count]
        )
        value = dot(h_ref[...], weight[kind])
        if kind != 1:
            row = V_BQ if kind == 0 else V_BV
            start = pl.multiple_of(group * width, LANES)
            value = value + v_ref[row : row + 1, pl.ds(start, width)]
        value = value.astype(BF16)
        for pair in range(per):
            out_ref[pair, :, :, kind * LANES : (kind + 1) * LANES] = value[
                :, pair * LANES : (pair + 1) * LANES
            ].reshape(seqs, rows, LANES)


def project(h1, vectors, parts, seqs, rows):
    arrays, offsets = parts
    tokens, features = h1.shape
    width = 2 * LANES
    groups = features // width
    pairs = features // LANES
    specs = []
    operands = []
    for kind in range(3):
        for array in arrays:
            specs.append(
                pl.BlockSpec((array.shape[0], width), lambda g, o, k=kind: (0, k * groups + g))
            )
            operands.append(array)
    return pl.pallas_call(
        functools.partial(qkv_kernel, len(arrays), seqs, rows),
        grid_spec=pltpu.PrefetchScalarGridSpec(
            num_scalar_prefetch=1,
            grid=(groups,),
            in_specs=[whole(h1.shape), whole(vectors.shape)] + specs,
            out_specs=[
                pl.BlockSpec((2, seqs, rows, 3 * LANES), lambda g, o: (g, 0, 0, 0)),
                whole(TOKEN.shape),
            ],
            scratch_shapes=[pltpu.VMEM((3, features, width), BF16)],
        ),
        out_shape=[jax.ShapeDtypeStruct((pairs, seqs, rows, 3 * LANES), BF16), TOKEN],
        compiler_params=params(),
        cost_estimate=cost(6 * tokens * features * features, 6 * features * features),
        name="project",
    )(offsets, h1, vectors, *operands)


def to_places(table, ctx_size, half, source, target):
    for device in range(ctx_size):
        pair = table[device]
        early = pl.multiple_of(pair * half, half)
        later = pl.multiple_of((2 * ctx_size - 1 - pair) * half, half)
        target[pl.ds(early, half), :] = source[device, 0, 0:half, :]
        target[pl.ds(later, half), :] = source[device, 0, half : 2 * half, :]


def both_heads(block):
    first = lax.broadcasted_iota(jnp.int32, block.shape, 0) < LANES // 2
    zero = jnp.zeros_like(block)
    return jnp.concatenate([jnp.where(first, block, zero), jnp.where(first, zero, block)], axis=1)


def stacked_heads(block):
    first = lax.broadcasted_iota(jnp.int32, block.shape, 1) < LANES // 2
    zero = jnp.zeros_like(block)
    return jnp.concatenate([jnp.where(first, block, zero), jnp.where(first, zero, block)], axis=0)


def flipped(block):
    return block.astype(F32).T.astype(BF16)


def band_mask(low, high, start_row, size):
    count = high - low
    key = lax.broadcasted_iota(jnp.int32, (count, 2 * size), 0) + low
    query = lax.broadcasted_iota(jnp.int32, (count, 2 * size), 1) % size + (high - size)
    return (key >= start_row) & (key <= query)


def attend_kernel(
    ctx_size, table, seq_ref, qkv_ref, start_ref, out_ref, lse_ref, held, query_t, value_t, mixed
):
    length = held.shape[0]
    half = length // (2 * ctx_size)
    size = LANES
    blocks = length // size
    reach = blocks // 2
    to_places(table, ctx_size, half, qkv_ref, held)
    for block in range(blocks):
        span = slice(block * size, (block + 1) * size)
        query_t[:, span] = (held[span, 0:LANES].astype(F32) * 0.125).T.astype(BF16)
        value_t[:, span] = flipped(held[span, 2 * LANES :])
    for block in range(blocks):
        low = max(0, block - reach) * size
        high = (block + 1) * size
        span = slice(block * size, high)
        scores = dot(held[low:high, LANES : 2 * LANES], both_heads(query_t[:, span]))
        start_row = start_ref[0, :, span]
        start_row = jnp.concatenate([start_row, start_row], axis=1)
        scores = jnp.where(band_mask(low, high, start_row, size), scores, MASKED)
        top = jnp.max(scores, axis=0, keepdims=True)
        weights = jnp.exp(scores - top)
        total = jnp.sum(weights, axis=0, keepdims=True)
        lse = top + jnp.log(total)
        probs = (weights * (1.0 / total)).astype(BF16)
        lse_ref[0, 0:1, span] = lse[:, :size]
        lse_ref[0, 1:2, span] = lse[:, size:]
        mixed_t = dot(value_t[:, low:high], probs)
        both = jnp.concatenate(
            [mixed_t[0 : LANES // 2, :size], mixed_t[LANES // 2 :, size:]], axis=0
        )
        mixed[span, :] = both.T.astype(BF16)
    for device in range(ctx_size):
        pair = table[device]
        early = pl.multiple_of(pair * half, half)
        later = pl.multiple_of((2 * ctx_size - 1 - pair) * half, half)
        out_ref[device, 0, 0:half, :] = mixed[pl.ds(early, half), :]
        out_ref[device, 0, half : 2 * half, :] = mixed[pl.ds(later, half), :]


def attend(table, unit_seqs, qkv, starts):
    ctx_size, units, rows, width = qkv.shape
    length = ctx_size * rows
    return pl.pallas_call(
        functools.partial(attend_kernel, ctx_size),
        grid_spec=pltpu.PrefetchScalarGridSpec(
            num_scalar_prefetch=2,
            grid=(units,),
            in_specs=[
                pl.BlockSpec((ctx_size, 1, rows, width), lambda u, t, s: (0, u, 0, 0)),
                pl.BlockSpec((1, 1, length), lambda u, t, s: (s[u], 0, 0)),
            ],
            out_specs=[
                pl.BlockSpec((ctx_size, 1, rows, LANES), lambda u, t, s: (0, u, 0, 0)),
                pl.BlockSpec((1, 2, length), lambda u, t, s: (u, 0, 0)),
            ],
            scratch_shapes=[
                pltpu.VMEM((length, width), BF16),
                pltpu.VMEM((LANES, length), BF16),
                pltpu.VMEM((LANES, length), BF16),
                pltpu.VMEM((length, LANES), BF16),
            ],
        ),
        out_shape=[
            jax.ShapeDtypeStruct((ctx_size, units, rows, LANES), BF16),
            jax.ShapeDtypeStruct((units, 2, length), F32),
        ],
        compiler_params=params(),
        cost_estimate=cost(units * length * length * 256, qkv.size * 4),
        name="attend",
    )(table, unit_seqs, qkv, starts)


def attend_back_kernel(
    ctx_size,
    table,
    seq_ref,
    qkv_ref,
    grad_ref,
    start_ref,
    lse_ref,
    out_ref,
    token_ref,
    held,
    grad,
    query_t,
    key_t,
    grad_t,
    query_grad,
    key_grad,
    value_grad,
):
    token_ref[...] = jnp.zeros_like(token_ref)
    length = held.shape[0]
    half = length // (2 * ctx_size)
    size = LANES
    blocks = length // size
    reach = blocks // 2
    to_places(table, ctx_size, half, qkv_ref, held)
    to_places(table, ctx_size, half, grad_ref, grad)
    for block in range(blocks):
        span = slice(block * size, (block + 1) * size)
        scaled = (held[span, 0:LANES].astype(F32) * 0.125).astype(BF16)
        held[span, 0:LANES] = scaled
        query_t[:, span] = flipped(scaled)
        key_t[:, span] = flipped(held[span, LANES : 2 * LANES])
        grad_t[:, span] = flipped(grad[span, :])
    for block in range(blocks):
        low = max(0, block - reach) * size
        high = (block + 1) * size
        span = slice(block * size, high)
        scores = dot(held[low:high, LANES : 2 * LANES], both_heads(query_t[:, span]))
        start_row = start_ref[0, :, span]
        start_row = jnp.concatenate([start_row, start_row], axis=1)
        scores = jnp.where(band_mask(low, high, start_row, size), scores, MASKED)
        lse = jnp.concatenate([lse_ref[0, 0:1, span], lse_ref[0, 1:2, span]], axis=1)
        probs = jnp.exp(scores - lse)
        prob_grad = dot(held[low:high, 2 * LANES :], both_heads(grad_t[:, span]))
        delta = jnp.sum(probs * prob_grad, axis=0, keepdims=True)
        score_grad = (probs * (prob_grad - delta)).astype(BF16)
        probs = probs.astype(BF16)
        new_value = dot(probs, stacked_heads(grad[span, :]))
        new_key = dot(score_grad, stacked_heads(held[span, 0:LANES]))
        if low < high - size:
            value_grad[low : high - size, :] += new_value[: high - size - low]
            key_grad[low : high - size, :] += new_key[: high - size - low]
        value_grad[span, :] = new_value[high - size - low :]
        key_grad[span, :] = new_key[high - size - low :]
        query_t_grad = dot(key_t[:, low:high], score_grad)
        both = jnp.concatenate(
            [query_t_grad[0 : LANES // 2, :size], query_t_grad[LANES // 2 :, size:]], axis=0
        )
        query_grad[span, :] = (both.T * 0.125).astype(BF16)
    for device in range(ctx_size):
        pair = table[device]
        early = pl.multiple_of(pair * half, half)
        later = pl.multiple_of((2 * ctx_size - 1 - pair) * half, half)
        for place, source in ((0, early), (half, later)):
            rows = pl.ds(source, half)
            out_ref[device, 0, place : place + half, 0:LANES] = query_grad[rows, :]
            out_ref[device, 0, place : place + half, LANES : 2 * LANES] = key_grad[
                rows, :
            ].astype(BF16)
            out_ref[device, 0, place : place + half, 2 * LANES :] = value_grad[rows, :].astype(
                BF16
            )


def attend_back(table, unit_seqs, qkv, grad, starts, lse):
    ctx_size, units, rows, width = qkv.shape
    length = ctx_size * rows
    return pl.pallas_call(
        functools.partial(attend_back_kernel, ctx_size),
        grid_spec=pltpu.PrefetchScalarGridSpec(
            num_scalar_prefetch=2,
            grid=(units,),
            in_specs=[
                pl.BlockSpec((ctx_size, 1, rows, width), lambda u, t, s: (0, u, 0, 0)),
                pl.BlockSpec((ctx_size, 1, rows, LANES), lambda u, t, s: (0, u, 0, 0)),
                pl.BlockSpec((1, 1, length), lambda u, t, s: (s[u], 0, 0)),
                pl.BlockSpec((1, 2, length), lambda u, t, s: (u, 0, 0)),
            ],
            out_specs=[
                pl.BlockSpec((ctx_size, 1, rows, width), lambda u, t, s: (0, u, 0, 0)),
                whole(TOKEN.shape),
            ],
            scratch_shapes=[
                pltpu.VMEM((length, width), BF16),
                pltpu.VMEM((length, LANES), BF16),
                pltpu.VMEM((LANES, length), BF16),
                pltpu.VMEM((LANES, length), BF16),
                pltpu.VMEM((LANES, length), BF16),
                pltpu.VMEM((length, LANES), BF16),
                pltpu.VMEM((length, LANES), F32),
                pltpu.VMEM((length, LANES), F32),
            ],
        ),
        out_shape=[jax.ShapeDtypeStruct(qkv.shape, BF16), TOKEN],
        compiler_params=params(),
        cost_estimate=cost(units * length * length * 640, qkv.size * 6),
        name="attend_back",
    )(table, unit_seqs, qkv, grad, starts, lse)


def branch_kernel(off_ref, att_ref, x_ref, v_ref, *refs):
    residual_ref, h2_ref, mixed_ref, weight = refs[-4:]
    pairs = att_ref.shape[0]
    tokens = x_ref.shape[0]
    for pair in range(pairs):
        mixed_ref[:, pair * LANES : (pair + 1) * LANES] = att_ref[pair].reshape(tokens, LANES)
    place_columns(weight, off_ref, refs[:-4])
    residual = (
        x_ref[...].astype(F32) + dot(mixed_ref[...], weight[...]) + v_ref[V_BO : V_BO + 1, :]
    )
    residual_ref[...] = residual
    hat, _ = norm_stats(residual)
    h2_ref[...] = (hat * v_ref[V_G2 : V_G2 + 1, :] + v_ref[V_B2 : V_B2 + 1, :]).astype(BF16)


def branch(att, x, vectors, parts):
    arrays, offsets = parts
    tokens, features = x.shape
    return pl.pallas_call(
        branch_kernel,
        grid_spec=pltpu.PrefetchScalarGridSpec(
            num_scalar_prefetch=1,
            grid=(1,),
            in_specs=[whole(att.shape), whole(x.shape), whole(vectors.shape)]
            + [whole(array.shape) for array in arrays],
            out_specs=[whole(x.shape)] * 3,
            scratch_shapes=[pltpu.VMEM((features, features), BF16)],
        ),
        out_shape=[
            jax.ShapeDtypeStruct(x.shape, F32),
            jax.ShapeDtypeStruct(x.shape, BF16),
            jax.ShapeDtypeStruct(x.shape, BF16),
        ],
        compiler_params=params(),
        cost_estimate=cost(2 * tokens * features * features, 2 * features * features),
        name="branch",
    )(offsets, att, x, vectors, *arrays)


def ffn_kernel(
    expand_count,
    shrink_count,
    steps,
    sc_ref,
    residual_ref,
    h2_ref,
    h2_other_ref,
    og_ref,
    og_other_ref,
    v_ref,
    eb_ref,
    *refs,
):
    expand_parts = refs[:expand_count]
    shrink_parts = refs[expand_count : expand_count + shrink_count]
    (
        send_ref,
        keep_ref,
        send_s,
        keep_s,
        send_e,
        keep_e,
        eb_grad_ref,
        sb_grad_ref,
        expand,
        shrink,
        total,
        back,
        h2,
        h2_t,
        og,
    ) = refs[expand_count + shrink_count :]
    step = pl.program_id(0)
    y_index = sc_ref[0]
    low_label = sc_ref[2]
    expand_offsets = [sc_ref[4 + i] for i in range(expand_count)]
    shrink_offsets = [sc_ref[4 + expand_count + i] for i in range(shrink_count)]
    tokens = h2_ref.shape[0]

    @pl.when(step == 0)
    def _():
        total[:tokens] = residual_ref[...] + v_ref[V_BS : V_BS + 1, :]
        total[tokens:] = jnp.zeros_like(residual_ref)
        back[...] = jnp.zeros_like(back)
        h2[:tokens] = h2_ref[...]
        h2[tokens:] = h2_other_ref[...]
        og[:tokens] = og_ref[...]
        og[tokens:] = og_other_ref[...]
        h2_t[...] = h2[...].astype(F32).T.astype(BF16)
        sb_grad_ref[...] = jnp.sum(og_ref[...].astype(F32), axis=0, keepdims=True)

    place_rows(expand, expand_offsets, expand_parts)
    place_columns(shrink, shrink_offsets, shrink_parts)
    pre = dot(h2[...], expand[...]) + eb_ref[...]
    root = math.sqrt(2.0 / math.pi)
    square = pre * pre
    curve = jnp.tanh(root * (pre + 0.044715 * (square * pre)))
    slope = 0.5 * (1.0 + curve)
    active = (pre * slope).astype(BF16)
    slope = slope + (0.5 * root) * pre * (1.0 - curve * curve) * (1.0 + 0.134145 * square)
    total[...] += dot(active, shrink[...])
    dpre = (dot_nt(og[...], shrink[...]) * slope).astype(BF16)
    eb_grad_ref[...] = jnp.sum(dpre.astype(F32), axis=0, keepdims=True)
    back[...] += dot_nt(dpre, expand[...])
    shrink_grad = dot_tn(active, og[...]).astype(BF16)
    expand_grad = dot(h2_t[...], dpre).astype(BF16)

    fsdp_half, _, subs, rows, columns = send_s.shape
    for part in range(2 * fsdp_half):
        there = slice(part * columns, (part + 1) * columns)
        place = part ^ y_index

        def store_s(target, there=there, place=place):
            for sub in range(subs):
                here = slice(sub * rows, (sub + 1) * rows)
                target[place & (fsdp_half - 1), 0, sub ^ low_label] = shrink_grad[here, there]

        pl.when(place < fsdp_half)(functools.partial(store_s, keep_s))
        pl.when(place >= fsdp_half)(functools.partial(store_s, send_s))
    for sub in range(subs):
        here = slice(sub * rows, (sub + 1) * rows)
        place = sub ^ low_label

        def store_e(target, here=here, place=place):
            for part in range(2 * fsdp_half):
                there = slice(part * columns, (part + 1) * columns)
                target[part ^ y_index, 0, place >> 1] = expand_grad[there, here]

        pl.when((place & 1) == 0)(functools.partial(store_e, keep_e))
        pl.when((place & 1) == 1)(functools.partial(store_e, send_e))

    @pl.when(step == steps - 1)
    def _():
        keep_ref[0] = back[:tokens]
        keep_ref[1] = total[:tokens]
        send_ref[0] = back[tokens:]
        send_ref[1] = total[tokens:]


def feed_scalars(place, hidden, width, expand_offsets, shrink_offsets):
    (_, ctx_size), y_index, c_index = place
    subs = width * ctx_size // hidden
    label = c_index >> 1
    first = [y_index, label >> bits_of(subs), label & (subs - 1), c_index & 1]
    return jnp.concatenate([jnp.stack(first), expand_offsets, shrink_offsets])


def feed_forward(
    scalars, residual, h2, h2_other, og, og_other, vectors, expand_bias, expand, shrink, sizes
):
    fsdp_size, ctx_size = sizes
    expand_arrays = expand[0]
    shrink_arrays = shrink[0]
    tokens, features = h2.shape
    hidden = expand_bias.shape[1]
    rows = hidden // ctx_size
    columns = features // fsdp_size
    width = WIDTH
    subs = width // rows
    steps = hidden // (2 * width)
    def chunk(array, dim):
        if array.shape[dim] == hidden:
            return lambda s, sc: sc[3] * steps + (s ^ sc[1])
        return lambda s, sc: s ^ sc[1]

    def columns_of(array):
        index = chunk(array, 1)
        return pl.BlockSpec((array.shape[0], width), lambda s, sc: (0, index(s, sc)))

    def rows_of(array):
        index = chunk(array, 0)
        return pl.BlockSpec((width, array.shape[1]), lambda s, sc: (index(s, sc), 0))

    grad_s = (fsdp_size // 2, steps, subs, rows, columns)
    grad_e = (fsdp_size, steps, subs // 2, columns, rows)

    def block(shape):
        return pl.BlockSpec((shape[0], 1) + shape[2:], lambda s, sc: (0, s, 0, 0, 0))

    full = whole(h2.shape)
    wide = jax.ShapeDtypeStruct((2,) + h2.shape, F32)
    return pl.pallas_call(
        functools.partial(ffn_kernel, len(expand_arrays), len(shrink_arrays), steps),
        grid_spec=pltpu.PrefetchScalarGridSpec(
            num_scalar_prefetch=1,
            grid=(steps,),
            in_specs=[full] * 5
            + [whole(vectors.shape), columns_of(expand_bias)]
            + [columns_of(array) for array in expand_arrays]
            + [rows_of(array) for array in shrink_arrays],
            out_specs=[whole(wide.shape)] * 2
            + [block(grad_s)] * 2
            + [block(grad_e)] * 2
            + [pl.BlockSpec((1, width), lambda s, sc: (0, s ^ sc[1])), whole((1, features))],
            scratch_shapes=[
                pltpu.VMEM((features, width), BF16),
                pltpu.VMEM((width, features), BF16),
                pltpu.VMEM((2 * tokens, features), F32),
                pltpu.VMEM((2 * tokens, features), F32),
                pltpu.VMEM((2 * tokens, features), BF16),
                pltpu.VMEM((features, 2 * tokens), BF16),
                pltpu.VMEM((2 * tokens, features), BF16),
            ],
        ),
        out_shape=[wide] * 2
        + [jax.ShapeDtypeStruct(grad_s, BF16)] * 2
        + [jax.ShapeDtypeStruct(grad_e, BF16)] * 2
        + [
            jax.ShapeDtypeStruct((1, hidden // 2), F32),
            jax.ShapeDtypeStruct((1, features), F32),
        ],
        compiler_params=params(),
        cost_estimate=cost(0, 0),
        name="feed_forward",
    )(
        scalars,
        residual,
        h2,
        h2_other,
        og,
        og_other,
        vectors,
        expand_bias,
        *expand_arrays,
        *shrink_arrays,
    )


def branch_back_kernel(
    part_count, seqs, rows, sc_ref, dh2_ref, dh2_other_ref, residual_ref, og_ref, mixed_ref, v_ref, *refs
):
    parts = refs[:part_count]
    dres_ref, dmixed_ref, keep_ref, send_ref, vec_ref, weight, rounded = refs[part_count:]
    place_columns(weight, sc_ref, parts)
    hat, rate = norm_stats(residual_ref[...])
    dh2 = dh2_ref[0] + dh2_other_ref[0]
    scaled = dh2 * v_ref[V_G2 : V_G2 + 1, :]
    first = jnp.mean(scaled, axis=-1, keepdims=True)
    second = jnp.mean(scaled * hat, axis=-1, keepdims=True)
    dres = og_ref[...].astype(F32) + rate * (scaled - first - hat * second)
    dres_ref[...] = dres
    rounded[...] = dres.astype(BF16)
    vec_ref[0:1, :] = jnp.sum(dh2 * hat, axis=0, keepdims=True)
    vec_ref[1:2, :] = jnp.sum(dh2, axis=0, keepdims=True)
    vec_ref[2:3, :] = jnp.sum(rounded[...].astype(F32), axis=0, keepdims=True)
    vec_ref[3:, :] = jnp.zeros((vec_ref.shape[0] - 3, vec_ref.shape[1]), F32)
    dmixed = dot_nt(rounded[...], weight[...]).astype(BF16)
    for pair in range(dmixed_ref.shape[0]):
        dmixed_ref[pair] = dmixed[:, pair * LANES : (pair + 1) * LANES].reshape(seqs, rows, LANES)
    fsdp_size, count, size, columns = keep_ref.shape
    grad = dot_tn(mixed_ref[...], rounded[...]).astype(BF16)
    y_index = sc_ref[part_count]
    label = sc_ref[part_count + 1]
    for number in range(2 * count):
        place = number ^ label

        def store(target, number=number, place=place):
            for part in range(fsdp_size):
                target[part ^ y_index, place >> 1] = grad[
                    number * size : (number + 1) * size, part * columns : (part + 1) * columns
                ]

        pl.when((place & 1) == 0)(functools.partial(store, keep_ref))
        pl.when((place & 1) == 1)(functools.partial(store, send_ref))


def branch_back(scalars, dh2, dh2_other, residual, og, mixed, vectors, parts, sizes, seqs, rows):
    fsdp_size, ctx_size = sizes
    arrays, offsets = parts
    tokens, features = residual.shape
    pairs = features // LANES
    grad = (fsdp_size, ctx_size // 2, features // ctx_size, features // fsdp_size)
    full = whole(residual.shape)
    half = pl.BlockSpec((1,) + residual.shape, lambda n, o: (0, 0, 0))
    return pl.pallas_call(
        functools.partial(branch_back_kernel, len(arrays), seqs, rows),
        grid_spec=pltpu.PrefetchScalarGridSpec(
            num_scalar_prefetch=1,
            grid=(1,),
            in_specs=[half] * 2 + [full] * 3 + [whole(vectors.shape)]
            + [whole(array.shape) for array in arrays],
            out_specs=[
                full,
                whole((pairs, seqs, rows, LANES)),
                whole(grad),
                whole(grad),
                whole((8, features)),
            ],
            scratch_shapes=[
                pltpu.VMEM((features, features), BF16),
                pltpu.VMEM((tokens, features), BF16),
            ],
        ),
        out_shape=[
            jax.ShapeDtypeStruct(residual.shape, F32),
            jax.ShapeDtypeStruct((pairs, seqs, rows, LANES), BF16),
            jax.ShapeDtypeStruct(grad, BF16),
            jax.ShapeDtypeStruct(grad, BF16),
            jax.ShapeDtypeStruct((8, features), F32),
        ],
        compiler_params=params(),
        cost_estimate=cost(4 * tokens * features * features, 8 * features * features),
        name="branch_back",
    )(scalars, dh2, dh2_other, residual, og, mixed, vectors, *arrays)


def input_terms_kernel(sc_ref, h_ref, d_ref, keep_ref, send_ref, token_ref):
    token_ref[...] = jnp.zeros_like(token_ref)
    left = h_ref[...].reshape(-1, h_ref.shape[-1])
    right = d_ref[...].reshape(-1, d_ref.shape[-1])
    value = dot_tn(left, right).astype(BF16)
    half, fsdp_size, rows, _ = keep_ref.shape
    per = value.shape[0] // rows
    for number in range(per):
        place = pl.program_id(0) * per + number
        part = (place // (2 * half)) ^ sc_ref[1]
        own = (place & (2 * half - 1)) ^ sc_ref[2]

        def store(target, number=number, part=part, own=own):
            target[own & (half - 1), part] = value[number * rows : (number + 1) * rows]

        pl.when(own < half)(functools.partial(store, keep_ref))
        pl.when(own >= half)(functools.partial(store, send_ref))


def input_weight_terms(gathered, dqkv, scalars, low, fsdp_size):
    ctx_size, units, rows, width = dqkv.shape
    features = gathered.shape[-1]
    block = 2 * LANES
    out = (low // 2, fsdp_size, features // (low * fsdp_size), width)
    return pl.pallas_call(
        input_terms_kernel,
        grid_spec=pltpu.PrefetchScalarGridSpec(
            num_scalar_prefetch=1,
            grid=(features // block,),
            in_specs=[
                pl.BlockSpec((ctx_size, units, rows, block), lambda g, s: (0, s[0], 0, g)),
                whole(dqkv.shape),
            ],
            out_specs=[whole(out), whole(out), whole(TOKEN.shape)],
        ),
        out_shape=[jax.ShapeDtypeStruct(out, BF16)] * 2 + [TOKEN],
        compiler_params=params(),
        cost_estimate=cost(0, 0),
        name="input_weight_terms",
    )(scalars, gathered, dqkv)


def entry_back_kernel(
    part_count,
    groups,
    off_ref,
    d_ref,
    x_ref,
    dres_ref,
    one_ref,
    two_ref,
    second_ref,
    sb_ref,
    eb_ref,
    v_ref,
    *refs,
):
    parts = refs[: 3 * part_count]
    out_ref, layer_ref, vec_ref, weight, back = refs[3 * part_count :]
    group = pl.program_id(0)
    tokens = x_ref.shape[0]
    width = weight.shape[-1]

    @pl.when(group == 0)
    def _():
        back[...] = jnp.zeros_like(back)
        layer_ref[...] = (one_ref[0] + two_ref[0]).astype(BF16)
        vec_ref[4:7, :] = second_ref[0:3, :]
        vec_ref[7:8, :] = sb_ref[...]
        count = vec_ref.shape[0] - 8
        core = off_ref[off_ref.shape[0] - 1]
        for row in range(count):
            here = eb_ref[:, (row % (count // 2)) * LANES * 8 : (row % (count // 2) + 1) * LANES * 8]
            mine = core == row // (count // 2)
            vec_ref[8 + row : 9 + row, :] = jnp.where(mine, here, jnp.zeros_like(here))

    for kind in range(3):
        place_rows(
            weight.at[kind], off_ref, parts[kind * part_count : (kind + 1) * part_count]
        )
        lanes = slice(kind * LANES, (kind + 1) * LANES)
        value = jnp.concatenate(
            [d_ref[pair, :, :, lanes].reshape(tokens, LANES) for pair in range(d_ref.shape[0])],
            axis=1,
        )
        back[...] += dot_nt(value, weight[kind])
        if kind != 1:
            row = 2 if kind == 0 else 3
            start = pl.multiple_of(group * width, LANES)
            vec_ref[row : row + 1, pl.ds(start, width)] = jnp.sum(
                value.astype(F32), axis=0, keepdims=True
            )

    @pl.when(group == groups - 1)
    def _():
        hat, rate = norm_stats(x_ref[...].astype(F32))
        dh1 = back[...]
        scaled = dh1 * v_ref[V_G1 : V_G1 + 1, :]
        first = jnp.mean(scaled, axis=-1, keepdims=True)
        second = jnp.mean(scaled * hat, axis=-1, keepdims=True)
        out_ref[...] = dres_ref[...] + rate * (scaled - first - hat * second)
        vec_ref[0:1, :] = jnp.sum(dh1 * hat, axis=0, keepdims=True)
        vec_ref[1:2, :] = jnp.sum(dh1, axis=0, keepdims=True)


def entry_back(dqkv, x, dres, one, two, sums, vectors, parts):
    arrays, offsets = parts
    tokens, features = x.shape
    pairs, seqs, rows, _ = dqkv.shape
    width = 2 * LANES
    vec = (8 + 2 * sums[2].shape[1] // features, features)
    groups = features // width
    specs = []
    operands = []
    for kind in range(3):
        for array in arrays:
            specs.append(
                pl.BlockSpec((array.shape[0], width), lambda g, o, k=kind: (0, k * groups + g))
            )
            operands.append(array)
    return pl.pallas_call(
        functools.partial(entry_back_kernel, len(arrays), groups),
        grid_spec=pltpu.PrefetchScalarGridSpec(
            num_scalar_prefetch=1,
            grid=(groups,),
            in_specs=[
                pl.BlockSpec((2, seqs, rows, 3 * LANES), lambda g, o: (g, 0, 0, 0)),
                whole(x.shape),
                whole(x.shape),
                pl.BlockSpec((1,) + x.shape, lambda g, o: (1, 0, 0)),
                pl.BlockSpec((1,) + x.shape, lambda g, o: (1, 0, 0)),
            ]
            + [whole(array.shape) for array in sums]
            + [whole(vectors.shape)]
            + specs,
            out_specs=[whole(x.shape), whole(x.shape), whole(vec)],
            scratch_shapes=[
                pltpu.VMEM((3, features, width), BF16),
                pltpu.VMEM((tokens, features), F32),
            ],
        ),
        out_shape=[
            jax.ShapeDtypeStruct(x.shape, F32),
            jax.ShapeDtypeStruct(x.shape, BF16),
            jax.ShapeDtypeStruct(vec, F32),
        ],
        compiler_params=params(),
        cost_estimate=cost(6 * tokens * features * features, 6 * features * features),
        name="entry_back",
    )(offsets, dqkv, x, dres, one, two, *sums, vectors, *operands)


def combine_kernel(one_ref, two_ref, send_ref, keep_ref):
    total = (one_ref[...].astype(F32) + two_ref[...].astype(F32)).astype(BF16)
    keep_ref[...] = total[:, 0]
    send_ref[...] = total[:, 1]


def last_kernel(one_ref, two_ref, out_ref):
    out_ref[...] = (one_ref[...].astype(F32) + two_ref[...].astype(F32)).astype(BF16)


def combine(one, two, outer):
    rows, columns = one.shape[-2:]
    shape = (outer, 2, one.size // (2 * outer * rows * columns), rows, columns)
    inner = shape[2]
    per = inner
    while per * rows * columns > 256 * 1024 and per % 2 == 0:
        per //= 2
    half = (outer, inner, rows, columns)
    block = pl.BlockSpec((1, 2, per, rows, columns), lambda a, b: (a, 0, b, 0, 0))
    out = pl.BlockSpec((1, per, rows, columns), lambda a, b: (a, b, 0, 0))
    return pl.pallas_call(
        combine_kernel,
        grid=(outer, inner // per),
        in_specs=[block, block],
        out_specs=[out, out],
        out_shape=[jax.ShapeDtypeStruct(half, BF16)] * 2,
        compiler_params=params(),
        cost_estimate=cost(0, 0),
        name="combine",
    )(one.reshape(shape), two.reshape(shape))


def add_last(one, two):
    rows, columns = one.shape[-2:]
    return pl.pallas_call(
        last_kernel,
        out_shape=jax.ShapeDtypeStruct((1, rows, columns), BF16),
        compiler_params=params(),
        cost_estimate=cost(0, 0),
        name="add_last",
    )(one.reshape(1, rows, columns), two.reshape(1, rows, columns))


def merge_kernel(one_ref, two_ref, out_ref):
    out_ref[:, 0] = one_ref[...]
    out_ref[:, 1] = two_ref[...]


def merge(one, two):
    count, rows, columns = one.shape
    block = pl.BlockSpec((1, rows, columns), lambda n: (n, 0, 0))
    return pl.pallas_call(
        merge_kernel,
        grid=(count,),
        in_specs=[block, block],
        out_specs=pl.BlockSpec((1, 2, rows, columns), lambda n: (n, 0, 0, 0)),
        out_shape=jax.ShapeDtypeStruct((count, 2, rows, columns), BF16),
        compiler_params=params(),
        cost_estimate=cost(0, 0),
        name="merge",
    )(one, two).reshape(2 * count, rows, columns)


def tiles(rows, width, columns):
    count = columns // LANES
    height = rows // count
    return height, [
        (across * height, down * LANES, down * height, across * LANES)
        for down in range(width // LANES)
        for across in range(count)
    ]


def pack_kernel(one_ref, two_ref, extra_ref, out_ref):
    rows, columns = one_ref.shape[1:]
    first = out_ref.shape[1] - rows
    out_ref[:, first:] = (one_ref[...].astype(F32) + two_ref[...].astype(F32)).astype(BF16)
    height, moves = tiles(*extra_ref.shape, columns)
    for row, column, to_row, to_column in moves:
        out_ref[0, to_row : to_row + height, to_column : to_column + LANES] = extra_ref[
            row : row + height, column : column + LANES
        ]


def pack(one, two, extra):
    rows, columns = one.shape[-2:]
    return pl.pallas_call(
        pack_kernel,
        out_shape=jax.ShapeDtypeStruct((1, rows + extra.size // columns, columns), BF16),
        compiler_params=params(),
        cost_estimate=cost(0, 0),
        name="pack",
    )(one.reshape(1, rows, columns), two.reshape(1, rows, columns), extra)


class Flow:
    def __init__(self, send, keep, first, labels, order, sizes):
        self.sizes = dict(fsdp=sizes[0], ctx=sizes[1])
        self.labels = list(labels)
        self.order = list(order)
        self.keep = keep
        self.spreading = None
        self.extra = None
        self.received = self.swap(send, first)

    def swap(self, value, label):
        return swap_bit(value, label[0], self.sizes[label[0]], label[1])

    def step(self, event):
        received = after(self.received, event)
        if self.order:
            label = self.order.pop(0)
            place = self.labels.index(label)
            self.labels.pop(place)
            send, self.keep = combine(self.keep, received, 1 << place)
            self.received = self.swap(send, label)
        elif self.spreading is None:
            if self.extra is None:
                self.keep = add_last(self.keep, received)
            else:
                self.keep = pack(self.keep, received, self.extra)
            self.received = None
        else:
            if self.spreading:
                self.keep = merge(self.keep, received)
                self.received = self.swap(self.keep, self.spreading.pop(0))
            else:
                self.far = received
                self.received = None
        return self

    def spread(self):
        self.spreading = [("ctx", bit) for bit in reversed(range(bits_of(self.sizes["ctx"])))]
        self.received = self.swap(self.keep, self.spreading.pop(0))


def finish_kernel(dim, label_ref, near_ref, far_ref, out_ref):
    count, height, _ = near_ref.shape
    rows, columns = out_ref.shape
    if dim == 0:
        rows = rows // count
    else:
        columns = columns // count
    first = height - rows
    low = label_ref[1] & (count - 1)

    def write(source):
        for number in range(count):
            place = number ^ low
            value = source[number, first:].astype(F32)
            if dim == 0:
                out_ref[pl.ds(pl.multiple_of(place * rows, LANES), rows), :] = value
            else:
                out_ref[:, pl.ds(pl.multiple_of(place * columns, LANES), columns)] = value

    pl.when(pl.program_id(0) == 0)(functools.partial(write, near_ref))
    pl.when(pl.program_id(0) == 1)(functools.partial(write, far_ref))


def finish(near, far, table, dim, rows, columns):
    half, height, width = near.shape
    group = half // 2
    shift = bits_of(group)
    if dim == 0:
        shape = (2 * half * rows, columns)
        out_spec = pl.BlockSpec(
            (group * rows, columns), lambda k, n, t: ((k ^ t[0]) * 2 + (n ^ (t[1] >> shift)), 0)
        )
    else:
        shape = (rows, 2 * half * columns)
        out_spec = pl.BlockSpec(
            (rows, group * columns), lambda k, n, t: (0, (k ^ t[0]) * 2 + (n ^ (t[1] >> shift)))
        )

    def block(which):
        return pl.BlockSpec(
            (group, height, width),
            lambda k, n, t: (jnp.where(k == which, n, 1 - which), 0, 0),
        )

    return pl.pallas_call(
        functools.partial(finish_kernel, dim),
        grid_spec=pltpu.PrefetchScalarGridSpec(
            num_scalar_prefetch=1,
            grid=(2, 2),
            in_specs=[block(0), block(1)],
            out_specs=out_spec,
        ),
        out_shape=jax.ShapeDtypeStruct(shape, F32),
        compiler_params=params(),
        cost_estimate=cost(0, 0),
        name="finish",
    )(table, near, far)


def finish_extra_kernel(rows, width, low_bits, label_ref, near_ref, far_ref, *refs):
    out_ref = refs[-1]
    half, _, columns = near_ref.shape
    height, moves = tiles(rows, width, columns)
    for number in range(2 * half):
        source = far_ref if number & 1 else near_ref
        owner = number ^ ((label_ref[1] << 1) | label_ref[0])
        if low_bits is None:
            place, begin, stride = owner, 0, LANES
        else:
            place = owner & ((1 << low_bits) - 1)
            begin = (owner >> low_bits) * LANES
            stride = out_ref.shape[1] // (width // LANES)
        for row, column, from_row, from_column in moves:
            down = pl.ds(pl.multiple_of(place * rows + row, 32), height)
            across = begin + (column // LANES) * stride
            if low_bits is not None:
                across = pl.multiple_of(across, LANES)
            out_ref[down, pl.ds(across, LANES)] = source[
                number >> 1, from_row : from_row + height, from_column : from_column + LANES
            ].astype(F32)


def finish_extra(near, far, table, rows, width, low_bits, shape, events=()):
    half, _, columns = near.shape
    block = pl.BlockSpec((half, rows * width // columns, columns), lambda n, t: (0, 0, 0))
    return pl.pallas_call(
        functools.partial(finish_extra_kernel, rows, width, low_bits),
        grid_spec=pltpu.PrefetchScalarGridSpec(
            num_scalar_prefetch=1,
            grid=(1,),
            in_specs=[block, block] + [whole(event.keep.shape) for event in events],
            out_specs=whole(shape),
        ),
        out_shape=jax.ShapeDtypeStruct(shape, F32),
        compiler_params=params(),
        cost_estimate=cost(0, 0),
        name="finish_extra",
    )(table, near, far, *[event.keep for event in events])


class Total:
    def __init__(self, value, labels, sizes):
        self.keep = value
        self.sizes = dict(fsdp=sizes[0], ctx=sizes[1])
        self.labels = list(labels)
        self.start()

    def start(self):
        self.received = None
        if self.labels:
            name, bit = self.labels.pop(0)
            self.received = swap_bit(self.keep, name, self.sizes[name], bit)

    def step(self, event):
        received = after(self.received, event)
        self.keep = pl.pallas_call(
            total_kernel,
            out_shape=jax.ShapeDtypeStruct(self.keep.shape, F32),
            compiler_params=params(),
            cost_estimate=cost(0, 0),
            name="total",
        )(self.keep, received)
        self.start()
        return self


def total_kernel(one_ref, two_ref, out_ref):
    out_ref[...] = one_ref[...] + two_ref[...]


def body(
    sizes,
    layer_input,
    output_grad,
    segments,
    assignment,
    first_gain,
    first_bias,
    input_weight,
    query_bias,
    value_bias,
    output_weight,
    output_bias,
    second_gain,
    second_bias,
    expand_weight,
    expand_bias,
    shrink_weight,
    shrink_bias,
):
    fsdp_size, ctx_size = sizes
    seqs, rows, features = layer_input.shape
    tokens = seqs * rows
    hidden = expand_weight.shape[1]
    pairs = features // LANES
    units = seqs * pairs // ctx_size
    y_index = lax.axis_index("fsdp").astype(jnp.int32)
    c_index = lax.axis_index("ctx").astype(jnp.int32)
    part = features // fsdp_size
    small = jnp.concatenate(
        [
            first_gain,
            first_bias,
            query_bias,
            value_bias,
            output_bias,
            second_gain,
            second_bias,
            shrink_bias,
            expand_bias,
        ]
    )
    small = small.reshape(1, -1)
    x = layer_input.reshape(tokens, features)
    og = output_grad.reshape(tokens, features)
    place = (sizes, y_index, c_index)
    core = c_index & 1
    starts = jnp.sum(
        (segments[:, None, :] < segments[:, :, None]).astype(jnp.int32), axis=-1
    )[:, None, :]
    unit_seqs = (c_index * units + jnp.arange(units, dtype=jnp.int32)) & (seqs - 1)
    input_gather = Gather(input_weight, 0, place, (1, 0))
    output_gather = Gather(output_weight, 1, place, (0,))
    expand_gather = Gather(expand_weight, 0, place, (1,), core)
    shrink_gather = Gather(shrink_weight, 1, place, (), core)
    gathers = (input_gather, output_gather, expand_gather, shrink_gather)

    group = ((c_index * units) & (seqs - 1)) >> bits_of(units)
    low_bits = bits_of(ctx_size // pairs)
    low = 1 << low_bits
    if fsdp_size == 2:
        owners = jnp.stack([y_index, 1 - y_index])
    else:
        owners = jnp.arange(fsdp_size, dtype=jnp.int32)

    ready = (
        x,
        small,
        starts,
        [gather.first for gather in gathers[1:]],
        [
            unit_seqs,
            owners,
            input_gather.offsets,
            output_gather.offsets,
            feed_scalars(place, hidden, WIDTH, expand_gather.offsets, shrink_gather.offsets),
            jnp.stack([core, c_index >> 1]),
            jnp.concatenate([output_gather.offsets, jnp.stack([y_index, c_index])]),
            jnp.concatenate([input_gather.offsets, core[None]]),
            jnp.stack([group, y_index, c_index & (low - 1)]),
        ],
    )
    x, small, starts, firsts, tables = lax.optimization_barrier(ready)
    for gather, first in zip(gathers[1:], firsts):
        gather.first = first
    unit_seqs, owners, input_gather.offsets, output_gather.offsets, *tables = tables
    feed_table, finish_table, back_table, entry_table, terms_table = tables

    input_gather.fetch()
    if fsdp_size == 2:
        small_other = Event(swap_bit(small, "fsdp", 2, 0))
        input_gather.keep = after(input_gather.keep, small_other)
        shards = [small, small_other.keep]
    else:
        full = lax.all_gather(small, "fsdp", axis=0)
        shards = [full[number] for number in range(fsdp_size)]
    h1, vectors, expand_vector = first_norm(x, shards, owners, hidden)
    other = Event(swap_bit(og, "ctx", ctx_size, 0))
    expand_gather.fetch(input_gather)
    input_gather.exchange()
    norm_done = Event(h1)
    input_gather.keep = after(input_gather.keep, norm_done)
    h1 = norm_done.keep
    input_gather.exchange()
    expand_first = Event(after(expand_gather.keep, input_gather))
    expand_gather.exchange()
    output_gather.fetch(expand_first)
    h1 = after(after(h1, other), expand_first)
    og_other = other.keep
    qkv, token = project(h1, vectors, input_gather.result(), seqs, rows)
    expand_gather.held[0] = expand_first.keep
    project_done = Event(token)
    shrink_gather.fetch(output_gather)
    output_gather.exchange()
    output_gather.keep = after(output_gather.keep, project_done)
    qkv = qkv.reshape(ctx_size, units, rows, 3 * LANES)
    qkv = lax.all_to_all(qkv, "ctx", 0, 0, tiled=True)
    qkv = after(qkv, output_gather)
    att, lse = attend(assignment, unit_seqs, qkv, starts)
    attend_done = Event(lse)
    shrink_gather.keep = after(shrink_gather.keep, attend_done)
    att = lax.all_to_all(att, "ctx", 0, 0, tiled=True)
    received = Event(after(after(att, expand_gather), shrink_gather))
    gathered = lax.all_gather(
        after(h1, received).reshape(seqs, rows, features), "ctx", axis=0
    )
    att = received.keep.reshape(pairs, seqs, rows, LANES)
    output_parts = output_gather.result()
    residual, h2, mixed = branch(att, x, vectors, output_parts)
    h2_other = swap_bit(h2, "ctx", ctx_size, 0)
    send, keep, send_s, keep_s, send_e, keep_e, eb_grad, sb_grad = feed_forward(
        feed_table,
        residual,
        h2,
        h2_other,
        og,
        og_other,
        vectors,
        expand_vector,
        expand_gather.result(),
        shrink_gather.result(),
        sizes,
    )
    other = swap_bit(send, "ctx", ctx_size, 0)

    every = [("fsdp", bit) for bit in reversed(range(bits_of(fsdp_size)))]
    high = [("ctx", bit) for bit in reversed(range(1, bits_of(ctx_size)))]
    flow_s = Flow(send_s, keep_s, every[0], every[1:] + high, every[1:] + high[::-1], sizes)
    flow_e = Flow(
        send_e, keep_e, high[-1], every + high[:-1], every + high[:-1][::-1], sizes
    )
    dres, dmixed, keep_o, send_o, vec_two = branch_back(
        back_table, keep, other, residual, og, mixed, vectors, output_parts, sizes, seqs, rows
    )
    branch_done = Event(vec_two)
    flow_o = Flow(send_o, keep_o, ("ctx", 0), every + high, every + high[::-1], sizes)
    dmixed = dmixed.reshape(ctx_size, units, rows, LANES)
    dmixed = lax.all_to_all(dmixed, "ctx", 0, 0, tiled=True)
    dqkv, token = attend_back(
        assignment, unit_seqs, qkv, dmixed, starts, attend_done.keep
    )
    back_done = Event(token)
    last = flow_s.step(back_done)
    last = flow_e.step(last)
    held = Event(after(dqkv, last))
    keep_i, send_i, token = input_weight_terms(gathered, held.keep, terms_table, low, fsdp_size)
    terms_done = Event(token)
    low_labels = [("ctx", bit) for bit in reversed(range(low_bits))]
    flow_i = Flow(
        send_i,
        keep_i,
        low_labels[0],
        low_labels[1:] + every,
        low_labels[1:] + every,
        sizes,
    )
    last = flow_o.step(terms_done)
    last = flow_i.step(last)
    last = flow_s.step(last)
    last = flow_e.step(last)
    dqkv = lax.all_to_all(dqkv, "ctx", 0, 0, tiled=True).reshape(pairs, seqs, rows, 3 * LANES)
    last = flow_o.step(last)
    while flow_i.received is not None:
        last = flow_i.step(last)
    flow_s.extra = flow_i.keep[0]
    while flow_s.order:
        last = flow_s.step(last)
    last = flow_s.step(last)
    flow_s.spread()
    input_grad, out, sums = entry_back(
        after(dqkv, last),
        x,
        dres,
        keep,
        other,
        [branch_done.keep, sb_grad, eb_grad],
        vectors,
        (input_gather.result()[0], entry_table),
    )
    totals = Total(sums, every + [("ctx", 0)] + high[::-1], sizes)
    last = flow_o.step(totals)
    if flow_e.order:
        last = flow_e.step(last)
    last = flow_s.step(last)
    last = flow_o.step(last)
    last = totals.step(last)
    while flow_e.order:
        last = flow_e.step(last)
    last = flow_s.step(last)
    while flow_o.received is not None:
        last = flow_o.step(last)
    flow_e.extra = flow_o.keep[0]
    last = flow_e.step(last)
    flow_e.spread()
    last = totals.step(last)
    last = flow_e.step(last)
    last = flow_e.step(last)
    while flow_s.spreading:
        last = flow_s.step(last)
    last = totals.step(last)
    last = flow_s.step(last)
    rows_s = hidden // ctx_size
    shrink_done = Event(finish(flow_s.keep, flow_s.far, finish_table, 0, rows_s, part))
    loose = [project_done, back_done, terms_done, branch_done]
    input_done = Event(
        finish_extra(
            flow_s.keep,
            flow_s.far,
            finish_table,
            part >> low_bits,
            3 * LANES,
            low_bits,
            (part, 3 * features),
            loose,
        )
    )
    last = totals.step(last)
    flow_e.received = after(flow_e.received, shrink_done)
    flow_e.received = after(flow_e.received, input_done)
    while flow_e.spreading:
        last = flow_e.step(last)
    while totals.received is not None:
        last = totals.step(last)
    last = flow_e.step(last)
    shrink_grad = shrink_done.keep
    input_grad_w = input_done.keep
    expand_grad = finish(flow_e.keep, flow_e.far, finish_table, 1, part, rows_s)
    output_grad_w = finish_extra(
        flow_e.keep,
        flow_e.far,
        finish_table,
        features // ctx_size,
        part,
        None,
        (features, part),
    )
    sums = totals.keep
    input_grad_w = finish_extra(
        flow_s.keep,
        flow_s.far,
        finish_table,
        part >> low_bits,
        3 * LANES,
        low_bits,
        (part, 3 * features),
        loose,
    )
    rows_s = hidden // ctx_size
    shrink_grad = finish(flow_s.keep, flow_s.far, finish_table, 0, rows_s, part)
    expand_grad = finish(flow_e.keep, flow_e.far, finish_table, 1, part, rows_s)
    output_grad_w = finish_extra(
        flow_e.keep,
        flow_e.far,
        finish_table,
        features // ctx_size,
        part,
        None,
        (features, part),
    )

    def own(vector):
        size = vector.shape[0] // fsdp_size
        return lax.dynamic_slice_in_dim(vector, y_index * size, size, 0)

    return (
        out.reshape(seqs, rows, features),
        input_grad.reshape(seqs, rows, features),
        own(sums[0]),
        own(sums[1]),
        input_grad_w,
        own(sums[2]),
        own(sums[3]),
        output_grad_w,
        own(sums[6]),
        own(sums[4]),
        own(sums[5]),
        expand_grad,
        own(sums[8:].reshape(-1)),
        shrink_grad,
        own(sums[7]),
    )


def solution(mesh):
    sizes = (mesh.shape["fsdp"], mesh.shape["ctx"])
    return jax.shard_map(
        functools.partial(body, sizes),
        mesh=mesh,
        in_specs=(
            P("fsdp", "ctx", None),
            P("fsdp", "ctx", None),
            P("fsdp", None),
            P(),
            P("fsdp"),
            P("fsdp"),
            P("fsdp", None),
            P("fsdp"),
            P("fsdp"),
            P(None, "fsdp"),
            P("fsdp"),
            P("fsdp"),
            P("fsdp"),
            P("fsdp", None),
            P("fsdp"),
            P(None, "fsdp"),
            P("fsdp"),
        ),
        out_specs=(
            P("fsdp", "ctx", None),
            P("fsdp", "ctx", None),
            P("fsdp"),
            P("fsdp"),
            P("fsdp", None),
            P("fsdp"),
            P("fsdp"),
            P(None, "fsdp"),
            P("fsdp"),
            P("fsdp"),
            P("fsdp"),
            P("fsdp", None),
            P("fsdp"),
            P(None, "fsdp"),
            P("fsdp"),
        ),
        check_vma=False,
    )
```

time: 605 us -> 493 us (0.81)
  waiting for transfers between devices: 348 us -> 250 us
  other arithmetic: 31.7 us -> 3.49 us
  local copies, waits for them, and re-layouts: 36.3 us -> 46.3 us
  Pallas kernels: 105 us -> 113 us
    ppermute x51 -> x41, waiting for transfers between devices: 308 us -> 213 us  [swap_bit(): return lax.ppermute(value, axis, [(i, i ^ 1 << bit) for i in range(size)])]
    all_to_all x1, waiting for transfers between devices: 0.01 us -> 18.7 us  [body(): dmixed = lax.all_to_all(dmixed, 'ctx', 0, 0, tiled=True)]
    add x27 -> x3, other arithmetic: 16 us -> 0.02 us  [__init__(): (1 - y_index) * extent + numbers * size]
    unnamed x95 -> x96, local copies, waits for them, and re-layouts: 17.1 us -> 32.6 us
    all_to_all x1, waiting for transfers between devices: 27.3 us -> 14 us  [body(): qkv = lax.all_to_all(qkv, 'ctx', 0, 0, tiled=True)]
    concatenate x13 -> x4, other arithmetic: 12.6 us -> 0.3 us  [the longest x2 0.15 us: __init__(): jnp.concatenate([order, (1 - y_index) * extent + numbers * size])]
    pallas_call x6 -> x32, Pallas kernels: 39.1 us -> 49.8 us  [the longest x11 15.1 us: combine(): pl.pallas_call(combine_kernel, grid=(outer, inner // per), in_specs=[bloc...]
    ppermute x51 -> x41, starting transfers between devices: 42.5 us -> 34.8 us  [swap_bit(): return lax.ppermute(value, axis, [(i, i ^ 1 << bit) for i in range(size)])]
  transfers between devices with their start and end apart: 56 -> 46, of which waited for: 25 -> 25; matrix products, arithmetic and copies ran while one was open for 8% -> 4% of each run, Pallas kernels for 16% -> 19%
where the time goes in v2:
time: 493 us; the launch traced here: 491 us
  waiting for transfers between devices  250 us (51%)
  Pallas kernels  113 us (23%)
  starting transfers between devices  63.1 us (13%)
  local copies, waits for them, and re-layouts  46.3 us (9%)
  between operations  14.6 us (3%)
    ppermute x41, waiting for transfers between devices, swap_bit(): return lax.ppermute(value, axis, [(i, i ^ 1 << bit) for i in range(size)])  213 us
    ppermute x41, starting transfers between devices, swap_bit(): return lax.ppermute(value, axis, [(i, i ^ 1 << bit) for i in range(size)])  34.8 us
    unnamed x96, local copies, waits for them, and re-layouts  32.6 us
    pallas_call x1, Pallas kernels, feed_forward(): pl.pallas_call(functools.partial(ffn_kernel, len(expand_arrays), len(shri...  22 us
    all_to_all x1, waiting for transfers between devices, body(): dmixed = lax.all_to_all(dmixed, 'ctx', 0, 0, tiled=True)  18.7 us
    pallas_call x11, Pallas kernels, combine(): pl.pallas_call(combine_kernel, grid=(outer, inner // per), in_specs=[bloc...  15.1 us
    pallas_call x2, Pallas kernels, finish(): pl.pallas_call(functools.partial(finish_kernel, dim), grid_spec=pltpu.Pre...  14.5 us
    all_to_all x1, waiting for transfers between devices, body(): qkv = lax.all_to_all(qkv, 'ctx', 0, 0, tiled=True)  14 us
  transfers between devices with their start and end apart: 46, of which 25 were waited for; matrix products, arithmetic and copies ran while one was open for 4% of the time, Pallas kernels for 19%

profile of v2, /device:TPU:0, one launch (start us, length us, event | category | flops | bytes accessed | tf_op | source)
XLA Modules:
  0.0 491.3 jit_solution(13322960574130621613)
XLA Ops:
  8.5 3.0 collective-permute-start
  11.5 3.1 convert_reduce_fusion
  22.4 2.3 dynamic_slice.56
  25.9 3.2 constant_dynamic-slice_fusion.9
  29.1 3.8 collective-permute-done.1.refs_1_
  35.9 14.9 %collective-permute-done.2.refs_2_.refs_7_.refs_12_ = bf16[128,3072]{1,0:T(8,128)(2,1)S(1)} collective-permute-done((bf16[128,3072]{1,0:T(8,128)(2,1)S(1)}, bf16[128,3072]{1,0:T(8,128)(2,1)S(1)}, u32[]{:S(2)}, u32[]{:S(2)}) %collective-permute-start.2) | collective-permute-done | bytes 786464 | tf_op jit(solution)/shard_map/ppermute | solution.py:41
  51.3 3.6 collective-permute-done.3.og_other_ref
  58.6 5.0 %project.1 = (bf16[8,4,64,384]{3,2,1,0:T(8,128)(2,1)S(1)}, f32[8,128]{1,0:T(8,128)S(1)}) custom-call(s32[5]{0:T(128)S(1)} %pad_add_fusion.1.off_ref, bf16[256,1024]{1,0:T(8,128)(2,1)S(1)} %get-tuple-element.234.h_ref, f32[8,1024]{1,0:T(8,128)S(1)} %get-tuple-element.188.v_ref, bf16[512,3072]{1,0:T(8,128)(2,1)} %refs_10_.3, ...), custom_call_target="tpu_custom_call" | custom-call | tf_op jit(solution)/shard_map/project/pallas_call | solution.py:220
  64.8 5.2 %all-to-all-start = ((bf16[16,2,64,384]{3,2,1,0:T(8,128)(2,1)}), bf16[16,2,64,384]{3,2,1,0:T(8,128)(2,1)}, u32[]{:S(2)}, u32[]{:S(2)}) async-start(bf16[16,2,64,384]{3,2,1,0:T(8,128)(2,1)} %bitcast.97), calls=%async_computation | async-start | bytes 3145728 | tf_op jit(solution)/shard_map/all_to_all | solution.py:1296
  70.5 13.8 %collective-permute-done.7.refs_1_ = bf16[1024,256]{1,0:T(8,128)(2,1)S(1)} collective-permute-done((bf16[1024,256]{1,0:T(8,128)(2,1)}, bf16[1024,256]{1,0:T(8,128)(2,1)S(1)}, u32[]{:S(2)}, u32[]{:S(2)}) %collective-permute-start.7) | collective-permute-done | bytes 524320 | tf_op jit(solution)/shard_map/ppermute | solution.py:41
  88.1 14.0 %all-to-all-done.qkv_ref = bf16[16,2,64,384]{3,2,1,0:T(8,128)(2,1)} async-done(((bf16[16,2,64,384]{3,2,1,0:T(8,128)(2,1)}), bf16[16,2,64,384]{3,2,1,0:T(8,128)(2,1)}, u32[]{:S(2)}, u32[]{:S(2)}) %all-to-all-start) | async-done | bytes 1572896 | tf_op jit(solution)/shard_map/all_to_all | solution.py:1296
  102.1 9.9 %attend.1 = (bf16[16,2,64,128]{3,2,1,0:T(8,128)(2,1)S(1)}, f32[2,2,1024]{2,1,0:T(2,128)S(1)}) custom-call(s32[16]{0:T(128)S(1)} %copy-done.38, s32[2]{0:T(128)S(1)} %add_and_fusion.seq_ref, bf16[16,2,64,384]{3,2,1,0:T(8,128)(2,1)} %all-to-all-done.qkv_ref, s32[4,1,1024]{2,1,0:T(1,128)S(1)} %broadcast_in_dim.2.start_ref), custom_call_target="tpu_custom_call" | custom-call | tf_op jit(solution)/shard_map/attend/pallas_call | solution.py:315
  112.9 9.2 %all-to-all-start.1 = ((bf16[16,2,64,128]{3,2,1,0:T(8,128)(2,1)}), bf16[16,2,64,128]{3,2,1,0:T(8,128)(2,1)}, u32[]{:S(2)}, u32[]{:S(2)}) async-start(bf16[16,2,64,128]{3,2,1,0:T(8,128)(2,1)} %copy-done.37), calls=%async_computation.1 | async-start | bytes 1048576 | tf_op jit(solution)/shard_map/all_to_all | solution.py:1301
  122.3 9.5 %collective-permute-done.10.refs_4_ = bf16[2048,512]{1,0:T(8,128)(2,1)} collective-permute-done((bf16[2048,512]{1,0:T(8,128)(2,1)}, bf16[2048,512]{1,0:T(8,128)(2,1)}, u32[]{:S(2)}, u32[]{:S(2)}) %collective-permute-start.10) | collective-permute-done | bytes 2097184 | tf_op jit(solution)/shard_map/ppermute | solution.py:41
  131.8 4.8 all-to-all-done.1
  140.9 3.0 branch.1
  144.0 1.9 collective-permute-done.11.h2_other_ref
  146.0 22.0 %feed_forward.1 = (f32[2,256,1024]{2,1,0:T(8,128)}, f32[2,256,1024]{2,1,0:T(8,128)}, bf16[1,4,2,256,512]{4,3,2,1,0:T(8,128)(2,1)}, bf16[1,4,2,256,512]{4,3,2,1,0...) custom-call(s32[9]{0:T(128)S(1)} %concatenate.23.sc_ref, ...), custom_call_target="tpu_custom_call" | custom-call | tf_op jit(solution)/shard_map/feed_forward/pallas_call | solution.py:637
  168.5 6.0 %collective-permute-done.12.dh2_other_ref.two_ref = f32[2,256,1024]{2,1,0:T(8,128)S(1)} collective-permute-done((f32[2,256,1024]{2,1,0:T(8,128)}, f32[2,256,1024]{2,1,0:T(8,128)S(1)}, u32[]{:S(2)}, u32[]{:S(2)}) %collective-permute-start.12) | collective-permute-done | bytes 2097184 | tf_op jit(solution)/shard_map/ppermute | solution.py:41
  175.9 5.3 %branch_back.1 = (f32[256,1024]{1,0:T(8,128)S(1)}, bf16[8,4,64,128]{3,2,1,0:T(8,128)(2,1)S(1)}, bf16[2,8,64,512]{3,2,1,0:T(8,128)(2,1)S(1)}, bf16[2,8,64,512]{3,2,1,0:T(8,128)(2,1)S(1)}, f32[8,1024]{1,0:T(8,128)S(1)}) custom-call(s32[5]{0:T(128)S(1)} %pad_add_fusion.4.sc_ref, f32[2,256,1024]{2,1,0:T(8,128)} %get-tuple-element.216.dh2_ref.one_ref, ...), custom_call_target="tpu_custom_call" | custom-call | tf_op jit(solution)/shard_map/branch_back/pallas_call | solution.py:730
  184.9 4.5 all-to-all-start.2
  191.0 18.7 %all-to-all-done.2.grad_ref = bf16[16,2,64,128]{3,2,1,0:T(8,128)(2,1)} async-done(((bf16[16,2,64,128]{3,2,1,0:T(8,128)(2,1)}), bf16[16,2,64,128]{3,2,1,0:T(8,128)(2,1)}, u32[]{:S(2)}, u32[]{:S(2)}) %all-to-all-start.2) | async-done | bytes 524320 | tf_op jit(solution)/shard_map/all_to_all | solution.py:1337
  209.6 10.4 %attend_back.1 = (bf16[16,2,64,384]{3,2,1,0:T(8,128)(2,1)S(1)}, f32[8,128]{1,0:T(8,128)S(1)}) custom-call(s32[16]{0:T(128)S(1)} %copy-done.38, s32[2]{0:T(128)S(1)} %add_and_fusion.seq_ref, bf16[16,2,64,384]{3,2,1,0:T(8,128)(2,1)} %all-to-all-done.qkv_ref, bf16[16,2,64,128]{3,2,1,0:T(8,128)(2,1)} %all-to-all-done.2.grad_ref, ...), custom_call_target="tpu_custom_call" | custom-call | tf_op jit(solution)/shard_map/attend_back/pallas_call | solution.py:423
  221.2 9.3 %all-to-all-start.3 = ((bf16[16,2,64,384]{3,2,1,0:T(8,128)(2,1)}), bf16[16,2,64,384]{3,2,1,0:T(8,128)(2,1)}, u32[]{:S(2)}, u32[]{:S(2)}) async-start(bf16[16,2,64,384]{3,2,1,0:T(8,128)(2,1)} %copy-done.4), calls=%async_computation.3 | async-start | bytes 3145728 | tf_op jit(solution)/shard_map/all_to_all | solution.py:1360
  232.4 3.8 combine.11
  237.9 14.8 %collective-permute-done.13 = bf16[2,4,1,512,256]{4,3,1,0,2:T(8,128)(2,1)} collective-permute-done((bf16[2,4,1,512,256]{4,3,1,0,2:T(8,128)(2,1)}, bf16[2,4,1,512,256]{4,3,1,0,2:T(8,128)(2,1)}, u32[]{:S(2)}, u32[]{:S(2)}) %collective-permute-start.13) | collective-permute-done | bytes 2097184 | tf_op jit(solution)/shard_map/ppermute | solution.py:41
  252.7 2.6 combine.12
  259.4 5.5 %input_weight_terms.1 = (bf16[1,2,256,384]{3,2,1,0:T(8,128)(2,1)S(1)}, bf16[1,2,256,384]{3,2,1,0:T(8,128)(2,1)S(1)}, f32[8,128]{1,0:T(8,128)S(1)}) custom-call(s32[3]{0:T(128)S(1)} %get-tuple-element.233.sc_ref, bf16[16,4,64,1024]{3,2,1,0:T(8,128)(2,1)} %all-gather.2.cloned.1.call-done.h_ref, bf16[16,2,64,384]{3,2,1,0:T(8,128)(2,1)S(1)} %copy-done.5), custom_call_target="tpu_custom_call" | custom-call | tf_op jit(solution)/shard_map/input_weight_terms/pallas_call | solution.py:786
  267.2 16.3 %collective-permute-done.16 = bf16[4,1,256,512]{3,2,1,0:T(8,128)(2,1)} collective-permute-done((bf16[4,1,256,512]{3,2,1,0:T(8,128)(2,1)}, bf16[4,1,256,512]{3,2,1,0:T(8,128)(2,1)}, u32[]{:S(2)}, u32[]{:S(2)}) %collective-permute-start.16) | collective-permute-done | bytes 1048608 | tf_op jit(solution)/shard_map/ppermute | solution.py:41
  287.8 2.0 combine.16
  289.8 4.0 collective-permute-done.21
  298.8 2.5 collective-permute-start.22
  302.8 9.9 %collective-permute-done.22 = bf16[1,1,256,512]{3,2,1,0:T(8,128)(2,1)S(1)} collective-permute-done((bf16[1,1,256,512]{3,2,1,0:T(8,128)(2,1)S(1)}, bf16[1,1,256,512]{3,2,1,0:T(8,128)(2,1)S(1)}, u32[]{:S(2)}, u32[]{:S(2)}) %collective-permute-start.22) | collective-permute-done | bytes 262176 | tf_op jit(solution)/shard_map/ppermute | solution.py:41
  316.8 8.2 %entry_back.1 = (f32[256,1024]{1,0:T(8,128)}, bf16[256,1024]{1,0:T(8,128)(2,1)}, f32[12,1024]{1,0:T(8,128)S(1)}) custom-call(s32[6]{0:T(128)S(1)} %pad_add_fusion.5.off_ref, bf16[8,4,64,384]{3,2,1,0:T(8,128)(2,1)} %bitcast.15.d_ref, bf16[256,1024]{1,0:T(8,128)(2,1)S(1)} %bitcast.86, f32[256,1024]{1,0:T(8,128)S(1)} %copy-done.23, ...), custom_call_target="tpu_custom_call" | custom-call | tf_op jit(solution)/shard_map/entry_back/pallas_call | solution.py:882
  327.1 9.0 %collective-permute-done.25.two_ref = bf16[1,448,512]{2,1,0:T(8,128)(2,1)} collective-permute-done((bf16[1,448,512]{2,1,0:T(8,128)(2,1)}, bf16[1,448,512]{2,1,0:T(8,128)(2,1)}, u32[]{:S(2)}, u32[]{:S(2)}) %collective-permute-start.25) | collective-permute-done | bytes 458784 | tf_op jit(solution)/shard_map/ppermute | solution.py:41
  340.9 20.4 %collective-permute-done.24 = bf16[2,1,64,512]{3,2,0,1:T(8,128)(2,1)S(1)} collective-permute-done((bf16[2,1,64,512]{3,2,0,1:T(8,128)(2,1)S(1)}, bf16[2,1,64,512]{3,2,0,1:T(8,128)(2,1)S(1)}, u32[]{:S(2)}, u32[]{:S(2)}) %collective-permute-start.24) | collective-permute-done | bytes 131104 | tf_op jit(solution)/shard_map/ppermute | solution.py:41
  362.6 2.9 collective-permute-start.31
  365.6 13.6 %collective-permute-done.32 = bf16[1,1,64,512]{3,2,1,0:T(8,128)(2,1)S(1)} collective-permute-done((bf16[1,1,64,512]{3,2,1,0:T(8,128)(2,1)S(1)}, bf16[1,1,64,512]{3,2,1,0:T(8,128)(2,1)S(1)}, u32[]{:S(2)}, u32[]{:S(2)}) %collective-permute-start.32) | collective-permute-done | bytes 65568 | tf_op jit(solution)/shard_map/ppermute | solution.py:41
  380.7 15.3 %collective-permute-done.33.two_ref = bf16[1,640,256]{2,1,0:T(8,128)(2,1)S(1)} collective-permute-done((bf16[1,640,256]{2,1,0:T(8,128)(2,1)S(1)}, bf16[1,640,256]{2,1,0:T(8,128)(2,1)S(1)}, u32[]{:S(2)}, u32[]{:S(2)}) %collective-permute-start.33) | collective-permute-done | bytes 327712 | tf_op jit(solution)/shard_map/ppermute | solution.py:41
  396.1 14.8 %collective-permute-done.34.two_ref = bf16[2,640,256]{2,1,0:T(8,128)(2,1)S(1)} collective-permute-done((bf16[2,640,256]{2,1,0:T(8,128)(2,1)S(1)}, bf16[2,640,256]{2,1,0:T(8,128)(2,1)S(1)}, u32[]{:S(2)}, u32[]{:S(2)}) %collective-permute-start.34) | collective-permute-done | bytes 655392 | tf_op jit(solution)/shard_map/ppermute | solution.py:41
  411.1 2.3 merge.10
  415.4 30.6 %collective-permute-done.37.two_ref = f32[12,1024]{1,0:T(8,128)S(1)} collective-permute-done((f32[12,1024]{1,0:T(8,128)S(1)}, f32[12,1024]{1,0:T(8,128)S(1)}, u32[]{:S(2)}, u32[]{:S(2)}) %collective-permute-start.37) | collective-permute-done | bytes 49184 | tf_op jit(solution)/shard_map/ppermute | solution.py:41
  446.3 4.0 collective-permute-done.38.two_ref
  454.0 2.0 copy-done
  456.0 7.5 %finish.4 = f32[4096,512]{1,0:T(8,128)} custom-call(s32[2]{0:T(128)S(1)} %get-tuple-element.315.label_ref, bf16[8,448,512]{2,1,0:T(8,128)(2,1)S(1)} %bitcast.75, bf16[8,448,512]{2,1,0:T(8,128)(2,1)} %copy-done.40), custom_call_target="tpu_custom_call" | custom-call | tf_op jit(solution)/shard_map/finish/pallas_call | solution.py:1094
  463.6 5.6 %finish_extra.3 = f32[512,3072]{1,0:T(8,128)} custom-call(s32[2]{0:T(128)S(1)} %get-tuple-element.315.label_ref, bf16[8,448,512]{2,1,0:T(8,128)(2,1)S(1)} %bitcast.76, bf16[8,448,512]{2,1,0:T(8,128)(2,1)} %copy-done.40, f32[8,128]{1,0:T(8,128)S(1)} %get-tuple-element.318.refs_0_, f32[8,128]{1,0:T(8,128)S(1)} %get-tuple-element.319.refs_1_, ...), custom_call_target="tpu_custom_call" | custom-call | tf_op jit(solution)/shard_map/finish_extra/pallas_call | solution.py:1135
  469.2 3.1 finish_extra.4
  472.3 6.9 %finish.3 = f32[512,4096]{1,0:T(8,128)} custom-call(s32[2]{0:T(128)S(1)} %get-tuple-element.315.label_ref, bf16[8,640,256]{2,1,0:T(8,128)(2,1)S(1)} %bitcast.79, bf16[8,640,256]{2,1,0:T(8,128)(2,1)} %collective-permute-done.39.far_ref), custom_call_target="tpu_custom_call" | custom-call | tf_op jit(solution)/shard_map/finish/pallas_call | solution.py:1094
  (209 shorter events, 82.8 us)
Async XLA Ops:
  8.5 24.4 %collective-permute-start = (bf16[128,3072]{1,0:T(8,128)(2,1)S(1)}, bf16[128,3072]{1,0:T(8,128)(2,1)S(1)}, u32[]{:S(2)}, u32[]{:S(2)}) collective-permute-start(bf16[128,3072]{1,0:T(8,128)(2,1)S(1)} %constant_dynamic-slice_fusion.8), channel_id=1, source_target_pairs={{0,16},{16,0},{1,17},{17,1},{2,18},{18,2},{3,19},{19,3},{4,20},{20... | collective-permute-start | bytes 2359304 | tf_op jit(solution)/shard_map/ppermute | solution.py:41
  29.1 3.8 collective-permute-start.1
  32.9 17.9 %collective-permute-start.2 = (bf16[128,3072]{1,0:T(8,128)(2,1)S(1)}, bf16[128,3072]{1,0:T(8,128)(2,1)S(1)}, u32[]{:S(2)}, u32[]{:S(2)}) collective-permute-start(bf16[128,3072]{1,0:T(8,128)(2,1)S(1)} %collective-permute-done.refs_1_.refs_6_.refs_11_), channel_id=1, source_target_pairs={{0,2},{1,3},{2,0},{3,1},{4,6},{5,7},{6,4},{7,5},{8,10},{9,11},{10,... | collective-permute-start | bytes 2359304 | tf_op jit(solution)/shard_map/ppermute | solution.py:41
  34.4 23.2 %collective-permute-start.4 = (bf16[256,2048]{1,0:T(8,128)(2,1)S(1)}, bf16[256,2048]{1,0:T(8,128)(2,1)S(1)}, u32[]{:S(2)}, u32[]{:S(2)}) collective-permute-start(bf16[256,2048]{1,0:T(8,128)(2,1)S(1)} %copy-done.42), channel_id=1, source_target_pairs={{0,16},{16,0},{1,17},{17,1},{2,18},{18,2},{3,19},{19,3},{4,20},{20... | collective-permute-start | bytes 3145736 | tf_op jit(solution)/shard_map/ppermute | solution.py:41
  50.8 6.8 %collective-permute-start.5 = (bf16[128,3072]{1,0:T(8,128)(2,1)S(1)}, bf16[128,3072]{1,0:T(8,128)(2,1)S(1)}, u32[]{:S(2)}, u32[]{:S(2)}) collective-permute-start(bf16[128,3072]{1,0:T(8,128)(2,1)S(1)} %collective-permute-done.2.refs_2_.refs_7_.refs_12_), channel_id=1, source_target_pairs={{0,1},{1,0},{2,3},{3,2},{4,5},{5,4},{6,7},{7,6},{8,9},{9,8},{10,11... | collective-permute-start | bytes 2359304 | tf_op jit(solution)/shard_map/ppermute | solution.py:41
  50.8 6.8 %collective-permute-start.6 = (bf16[128,3072]{1,0:T(8,128)(2,1)S(1)}, bf16[128,3072]{1,0:T(8,128)(2,1)S(1)}, u32[]{:S(2)}, u32[]{:S(2)}) collective-permute-start(bf16[128,3072]{1,0:T(8,128)(2,1)S(1)} %collective-permute-done.refs_1_.refs_6_.refs_11_), channel_id=1, source_target_pairs={{0,1},{1,0},{2,3},{3,2},{4,5},{5,4},{6,7},{7,6},{8,9},{9,8},{10,11... | collective-permute-start | bytes 2359304 | tf_op jit(solution)/shard_map/ppermute | solution.py:41
  51.3 3.6 collective-permute-start.3
  64.8 37.4 %copy-start.38 = (s32[16]{0:T(128)S(1)}, s32[16]{0:T(128)}, u32[]{:S(2)}) copy-start(s32[16]{0:T(128)} %table.3) | copy-start | bytes 196
  64.8 37.4 %all-to-all-start = ((bf16[16,2,64,384]{3,2,1,0:T(8,128)(2,1)}), bf16[16,2,64,384]{3,2,1,0:T(8,128)(2,1)}, u32[]{:S(2)}, u32[]{:S(2)}) async-start(bf16[16,2,64,384]{3,2,1,0:T(8,128)(2,1)} %bitcast.97), calls=%async_computation | async-start | bytes 3145728 | tf_op jit(solution)/shard_map/all_to_all | solution.py:1296
  69.9 14.4 %collective-permute-start.7 = (bf16[1024,256]{1,0:T(8,128)(2,1)}, bf16[1024,256]{1,0:T(8,128)(2,1)S(1)}, u32[]{:S(2)}, u32[]{:S(2)}) collective-permute-start(bf16[1024,256]{1,0:T(8,128)(2,1)} %constant_dynamic-slice_fusion.10), channel_id=1, source_target_pairs={{0,16},{16,0},{1,17},{17,1},{2,18},{18,2},{3,19},{19,3},{4,20},{20... | collective-permute-start | bytes 1572872 | tf_op jit(solution)/shard_map/ppermute | solution.py:41
  84.3 47.4 %collective-permute-start.10 = (bf16[2048,512]{1,0:T(8,128)(2,1)}, bf16[2048,512]{1,0:T(8,128)(2,1)}, u32[]{:S(2)}, u32[]{:S(2)}) collective-permute-start(bf16[2048,512]{1,0:T(8,128)(2,1)} %constant_dynamic-slice_fusion.9), channel_id=1, source_target_pairs={{0,16},{16,0},{1,17},{17,1},{2,18},{18,2},{3,19},{19,3},{4,20},{20... | collective-permute-start | bytes 6291464 | tf_op jit(solution)/shard_map/ppermute | solution.py:41
  84.8 2.5 collective-permute-start.8
  85.6 46.1 %collective-permute-start.9 = (bf16[256,2048]{1,0:T(8,128)(2,1)}, bf16[256,2048]{1,0:T(8,128)(2,1)}, u32[]{:S(2)}, u32[]{:S(2)}) collective-permute-start(bf16[256,2048]{1,0:T(8,128)(2,1)} %copy-done.30), channel_id=1, source_target_pairs={{0,2},{1,3},{2,0},{3,1},{4,6},{5,7},{6,4},{7,5},{8,10},{9,11},{10,... | collective-permute-start | bytes 3145736 | tf_op jit(solution)/shard_map/ppermute | solution.py:41
  112.9 23.7 %all-to-all-start.1 = ((bf16[16,2,64,128]{3,2,1,0:T(8,128)(2,1)}), bf16[16,2,64,128]{3,2,1,0:T(8,128)(2,1)}, u32[]{:S(2)}, u32[]{:S(2)}) async-start(bf16[16,2,64,128]{3,2,1,0:T(8,128)(2,1)} %copy-done.37), calls=%async_computation.1 | async-start | bytes 1048576 | tf_op jit(solution)/shard_map/all_to_all | solution.py:1301
  122.0 135.9 %all-gather.2.cloned.1.call-start = ((), (), s32[]{:S(2)}) async-start(), calls=%async_computation.4 | async-start | bytes 8912896 | tf_op jit(solution)/shard_map/all_gather | solution.py:1303
  144.0 2.0 collective-permute-start.11
  146.0 29.9 %copy-start.17 = (bf16[1024,256]{1,0:T(8,128)(2,1)S(1)}, bf16[1024,256]{1,0:T(8,128)(2,1)}, u32[]{:S(2)}) copy-start(bf16[1024,256]{1,0:T(8,128)(2,1)} %copy-done.15) | copy-start | bytes 1572868
  167.9 6.6 %collective-permute-start.12 = (f32[2,256,1024]{2,1,0:T(8,128)}, f32[2,256,1024]{2,1,0:T(8,128)S(1)}, u32[]{:S(2)}, u32[]{:S(2)}) collective-permute-start(f32[2,256,1024]{2,1,0:T(8,128)} %get-tuple-element.217), channel_id=1, source_target_pairs={{0,1},{1,0},{2,3},{3,2},{4,5},{5,4},{6,7},{7,6},{8,9},{9,8},{10,11... | collective-permute-start | bytes 6291464 | tf_op jit(solution)/shard_map/ppermute | solution.py:41
  168.1 62.7 %collective-permute-start.14 = (bf16[1,4,2,256,512]{4,3,2,1,0:T(8,128)(2,1)}, bf16[1,4,2,256,512]{4,3,2,1,0:T(8,128)(2,1)}, u32[]{:S(2)}, u32[]{:S(2)}) collective-permute-start(bf16[1,4,2,256,512]{4,3,2,1,0:T(8,128)(2,1)} %get-tuple-element.225), channel_id=1, source_target_pairs={{0,16},{16,0},{1,17},{17,1},{2,18},{18,2},{3,19},{19,3},{4,20},{20... | collective-permute-start | bytes 6291464 | tf_op jit(solution)/shard_map/ppermute | solution.py:41
  184.9 24.7 %all-to-all-start.2 = ((bf16[16,2,64,128]{3,2,1,0:T(8,128)(2,1)}), bf16[16,2,64,128]{3,2,1,0:T(8,128)(2,1)}, u32[]{:S(2)}, u32[]{:S(2)}) async-start(bf16[16,2,64,128]{3,2,1,0:T(8,128)(2,1)} %bitcast.107), calls=%async_computation.2 | async-start | bytes 1048576 | tf_op jit(solution)/shard_map/all_to_all | solution.py:1337
  189.4 63.4 %collective-permute-start.13 = (bf16[2,4,1,512,256]{4,3,1,0,2:T(8,128)(2,1)}, bf16[2,4,1,512,256]{4,3,1,0,2:T(8,128)(2,1)}, u32[]{:S(2)}, u32[]{:S(2)}) collective-permute-start(bf16[2,4,1,512,256]{4,3,1,0,2:T(8,128)(2,1)} %bitcast.133), channel_id=1, source_target_pairs={{0,2},{1,3},{2,0},{3,1},{4,6},{5,7},{6,4},{7,5},{8,10},{9,11},{10,... | collective-permute-start | bytes 6291464 | tf_op jit(solution)/shard_map/ppermute | solution.py:41
  221.2 93.3 %all-to-all-start.3 = ((bf16[16,2,64,384]{3,2,1,0:T(8,128)(2,1)}), bf16[16,2,64,384]{3,2,1,0:T(8,128)(2,1)}, u32[]{:S(2)}, u32[]{:S(2)}) async-start(bf16[16,2,64,384]{3,2,1,0:T(8,128)(2,1)} %copy-done.4), calls=%async_computation.3 | async-start | bytes 3145728 | tf_op jit(solution)/shard_map/all_to_all | solution.py:1360
  230.5 34.5 %collective-permute-start.18 = (bf16[2,8,64,512]{3,2,1,0:T(8,128)(2,1)}, bf16[2,8,64,512]{3,2,1,0:T(8,128)(2,1)}, u32[]{:S(2)}, u32[]{:S(2)}) collective-permute-start(bf16[2,8,64,512]{3,2,1,0:T(8,128)(2,1)} %copy-done.39), channel_id=1, source_target_pairs={{0,1},{1,0},{2,3},{3,2},{4,5},{5,4},{6,7},{7,6},{8,9},{9,8},{10,11... | collective-permute-start | bytes 3145736 | tf_op jit(solution)/shard_map/ppermute | solution.py:41
  236.2 47.2 %collective-permute-start.16 = (bf16[4,1,256,512]{3,2,1,0:T(8,128)(2,1)}, bf16[4,1,256,512]{3,2,1,0:T(8,128)(2,1)}, u32[]{:S(2)}, u32[]{:S(2)}) collective-permute-start(bf16[4,1,256,512]{3,2,1,0:T(8,128)(2,1)} %get-tuple-element.232), channel_id=1, source_target_pairs={{0,2},{1,3},{2,0},{3,1},{4,6},{5,7},{6,4},{7,5},{8,10},{9,11},{10,... | collective-permute-start | bytes 3145736 | tf_op jit(solution)/shard_map/ppermute | solution.py:41
  256.4 31.5 %collective-permute-start.15 = (bf16[1,4,512,256]{3,2,1,0:T(8,128)(2,1)}, bf16[1,4,512,256]{3,2,1,0:T(8,128)(2,1)}, u32[]{:S(2)}, u32[]{:S(2)}) collective-permute-start(bf16[1,4,512,256]{3,2,1,0:T(8,128)(2,1)} %get-tuple-element.230), channel_id=1, source_target_pairs={{0,16},{16,0},{1,17},{17,1},{2,18},{18,2},{3,19},{19,3},{4,20},{20... | collective-permute-start | bytes 3145736 | tf_op jit(solution)/shard_map/ppermute | solution.py:41
  264.9 2.2 collective-permute-start.17
  266.6 27.3 %collective-permute-start.21 = (bf16[1,8,64,512]{3,2,1,0:T(8,128)(2,1)S(1)}, bf16[1,8,64,512]{3,2,1,0:T(8,128)(2,1)S(1)}, u32[]{:S(2)}, u32[]{:S(2)}) collective-permute-start(bf16[1,8,64,512]{3,2,1,0:T(8,128)(2,1)S(1)} %get-tuple-element.253), channel_id=1, source_target_pairs={{0,16},{16,0},{1,17},{17,1},{2,18},{18,2},{3,19},{19,3},{4,20},{20... | collective-permute-start | bytes 1572872 | tf_op jit(solution)/shard_map/ppermute | solution.py:41
  284.8 13.8 %collective-permute-start.19 = (bf16[2,1,256,512]{3,2,0,1:T(8,128)(2,1)S(1)}, bf16[2,1,256,512]{3,2,0,1:T(8,128)(2,1)S(1)}, u32[]{:S(2)}, u32[]{:S(2)}) collective-permute-start(bf16[2,1,256,512]{3,2,0,1:T(8,128)(2,1)S(1)} %bitcast.122), channel_id=1, source_target_pairs={{0,4},{1,5},{2,6},{3,7},{4,0},{5,1},{6,2},{7,3},{8,12},{9,13},{10,... | collective-permute-start | bytes 1572872 | tf_op jit(solution)/shard_map/ppermute | solution.py:41
  286.4 10.5 %collective-permute-start.20 = (bf16[1,1,256,384]{3,2,1,0:T(8,128)(2,1)S(1)}, bf16[1,1,256,384]{3,2,1,0:T(8,128)(2,1)S(1)}, u32[]{:S(2)}, u32[]{:S(2)}) collective-permute-start(bf16[1,1,256,384]{3,2,1,0:T(8,128)(2,1)S(1)} %get-tuple-element.251), channel_id=1, source_target_pairs={{0,16},{16,0},{1,17},{17,1},{2,18},{18,2},{3,19},{19,3},{4,20},{20... | collective-permute-start | bytes 589832 | tf_op jit(solution)/shard_map/ppermute | solution.py:41
  298.8 14.0 %collective-permute-start.22 = (bf16[1,1,256,512]{3,2,1,0:T(8,128)(2,1)S(1)}, bf16[1,1,256,512]{3,2,1,0:T(8,128)(2,1)S(1)}, u32[]{:S(2)}, u32[]{:S(2)}) collective-permute-start(bf16[1,1,256,512]{3,2,1,0:T(8,128)(2,1)S(1)} %get-tuple-element.261), channel_id=1, source_target_pairs={{0,8},{1,9},{2,10},{3,11},{4,12},{5,13},{6,14},{7,15},{8,0},{9,1},... | collective-permute-start | bytes 786440 | tf_op jit(solution)/shard_map/ppermute | solution.py:41
  301.2 24.7 %collective-permute-start.26 = (bf16[2,1,512,256]{3,2,0,1:T(8,128)(2,1)}, bf16[2,1,512,256]{3,2,0,1:T(8,128)(2,1)}, u32[]{:S(2)}, u32[]{:S(2)}) collective-permute-start(bf16[2,1,512,256]{3,2,0,1:T(8,128)(2,1)} %bitcast.46), channel_id=1, source_target_pairs={{0,4},{1,5},{2,6},{3,7},{4,0},{5,1},{6,2},{7,3},{8,12},{9,13},{10,... | collective-permute-start | bytes 1572872 | tf_op jit(solution)/shard_map/ppermute | solution.py:41
  313.6 22.5 %collective-permute-start.25 = (bf16[1,448,512]{2,1,0:T(8,128)(2,1)}, bf16[1,448,512]{2,1,0:T(8,128)(2,1)}, u32[]{:S(2)}, u32[]{:S(2)}) collective-permute-start(bf16[1,448,512]{2,1,0:T(8,128)(2,1)} %pack.2.one_ref), channel_id=1, source_target_pairs={{0,8},{1,9},{2,10},{3,11},{4,12},{5,13},{6,14},{7,15},{8,0},{9,1},... | collective-permute-start | bytes 1376264 | tf_op jit(solution)/shard_map/ppermute | solution.py:41
  313.6 11.3 %collective-permute-start.23 = (bf16[4,1,64,512]{3,2,1,0:T(8,128)(2,1)}, bf16[4,1,64,512]{3,2,1,0:T(8,128)(2,1)}, u32[]{:S(2)}, u32[]{:S(2)}) collective-permute-start(bf16[4,1,64,512]{3,2,1,0:T(8,128)(2,1)} %get-tuple-element.273), channel_id=1, source_target_pairs={{0,2},{1,3},{2,0},{3,1},{4,6},{5,7},{6,4},{7,5},{8,10},{9,11},{10,... | collective-permute-start | bytes 786440 | tf_op jit(solution)/shard_map/ppermute | solution.py:41
  337.3 24.0 %collective-permute-start.27 = (bf16[2,448,512]{2,1,0:T(8,128)(2,1)S(1)}, bf16[2,448,512]{2,1,0:T(8,128)(2,1)S(1)}, u32[]{:S(2)}, u32[]{:S(2)}) collective-permute-start(bf16[2,448,512]{2,1,0:T(8,128)(2,1)S(1)} %bitcast.87), channel_id=1, source_target_pairs={{0,4},{1,5},{2,6},{3,7},{4,0},{5,1},{6,2},{7,3},{8,12},{9,13},{10,... | collective-permute-start | bytes 2752520 | tf_op jit(solution)/shard_map/ppermute | solution.py:41
  338.4 22.9 %collective-permute-start.24 = (bf16[2,1,64,512]{3,2,0,1:T(8,128)(2,1)S(1)}, bf16[2,1,64,512]{3,2,0,1:T(8,128)(2,1)S(1)}, u32[]{:S(2)}, u32[]{:S(2)}) collective-permute-start(bf16[2,1,64,512]{3,2,0,1:T(8,128)(2,1)S(1)} %bitcast.123), channel_id=1, source_target_pairs={{0,4},{1,5},{2,6},{3,7},{4,0},{5,1},{6,2},{7,3},{8,12},{9,13},{10,... | collective-permute-start | bytes 393224 | tf_op jit(solution)/shard_map/ppermute | solution.py:41
  339.4 21.9 %collective-permute-start.28 = (f32[12,1024]{1,0:T(8,128)S(1)}, f32[12,1024]{1,0:T(8,128)S(1)}, u32[]{:S(2)}, u32[]{:S(2)}) collective-permute-start(f32[12,1024]{1,0:T(8,128)S(1)} %get-tuple-element.285.one_ref), channel_id=1, source_target_pairs={{0,16},{16,0},{1,17},{17,1},{2,18},{18,2},{3,19},{19,3},{4,20},{20... | collective-permute-start | bytes 147464 | tf_op jit(solution)/shard_map/ppermute | solution.py:41
  361.5 49.5 %collective-permute-start.29 = (bf16[4,448,512]{2,1,0:T(8,128)(2,1)S(1)}, bf16[4,448,512]{2,1,0:T(8,128)(2,1)S(1)}, u32[]{:S(2)}, u32[]{:S(2)}) collective-permute-start(bf16[4,448,512]{2,1,0:T(8,128)(2,1)S(1)} %bitcast.80), channel_id=1, source_target_pairs={{0,2},{1,3},{2,0},{3,1},{4,6},{5,7},{6,4},{7,5},{8,10},{9,11},{10,... | collective-permute-start | bytes 5505032 | tf_op jit(solution)/shard_map/ppermute | solution.py:41
  362.6 16.6 %collective-permute-start.31 = (bf16[1,1,512,256]{3,2,1,0:T(8,128)(2,1)S(1)}, bf16[1,1,512,256]{3,2,1,0:T(8,128)(2,1)S(1)}, u32[]{:S(2)}, u32[]{:S(2)}) collective-permute-start(bf16[1,1,512,256]{3,2,1,0:T(8,128)(2,1)S(1)} %get-tuple-element.292), channel_id=1, source_target_pairs={{0,8},{1,9},{2,10},{3,11},{4,12},{5,13},{6,14},{7,15},{8,0},{9,1},... | collective-permute-start | bytes 786440 | tf_op jit(solution)/shard_map/ppermute | solution.py:41
  365.5 13.6 %collective-permute-start.32 = (bf16[1,1,64,512]{3,2,1,0:T(8,128)(2,1)S(1)}, bf16[1,1,64,512]{3,2,1,0:T(8,128)(2,1)S(1)}, u32[]{:S(2)}, u32[]{:S(2)}) collective-permute-start(bf16[1,1,64,512]{3,2,1,0:T(8,128)(2,1)S(1)} %get-tuple-element.294), channel_id=1, source_target_pairs={{0,8},{1,9},{2,10},{3,11},{4,12},{5,13},{6,14},{7,15},{8,0},{9,1},... | collective-permute-start | bytes 196616 | tf_op jit(solution)/shard_map/ppermute | solution.py:41
  379.3 16.7 %collective-permute-start.33 = (bf16[1,640,256]{2,1,0:T(8,128)(2,1)S(1)}, bf16[1,640,256]{2,1,0:T(8,128)(2,1)S(1)}, u32[]{:S(2)}, u32[]{:S(2)}) collective-permute-start(bf16[1,640,256]{2,1,0:T(8,128)(2,1)S(1)} %pack.3.one_ref), channel_id=1, source_target_pairs={{0,8},{1,9},{2,10},{3,11},{4,12},{5,13},{6,14},{7,15},{8,0},{9,1},... | collective-permute-start | bytes 983048 | tf_op jit(solution)/shard_map/ppermute | solution.py:41
  379.4 1.3 collective-permute-start.30
  396.0 14.9 %collective-permute-start.34 = (bf16[2,640,256]{2,1,0:T(8,128)(2,1)S(1)}, bf16[2,640,256]{2,1,0:T(8,128)(2,1)S(1)}, u32[]{:S(2)}, u32[]{:S(2)}) collective-permute-start(bf16[2,640,256]{2,1,0:T(8,128)(2,1)S(1)} %bitcast.89), channel_id=1, source_target_pairs={{0,4},{1,5},{2,6},{3,7},{4,0},{5,1},{6,2},{7,3},{8,12},{9,13},{10,... | collective-permute-start | bytes 1966088 | tf_op jit(solution)/shard_map/ppermute | solution.py:41
  413.4 36.9 %collective-permute-start.36 = (bf16[8,448,512]{2,1,0:T(8,128)(2,1)}, bf16[8,448,512]{2,1,0:T(8,128)(2,1)S(1)}, u32[]{:S(2)}, u32[]{:S(2)}) collective-permute-start(bf16[8,448,512]{2,1,0:T(8,128)(2,1)} %bitcast.74), channel_id=1, source_target_pairs={{0,1},{1,0},{2,3},{3,2},{4,5},{5,4},{6,7},{7,6},{8,9},{9,8},{10,11... | collective-permute-start | bytes 11010056 | tf_op jit(solution)/shard_map/ppermute | solution.py:41
  413.4 36.9 %collective-permute-start.35 = (bf16[4,640,256]{2,1,0:T(8,128)(2,1)S(1)}, bf16[4,640,256]{2,1,0:T(8,128)(2,1)S(1)}, u32[]{:S(2)}, u32[]{:S(2)}) collective-permute-start(bf16[4,640,256]{2,1,0:T(8,128)(2,1)S(1)} %bitcast.82), channel_id=1, source_target_pairs={{0,2},{1,3},{2,0},{3,1},{4,6},{5,7},{6,4},{7,5},{8,10},{9,11},{10,... | collective-permute-start | bytes 3932168 | tf_op jit(solution)/shard_map/ppermute | solution.py:41
  414.8 31.1 %collective-permute-start.37 = (f32[12,1024]{1,0:T(8,128)S(1)}, f32[12,1024]{1,0:T(8,128)S(1)}, u32[]{:S(2)}, u32[]{:S(2)}) collective-permute-start(f32[12,1024]{1,0:T(8,128)S(1)} %total.6.one_ref), channel_id=1, source_target_pairs={{0,2},{1,3},{2,0},{3,1},{4,6},{5,7},{6,4},{7,5},{8,10},{9,11},{10,... | collective-permute-start | bytes 147464 | tf_op jit(solution)/shard_map/ppermute | solution.py:41
  446.0 4.3 collective-permute-start.38
  452.1 17.0 %collective-permute-start.39 = (bf16[8,640,256]{2,1,0:T(8,128)(2,1)S(1)}, bf16[8,640,256]{2,1,0:T(8,128)(2,1)}, u32[]{:S(2)}, u32[]{:S(2)}) collective-permute-start(bf16[8,640,256]{2,1,0:T(8,128)(2,1)S(1)} %bitcast.77), channel_id=1, source_target_pairs={{0,1},{1,0},{2,3},{3,2},{4,5},{5,4},{6,7},{7,6},{8,9},{9,8},{10,11... | collective-permute-start | bytes 7864328 | tf_op jit(solution)/shard_map/ppermute | solution.py:41
  452.1 17.0 %collective-permute-start.40 = (f32[12,1024]{1,0:T(8,128)S(1)}, f32[12,1024]{1,0:T(8,128)S(1)}, u32[]{:S(2)}, u32[]{:S(2)}) collective-permute-start(f32[12,1024]{1,0:T(8,128)S(1)} %total.8.one_ref), channel_id=1, source_target_pairs={{0,8},{1,9},{2,10},{3,11},{4,12},{5,13},{6,14},{7,15},{8,0},{9,1},... | collective-permute-start | bytes 147464 | tf_op jit(solution)/shard_map/ppermute | solution.py:41
  (41 other events, 310.5 us)
Sparse Core Ops, SparseCore 0:
  136.7 82.2 all-gather.1

commit v3 on v2

--- a/solution.py
+++ b/solution.py
@@ -1006,6 +1006,47 @@
     )(one.reshape(1, rows, columns), two.reshape(1, rows, columns), extra)
 
 
+def join_kernel(one_ref, two_ref, extra_one_ref, extra_two_ref, send_ref, keep_ref):
+    rows, columns = one_ref.shape[-2:]
+    height, moves = tiles(*extra_one_ref.shape[-2:], columns)
+    first = keep_ref.shape[1] - rows
+    for half, target in ((0, keep_ref), (1, send_ref)):
+        value = one_ref[0, half].astype(F32) + two_ref[0, half].astype(F32)
+        target[0, first:] = value.astype(BF16)
+        value = extra_one_ref[0, half].astype(F32) + extra_two_ref[0, half].astype(F32)
+        value = value.astype(BF16)
+        for row, column, to_row, to_column in moves:
+            target[0, to_row : to_row + height, to_column : to_column + LANES] = value[
+                row : row + height, column : column + LANES
+            ]
+
+
+def join(one, two, extra_one, extra_two, outer):
+    rows, columns = one.shape[-2:]
+    extra_rows, extra_columns = extra_one.shape[-2:]
+    height = rows + extra_rows * extra_columns // columns
+    block = pl.BlockSpec((1, 2, rows, columns), lambda n: (n, 0, 0, 0))
+    extra = pl.BlockSpec((1, 2, extra_rows, extra_columns), lambda n: (n, 0, 0, 0))
+    out = pl.BlockSpec((1, height, columns), lambda n: (n, 0, 0))
+    shape = (outer, 2, rows, columns)
+    extra_shape = (outer, 2, extra_rows, extra_columns)
+    return pl.pallas_call(
+        join_kernel,
+        grid=(outer,),
+        in_specs=[block, block, extra, extra],
+        out_specs=[out, out],
+        out_shape=[jax.ShapeDtypeStruct((outer, height, columns), BF16)] * 2,
+        compiler_params=params(),
+        cost_estimate=cost(0, 0),
+        name="join",
+    )(
+        one.reshape(shape),
+        two.reshape(shape),
+        extra_one.reshape(extra_shape),
+        extra_two.reshape(extra_shape),
+    )
+
+
 class Flow:
     def __init__(self, send, keep, first, labels, order, sizes):
         self.sizes = dict(fsdp=sizes[0], ctx=sizes[1])
@@ -1042,13 +1083,35 @@
                 self.received = None
         return self
 
-    def spread(self):
-        self.spreading = [("ctx", bit) for bit in reversed(range(bits_of(self.sizes["ctx"])))]
+    def join(self, other, event):
+        received = after(self.received, event)
+        label = self.order.pop(0)
+        assert self.labels[-1] == label
+        self.labels.pop()
+        send, self.keep = join(
+            self.keep, received, other.keep, other.received, 1 << len(self.labels)
+        )
+        self.received = self.swap(send, label)
+        other.received = None
+        return self
+
+    def spread(self, bits):
+        self.spreading = [("ctx", bit) for bit in bits]
         self.received = self.swap(self.keep, self.spreading.pop(0))
 
 
-def finish_kernel(dim, label_ref, near_ref, far_ref, out_ref):
-    count, height, _ = near_ref.shape
+def places(bits):
+    count = len(bits) - 1
+    return [
+        sum(((number >> (count - 1 - turn)) & 1) << (bits[turn] - 1) for turn in range(count))
+        for number in range(1 << count)
+    ]
+
+
+def finish_kernel(dim, order, label_ref, source, *refs):
+    out_ref, token_ref = refs[-2:]
+    token_ref[...] = jnp.zeros_like(token_ref)
+    count, height, _ = source.shape
     rows, columns = out_ref.shape
     if dim == 0:
         rows = rows // count
@@ -1056,63 +1119,57 @@
         columns = columns // count
     first = height - rows
     low = label_ref[1] & (count - 1)
-
-    def write(source):
-        for number in range(count):
-            place = number ^ low
-            value = source[number, first:].astype(F32)
-            if dim == 0:
-                out_ref[pl.ds(pl.multiple_of(place * rows, LANES), rows), :] = value
-            else:
-                out_ref[:, pl.ds(pl.multiple_of(place * columns, LANES), columns)] = value
-
-    pl.when(pl.program_id(0) == 0)(functools.partial(write, near_ref))
-    pl.when(pl.program_id(0) == 1)(functools.partial(write, far_ref))
-
-
-def finish(near, far, table, dim, rows, columns):
-    half, height, width = near.shape
-    group = half // 2
+    for number in range(count):
+        place = order[number] ^ low
+        value = source[number, first:].astype(F32)
+        if dim == 0:
+            out_ref[pl.ds(pl.multiple_of(place * rows, LANES), rows), :] = value
+        else:
+            out_ref[:, pl.ds(pl.multiple_of(place * columns, LANES), columns)] = value
+
+
+def finish(source, before, other, table, dim, rows, columns, bits):
+    half, height, width = source.shape
+    order = places(bits)
+    group = half // 2 if bits[0] == max(bits) else half
+    count = half // group
     shift = bits_of(group)
+
+    def index(n, t):
+        return (other ^ t[0]) * count + (n ^ (t[1] >> shift))
+
     if dim == 0:
         shape = (2 * half * rows, columns)
-        out_spec = pl.BlockSpec(
-            (group * rows, columns), lambda k, n, t: ((k ^ t[0]) * 2 + (n ^ (t[1] >> shift)), 0)
-        )
+        out_spec = pl.BlockSpec((group * rows, columns), lambda n, t: (index(n, t), 0))
     else:
         shape = (rows, 2 * half * columns)
-        out_spec = pl.BlockSpec(
-            (rows, group * columns), lambda k, n, t: (0, (k ^ t[0]) * 2 + (n ^ (t[1] >> shift)))
-        )
-
-    def block(which):
-        return pl.BlockSpec(
-            (group, height, width),
-            lambda k, n, t: (jnp.where(k == which, n, 1 - which), 0, 0),
-        )
-
+        out_spec = pl.BlockSpec((rows, group * columns), lambda n, t: (0, index(n, t)))
+    earlier = [] if before is None else [before]
     return pl.pallas_call(
-        functools.partial(finish_kernel, dim),
+        functools.partial(finish_kernel, dim, order[:group]),
         grid_spec=pltpu.PrefetchScalarGridSpec(
             num_scalar_prefetch=1,
-            grid=(2, 2),
-            in_specs=[block(0), block(1)],
-            out_specs=out_spec,
+            grid=(count,),
+            in_specs=[pl.BlockSpec((group, height, width), lambda n, t: (n, 0, 0))]
+            + [pl.BlockSpec(memory_space=pl.ANY) for _ in earlier],
+            out_specs=[out_spec, whole(TOKEN.shape)],
         ),
-        out_shape=jax.ShapeDtypeStruct(shape, F32),
+        out_shape=[jax.ShapeDtypeStruct(shape, F32), TOKEN],
+        input_output_aliases={2: 0} if earlier else {},
         compiler_params=params(),
         cost_estimate=cost(0, 0),
         name="finish",
-    )(table, near, far)
-
-
-def finish_extra_kernel(rows, width, low_bits, label_ref, near_ref, far_ref, *refs):
-    out_ref = refs[-1]
+    )(table, source, *earlier)
+
+
+def finish_extra_kernel(rows, width, low_bits, order, label_ref, near_ref, far_ref, *refs):
+    out_ref, token_ref = refs[-2:]
+    token_ref[...] = jnp.zeros_like(token_ref)
     half, _, columns = near_ref.shape
     height, moves = tiles(rows, width, columns)
     for number in range(2 * half):
         source = far_ref if number & 1 else near_ref
-        owner = number ^ ((label_ref[1] << 1) | label_ref[0])
+        owner = ((order[number >> 1] << 1) | (number & 1)) ^ ((label_ref[1] << 1) | label_ref[0])
         if low_bits is None:
             place, begin, stride = owner, 0, LANES
         else:
@@ -1129,18 +1186,18 @@
             ].astype(F32)
 
 
-def finish_extra(near, far, table, rows, width, low_bits, shape, events=()):
+def finish_extra(near, far, table, rows, width, low_bits, shape, bits, events=()):
     half, _, columns = near.shape
     block = pl.BlockSpec((half, rows * width // columns, columns), lambda n, t: (0, 0, 0))
     return pl.pallas_call(
-        functools.partial(finish_extra_kernel, rows, width, low_bits),
+        functools.partial(finish_extra_kernel, rows, width, low_bits, places(bits)),
         grid_spec=pltpu.PrefetchScalarGridSpec(
             num_scalar_prefetch=1,
             grid=(1,),
             in_specs=[block, block] + [whole(event.keep.shape) for event in events],
-            out_specs=whole(shape),
+            out_specs=[whole(shape), whole(TOKEN.shape)],
         ),
-        out_shape=jax.ShapeDtypeStruct(shape, F32),
+        out_shape=[jax.ShapeDtypeStruct(shape, F32), TOKEN],
         compiler_params=params(),
         cost_estimate=cost(0, 0),
         name="finish_extra",
@@ -1284,8 +1341,7 @@
     expand_first = Event(after(expand_gather.keep, input_gather))
     expand_gather.exchange()
     output_gather.fetch(expand_first)
-    h1 = after(after(h1, other), expand_first)
-    og_other = other.keep
+    h1 = after(h1, expand_first)
     qkv, token = project(h1, vectors, input_gather.result(), seqs, rows)
     expand_gather.held[0] = expand_first.keep
     project_done = Event(token)
@@ -1294,7 +1350,8 @@
     output_gather.keep = after(output_gather.keep, project_done)
     qkv = qkv.reshape(ctx_size, units, rows, 3 * LANES)
     qkv = lax.all_to_all(qkv, "ctx", 0, 0, tiled=True)
-    qkv = after(qkv, output_gather)
+    qkv = after(after(qkv, output_gather), other)
+    og_other = other.keep
     att, lse = attend(assignment, unit_seqs, qkv, starts)
     attend_done = Event(lse)
     shrink_gather.keep = after(shrink_gather.keep, attend_done)
@@ -1325,13 +1382,16 @@
     every = [("fsdp", bit) for bit in reversed(range(bits_of(fsdp_size)))]
     high = [("ctx", bit) for bit in reversed(range(1, bits_of(ctx_size)))]
     flow_s = Flow(send_s, keep_s, every[0], every[1:] + high, every[1:] + high[::-1], sizes)
+    dres, dmixed, keep_o, send_o, vec_two = branch_back(
+        back_table, keep, other, residual, og, mixed, vectors, output_parts, sizes, seqs, rows
+    )
+    branch_done = Event(vec_two)
+    send_e = after(send_e, branch_done)
     flow_e = Flow(
         send_e, keep_e, high[-1], every + high[:-1], every + high[:-1][::-1], sizes
     )
-    dres, dmixed, keep_o, send_o, vec_two = branch_back(
-        back_table, keep, other, residual, og, mixed, vectors, output_parts, sizes, seqs, rows
-    )
-    branch_done = Event(vec_two)
+    spread_s = [bit for _, bit in high] + [0]
+    spread_e = [1] + [bit for bit in spread_s if bit > 1] + [0]
     flow_o = Flow(send_o, keep_o, ("ctx", 0), every + high, every + high[::-1], sizes)
     dmixed = dmixed.reshape(ctx_size, units, rows, LANES)
     dmixed = lax.all_to_all(dmixed, "ctx", 0, 0, tiled=True)
@@ -1340,7 +1400,6 @@
     )
     back_done = Event(token)
     last = flow_s.step(back_done)
-    last = flow_e.step(last)
     held = Event(after(dqkv, last))
     keep_i, send_i, token = input_weight_terms(gathered, held.keep, terms_table, low, fsdp_size)
     terms_done = Event(token)
@@ -1353,19 +1412,26 @@
         low_labels[1:] + every,
         sizes,
     )
-    last = flow_o.step(terms_done)
+    last = flow_e.step(terms_done)
     last = flow_i.step(last)
+    last = flow_o.step(last)
     last = flow_s.step(last)
-    last = flow_e.step(last)
+    while ("fsdp", 0) in flow_e.order:
+        last = flow_e.step(last)
     dqkv = lax.all_to_all(dqkv, "ctx", 0, 0, tiled=True).reshape(pairs, seqs, rows, 3 * LANES)
     last = flow_o.step(last)
     while flow_i.received is not None:
         last = flow_i.step(last)
+    last = flow_s.step(last)
+    while len(flow_o.order) > len(flow_e.order):
+        last = flow_o.step(last)
+    flow_o.received = after(flow_o.received, last)
+    last = flow_e.join(flow_o, last)
     flow_s.extra = flow_i.keep[0]
     while flow_s.order:
         last = flow_s.step(last)
     last = flow_s.step(last)
-    flow_s.spread()
+    flow_s.spread(spread_s)
     input_grad, out, sums = entry_back(
         after(dqkv, last),
         x,
@@ -1376,55 +1442,55 @@
         vectors,
         (input_gather.result()[0], entry_table),
     )
-    totals = Total(sums, every + [("ctx", 0)] + high[::-1], sizes)
-    last = flow_o.step(totals)
-    if flow_e.order:
-        last = flow_e.step(last)
-    last = flow_s.step(last)
-    last = flow_o.step(last)
-    last = totals.step(last)
+    totals = Total(sums, every + high[::-1] + [("ctx", 0)], sizes)
+    last = totals
     while flow_e.order:
         last = flow_e.step(last)
     last = flow_s.step(last)
-    while flow_o.received is not None:
-        last = flow_o.step(last)
-    flow_e.extra = flow_o.keep[0]
+    for _ in range(len(every) + 2):
+        last = totals.step(last)
     last = flow_e.step(last)
-    flow_e.spread()
+    flow_e.spread(spread_e)
+    while totals.labels:
+        last = totals.step(last)
+    last = flow_e.step(last)
+    last = flow_s.step(last)
+    while len(flow_e.spreading) > 1:
+        last = flow_e.step(last)
     last = totals.step(last)
-    last = flow_e.step(last)
-    last = flow_e.step(last)
     while flow_s.spreading:
         last = flow_s.step(last)
-    last = totals.step(last)
-    last = flow_s.step(last)
     rows_s = hidden // ctx_size
-    shrink_done = Event(finish(flow_s.keep, flow_s.far, finish_table, 0, rows_s, part))
-    loose = [project_done, back_done, terms_done, branch_done]
-    input_done = Event(
-        finish_extra(
-            flow_s.keep,
-            flow_s.far,
-            finish_table,
-            part >> low_bits,
-            3 * LANES,
-            low_bits,
-            (part, 3 * features),
-            loose,
-        )
-    )
-    last = totals.step(last)
+    shrink_grad, token = finish(flow_s.keep, None, 0, finish_table, 0, rows_s, part, spread_s)
+    shrink_done = Event(token)
     flow_e.received = after(flow_e.received, shrink_done)
-    flow_e.received = after(flow_e.received, input_done)
     while flow_e.spreading:
         last = flow_e.step(last)
-    while totals.received is not None:
-        last = totals.step(last)
+    last = flow_s.step(last)
+    shrink_grad, token = finish(
+        flow_s.far, shrink_grad, 1, finish_table, 0, rows_s, part, spread_s
+    )
+    input_grad_w, token = finish_extra(
+        flow_s.keep,
+        flow_s.far,
+        finish_table,
+        part >> low_bits,
+        3 * LANES,
+        low_bits,
+        (part, 3 * features),
+        spread_s,
+    )
+    input_done = Event(token)
+    expand_grad, _ = finish(
+        flow_e.keep, None, 0, finish_table, 1, part, rows_s, spread_e
+    )
+    flow_e.received = after(flow_e.received, input_done)
     last = flow_e.step(last)
-    shrink_grad = shrink_done.keep
-    input_grad_w = input_done.keep
-    expand_grad = finish(flow_e.keep, flow_e.far, finish_table, 1, part, rows_s)
-    output_grad_w = finish_extra(
+    expand_grad, token = finish(
+        flow_e.far, expand_grad, 1, finish_table, 1, part, rows_s, spread_e
+    )
+    expand_done = Event(token)
+    output_grad_w, _ = finish_extra(
         flow_e.keep,
         flow_e.far,
         finish_table,
@@ -1432,30 +1498,10 @@
         part,
         None,
         (features, part),
+        spread_e,
+        [project_done, back_done, terms_done, branch_done, shrink_done, input_done, expand_done],
     )
     sums = totals.keep
-    input_grad_w = finish_extra(
-        flow_s.keep,
-        flow_s.far,
-        finish_table,
-        part >> low_bits,
-        3 * LANES,
-        low_bits,
-        (part, 3 * features),
-        loose,
-    )
-    rows_s = hidden // ctx_size
-    shrink_grad = finish(flow_s.keep, flow_s.far, finish_table, 0, rows_s, part)
-    expand_grad = finish(flow_e.keep, flow_e.far, finish_table, 1, part, rows_s)
-    output_grad_w = finish_extra(
-        flow_e.keep,
-        flow_e.far,
-        finish_table,
-        features // ctx_size,
-        part,
-        None,
-        (features, part),
-    )
 
     def own(vector):
         size = vector.shape[0] // fsdp_size

time: 493 us -> 471 us (0.955)
  waiting for transfers between devices: 250 us -> 228 us
  starting transfers between devices: 63.1 us -> 69.3 us
    ppermute x41 -> x39, waiting for transfers between devices: 213 us -> 191 us  [swap_bit(): return lax.ppermute(value, axis, [(i, i ^ 1 << bit) for i in range(size)])]
    ppermute x41 -> x39, starting transfers between devices: 34.8 us -> 41.3 us  [swap_bit(): return lax.ppermute(value, axis, [(i, i ^ 1 << bit) for i in range(size)])]
    pallas_call x11 -> x8, Pallas kernels: 15.1 us -> 10 us  [combine(): pl.pallas_call(combine_kernel, grid=(outer, inner // per), in_specs=[bloc...]
    unnamed x96 -> x82, local copies, waits for them, and re-layouts: 32.6 us -> 30.3 us
    pallas_call x2 -> x5, Pallas kernels: 14.5 us -> 15.6 us  [the longest x4 14.6 us: finish(): pl.pallas_call(functools.partial(finish_kernel, dim, order[:group]), grid...]
  transfers between devices with their start and end apart: 46 -> 44, of which waited for: 25 -> 27; matrix products, arithmetic and copies ran while one was open for 4% -> 5% of each run, Pallas kernels for 19% -> 20%
where the time goes in v3:
time: 471 us; the launch traced here: 469 us
  waiting for transfers between devices  228 us (48%)
  Pallas kernels  110 us (23%)
  starting transfers between devices  69.3 us (15%)
  local copies, waits for them, and re-layouts  43.8 us (9%)
  between operations  14.5 us (3%)
    ppermute x39, waiting for transfers between devices, swap_bit(): return lax.ppermute(value, axis, [(i, i ^ 1 << bit) for i in range(size)])  191 us
    ppermute x39, starting transfers between devices, swap_bit(): return lax.ppermute(value, axis, [(i, i ^ 1 << bit) for i in range(size)])  41.3 us
    unnamed x82, local copies, waits for them, and re-layouts  30.3 us
    pallas_call x1, Pallas kernels, feed_forward(): pl.pallas_call(functools.partial(ffn_kernel, len(expand_arrays), len(shri...  22.2 us
    all_to_all x1, waiting for transfers between devices, body(): dmixed = lax.all_to_all(dmixed, 'ctx', 0, 0, tiled=True)  18.8 us
    pallas_call x4, Pallas kernels, finish(): pl.pallas_call(functools.partial(finish_kernel, dim, order[:group]), grid...  14.6 us
    all_to_all x1, waiting for transfers between devices, body(): qkv = lax.all_to_all(qkv, 'ctx', 0, 0, tiled=True)  13.5 us
    pallas_call x1, Pallas kernels, attend_back(): pl.pallas_call(functools.partial(attend_back_kernel, ctx_size), grid_spec...  10.4 us
  transfers between devices with their start and end apart: 44, of which 27 were waited for; matrix products, arithmetic and copies ran while one was open for 5% of the time, Pallas kernels for 20%

profile of v3, /device:TPU:0, one launch (start us, length us, event | category | flops | bytes accessed | tf_op | source)
XLA Modules:
  0.0 468.7 jit_solution(7149722415886464846)
XLA Ops:
  8.5 3.0 collective-permute-start
  11.6 3.1 convert_reduce_fusion
  25.9 3.1 constant_dynamic-slice_fusion.9
  29.0 3.8 collective-permute-done.1.refs_1_
  35.8 14.9 %collective-permute-done.2.refs_2_.refs_7_.refs_12_ = bf16[128,3072]{1,0:T(8,128)(2,1)S(1)} collective-permute-done((bf16[128,3072]{1,0:T(8,128)(2,1)S(1)}, bf16[128,3072]{1,0:T(8,128)(2,1)S(1)}, u32[]{:S(2)}, u32[]{:S(2)}) %collective-permute-start.2) | collective-permute-done | bytes 786464 | tf_op jit(solution)/shard_map/ppermute | solution.py:41
  51.2 6.5 %collective-permute-done.3.refs_1_ = bf16[256,2048]{1,0:T(8,128)(2,1)S(1)} collective-permute-done((bf16[256,2048]{1,0:T(8,128)(2,1)}, bf16[256,2048]{1,0:T(8,128)(2,1)S(1)}, u32[]{:S(2)}, u32[]{:S(2)}) %collective-permute-start.3) | collective-permute-done | bytes 1048608 | tf_op jit(solution)/shard_map/ppermute | solution.py:41
  58.7 5.0 %project.1 = (bf16[8,4,64,384]{3,2,1,0:T(8,128)(2,1)S(1)}, f32[8,128]{1,0:T(8,128)S(1)}) custom-call(s32[5]{0:T(128)S(1)} %pad_add_fusion.1.off_ref, bf16[256,1024]{1,0:T(8,128)(2,1)S(1)} %get-tuple-element.235.h_ref, f32[8,1024]{1,0:T(8,128)S(1)} %get-tuple-element.195.v_ref, bf16[512,3072]{1,0:T(8,128)(2,1)} %refs_10_.3, ...), custom_call_target="tpu_custom_call" | custom-call | tf_op jit(solution)/shard_map/project/pallas_call | solution.py:220
  64.9 5.2 %all-to-all-start = ((bf16[16,2,64,384]{3,2,1,0:T(8,128)(2,1)}), bf16[16,2,64,384]{3,2,1,0:T(8,128)(2,1)}, u32[]{:S(2)}, u32[]{:S(2)}) async-start(bf16[16,2,64,384]{3,2,1,0:T(8,128)(2,1)} %bitcast.90), calls=%async_computation | async-start | bytes 3145728 | tf_op jit(solution)/shard_map/all_to_all | solution.py:1352
  70.6 13.8 %collective-permute-done.6.refs_1_ = bf16[1024,256]{1,0:T(8,128)(2,1)S(1)} collective-permute-done((bf16[1024,256]{1,0:T(8,128)(2,1)}, bf16[1024,256]{1,0:T(8,128)(2,1)S(1)}, u32[]{:S(2)}, u32[]{:S(2)}) %collective-permute-start.6) | collective-permute-done | bytes 524320 | tf_op jit(solution)/shard_map/ppermute | solution.py:41
  88.7 13.5 %all-to-all-done.qkv_ref = bf16[16,2,64,384]{3,2,1,0:T(8,128)(2,1)} async-done(((bf16[16,2,64,384]{3,2,1,0:T(8,128)(2,1)}), bf16[16,2,64,384]{3,2,1,0:T(8,128)(2,1)}, u32[]{:S(2)}, u32[]{:S(2)}) %all-to-all-start) | async-done | bytes 1572896 | tf_op jit(solution)/shard_map/all_to_all | solution.py:1352
  102.2 10.0 %attend.1 = (bf16[16,2,64,128]{3,2,1,0:T(8,128)(2,1)S(1)}, f32[2,2,1024]{2,1,0:T(2,128)S(1)}) custom-call(s32[16]{0:T(128)S(1)} %copy-done.33, s32[2]{0:T(128)S(1)} %add_and_fusion.seq_ref, bf16[16,2,64,384]{3,2,1,0:T(8,128)(2,1)} %all-to-all-done.qkv_ref, s32[4,1,1024]{2,1,0:T(1,128)S(1)} %broadcast_in_dim.2.start_ref), custom_call_target="tpu_custom_call" | custom-call | tf_op jit(solution)/shard_map/attend/pallas_call | solution.py:315
  113.0 9.2 %all-to-all-start.1 = ((bf16[16,2,64,128]{3,2,1,0:T(8,128)(2,1)}), bf16[16,2,64,128]{3,2,1,0:T(8,128)(2,1)}, u32[]{:S(2)}, u32[]{:S(2)}) async-start(bf16[16,2,64,128]{3,2,1,0:T(8,128)(2,1)} %copy-done.32), calls=%async_computation.1 | async-start | bytes 1048576 | tf_op jit(solution)/shard_map/all_to_all | solution.py:1358
  122.4 9.5 %collective-permute-done.10.refs_4_ = bf16[2048,512]{1,0:T(8,128)(2,1)} collective-permute-done((bf16[2048,512]{1,0:T(8,128)(2,1)}, bf16[2048,512]{1,0:T(8,128)(2,1)}, u32[]{:S(2)}, u32[]{:S(2)}) %collective-permute-start.10) | collective-permute-done | bytes 2097184 | tf_op jit(solution)/shard_map/ppermute | solution.py:41
  131.9 4.8 %all-to-all-done.1 = bf16[16,2,64,128]{3,2,1,0:T(8,128)(2,1)} async-done(((bf16[16,2,64,128]{3,2,1,0:T(8,128)(2,1)}), bf16[16,2,64,128]{3,2,1,0:T(8,128)(2,1)}, u32[]{:S(2)}, u32[]{:S(2)}) %all-to-all-start.1) | async-done | bytes 524320 | tf_op jit(solution)/shard_map/all_to_all | solution.py:1358
  141.0 2.8 branch.1
  145.9 22.2 %feed_forward.1 = (f32[2,256,1024]{2,1,0:T(8,128)}, f32[2,256,1024]{2,1,0:T(8,128)}, bf16[1,4,2,256,512]{4,3,2,1,0:T(8,128)(2,1)}, bf16[1,4,2,256,512]{4,3,2,1,0...) custom-call(s32[9]{0:T(128)S(1)} %concatenate.23.sc_ref, ...), custom_call_target="tpu_custom_call" | custom-call | tf_op jit(solution)/shard_map/feed_forward/pallas_call | solution.py:637
  168.8 5.8 %collective-permute-done.12.dh2_other_ref.two_ref = f32[2,256,1024]{2,1,0:T(8,128)S(1)} collective-permute-done((f32[2,256,1024]{2,1,0:T(8,128)}, f32[2,256,1024]{2,1,0:T(8,128)S(1)}, u32[]{:S(2)}, u32[]{:S(2)}) %collective-permute-start.12) | collective-permute-done | bytes 2097184 | tf_op jit(solution)/shard_map/ppermute | solution.py:41
  175.9 5.3 %branch_back.1 = (f32[256,1024]{1,0:T(8,128)S(1)}, bf16[8,4,64,128]{3,2,1,0:T(8,128)(2,1)S(1)}, bf16[2,8,64,512]{3,2,1,0:T(8,128)(2,1)S(1)}, bf16[2,8,64,512]{3,2,1,0:T(8,128)(2,1)S(1)}, f32[8,1024]{1,0:T(8,128)S(1)}) custom-call(s32[5]{0:T(128)S(1)} %pad_add_fusion.4.sc_ref, f32[2,256,1024]{2,1,0:T(8,128)} %get-tuple-element.224.dh2_ref.one_ref, ...), custom_call_target="tpu_custom_call" | custom-call | tf_op jit(solution)/shard_map/branch_back/pallas_call | solution.py:730
  185.0 4.2 all-to-all-start.2
  191.0 18.8 %all-to-all-done.2.grad_ref = bf16[16,2,64,128]{3,2,1,0:T(8,128)(2,1)} async-done(((bf16[16,2,64,128]{3,2,1,0:T(8,128)(2,1)}), bf16[16,2,64,128]{3,2,1,0:T(8,128)(2,1)}, u32[]{:S(2)}, u32[]{:S(2)}) %all-to-all-start.2) | async-done | bytes 524320 | tf_op jit(solution)/shard_map/all_to_all | solution.py:1397
  209.8 10.4 %attend_back.1 = (bf16[16,2,64,384]{3,2,1,0:T(8,128)(2,1)S(1)}, f32[8,128]{1,0:T(8,128)S(1)}) custom-call(s32[16]{0:T(128)S(1)} %copy-done.33, s32[2]{0:T(128)S(1)} %add_and_fusion.seq_ref, bf16[16,2,64,384]{3,2,1,0:T(8,128)(2,1)} %all-to-all-done.qkv_ref, bf16[16,2,64,128]{3,2,1,0:T(8,128)(2,1)} %all-to-all-done.2.grad_ref, ...), custom_call_target="tpu_custom_call" | custom-call | tf_op jit(solution)/shard_map/attend_back/pallas_call | solution.py:423
  221.3 9.2 %all-to-all-start.3 = ((bf16[16,2,64,384]{3,2,1,0:T(8,128)(2,1)}), bf16[16,2,64,384]{3,2,1,0:T(8,128)(2,1)}, u32[]{:S(2)}, u32[]{:S(2)}) async-start(bf16[16,2,64,384]{3,2,1,0:T(8,128)(2,1)} %copy-done.4), calls=%async_computation.3 | async-start | bytes 3145728 | tf_op jit(solution)/shard_map/all_to_all | solution.py:1421
  232.5 3.6 combine.8
  240.2 5.6 %input_weight_terms.1 = (bf16[1,2,256,384]{3,2,1,0:T(8,128)(2,1)S(1)}, bf16[1,2,256,384]{3,2,1,0:T(8,128)(2,1)S(1)}, f32[8,128]{1,0:T(8,128)S(1)}) custom-call(s32[3]{0:T(128)S(1)} %get-tuple-element.234.sc_ref, bf16[16,4,64,1024]{3,2,1,0:T(8,128)(2,1)} %all-gather.2.cloned.1.call-done.h_ref, bf16[16,2,64,384]{3,2,1,0:T(8,128)(2,1)S(1)} %copy-done.5), custom_call_target="tpu_custom_call" | custom-call | tf_op jit(solution)/shard_map/input_weight_terms/pallas_call | solution.py:786
  245.9 6.9 %collective-permute-done.13 = bf16[2,4,1,512,256]{4,3,1,0,2:T(8,128)(2,1)} collective-permute-done((bf16[2,4,1,512,256]{4,3,1,0,2:T(8,128)(2,1)}, bf16[2,4,1,512,256]{4,3,1,0,2:T(8,128)(2,1)}, u32[]{:S(2)}, u32[]{:S(2)}) %collective-permute-start.13) | collective-permute-done | bytes 2097184 | tf_op jit(solution)/shard_map/ppermute | solution.py:41
  258.5 25.0 %collective-permute-done.16 = bf16[4,1,256,512]{3,2,1,0:T(8,128)(2,1)} collective-permute-done((bf16[4,1,256,512]{3,2,1,0:T(8,128)(2,1)}, bf16[4,1,256,512]{3,2,1,0:T(8,128)(2,1)}, u32[]{:S(2)}, u32[]{:S(2)}) %collective-permute-start.16) | collective-permute-done | bytes 1048608 | tf_op jit(solution)/shard_map/ppermute | solution.py:41
  287.9 4.2 collective-permute-done.19
  295.2 3.5 collective-permute-done.21
  298.8 2.5 collective-permute-start.23
  303.8 9.0 %collective-permute-done.23 = bf16[1,1,256,512]{3,2,1,0:T(8,128)(2,1)S(1)} collective-permute-done((bf16[1,1,256,512]{3,2,1,0:T(8,128)(2,1)S(1)}, bf16[1,1,256,512]{3,2,1,0:T(8,128)(2,1)S(1)}, u32[]{:S(2)}, u32[]{:S(2)}) %collective-permute-start.23) | collective-permute-done | bytes 262176 | tf_op jit(solution)/shard_map/ppermute | solution.py:41
  316.0 8.2 %entry_back.1 = (f32[256,1024]{1,0:T(8,128)}, bf16[256,1024]{1,0:T(8,128)(2,1)}, f32[12,1024]{1,0:T(8,128)S(1)}) custom-call(s32[6]{0:T(128)S(1)} %pad_add_fusion.5.off_ref, bf16[8,4,64,384]{3,2,1,0:T(8,128)(2,1)} %bitcast.15.d_ref, bf16[256,1024]{1,0:T(8,128)(2,1)S(1)} %bitcast.79, f32[256,1024]{1,0:T(8,128)S(1)} %copy-done.22, ...), custom_call_target="tpu_custom_call" | custom-call | tf_op jit(solution)/shard_map/entry_back/pallas_call | solution.py:882
  324.1 4.3 collective-permute-done.26
  329.7 6.5 %collective-permute-done.25.two_ref = bf16[1,448,512]{2,1,0:T(8,128)(2,1)} collective-permute-done((bf16[1,448,512]{2,1,0:T(8,128)(2,1)}, bf16[1,448,512]{2,1,0:T(8,128)(2,1)}, u32[]{:S(2)}, u32[]{:S(2)}) %collective-permute-start.25) | collective-permute-done | bytes 458784 | tf_op jit(solution)/shard_map/ppermute | solution.py:41
  338.9 3.4 collective-permute-start.31
  343.8 2.8 collective-permute-done.24.two_ref
  347.2 3.7 collective-permute-done.28.two_ref
  351.1 15.9 %collective-permute-done.29.two_ref = f32[12,1024]{1,0:T(8,128)S(1)} collective-permute-done((f32[12,1024]{1,0:T(8,128)S(1)}, f32[12,1024]{1,0:T(8,128)S(1)}, u32[]{:S(2)}, u32[]{:S(2)}) %collective-permute-start.29) | collective-permute-done | bytes 49184 | tf_op jit(solution)/shard_map/ppermute | solution.py:41
  367.7 3.4 collective-permute-start.30
  375.9 3.7 collective-permute-start.35
  379.5 26.2 %collective-permute-done.35.two_ref = bf16[2,640,256]{2,1,0:T(8,128)(2,1)S(1)} collective-permute-done((bf16[2,640,256]{2,1,0:T(8,128)(2,1)S(1)}, bf16[2,640,256]{2,1,0:T(8,128)(2,1)S(1)}, u32[]{:S(2)}, u32[]{:S(2)}) %collective-permute-start.35) | collective-permute-done | bytes 655392 | tf_op jit(solution)/shard_map/ppermute | solution.py:41
  408.0 6.1 %collective-permute-done.33.two_ref = bf16[4,448,512]{2,1,0:T(8,128)(2,1)S(1)} collective-permute-done((bf16[4,448,512]{2,1,0:T(8,128)(2,1)S(1)}, bf16[4,448,512]{2,1,0:T(8,128)(2,1)S(1)}, u32[]{:S(2)}, u32[]{:S(2)}) %collective-permute-start.33) | collective-permute-done | bytes 1835040 | tf_op jit(solution)/shard_map/ppermute | solution.py:41
  418.4 2.7 finish.4
  421.1 14.5 %collective-permute-done.36.two_ref = bf16[4,640,256]{2,1,0:T(8,128)(2,1)S(1)} collective-permute-done((bf16[4,640,256]{2,1,0:T(8,128)(2,1)S(1)}, bf16[4,640,256]{2,1,0:T(8,128)(2,1)S(1)}, u32[]{:S(2)}, u32[]{:S(2)}) %collective-permute-start.36) | collective-permute-done | bytes 1310752 | tf_op jit(solution)/shard_map/ppermute | solution.py:41
  441.3 4.5 finish.7
  445.7 5.6 %finish_extra.2 = (f32[512,3072]{1,0:T(8,128)}, f32[8,128]{1,0:T(8,128)S(1)}) custom-call(s32[2]{0:T(128)S(1)} %get-tuple-element.314.label_ref, bf16[8,448,512]{2,1,0:T(8,128)(2,1)S(1)} %bitcast.69, bf16[8,448,512]{2,1,0:T(8,128)(2,1)} %collective-permute-done.37.far_ref.source), custom_call_target="tpu_custom_call" | custom-call | tf_op jit(solution)/shard_map/finish_extra/pallas_call | solution.py:1192
  451.4 2.9 finish.5
  454.2 4.6 finish.6
  458.8 3.1 finish_extra.3
  (190 shorter events, 87.7 us)
Async XLA Ops:
  8.5 24.3 %collective-permute-start = (bf16[128,3072]{1,0:T(8,128)(2,1)S(1)}, bf16[128,3072]{1,0:T(8,128)(2,1)S(1)}, u32[]{:S(2)}, u32[]{:S(2)}) collective-permute-start(bf16[128,3072]{1,0:T(8,128)(2,1)S(1)} %constant_dynamic-slice_fusion.8), channel_id=1, source_target_pairs={{0,16},{16,0},{1,17},{17,1},{2,18},{18,2},{3,19},{19,3},{4,20},{20... | collective-permute-start | bytes 2359304 | tf_op jit(solution)/shard_map/ppermute | solution.py:41
  29.0 3.8 collective-permute-start.1
  32.8 17.9 %collective-permute-start.2 = (bf16[128,3072]{1,0:T(8,128)(2,1)S(1)}, bf16[128,3072]{1,0:T(8,128)(2,1)S(1)}, u32[]{:S(2)}, u32[]{:S(2)}) collective-permute-start(bf16[128,3072]{1,0:T(8,128)(2,1)S(1)} %collective-permute-done.refs_1_.refs_6_.refs_11_), channel_id=1, source_target_pairs={{0,2},{1,3},{2,0},{3,1},{4,6},{5,7},{6,4},{7,5},{8,10},{9,11},{10,... | collective-permute-start | bytes 2359304 | tf_op jit(solution)/shard_map/ppermute | solution.py:41
  34.3 23.4 %collective-permute-start.3 = (bf16[256,2048]{1,0:T(8,128)(2,1)}, bf16[256,2048]{1,0:T(8,128)(2,1)S(1)}, u32[]{:S(2)}, u32[]{:S(2)}) collective-permute-start(bf16[256,2048]{1,0:T(8,128)(2,1)} %dynamic_slice.56), channel_id=1, source_target_pairs={{0,16},{16,0},{1,17},{17,1},{2,18},{18,2},{3,19},{19,3},{4,20},{20... | collective-permute-start | bytes 3145736 | tf_op jit(solution)/shard_map/ppermute | solution.py:41
  50.7 7.0 %collective-permute-start.4 = (bf16[128,3072]{1,0:T(8,128)(2,1)S(1)}, bf16[128,3072]{1,0:T(8,128)(2,1)S(1)}, u32[]{:S(2)}, u32[]{:S(2)}) collective-permute-start(bf16[128,3072]{1,0:T(8,128)(2,1)S(1)} %collective-permute-done.2.refs_2_.refs_7_.refs_12_), channel_id=1, source_target_pairs={{0,1},{1,0},{2,3},{3,2},{4,5},{5,4},{6,7},{7,6},{8,9},{9,8},{10,11... | collective-permute-start | bytes 2359304 | tf_op jit(solution)/shard_map/ppermute | solution.py:41
  50.7 7.0 %collective-permute-start.5 = (bf16[128,3072]{1,0:T(8,128)(2,1)S(1)}, bf16[128,3072]{1,0:T(8,128)(2,1)S(1)}, u32[]{:S(2)}, u32[]{:S(2)}) collective-permute-start(bf16[128,3072]{1,0:T(8,128)(2,1)S(1)} %collective-permute-done.refs_1_.refs_6_.refs_11_), channel_id=1, source_target_pairs={{0,1},{1,0},{2,3},{3,2},{4,5},{5,4},{6,7},{7,6},{8,9},{9,8},{10,11... | collective-permute-start | bytes 2359304 | tf_op jit(solution)/shard_map/ppermute | solution.py:41
  64.9 37.4 %copy-start.33 = (s32[16]{0:T(128)S(1)}, s32[16]{0:T(128)}, u32[]{:S(2)}) copy-start(s32[16]{0:T(128)} %table.3) | copy-start | bytes 196
  64.9 37.4 %all-to-all-start = ((bf16[16,2,64,384]{3,2,1,0:T(8,128)(2,1)}), bf16[16,2,64,384]{3,2,1,0:T(8,128)(2,1)}, u32[]{:S(2)}, u32[]{:S(2)}) async-start(bf16[16,2,64,384]{3,2,1,0:T(8,128)(2,1)} %bitcast.90), calls=%async_computation | async-start | bytes 3145728 | tf_op jit(solution)/shard_map/all_to_all | solution.py:1352
  70.0 14.4 %collective-permute-start.6 = (bf16[1024,256]{1,0:T(8,128)(2,1)}, bf16[1024,256]{1,0:T(8,128)(2,1)S(1)}, u32[]{:S(2)}, u32[]{:S(2)}) collective-permute-start(bf16[1024,256]{1,0:T(8,128)(2,1)} %constant_dynamic-slice_fusion.10), channel_id=1, source_target_pairs={{0,16},{16,0},{1,17},{17,1},{2,18},{18,2},{3,19},{19,3},{4,20},{20... | collective-permute-start | bytes 1572872 | tf_op jit(solution)/shard_map/ppermute | solution.py:41
  84.4 47.4 %collective-permute-start.10 = (bf16[2048,512]{1,0:T(8,128)(2,1)}, bf16[2048,512]{1,0:T(8,128)(2,1)}, u32[]{:S(2)}, u32[]{:S(2)}) collective-permute-start(bf16[2048,512]{1,0:T(8,128)(2,1)} %constant_dynamic-slice_fusion.9), channel_id=1, source_target_pairs={{0,16},{16,0},{1,17},{17,1},{2,18},{18,2},{3,19},{19,3},{4,20},{20... | collective-permute-start | bytes 6291464 | tf_op jit(solution)/shard_map/ppermute | solution.py:41
  84.9 3.0 collective-permute-start.7
  85.7 16.5 %collective-permute-start.8 = (bf16[256,1024]{1,0:T(8,128)(2,1)}, bf16[256,1024]{1,0:T(8,128)(2,1)}, u32[]{:S(2)}, u32[]{:S(2)}) collective-permute-start(bf16[256,1024]{1,0:T(8,128)(2,1)} %bitcast.84), channel_id=1, source_target_pairs={{0,1},{1,0},{2,3},{3,2},{4,5},{5,4},{6,7},{7,6},{8,9},{9,8},{10,11... | collective-permute-start | bytes 1572872 | tf_op jit(solution)/shard_map/ppermute | solution.py:41
  86.3 45.6 %collective-permute-start.9 = (bf16[256,2048]{1,0:T(8,128)(2,1)}, bf16[256,2048]{1,0:T(8,128)(2,1)}, u32[]{:S(2)}, u32[]{:S(2)}) collective-permute-start(bf16[256,2048]{1,0:T(8,128)(2,1)} %copy-done.27), channel_id=1, source_target_pairs={{0,2},{1,3},{2,0},{3,1},{4,6},{5,7},{6,4},{7,5},{8,10},{9,11},{10,... | collective-permute-start | bytes 3145736 | tf_op jit(solution)/shard_map/ppermute | solution.py:41
  113.0 23.7 %all-to-all-start.1 = ((bf16[16,2,64,128]{3,2,1,0:T(8,128)(2,1)}), bf16[16,2,64,128]{3,2,1,0:T(8,128)(2,1)}, u32[]{:S(2)}, u32[]{:S(2)}) async-start(bf16[16,2,64,128]{3,2,1,0:T(8,128)(2,1)} %copy-done.32), calls=%async_computation.1 | async-start | bytes 1048576 | tf_op jit(solution)/shard_map/all_to_all | solution.py:1358
  122.1 116.7 %all-gather.2.cloned.1.call-start = ((), (), s32[]{:S(2)}) async-start(), calls=%async_computation.4 | async-start | bytes 8912896 | tf_op jit(solution)/shard_map/all_gather | solution.py:1360
  143.9 2.0 collective-permute-start.11
  145.9 30.0 %copy-start.16 = (bf16[1024,256]{1,0:T(8,128)(2,1)S(1)}, bf16[1024,256]{1,0:T(8,128)(2,1)}, u32[]{:S(2)}) copy-start(bf16[1024,256]{1,0:T(8,128)(2,1)} %copy-done.14) | copy-start | bytes 1572868
  145.9 30.0 %copy-start.19 = (bf16[1024,256]{1,0:T(8,128)(2,1)S(1)}, bf16[1024,256]{1,0:T(8,128)(2,1)}, u32[]{:S(2)}) copy-start(bf16[1024,256]{1,0:T(8,128)(2,1)} %copy-done.17) | copy-start | bytes 1572868
  168.1 6.5 %collective-permute-start.12 = (f32[2,256,1024]{2,1,0:T(8,128)}, f32[2,256,1024]{2,1,0:T(8,128)S(1)}, u32[]{:S(2)}, u32[]{:S(2)}) collective-permute-start(f32[2,256,1024]{2,1,0:T(8,128)} %get-tuple-element.225), channel_id=1, source_target_pairs={{0,1},{1,0},{2,3},{3,2},{4,5},{5,4},{6,7},{7,6},{8,9},{9,8},{10,11... | collective-permute-start | bytes 6291464 | tf_op jit(solution)/shard_map/ppermute | solution.py:41
  168.3 62.6 %collective-permute-start.14 = (bf16[1,4,2,256,512]{4,3,2,1,0:T(8,128)(2,1)}, bf16[1,4,2,256,512]{4,3,2,1,0:T(8,128)(2,1)}, u32[]{:S(2)}, u32[]{:S(2)}) collective-permute-start(bf16[1,4,2,256,512]{4,3,2,1,0:T(8,128)(2,1)} %get-tuple-element.237), channel_id=1, source_target_pairs={{0,16},{16,0},{1,17},{17,1},{2,18},{18,2},{3,19},{19,3},{4,20},{20... | collective-permute-start | bytes 6291464 | tf_op jit(solution)/shard_map/ppermute | solution.py:41
  185.0 24.8 %all-to-all-start.2 = ((bf16[16,2,64,128]{3,2,1,0:T(8,128)(2,1)}), bf16[16,2,64,128]{3,2,1,0:T(8,128)(2,1)}, u32[]{:S(2)}, u32[]{:S(2)}) async-start(bf16[16,2,64,128]{3,2,1,0:T(8,128)(2,1)} %bitcast.101), calls=%async_computation.2 | async-start | bytes 1048576 | tf_op jit(solution)/shard_map/all_to_all | solution.py:1397
  189.2 63.6 %collective-permute-start.13 = (bf16[2,4,1,512,256]{4,3,1,0,2:T(8,128)(2,1)}, bf16[2,4,1,512,256]{4,3,1,0,2:T(8,128)(2,1)}, u32[]{:S(2)}, u32[]{:S(2)}) collective-permute-start(bf16[2,4,1,512,256]{4,3,1,0,2:T(8,128)(2,1)} %bitcast.122), channel_id=1, source_target_pairs={{0,2},{1,3},{2,0},{3,1},{4,6},{5,7},{6,4},{7,5},{8,10},{9,11},{10,... | collective-permute-start | bytes 6291464 | tf_op jit(solution)/shard_map/ppermute | solution.py:41
  221.3 92.4 %all-to-all-start.3 = ((bf16[16,2,64,384]{3,2,1,0:T(8,128)(2,1)}), bf16[16,2,64,384]{3,2,1,0:T(8,128)(2,1)}, u32[]{:S(2)}, u32[]{:S(2)}) async-start(bf16[16,2,64,384]{3,2,1,0:T(8,128)(2,1)} %copy-done.4), calls=%async_computation.3 | async-start | bytes 3145728 | tf_op jit(solution)/shard_map/all_to_all | solution.py:1421
  230.5 26.0 %collective-permute-start.17 = (bf16[2,8,64,512]{3,2,1,0:T(8,128)(2,1)}, bf16[2,8,64,512]{3,2,1,0:T(8,128)(2,1)}, u32[]{:S(2)}, u32[]{:S(2)}) collective-permute-start(bf16[2,8,64,512]{3,2,1,0:T(8,128)(2,1)} %copy-done.34), channel_id=1, source_target_pairs={{0,1},{1,0},{2,3},{3,2},{4,5},{5,4},{6,7},{7,6},{8,9},{9,8},{10,11... | collective-permute-start | bytes 3145736 | tf_op jit(solution)/shard_map/ppermute | solution.py:41
  237.1 46.4 %collective-permute-start.16 = (bf16[4,1,256,512]{3,2,1,0:T(8,128)(2,1)}, bf16[4,1,256,512]{3,2,1,0:T(8,128)(2,1)}, u32[]{:S(2)}, u32[]{:S(2)}) collective-permute-start(bf16[4,1,256,512]{3,2,1,0:T(8,128)(2,1)} %get-tuple-element.245), channel_id=1, source_target_pairs={{0,2},{1,3},{2,0},{3,1},{4,6},{5,7},{6,4},{7,5},{8,10},{9,11},{10,... | collective-permute-start | bytes 3145736 | tf_op jit(solution)/shard_map/ppermute | solution.py:41
  245.8 10.6 %collective-permute-start.18 = (bf16[1,2,256,384]{3,2,1,0:T(8,128)(2,1)S(1)}, bf16[1,2,256,384]{3,2,1,0:T(8,128)(2,1)S(1)}, u32[]{:S(2)}, u32[]{:S(2)}) collective-permute-start(bf16[1,2,256,384]{3,2,1,0:T(8,128)(2,1)S(1)} %get-tuple-element.249), channel_id=1, source_target_pairs={{0,1},{1,0},{2,3},{3,2},{4,5},{5,4},{6,7},{7,6},{8,9},{9,8},{10,11... | collective-permute-start | bytes 1179656 | tf_op jit(solution)/shard_map/ppermute | solution.py:41
  254.8 28.8 %copy-start.26 = (bf16[4,1,256,512]{3,2,1,0:T(8,128)(2,1)S(1)}, bf16[4,1,256,512]{3,2,1,0:T(8,128)(2,1)}, u32[]{:S(2)}) copy-start(bf16[4,1,256,512]{3,2,1,0:T(8,128)(2,1)} %copy-done.25) | copy-start | bytes 3145732
  254.8 46.5 %collective-permute-start.15 = (bf16[1,4,512,256]{3,2,1,0:T(8,128)(2,1)S(1)}, bf16[1,4,512,256]{3,2,1,0:T(8,128)(2,1)S(1)}, u32[]{:S(2)}, u32[]{:S(2)}) collective-permute-start(bf16[1,4,512,256]{3,2,1,0:T(8,128)(2,1)S(1)} %get-tuple-element.244), channel_id=1, source_target_pairs={{0,16},{16,0},{1,17},{17,1},{2,18},{18,2},{3,19},{19,3},{4,20},{20... | collective-permute-start | bytes 3145736 | tf_op jit(solution)/shard_map/ppermute | solution.py:41
  258.0 34.1 %collective-permute-start.19 = (bf16[1,8,64,512]{3,2,1,0:T(8,128)(2,1)S(1)}, bf16[1,8,64,512]{3,2,1,0:T(8,128)(2,1)S(1)}, u32[]{:S(2)}, u32[]{:S(2)}) collective-permute-start(bf16[1,8,64,512]{3,2,1,0:T(8,128)(2,1)S(1)} %get-tuple-element.256), channel_id=1, source_target_pairs={{0,16},{16,0},{1,17},{17,1},{2,18},{18,2},{3,19},{19,3},{4,20},{20... | collective-permute-start | bytes 1572872 | tf_op jit(solution)/shard_map/ppermute | solution.py:41
  284.9 13.8 %collective-permute-start.21 = (bf16[2,1,256,512]{3,2,0,1:T(8,128)(2,1)S(1)}, bf16[2,1,256,512]{3,2,0,1:T(8,128)(2,1)S(1)}, u32[]{:S(2)}, u32[]{:S(2)}) collective-permute-start(bf16[2,1,256,512]{3,2,0,1:T(8,128)(2,1)S(1)} %bitcast.112), channel_id=1, source_target_pairs={{0,4},{1,5},{2,6},{3,7},{4,0},{5,1},{6,2},{7,3},{8,12},{9,13},{10,... | collective-permute-start | bytes 1572872 | tf_op jit(solution)/shard_map/ppermute | solution.py:41
  286.4 8.7 %collective-permute-start.22 = (bf16[1,1,256,384]{3,2,1,0:T(8,128)(2,1)S(1)}, bf16[1,1,256,384]{3,2,1,0:T(8,128)(2,1)S(1)}, u32[]{:S(2)}, u32[]{:S(2)}) collective-permute-start(bf16[1,1,256,384]{3,2,1,0:T(8,128)(2,1)S(1)} %get-tuple-element.265), channel_id=1, source_target_pairs={{0,16},{16,0},{1,17},{17,1},{2,18},{18,2},{3,19},{19,3},{4,20},{20... | collective-permute-start | bytes 589832 | tf_op jit(solution)/shard_map/ppermute | solution.py:41
  292.3 9.0 %collective-permute-start.20 = (bf16[4,1,64,512]{3,2,1,0:T(8,128)(2,1)S(1)}, bf16[4,1,64,512]{3,2,1,0:T(8,128)(2,1)S(1)}, u32[]{:S(2)}, u32[]{:S(2)}) collective-permute-start(bf16[4,1,64,512]{3,2,1,0:T(8,128)(2,1)S(1)} %get-tuple-element.261), channel_id=1, source_target_pairs={{0,2},{1,3},{2,0},{3,1},{4,6},{5,7},{6,4},{7,5},{8,10},{9,11},{10,... | collective-permute-start | bytes 786440 | tf_op jit(solution)/shard_map/ppermute | solution.py:41
  298.8 14.0 %collective-permute-start.23 = (bf16[1,1,256,512]{3,2,1,0:T(8,128)(2,1)S(1)}, bf16[1,1,256,512]{3,2,1,0:T(8,128)(2,1)S(1)}, u32[]{:S(2)}, u32[]{:S(2)}) collective-permute-start(bf16[1,1,256,512]{3,2,1,0:T(8,128)(2,1)S(1)} %get-tuple-element.272), channel_id=1, source_target_pairs={{0,8},{1,9},{2,10},{3,11},{4,12},{5,13},{6,14},{7,15},{8,0},{9,1},... | collective-permute-start | bytes 786440 | tf_op jit(solution)/shard_map/ppermute | solution.py:41
  302.3 26.2 %collective-permute-start.26 = (bf16[2,640,256]{2,1,0:T(8,128)(2,1)}, bf16[2,640,256]{2,1,0:T(8,128)(2,1)}, u32[]{:S(2)}, u32[]{:S(2)}) collective-permute-start(bf16[2,640,256]{2,1,0:T(8,128)(2,1)} %get-tuple-element.290), channel_id=1, source_target_pairs={{0,4},{1,5},{2,6},{3,7},{4,0},{5,1},{6,2},{7,3},{8,12},{9,13},{10,... | collective-permute-start | bytes 1966088 | tf_op jit(solution)/shard_map/ppermute | solution.py:41
  313.7 22.5 %collective-permute-start.25 = (bf16[1,448,512]{2,1,0:T(8,128)(2,1)}, bf16[1,448,512]{2,1,0:T(8,128)(2,1)}, u32[]{:S(2)}, u32[]{:S(2)}) collective-permute-start(bf16[1,448,512]{2,1,0:T(8,128)(2,1)} %pack.1.one_ref), channel_id=1, source_target_pairs={{0,8},{1,9},{2,10},{3,11},{4,12},{5,13},{6,14},{7,15},{8,0},{9,1},... | collective-permute-start | bytes 1376264 | tf_op jit(solution)/shard_map/ppermute | solution.py:41
  337.4 37.4 %collective-permute-start.27 = (bf16[2,448,512]{2,1,0:T(8,128)(2,1)S(1)}, bf16[2,448,512]{2,1,0:T(8,128)(2,1)S(1)}, u32[]{:S(2)}, u32[]{:S(2)}) collective-permute-start(bf16[2,448,512]{2,1,0:T(8,128)(2,1)S(1)} %bitcast.80), channel_id=1, source_target_pairs={{0,4},{1,5},{2,6},{3,7},{4,0},{5,1},{6,2},{7,3},{8,12},{9,13},{10,... | collective-permute-start | bytes 2752520 | tf_op jit(solution)/shard_map/ppermute | solution.py:41
  338.9 28.1 %collective-permute-start.31 = (bf16[1,1,640,256]{3,2,1,0:T(8,128)(2,1)S(1)}, bf16[1,1,640,256]{3,2,1,0:T(8,128)(2,1)S(1)}, u32[]{:S(2)}, u32[]{:S(2)}) collective-permute-start(bf16[1,1,640,256]{3,2,1,0:T(8,128)(2,1)S(1)} %get-tuple-element.302), channel_id=1, source_target_pairs={{0,8},{1,9},{2,10},{3,11},{4,12},{5,13},{6,14},{7,15},{8,0},{9,1},... | collective-permute-start | bytes 983048 | tf_op jit(solution)/shard_map/ppermute | solution.py:41
  342.3 4.3 collective-permute-start.24
  346.6 4.3 collective-permute-start.28
  350.9 16.1 %collective-permute-start.29 = (f32[12,1024]{1,0:T(8,128)S(1)}, f32[12,1024]{1,0:T(8,128)S(1)}, u32[]{:S(2)}, u32[]{:S(2)}) collective-permute-start(f32[12,1024]{1,0:T(8,128)S(1)} %total.6.one_ref), channel_id=1, source_target_pairs={{0,4},{1,5},{2,6},{3,7},{4,0},{5,1},{6,2},{7,3},{8,12},{9,13},{10,... | collective-permute-start | bytes 147464 | tf_op jit(solution)/shard_map/ppermute | solution.py:41
  367.1 7.6 %collective-permute-start.32 = (bf16[1,640,256]{2,1,0:T(8,128)(2,1)S(1)}, bf16[1,640,256]{2,1,0:T(8,128)(2,1)S(1)}, u32[]{:S(2)}, u32[]{:S(2)}) collective-permute-start(bf16[1,640,256]{2,1,0:T(8,128)(2,1)S(1)} %add_last.3.one_ref), channel_id=1, source_target_pairs={{0,2},{1,3},{2,0},{3,1},{4,6},{5,7},{6,4},{7,5},{8,10},{9,11},{10,... | collective-permute-start | bytes 983048 | tf_op jit(solution)/shard_map/ppermute | solution.py:41
  367.7 5.6 %collective-permute-start.30 = (f32[12,1024]{1,0:T(8,128)S(1)}, f32[12,1024]{1,0:T(8,128)S(1)}, u32[]{:S(2)}, u32[]{:S(2)}) collective-permute-start(f32[12,1024]{1,0:T(8,128)S(1)} %total.7.one_ref), channel_id=1, source_target_pairs={{0,8},{1,9},{2,10},{3,11},{4,12},{5,13},{6,14},{7,15},{8,0},{9,1},... | collective-permute-start | bytes 147464 | tf_op jit(solution)/shard_map/ppermute | solution.py:41
  375.0 39.1 %collective-permute-start.33 = (bf16[4,448,512]{2,1,0:T(8,128)(2,1)S(1)}, bf16[4,448,512]{2,1,0:T(8,128)(2,1)S(1)}, u32[]{:S(2)}, u32[]{:S(2)}) collective-permute-start(bf16[4,448,512]{2,1,0:T(8,128)(2,1)S(1)} %bitcast.73), channel_id=1, source_target_pairs={{0,2},{1,3},{2,0},{3,1},{4,6},{5,7},{6,4},{7,5},{8,10},{9,11},{10,... | collective-permute-start | bytes 5505032 | tf_op jit(solution)/shard_map/ppermute | solution.py:41
  375.9 29.9 %collective-permute-start.35 = (bf16[2,640,256]{2,1,0:T(8,128)(2,1)S(1)}, bf16[2,640,256]{2,1,0:T(8,128)(2,1)S(1)}, u32[]{:S(2)}, u32[]{:S(2)}) collective-permute-start(bf16[2,640,256]{2,1,0:T(8,128)(2,1)S(1)} %bitcast.82), channel_id=1, source_target_pairs={{0,8},{1,9},{2,10},{3,11},{4,12},{5,13},{6,14},{7,15},{8,0},{9,1},... | collective-permute-start | bytes 1966088 | tf_op jit(solution)/shard_map/ppermute | solution.py:41
  405.9 29.7 %collective-permute-start.36 = (bf16[4,640,256]{2,1,0:T(8,128)(2,1)S(1)}, bf16[4,640,256]{2,1,0:T(8,128)(2,1)S(1)}, u32[]{:S(2)}, u32[]{:S(2)}) collective-permute-start(bf16[4,640,256]{2,1,0:T(8,128)(2,1)S(1)} %bitcast.75), channel_id=1, source_target_pairs={{0,4},{1,5},{2,6},{3,7},{4,0},{5,1},{6,2},{7,3},{8,12},{9,13},{10,... | collective-permute-start | bytes 3932168 | tf_op jit(solution)/shard_map/ppermute | solution.py:41
  406.7 1.3 collective-permute-start.34
  416.4 24.9 %collective-permute-start.37 = (bf16[8,448,512]{2,1,0:T(8,128)(2,1)}, bf16[8,448,512]{2,1,0:T(8,128)(2,1)}, u32[]{:S(2)}, u32[]{:S(2)}) collective-permute-start(bf16[8,448,512]{2,1,0:T(8,128)(2,1)} %bitcast.67), channel_id=1, source_target_pairs={{0,1},{1,0},{2,3},{3,2},{4,5},{5,4},{6,7},{7,6},{8,9},{9,8},{10,11... | collective-permute-start | bytes 11010056 | tf_op jit(solution)/shard_map/ppermute | solution.py:41
  435.9 15.5 %collective-permute-start.38 = (bf16[8,640,256]{2,1,0:T(8,128)(2,1)S(1)}, bf16[8,640,256]{2,1,0:T(8,128)(2,1)}, u32[]{:S(2)}, u32[]{:S(2)}) collective-permute-start(bf16[8,640,256]{2,1,0:T(8,128)(2,1)S(1)} %bitcast.70), channel_id=1, source_target_pairs={{0,1},{1,0},{2,3},{3,2},{4,5},{5,4},{6,7},{7,6},{8,9},{9,8},{10,11... | collective-permute-start | bytes 7864328 | tf_op jit(solution)/shard_map/ppermute | solution.py:41
  (32 other events, 156.7 us)
Sparse Core Ops, SparseCore 0:
  136.8 82.1 all-gather.1

commit v4 on v3

--- a/solution.py
+++ b/solution.py
@@ -509,8 +509,10 @@
     expand_parts = refs[:expand_count]
     shrink_parts = refs[expand_count : expand_count + shrink_count]
     (
-        send_ref,
-        keep_ref,
+        dh2_send,
+        dh2_keep,
+        out_send,
+        out_keep,
         send_s,
         keep_s,
         send_e,
@@ -565,31 +567,22 @@
         there = slice(part * columns, (part + 1) * columns)
         place = part ^ y_index
 
-        def store_s(target, there=there, place=place):
+        def store(target_s, target_e, there=there, place=place):
             for sub in range(subs):
                 here = slice(sub * rows, (sub + 1) * rows)
-                target[place & (fsdp_half - 1), 0, sub ^ low_label] = shrink_grad[here, there]
-
-        pl.when(place < fsdp_half)(functools.partial(store_s, keep_s))
-        pl.when(place >= fsdp_half)(functools.partial(store_s, send_s))
-    for sub in range(subs):
-        here = slice(sub * rows, (sub + 1) * rows)
-        place = sub ^ low_label
-
-        def store_e(target, here=here, place=place):
-            for part in range(2 * fsdp_half):
-                there = slice(part * columns, (part + 1) * columns)
-                target[part ^ y_index, 0, place >> 1] = expand_grad[there, here]
-
-        pl.when((place & 1) == 0)(functools.partial(store_e, keep_e))
-        pl.when((place & 1) == 1)(functools.partial(store_e, send_e))
+                index = (place & (fsdp_half - 1), 0, sub ^ low_label)
+                target_s[index] = shrink_grad[here, there]
+                target_e[index] = expand_grad[there, here]
+
+        pl.when(place < fsdp_half)(functools.partial(store, keep_s, keep_e))
+        pl.when(place >= fsdp_half)(functools.partial(store, send_s, send_e))
 
     @pl.when(step == steps - 1)
     def _():
-        keep_ref[0] = back[:tokens]
-        keep_ref[1] = total[:tokens]
-        send_ref[0] = back[tokens:]
-        send_ref[1] = total[tokens:]
+        dh2_keep[...] = back[:tokens]
+        out_keep[...] = total[:tokens]
+        dh2_send[...] = back[tokens:]
+        out_send[...] = total[tokens:]
 
 
 def feed_scalars(place, hidden, width, expand_offsets, shrink_offsets):
@@ -627,13 +620,13 @@
         return pl.BlockSpec((width, array.shape[1]), lambda s, sc: (index(s, sc), 0))
 
     grad_s = (fsdp_size // 2, steps, subs, rows, columns)
-    grad_e = (fsdp_size, steps, subs // 2, columns, rows)
+    grad_e = (fsdp_size // 2, steps, subs, columns, rows)
 
     def block(shape):
         return pl.BlockSpec((shape[0], 1) + shape[2:], lambda s, sc: (0, s, 0, 0, 0))
 
     full = whole(h2.shape)
-    wide = jax.ShapeDtypeStruct((2,) + h2.shape, F32)
+    wide = jax.ShapeDtypeStruct(h2.shape, F32)
     return pl.pallas_call(
         functools.partial(ffn_kernel, len(expand_arrays), len(shrink_arrays), steps),
         grid_spec=pltpu.PrefetchScalarGridSpec(
@@ -643,7 +636,7 @@
             + [whole(vectors.shape), columns_of(expand_bias)]
             + [columns_of(array) for array in expand_arrays]
             + [rows_of(array) for array in shrink_arrays],
-            out_specs=[whole(wide.shape)] * 2
+            out_specs=[full] * 4
             + [block(grad_s)] * 2
             + [block(grad_e)] * 2
             + [pl.BlockSpec((1, width), lambda s, sc: (0, s ^ sc[1])), whole((1, features))],
@@ -657,7 +650,7 @@
                 pltpu.VMEM((2 * tokens, features), BF16),
             ],
         ),
-        out_shape=[wide] * 2
+        out_shape=[wide] * 4
         + [jax.ShapeDtypeStruct(grad_s, BF16)] * 2
         + [jax.ShapeDtypeStruct(grad_e, BF16)] * 2
         + [
@@ -688,7 +681,7 @@
     dres_ref, dmixed_ref, keep_ref, send_ref, vec_ref, weight, rounded = refs[part_count:]
     place_columns(weight, sc_ref, parts)
     hat, rate = norm_stats(residual_ref[...])
-    dh2 = dh2_ref[0] + dh2_other_ref[0]
+    dh2 = dh2_ref[...] + dh2_other_ref[...]
     scaled = dh2 * v_ref[V_G2 : V_G2 + 1, :]
     first = jnp.mean(scaled, axis=-1, keepdims=True)
     second = jnp.mean(scaled * hat, axis=-1, keepdims=True)
@@ -726,13 +719,12 @@
     pairs = features // LANES
     grad = (fsdp_size, ctx_size // 2, features // ctx_size, features // fsdp_size)
     full = whole(residual.shape)
-    half = pl.BlockSpec((1,) + residual.shape, lambda n, o: (0, 0, 0))
     return pl.pallas_call(
         functools.partial(branch_back_kernel, len(arrays), seqs, rows),
         grid_spec=pltpu.PrefetchScalarGridSpec(
             num_scalar_prefetch=1,
             grid=(1,),
-            in_specs=[half] * 2 + [full] * 3 + [whole(vectors.shape)]
+            in_specs=[full] * 5 + [whole(vectors.shape)]
             + [whole(array.shape) for array in arrays],
             out_specs=[
                 full,
@@ -825,7 +817,7 @@
     @pl.when(group == 0)
     def _():
         back[...] = jnp.zeros_like(back)
-        layer_ref[...] = (one_ref[0] + two_ref[0]).astype(BF16)
+        layer_ref[...] = (one_ref[...] + two_ref[...]).astype(BF16)
         vec_ref[4:7, :] = second_ref[0:3, :]
         vec_ref[7:8, :] = sb_ref[...]
         count = vec_ref.shape[0] - 8
@@ -888,8 +880,8 @@
                 pl.BlockSpec((2, seqs, rows, 3 * LANES), lambda g, o: (g, 0, 0, 0)),
                 whole(x.shape),
                 whole(x.shape),
-                pl.BlockSpec((1,) + x.shape, lambda g, o: (1, 0, 0)),
-                pl.BlockSpec((1,) + x.shape, lambda g, o: (1, 0, 0)),
+                whole(x.shape),
+                whole(x.shape),
             ]
             + [whole(array.shape) for array in sums]
             + [whole(vectors.shape)]
@@ -1128,7 +1120,7 @@
             out_ref[:, pl.ds(pl.multiple_of(place * columns, LANES), columns)] = value
 
 
-def finish(source, before, other, table, dim, rows, columns, bits):
+def finish(source, before, other, table, dim, rows, columns, bits, events=()):
     half, height, width = source.shape
     order = places(bits)
     group = half // 2 if bits[0] == max(bits) else half
@@ -1151,7 +1143,8 @@
             num_scalar_prefetch=1,
             grid=(count,),
             in_specs=[pl.BlockSpec((group, height, width), lambda n, t: (n, 0, 0))]
-            + [pl.BlockSpec(memory_space=pl.ANY) for _ in earlier],
+            + [pl.BlockSpec(memory_space=pl.ANY) for _ in earlier]
+            + [whole(event.shape) for event in events],
             out_specs=[out_spec, whole(TOKEN.shape)],
         ),
         out_shape=[jax.ShapeDtypeStruct(shape, F32), TOKEN],
@@ -1159,10 +1152,10 @@
         compiler_params=params(),
         cost_estimate=cost(0, 0),
         name="finish",
-    )(table, source, *earlier)
-
-
-def finish_extra_kernel(rows, width, low_bits, order, label_ref, near_ref, far_ref, *refs):
+    )(table, source, *earlier, *events)
+
+
+def finish_rows_kernel(rows, width, low_bits, order, label_ref, near_ref, far_ref, *refs):
     out_ref, token_ref = refs[-2:]
     token_ref[...] = jnp.zeros_like(token_ref)
     half, _, columns = near_ref.shape
@@ -1186,16 +1179,57 @@
             ].astype(F32)
 
 
-def finish_extra(near, far, table, rows, width, low_bits, shape, bits, events=()):
+def finish_rows(near, far, table, rows, width, low_bits, shape, bits, events=()):
     half, _, columns = near.shape
     block = pl.BlockSpec((half, rows * width // columns, columns), lambda n, t: (0, 0, 0))
     return pl.pallas_call(
-        functools.partial(finish_extra_kernel, rows, width, low_bits, places(bits)),
+        functools.partial(finish_rows_kernel, rows, width, low_bits, places(bits)),
         grid_spec=pltpu.PrefetchScalarGridSpec(
             num_scalar_prefetch=1,
             grid=(1,),
             in_specs=[block, block] + [whole(event.keep.shape) for event in events],
             out_specs=[whole(shape), whole(TOKEN.shape)],
+        ),
+        out_shape=[jax.ShapeDtypeStruct(shape, F32), TOKEN],
+        compiler_params=params(),
+        cost_estimate=cost(0, 0),
+        name="finish_rows",
+    )(table, near, far, *[event.keep for event in events])
+
+
+def finish_extra_kernel(rows, low_bits, order, label_ref, near_ref, far_ref, *refs):
+    out_ref, token_ref = refs[-2:]
+    token_ref[...] = jnp.zeros_like(token_ref)
+    half, height, columns = near_ref.shape
+    for number in range(2 * half):
+        source = far_ref if number & 1 else near_ref
+        owner = ((order[number >> 1] << 1) | (number & 1)) ^ ((label_ref[1] << 1) | label_ref[0])
+        if low_bits is None:
+            place, begin = owner, 0
+        else:
+            place = owner & ((1 << low_bits) - 1)
+            begin = pl.multiple_of((owner >> low_bits) * LANES, LANES)
+        for across in range(columns // LANES):
+            down = pl.multiple_of(place * rows + across * height, 32)
+            out_ref[pl.ds(down, height), pl.ds(begin, LANES)] = source[
+                number >> 1, :, across * LANES : (across + 1) * LANES
+            ].astype(F32)
+
+
+def finish_extra(near, far, table, rows, width, low_bits, shape, bits, events=()):
+    half, _, columns = near.shape
+    steps = width // LANES
+    block = pl.BlockSpec((half, rows * LANES // columns, columns), lambda n, t: (0, n, 0))
+    return pl.pallas_call(
+        functools.partial(finish_extra_kernel, rows, low_bits, places(bits)),
+        grid_spec=pltpu.PrefetchScalarGridSpec(
+            num_scalar_prefetch=1,
+            grid=(steps,),
+            in_specs=[block, block] + [whole(event.keep.shape) for event in events],
+            out_specs=[
+                pl.BlockSpec((shape[0], shape[1] // steps), lambda n, t: (0, n)),
+                whole(TOKEN.shape),
+            ],
         ),
         out_shape=[jax.ShapeDtypeStruct(shape, F32), TOKEN],
         compiler_params=params(),
@@ -1289,7 +1323,6 @@
     output_gather = Gather(output_weight, 1, place, (0,))
     expand_gather = Gather(expand_weight, 0, place, (1,), core)
     shrink_gather = Gather(shrink_weight, 1, place, (), core)
-    gathers = (input_gather, output_gather, expand_gather, shrink_gather)
 
     group = ((c_index * units) & (seqs - 1)) >> bits_of(units)
     low_bits = bits_of(ctx_size // pairs)
@@ -1299,11 +1332,18 @@
     else:
         owners = jnp.arange(fsdp_size, dtype=jnp.int32)
 
+    small, expand_gather.first = lax.optimization_barrier((small, expand_gather.first))
+    input_gather.fetch()
+    if fsdp_size == 2:
+        shards = [small, swap_bit(small, "fsdp", 2, 0)]
+    else:
+        full = lax.all_gather(small, "fsdp", axis=0)
+        shards = [full[number] for number in range(fsdp_size)]
     ready = (
         x,
-        small,
+        shards[-1],
         starts,
-        [gather.first for gather in gathers[1:]],
+        [gather.first for gather in (output_gather, shrink_gather)],
         [
             unit_seqs,
             owners,
@@ -1316,20 +1356,15 @@
             jnp.stack([group, y_index, c_index & (low - 1)]),
         ],
     )
-    x, small, starts, firsts, tables = lax.optimization_barrier(ready)
-    for gather, first in zip(gathers[1:], firsts):
+    x, shards[-1], starts, firsts, tables = lax.optimization_barrier(ready)
+    for gather, first in zip((output_gather, shrink_gather), firsts):
         gather.first = first
     unit_seqs, owners, input_gather.offsets, output_gather.offsets, *tables = tables
     feed_table, finish_table, back_table, entry_table, terms_table = tables
 
-    input_gather.fetch()
-    if fsdp_size == 2:
-        small_other = Event(swap_bit(small, "fsdp", 2, 0))
-        input_gather.keep = after(input_gather.keep, small_other)
-        shards = [small, small_other.keep]
-    else:
-        full = lax.all_gather(small, "fsdp", axis=0)
-        shards = [full[number] for number in range(fsdp_size)]
+    small_done = Event(shards[-1])
+    input_gather.keep = after(input_gather.keep, small_done)
+    shards[-1] = small_done.keep
     h1, vectors, expand_vector = first_norm(x, shards, owners, hidden)
     other = Event(swap_bit(og, "ctx", ctx_size, 0))
     expand_gather.fetch(input_gather)
@@ -1364,7 +1399,7 @@
     output_parts = output_gather.result()
     residual, h2, mixed = branch(att, x, vectors, output_parts)
     h2_other = swap_bit(h2, "ctx", ctx_size, 0)
-    send, keep, send_s, keep_s, send_e, keep_e, eb_grad, sb_grad = feed_forward(
+    dh2_send, dh2_keep, out_send, out_keep, send_s, keep_s, send_e, keep_e, eb_grad, sb_grad = feed_forward(
         feed_table,
         residual,
         h2,
@@ -1377,21 +1412,20 @@
         shrink_gather.result(),
         sizes,
     )
-    other = swap_bit(send, "ctx", ctx_size, 0)
+    dh2_other = swap_bit(dh2_send, "ctx", ctx_size, 0)
+    out_other = swap_bit(out_send, "ctx", ctx_size, 0)
 
     every = [("fsdp", bit) for bit in reversed(range(bits_of(fsdp_size)))]
     high = [("ctx", bit) for bit in reversed(range(1, bits_of(ctx_size)))]
     flow_s = Flow(send_s, keep_s, every[0], every[1:] + high, every[1:] + high[::-1], sizes)
     dres, dmixed, keep_o, send_o, vec_two = branch_back(
-        back_table, keep, other, residual, og, mixed, vectors, output_parts, sizes, seqs, rows
+        back_table, dh2_keep, dh2_other, residual, og, mixed, vectors, output_parts, sizes, seqs, rows
     )
     branch_done = Event(vec_two)
     send_e = after(send_e, branch_done)
-    flow_e = Flow(
-        send_e, keep_e, high[-1], every + high[:-1], every + high[:-1][::-1], sizes
-    )
+    flow_e = Flow(send_e, keep_e, every[0], every[1:] + high, every[1:] + high[::-1], sizes)
     spread_s = [bit for _, bit in high] + [0]
-    spread_e = [1] + [bit for bit in spread_s if bit > 1] + [0]
+    spread_e = spread_s
     flow_o = Flow(send_o, keep_o, ("ctx", 0), every + high, every + high[::-1], sizes)
     dmixed = dmixed.reshape(ctx_size, units, rows, LANES)
     dmixed = lax.all_to_all(dmixed, "ctx", 0, 0, tiled=True)
@@ -1400,7 +1434,9 @@
     )
     back_done = Event(token)
     last = flow_s.step(back_done)
-    held = Event(after(dqkv, last))
+    out_done = Event(out_other)
+    held = Event(after(after(dqkv, last), out_done))
+    out_other = out_done.keep
     keep_i, send_i, token = input_weight_terms(gathered, held.keep, terms_table, low, fsdp_size)
     terms_done = Event(token)
     low_labels = [("ctx", bit) for bit in reversed(range(low_bits))]
@@ -1412,11 +1448,10 @@
         low_labels[1:] + every,
         sizes,
     )
-    last = flow_e.step(terms_done)
-    last = flow_i.step(last)
+    last = flow_i.step(terms_done)
     last = flow_o.step(last)
     last = flow_s.step(last)
-    while ("fsdp", 0) in flow_e.order:
+    while len(flow_e.order) >= len(high):
         last = flow_e.step(last)
     dqkv = lax.all_to_all(dqkv, "ctx", 0, 0, tiled=True).reshape(pairs, seqs, rows, 3 * LANES)
     last = flow_o.step(last)
@@ -1436,8 +1471,8 @@
         after(dqkv, last),
         x,
         dres,
-        keep,
-        other,
+        out_keep,
+        out_other,
         [branch_done.keep, sb_grad, eb_grad],
         vectors,
         (input_gather.result()[0], entry_table),
@@ -1451,25 +1486,38 @@
         last = totals.step(last)
     last = flow_e.step(last)
     flow_e.spread(spread_e)
-    while totals.labels:
+    last = flow_s.step(last)
+    last = flow_e.step(last)
+    while totals.received is not None:
         last = totals.step(last)
-    last = flow_e.step(last)
-    last = flow_s.step(last)
     while len(flow_e.spreading) > 1:
         last = flow_e.step(last)
-    last = totals.step(last)
     while flow_s.spreading:
         last = flow_s.step(last)
     rows_s = hidden // ctx_size
-    shrink_grad, token = finish(flow_s.keep, None, 0, finish_table, 0, rows_s, part, spread_s)
-    shrink_done = Event(token)
-    flow_e.received = after(flow_e.received, shrink_done)
-    while flow_e.spreading:
-        last = flow_e.step(last)
+    sums = totals.keep
+    own_sums = lax.dynamic_slice_in_dim(sums[:8], y_index * part, part, 1)
+    hidden_part = hidden // fsdp_size
+    own_hidden = lax.dynamic_slice_in_dim(
+        sums[8:].reshape(1, hidden), y_index * hidden_part, hidden_part, 1
+    )
+    shrink_grad, token = finish(
+        flow_s.keep,
+        None,
+        0,
+        finish_table,
+        0,
+        rows_s,
+        part,
+        spread_s,
+        [own_sums, own_hidden],
+    )
+    flow_s.received = after(flow_s.received, Event(token))
     last = flow_s.step(last)
     shrink_grad, token = finish(
         flow_s.far, shrink_grad, 1, finish_table, 0, rows_s, part, spread_s
     )
+    shrink_done = Event(token)
     input_grad_w, token = finish_extra(
         flow_s.keep,
         flow_s.far,
@@ -1481,16 +1529,20 @@
         spread_s,
     )
     input_done = Event(token)
-    expand_grad, _ = finish(
+    flow_e.received = after(flow_e.received, shrink_done)
+    flow_e.received = after(flow_e.received, input_done)
+    while flow_e.spreading:
+        last = flow_e.step(last)
+    expand_grad, token = finish(
         flow_e.keep, None, 0, finish_table, 1, part, rows_s, spread_e
     )
-    flow_e.received = after(flow_e.received, input_done)
+    flow_e.received = after(flow_e.received, Event(token))
     last = flow_e.step(last)
     expand_grad, token = finish(
         flow_e.far, expand_grad, 1, finish_table, 1, part, rows_s, spread_e
     )
     expand_done = Event(token)
-    output_grad_w, _ = finish_extra(
+    output_grad_w, _ = finish_rows(
         flow_e.keep,
         flow_e.far,
         finish_table,
@@ -1501,28 +1553,22 @@
         spread_e,
         [project_done, back_done, terms_done, branch_done, shrink_done, input_done, expand_done],
     )
-    sums = totals.keep
-
-    def own(vector):
-        size = vector.shape[0] // fsdp_size
-        return lax.dynamic_slice_in_dim(vector, y_index * size, size, 0)
-
     return (
         out.reshape(seqs, rows, features),
         input_grad.reshape(seqs, rows, features),
-        own(sums[0]),
-        own(sums[1]),
+        own_sums[0],
+        own_sums[1],
         input_grad_w,
-        own(sums[2]),
-        own(sums[3]),
+        own_sums[2],
+        own_sums[3],
         output_grad_w,
-        own(sums[6]),
-        own(sums[4]),
-        own(sums[5]),
+        own_sums[6],
+        own_sums[4],
+        own_sums[5],
         expand_grad,
-        own(sums[8:].reshape(-1)),
+        own_hidden[0],
         shrink_grad,
-        own(sums[7]),
+        own_sums[7],
     )
 
 

time: 471 us -> 462 us (0.981)
  waiting for transfers between devices: 228 us -> 219 us
    ppermute x39 -> x40, waiting for transfers between devices: 191 us -> 182 us  [swap_bit(): return lax.ppermute(value, axis, [(i, i ^ 1 << bit) for i in range(size)])]
    unnamed x82 -> x96, local copies, waits for them, and re-layouts: 30.3 us -> 36.4 us
    dynamic_slice x9 -> x2, local copies, waits for them, and re-layouts: 5.24 us -> 0.02 us  [the longest x1 0.01 us: body(): lax.dynamic_slice_in_dim(sums[8:].reshape(1, hidden), y_index * hidden_pa...]
    ppermute x39 -> x40, starting transfers between devices: 41.3 us -> 41.9 us  [swap_bit(): return lax.ppermute(value, axis, [(i, i ^ 1 << bit) for i in range(size)])]
  transfers between devices with their start and end apart: 44 -> 45, of which waited for: 27 -> 27; matrix products, arithmetic and copies ran while one was open for 5% -> 4% of each run, Pallas kernels for 20% -> 20%
where the time goes in v4:
time: 462 us; the launch traced here: 460 us
  waiting for transfers between devices  219 us (47%)
  Pallas kernels  108 us (23%)
  starting transfers between devices  70.4 us (15%)
  local copies, waits for them, and re-layouts  45.4 us (10%)
  between operations  14.6 us (3%)
    ppermute x40, waiting for transfers between devices, swap_bit(): return lax.ppermute(value, axis, [(i, i ^ 1 << bit) for i in range(size)])  182 us
    ppermute x40, starting transfers between devices, swap_bit(): return lax.ppermute(value, axis, [(i, i ^ 1 << bit) for i in range(size)])  41.9 us
    unnamed x96, local copies, waits for them, and re-layouts  36.4 us
    pallas_call x1, Pallas kernels, feed_forward(): pl.pallas_call(functools.partial(ffn_kernel, len(expand_arrays), len(shri...  21.6 us
    all_to_all x1, waiting for transfers between devices, body(): dmixed = lax.all_to_all(dmixed, 'ctx', 0, 0, tiled=True)  19.8 us
    pallas_call x4, Pallas kernels, finish(): pl.pallas_call(functools.partial(finish_kernel, dim, order[:group]), grid...  13.7 us
    all_to_all x1, waiting for transfers between devices, body(): qkv = lax.all_to_all(qkv, 'ctx', 0, 0, tiled=True)  12.5 us
    pallas_call x8, Pallas kernels, combine(): pl.pallas_call(combine_kernel, grid=(outer, inner // per), in_specs=[bloc...  10.6 us
  transfers between devices with their start and end apart: 45, of which 27 were waited for; matrix products, arithmetic and copies ran while one was open for 4% of the time, Pallas kernels for 20%

profile of v4, /device:TPU:0, one launch (start us, length us, event | category | flops | bytes accessed | tf_op | source)
XLA Modules:
  0.0 459.9 jit_solution(11769150278498423786)
XLA Ops:
  8.5 3.0 collective-permute-start.1
  19.1 2.3 dynamic_slice.18
  22.6 3.1 constant_dynamic-slice_fusion.4
  25.7 2.3 convert_reduce_fusion
  33.8 14.5 %collective-permute-done.2.refs_2_.refs_7_.refs_12_ = bf16[128,3072]{1,0:T(8,128)(2,1)S(1)} collective-permute-done((bf16[128,3072]{1,0:T(8,128)(2,1)S(1)}, bf16[128,3072]{1,0:T(8,128)(2,1)S(1)}, u32[]{:S(2)}, u32[]{:S(2)}) %collective-permute-start.2) | collective-permute-done | bytes 786464 | tf_op jit(solution)/shard_map/ppermute | solution.py:41
  48.8 6.4 %collective-permute-done.3.refs_1_ = bf16[256,2048]{1,0:T(8,128)(2,1)S(1)} collective-permute-done((bf16[256,2048]{1,0:T(8,128)(2,1)}, bf16[256,2048]{1,0:T(8,128)(2,1)S(1)}, u32[]{:S(2)}, u32[]{:S(2)}) %collective-permute-start.3) | collective-permute-done | bytes 1048608 | tf_op jit(solution)/shard_map/ppermute | solution.py:41
  56.2 5.0 %project.1 = (bf16[8,4,64,384]{3,2,1,0:T(8,128)(2,1)S(1)}, f32[8,128]{1,0:T(8,128)S(1)}) custom-call(s32[5]{0:T(128)S(1)} %pad_add_fusion.1.off_ref, bf16[256,1024]{1,0:T(8,128)(2,1)S(1)} %get-tuple-element.250.h_ref, f32[8,1024]{1,0:T(8,128)S(1)} %get-tuple-element.201.v_ref, bf16[512,3072]{1,0:T(8,128)(2,1)} %refs_10_.3, ...), custom_call_target="tpu_custom_call" | custom-call | tf_op jit(solution)/shard_map/project/pallas_call | solution.py:220
  62.4 5.2 %all-to-all-start = ((bf16[16,2,64,384]{3,2,1,0:T(8,128)(2,1)}), bf16[16,2,64,384]{3,2,1,0:T(8,128)(2,1)}, u32[]{:S(2)}, u32[]{:S(2)}) async-start(bf16[16,2,64,384]{3,2,1,0:T(8,128)(2,1)} %bitcast.89), calls=%async_computation | async-start | bytes 3145728 | tf_op jit(solution)/shard_map/all_to_all | solution.py:1387
  69.2 12.8 %collective-permute-done.6.refs_1_ = bf16[1024,256]{1,0:T(8,128)(2,1)S(1)} collective-permute-done((bf16[1024,256]{1,0:T(8,128)(2,1)}, bf16[1024,256]{1,0:T(8,128)(2,1)S(1)}, u32[]{:S(2)}, u32[]{:S(2)}) %collective-permute-start.6) | collective-permute-done | bytes 524320 | tf_op jit(solution)/shard_map/ppermute | solution.py:41
  87.3 12.5 %all-to-all-done.qkv_ref = bf16[16,2,64,384]{3,2,1,0:T(8,128)(2,1)} async-done(((bf16[16,2,64,384]{3,2,1,0:T(8,128)(2,1)}), bf16[16,2,64,384]{3,2,1,0:T(8,128)(2,1)}, u32[]{:S(2)}, u32[]{:S(2)}) %all-to-all-start) | async-done | bytes 1572896 | tf_op jit(solution)/shard_map/all_to_all | solution.py:1387
  99.8 9.9 %attend.1 = (bf16[16,2,64,128]{3,2,1,0:T(8,128)(2,1)S(1)}, f32[2,2,1024]{2,1,0:T(2,128)S(1)}) custom-call(s32[16]{0:T(128)S(1)} %copy-done.37, s32[2]{0:T(128)S(1)} %add_and_fusion.seq_ref, bf16[16,2,64,384]{3,2,1,0:T(8,128)(2,1)} %all-to-all-done.qkv_ref, s32[4,1,1024]{2,1,0:T(1,128)S(1)} %broadcast_in_dim.2.start_ref), custom_call_target="tpu_custom_call" | custom-call | tf_op jit(solution)/shard_map/attend/pallas_call | solution.py:315
  110.5 9.2 %all-to-all-start.1 = ((bf16[16,2,64,128]{3,2,1,0:T(8,128)(2,1)}), bf16[16,2,64,128]{3,2,1,0:T(8,128)(2,1)}, u32[]{:S(2)}, u32[]{:S(2)}) async-start(bf16[16,2,64,128]{3,2,1,0:T(8,128)(2,1)} %copy-done.35), calls=%async_computation.1 | async-start | bytes 1048576 | tf_op jit(solution)/shard_map/all_to_all | solution.py:1393
  119.9 9.5 %collective-permute-done.10.refs_4_ = bf16[2048,512]{1,0:T(8,128)(2,1)} collective-permute-done((bf16[2048,512]{1,0:T(8,128)(2,1)}, bf16[2048,512]{1,0:T(8,128)(2,1)}, u32[]{:S(2)}, u32[]{:S(2)}) %collective-permute-start.10) | collective-permute-done | bytes 2097184 | tf_op jit(solution)/shard_map/ppermute | solution.py:41
  129.4 4.8 %all-to-all-done.1 = bf16[16,2,64,128]{3,2,1,0:T(8,128)(2,1)} async-done(((bf16[16,2,64,128]{3,2,1,0:T(8,128)(2,1)}), bf16[16,2,64,128]{3,2,1,0:T(8,128)(2,1)}, u32[]{:S(2)}, u32[]{:S(2)}) %all-to-all-start.1) | async-done | bytes 524320 | tf_op jit(solution)/shard_map/all_to_all | solution.py:1393
  138.6 2.8 branch.1
  144.3 21.6 %feed_forward.1 = (f32[256,1024]{1,0:T(8,128)S(1)}, f32[256,1024]{1,0:T(8,128)S(1)}, f32[256,1024]{1,0:T(8,128)S(1)}, f32[256,1024]{1,0:T(8,128)}, bf16[1,4,2,25...) custom-call(s32[9]{0:T(128)S(1)} %concatenate.23.sc_ref, ...), custom_call_target="tpu_custom_call" | custom-call | tf_op jit(solution)/shard_map/feed_forward/pallas_call | solution.py:630
  172.4 5.3 %branch_back.1 = (f32[256,1024]{1,0:T(8,128)S(1)}, bf16[8,4,64,128]{3,2,1,0:T(8,128)(2,1)S(1)}, bf16[2,8,64,512]{3,2,1,0:T(8,128)(2,1)S(1)}, bf16[2,8,64,512]{3,2,1,0:T(8,128)(2,1)S(1)}, f32[8,1024]{1,0:T(8,128)S(1)}) custom-call(s32[5]{0:T(128)S(1)} %pad_add_fusion.4.sc_ref, f32[256,1024]{1,0:T(8,128)} %copy-done.24, f32[256,1024]{1,0:T(8,128)} %copy-done.40, ...), custom_call_target="tpu_custom_call" | custom-call | tf_op jit(solution)/shard_map/branch_back/pallas_call | solution.py:722
  181.4 4.5 all-to-all-start.2
  187.6 19.8 %all-to-all-done.2.grad_ref = bf16[16,2,64,128]{3,2,1,0:T(8,128)(2,1)} async-done(((bf16[16,2,64,128]{3,2,1,0:T(8,128)(2,1)}), bf16[16,2,64,128]{3,2,1,0:T(8,128)(2,1)}, u32[]{:S(2)}, u32[]{:S(2)}) %all-to-all-start.2) | async-done | bytes 524320 | tf_op jit(solution)/shard_map/all_to_all | solution.py:1431
  207.4 10.4 %attend_back.1 = (bf16[16,2,64,384]{3,2,1,0:T(8,128)(2,1)S(1)}, f32[8,128]{1,0:T(8,128)S(1)}) custom-call(s32[16]{0:T(128)S(1)} %copy-done.37, s32[2]{0:T(128)S(1)} %add_and_fusion.seq_ref, bf16[16,2,64,384]{3,2,1,0:T(8,128)(2,1)} %all-to-all-done.qkv_ref, bf16[16,2,64,128]{3,2,1,0:T(8,128)(2,1)} %all-to-all-done.2.grad_ref, ...), custom_call_target="tpu_custom_call" | custom-call | tf_op jit(solution)/shard_map/attend_back/pallas_call | solution.py:423
  218.9 9.5 %all-to-all-start.3 = ((bf16[16,2,64,384]{3,2,1,0:T(8,128)(2,1)}), bf16[16,2,64,384]{3,2,1,0:T(8,128)(2,1)}, u32[]{:S(2)}, u32[]{:S(2)}) async-start(bf16[16,2,64,384]{3,2,1,0:T(8,128)(2,1)} %copy-done.3), calls=%async_computation.3 | async-start | bytes 3145728 | tf_op jit(solution)/shard_map/all_to_all | solution.py:1456
  230.4 3.6 combine.8
  238.1 5.6 %input_weight_terms.1 = (bf16[1,2,256,384]{3,2,1,0:T(8,128)(2,1)S(1)}, bf16[1,2,256,384]{3,2,1,0:T(8,128)(2,1)S(1)}, f32[8,128]{1,0:T(8,128)S(1)}) custom-call(s32[3]{0:T(128)S(1)} %get-tuple-element.249.sc_ref, bf16[16,4,64,1024]{3,2,1,0:T(8,128)(2,1)} %all-gather.2.cloned.1.call-done.h_ref, bf16[16,2,64,384]{3,2,1,0:T(8,128)(2,1)S(1)} %copy-done.4), custom_call_target="tpu_custom_call" | custom-call | tf_op jit(solution)/shard_map/input_weight_terms/pallas_call | solution.py:778
  247.1 23.9 %collective-permute-done.15 = bf16[4,1,256,512]{3,2,1,0:T(8,128)(2,1)} collective-permute-done((bf16[4,1,256,512]{3,2,1,0:T(8,128)(2,1)}, bf16[4,1,256,512]{3,2,1,0:T(8,128)(2,1)}, u32[]{:S(2)}, u32[]{:S(2)}) %collective-permute-start.15) | collective-permute-done | bytes 1048608 | tf_op jit(solution)/shard_map/ppermute | solution.py:41
  272.3 2.6 combine.12
  274.9 2.1 collective-permute-start.19
  280.4 11.4 %collective-permute-done.20 = bf16[1,8,64,512]{3,2,1,0:T(8,128)(2,1)S(1)} collective-permute-done((bf16[1,8,64,512]{3,2,1,0:T(8,128)(2,1)S(1)}, bf16[1,8,64,512]{3,2,1,0:T(8,128)(2,1)S(1)}, u32[]{:S(2)}, u32[]{:S(2)}) %collective-permute-start.20) | collective-permute-done | bytes 524320 | tf_op jit(solution)/shard_map/ppermute | solution.py:41
  292.1 2.4 collective-permute-done.23
  296.1 9.5 %collective-permute-done.21 = bf16[4,1,64,512]{3,2,1,0:T(8,128)(2,1)S(1)} collective-permute-done((bf16[4,1,64,512]{3,2,1,0:T(8,128)(2,1)S(1)}, bf16[4,1,64,512]{3,2,1,0:T(8,128)(2,1)S(1)}, u32[]{:S(2)}, u32[]{:S(2)}) %collective-permute-start.21) | collective-permute-done | bytes 262176 | tf_op jit(solution)/shard_map/ppermute | solution.py:41
  309.0 2.1 collective-permute-start.25
  314.6 7.8 %entry_back.1 = (f32[256,1024]{1,0:T(8,128)}, bf16[256,1024]{1,0:T(8,128)(2,1)}, f32[12,1024]{1,0:T(8,128)S(1)}) custom-call(s32[6]{0:T(128)S(1)} %pad_add_fusion.5.off_ref, bf16[8,4,64,384]{3,2,1,0:T(8,128)(2,1)} %bitcast.15.d_ref, bf16[256,1024]{1,0:T(8,128)(2,1)S(1)} %bitcast.78, f32[256,1024]{1,0:T(8,128)S(1)} %copy-done.31, f32[256,1024]{1,0:T(8,128)S(1)} %copy-done.29, ...), custom_call_target="tpu_custom_call" | custom-call | tf_op jit(solution)/shard_map/entry_back/pallas_call | solution.py:874
  322.5 10.2 %collective-permute-done.26 = bf16[2,640,256]{2,1,0:T(8,128)(2,1)} collective-permute-done((bf16[2,640,256]{2,1,0:T(8,128)(2,1)}, bf16[2,640,256]{2,1,0:T(8,128)(2,1)}, u32[]{:S(2)}, u32[]{:S(2)}) %collective-permute-start.26) | collective-permute-done | bytes 655392 | tf_op jit(solution)/shard_map/ppermute | solution.py:41
  336.5 2.1 collective-permute-start.28
  340.2 2.6 collective-permute-done.29.two_ref
  344.1 3.1 collective-permute-done.30.two_ref
  347.3 16.9 %collective-permute-done.31.two_ref = f32[12,1024]{1,0:T(8,128)S(1)} collective-permute-done((f32[12,1024]{1,0:T(8,128)S(1)}, f32[12,1024]{1,0:T(8,128)S(1)}, u32[]{:S(2)}, u32[]{:S(2)}) %collective-permute-start.31) | collective-permute-done | bytes 49184 | tf_op jit(solution)/shard_map/ppermute | solution.py:41
  367.2 14.4 %collective-permute-done.32.two_ref = bf16[1,640,256]{2,1,0:T(8,128)(2,1)S(1)} collective-permute-done((bf16[1,640,256]{2,1,0:T(8,128)(2,1)S(1)}, bf16[1,640,256]{2,1,0:T(8,128)(2,1)S(1)}, u32[]{:S(2)}, u32[]{:S(2)}) %collective-permute-start.32) | collective-permute-done | bytes 327712 | tf_op jit(solution)/shard_map/ppermute | solution.py:41
  381.8 2.5 collective-permute-start.34
  384.3 12.9 %collective-permute-done.34.two_ref = f32[12,1024]{1,0:T(8,128)S(1)} collective-permute-done((f32[12,1024]{1,0:T(8,128)S(1)}, f32[12,1024]{1,0:T(8,128)S(1)}, u32[]{:S(2)}, u32[]{:S(2)}) %collective-permute-start.34) | collective-permute-done | bytes 49184 | tf_op jit(solution)/shard_map/ppermute | solution.py:41
  399.5 5.3 %collective-permute-done.36.two_ref = bf16[4,448,512]{2,1,0:T(8,128)(2,1)S(1)} collective-permute-done((bf16[4,448,512]{2,1,0:T(8,128)(2,1)S(1)}, bf16[4,448,512]{2,1,0:T(8,128)(2,1)S(1)}, u32[]{:S(2)}, u32[]{:S(2)}) %collective-permute-start.36) | collective-permute-done | bytes 1835040 | tf_op jit(solution)/shard_map/ppermute | solution.py:41
  404.8 2.3 merge.10
  410.7 2.7 finish.4
  413.8 5.0 %finish_extra.1 = (f32[512,3072]{1,0:T(8,128)}, f32[8,128]{1,0:T(8,128)S(1)}) custom-call(s32[2]{0:T(128)S(1)} %get-tuple-element.322.label_ref, bf16[8,448,512]{2,1,0:T(8,128)(2,1)S(1)} %bitcast.68, bf16[8,448,512]{2,1,0:T(8,128)(2,1)} %collective-permute-done.37.far_ref.source), custom_call_target="tpu_custom_call" | custom-call | tf_op jit(solution)/shard_map/finish_extra/pallas_call | solution.py:1223
  418.8 4.2 finish.5
  423.0 15.3 %collective-permute-done.38.two_ref = bf16[4,640,256]{2,1,0:T(8,128)(2,1)S(1)} collective-permute-done((bf16[4,640,256]{2,1,0:T(8,128)(2,1)S(1)}, bf16[4,640,256]{2,1,0:T(8,128)(2,1)S(1)}, u32[]{:S(2)}, u32[]{:S(2)}) %collective-permute-start.38) | collective-permute-done | bytes 1310752 | tf_op jit(solution)/shard_map/ppermute | solution.py:41
  441.7 2.7 finish.6
  446.0 4.0 finish.7
  450.0 3.1 finish_rows.1
  (200 shorter events, 90.8 us)
Async XLA Ops:
  8.5 21.1 %collective-permute-start.1 = (bf16[128,3072]{1,0:T(8,128)(2,1)S(1)}, bf16[128,3072]{1,0:T(8,128)(2,1)S(1)}, u32[]{:S(2)}, u32[]{:S(2)}) collective-permute-start(bf16[128,3072]{1,0:T(8,128)(2,1)S(1)} %constant_dynamic-slice_fusion.3), channel_id=1, source_target_pairs={{0,16},{16,0},{1,17},{17,1},{2,18},{18,2},{3,19},{19,3},{4,20},{20... | collective-permute-start | bytes 2359304 | tf_op jit(solution)/shard_map/ppermute | solution.py:41
  21.4 8.2 %collective-permute-start = (bf16[1,6144]{1,0:T(2,128)(2,1)S(1)}, bf16[1,6144]{1,0:T(2,128)(2,1)S(1)}, u32[]{:S(2)}, u32[]{:S(2)}) collective-permute-start(bf16[1,6144]{1,0:T(2,128)(2,1)S(1)} %reshape.159.refs_0_), channel_id=1, source_target_pairs={{0,16},{16,0},{1,17},{17,1},{2,18},{18,2},{3,19},{19,3},{4,20},{20... | collective-permute-start | bytes 36872 | tf_op jit(solution)/shard_map/ppermute | solution.py:41
  29.6 18.7 %collective-permute-start.2 = (bf16[128,3072]{1,0:T(8,128)(2,1)S(1)}, bf16[128,3072]{1,0:T(8,128)(2,1)S(1)}, u32[]{:S(2)}, u32[]{:S(2)}) collective-permute-start(bf16[128,3072]{1,0:T(8,128)(2,1)S(1)} %collective-permute-done.1.refs_1_.refs_6_.refs_11_), channel_id=1, source_target_pairs={{0,2},{1,3},{2,0},{3,1},{4,6},{5,7},{6,4},{7,5},{8,10},{9,11},{10,... | collective-permute-start | bytes 2359304 | tf_op jit(solution)/shard_map/ppermute | solution.py:41
  31.3 24.0 %collective-permute-start.3 = (bf16[256,2048]{1,0:T(8,128)(2,1)}, bf16[256,2048]{1,0:T(8,128)(2,1)S(1)}, u32[]{:S(2)}, u32[]{:S(2)}) collective-permute-start(bf16[256,2048]{1,0:T(8,128)(2,1)} %dynamic_slice.18), channel_id=1, source_target_pairs={{0,16},{16,0},{1,17},{17,1},{2,18},{18,2},{3,19},{19,3},{4,20},{20... | collective-permute-start | bytes 3145736 | tf_op jit(solution)/shard_map/ppermute | solution.py:41
  48.3 6.9 %collective-permute-start.4 = (bf16[128,3072]{1,0:T(8,128)(2,1)S(1)}, bf16[128,3072]{1,0:T(8,128)(2,1)S(1)}, u32[]{:S(2)}, u32[]{:S(2)}) collective-permute-start(bf16[128,3072]{1,0:T(8,128)(2,1)S(1)} %collective-permute-done.2.refs_2_.refs_7_.refs_12_), channel_id=1, source_target_pairs={{0,1},{1,0},{2,3},{3,2},{4,5},{5,4},{6,7},{7,6},{8,9},{9,8},{10,11... | collective-permute-start | bytes 2359304 | tf_op jit(solution)/shard_map/ppermute | solution.py:41
  48.3 6.9 %collective-permute-start.5 = (bf16[128,3072]{1,0:T(8,128)(2,1)S(1)}, bf16[128,3072]{1,0:T(8,128)(2,1)S(1)}, u32[]{:S(2)}, u32[]{:S(2)}) collective-permute-start(bf16[128,3072]{1,0:T(8,128)(2,1)S(1)} %collective-permute-done.1.refs_1_.refs_6_.refs_11_), channel_id=1, source_target_pairs={{0,1},{1,0},{2,3},{3,2},{4,5},{5,4},{6,7},{7,6},{8,9},{9,8},{10,11... | collective-permute-start | bytes 2359304 | tf_op jit(solution)/shard_map/ppermute | solution.py:41
  62.4 37.4 %copy-start.37 = (s32[16]{0:T(128)S(1)}, s32[16]{0:T(128)}, u32[]{:S(2)}) copy-start(s32[16]{0:T(128)} %table.3) | copy-start | bytes 196
  62.4 37.3 %all-to-all-start = ((bf16[16,2,64,384]{3,2,1,0:T(8,128)(2,1)}), bf16[16,2,64,384]{3,2,1,0:T(8,128)(2,1)}, u32[]{:S(2)}, u32[]{:S(2)}) async-start(bf16[16,2,64,384]{3,2,1,0:T(8,128)(2,1)} %bitcast.89), calls=%async_computation | async-start | bytes 3145728 | tf_op jit(solution)/shard_map/all_to_all | solution.py:1387
  67.6 14.4 %collective-permute-start.6 = (bf16[1024,256]{1,0:T(8,128)(2,1)}, bf16[1024,256]{1,0:T(8,128)(2,1)S(1)}, u32[]{:S(2)}, u32[]{:S(2)}) collective-permute-start(bf16[1024,256]{1,0:T(8,128)(2,1)} %constant_dynamic-slice_fusion.5), channel_id=1, source_target_pairs={{0,16},{16,0},{1,17},{17,1},{2,18},{18,2},{3,19},{19,3},{4,20},{20... | collective-permute-start | bytes 1572872 | tf_op jit(solution)/shard_map/ppermute | solution.py:41
  82.0 47.4 %collective-permute-start.10 = (bf16[2048,512]{1,0:T(8,128)(2,1)}, bf16[2048,512]{1,0:T(8,128)(2,1)}, u32[]{:S(2)}, u32[]{:S(2)}) collective-permute-start(bf16[2048,512]{1,0:T(8,128)(2,1)} %constant_dynamic-slice_fusion.4), channel_id=1, source_target_pairs={{0,16},{16,0},{1,17},{17,1},{2,18},{18,2},{3,19},{19,3},{4,20},{20... | collective-permute-start | bytes 6291464 | tf_op jit(solution)/shard_map/ppermute | solution.py:41
  83.5 3.0 collective-permute-start.7
  84.3 15.4 %collective-permute-start.8 = (bf16[256,1024]{1,0:T(8,128)(2,1)}, bf16[256,1024]{1,0:T(8,128)(2,1)}, u32[]{:S(2)}, u32[]{:S(2)}) collective-permute-start(bf16[256,1024]{1,0:T(8,128)(2,1)} %bitcast.83), channel_id=1, source_target_pairs={{0,1},{1,0},{2,3},{3,2},{4,5},{5,4},{6,7},{7,6},{8,9},{9,8},{10,11... | collective-permute-start | bytes 1572872 | tf_op jit(solution)/shard_map/ppermute | solution.py:41
  84.8 44.6 %collective-permute-start.9 = (bf16[256,2048]{1,0:T(8,128)(2,1)}, bf16[256,2048]{1,0:T(8,128)(2,1)}, u32[]{:S(2)}, u32[]{:S(2)}) collective-permute-start(bf16[256,2048]{1,0:T(8,128)(2,1)} %copy-done.41), channel_id=1, source_target_pairs={{0,2},{1,3},{2,0},{3,1},{4,6},{5,7},{6,4},{7,5},{8,10},{9,11},{10,... | collective-permute-start | bytes 3145736 | tf_op jit(solution)/shard_map/ppermute | solution.py:41
  110.5 23.7 %all-to-all-start.1 = ((bf16[16,2,64,128]{3,2,1,0:T(8,128)(2,1)}), bf16[16,2,64,128]{3,2,1,0:T(8,128)(2,1)}, u32[]{:S(2)}, u32[]{:S(2)}) async-start(bf16[16,2,64,128]{3,2,1,0:T(8,128)(2,1)} %copy-done.35), calls=%async_computation.1 | async-start | bytes 1048576 | tf_op jit(solution)/shard_map/all_to_all | solution.py:1393
  119.7 117.0 %all-gather.2.cloned.1.call-start = ((), (), s32[]{:S(2)}) async-start(), calls=%async_computation.4 | async-start | bytes 8912896 | tf_op jit(solution)/shard_map/all_gather | solution.py:1395
  142.4 1.9 collective-permute-start.11
  167.8 3.6 collective-permute-start.12
  168.0 60.8 %collective-permute-start.14 = (bf16[1,4,2,256,512]{4,3,2,1,0:T(8,128)(2,1)}, bf16[1,4,2,256,512]{4,3,2,1,0:T(8,128)(2,1)}, u32[]{:S(2)}, u32[]{:S(2)}) collective-permute-start(bf16[1,4,2,256,512]{4,3,2,1,0:T(8,128)(2,1)} %get-tuple-element.241), channel_id=1, source_target_pairs={{0,16},{16,0},{1,17},{17,1},{2,18},{18,2},{3,19},{19,3},{4,20},{20... | collective-permute-start | bytes 6291464 | tf_op jit(solution)/shard_map/ppermute | solution.py:41
  181.4 26.0 %all-to-all-start.2 = ((bf16[16,2,64,128]{3,2,1,0:T(8,128)(2,1)}), bf16[16,2,64,128]{3,2,1,0:T(8,128)(2,1)}, u32[]{:S(2)}, u32[]{:S(2)}) async-start(bf16[16,2,64,128]{3,2,1,0:T(8,128)(2,1)} %bitcast.99), calls=%async_computation.2 | async-start | bytes 1048576 | tf_op jit(solution)/shard_map/all_to_all | solution.py:1431
  185.8 86.4 %collective-permute-start.13 = (bf16[1,4,2,512,256]{4,3,2,1,0:T(8,128)(2,1)}, bf16[1,4,2,512,256]{4,3,2,1,0:T(8,128)(2,1)}, u32[]{:S(2)}, u32[]{:S(2)}) collective-permute-start(bf16[1,4,2,512,256]{4,3,2,1,0:T(8,128)(2,1)} %get-tuple-element.239), channel_id=1, source_target_pairs={{0,16},{16,0},{1,17},{17,1},{2,18},{18,2},{3,19},{19,3},{4,20},{20... | collective-permute-start | bytes 6291464 | tf_op jit(solution)/shard_map/ppermute | solution.py:41
  187.6 49.1 %collective-permute-start.17 = (f32[256,1024]{1,0:T(8,128)}, f32[256,1024]{1,0:T(8,128)}, u32[]{:S(2)}, u32[]{:S(2)}) collective-permute-start(f32[256,1024]{1,0:T(8,128)} %copy-done.38), channel_id=1, source_target_pairs={{0,1},{1,0},{2,3},{3,2},{4,5},{5,4},{6,7},{7,6},{8,9},{9,8},{10,11... | collective-permute-start | bytes 3145736 | tf_op jit(solution)/shard_map/ppermute | solution.py:41
  218.9 92.2 %all-to-all-start.3 = ((bf16[16,2,64,384]{3,2,1,0:T(8,128)(2,1)}), bf16[16,2,64,384]{3,2,1,0:T(8,128)(2,1)}, u32[]{:S(2)}, u32[]{:S(2)}) async-start(bf16[16,2,64,384]{3,2,1,0:T(8,128)(2,1)} %copy-done.3), calls=%async_computation.3 | async-start | bytes 3145728 | tf_op jit(solution)/shard_map/all_to_all | solution.py:1456
  228.4 17.1 %collective-permute-start.16 = (bf16[2,8,64,512]{3,2,1,0:T(8,128)(2,1)}, bf16[2,8,64,512]{3,2,1,0:T(8,128)(2,1)}, u32[]{:S(2)}, u32[]{:S(2)}) collective-permute-start(bf16[2,8,64,512]{3,2,1,0:T(8,128)(2,1)} %copy-done.39), channel_id=1, source_target_pairs={{0,1},{1,0},{2,3},{3,2},{4,5},{5,4},{6,7},{7,6},{8,9},{9,8},{10,11... | collective-permute-start | bytes 3145736 | tf_op jit(solution)/shard_map/ppermute | solution.py:41
  235.0 35.9 %collective-permute-start.15 = (bf16[4,1,256,512]{3,2,1,0:T(8,128)(2,1)}, bf16[4,1,256,512]{3,2,1,0:T(8,128)(2,1)}, u32[]{:S(2)}, u32[]{:S(2)}) collective-permute-start(bf16[4,1,256,512]{3,2,1,0:T(8,128)(2,1)} %get-tuple-element.246), channel_id=1, source_target_pairs={{0,2},{1,3},{2,0},{3,1},{4,6},{5,7},{6,4},{7,5},{8,10},{9,11},{10,... | collective-permute-start | bytes 3145736 | tf_op jit(solution)/shard_map/ppermute | solution.py:41
  238.1 32.8 %copy-start.28 = (bf16[4,1,256,512]{3,2,1,0:T(8,128)(2,1)S(1)}, bf16[4,1,256,512]{3,2,1,0:T(8,128)(2,1)}, u32[]{:S(2)}) copy-start(bf16[4,1,256,512]{3,2,1,0:T(8,128)(2,1)} %copy-done.27) | copy-start | bytes 3145732
  243.7 28.6 %copy-start.13 = (bf16[1,4,2,512,256]{4,3,2,1,0:T(8,128)(2,1)S(1)}, bf16[1,4,2,512,256]{4,3,2,1,0:T(8,128)(2,1)}, u32[]{:S(2)}) copy-start(bf16[1,4,2,512,256]{4,3,2,1,0:T(8,128)(2,1)} %get-tuple-element.236) | copy-start | bytes 6291460
  243.7 1.8 collective-permute-start.18
  274.9 30.8 %collective-permute-start.19 = (bf16[4,1,512,256]{3,2,1,0:T(8,128)(2,1)S(1)}, bf16[4,1,512,256]{3,2,1,0:T(8,128)(2,1)S(1)}, u32[]{:S(2)}, u32[]{:S(2)}) collective-permute-start(bf16[4,1,512,256]{3,2,1,0:T(8,128)(2,1)S(1)} %get-tuple-element.264), channel_id=1, source_target_pairs={{0,2},{1,3},{2,0},{3,1},{4,6},{5,7},{6,4},{7,5},{8,10},{9,11},{10,... | collective-permute-start | bytes 3145736 | tf_op jit(solution)/shard_map/ppermute | solution.py:41
  276.9 14.9 %collective-permute-start.20 = (bf16[1,8,64,512]{3,2,1,0:T(8,128)(2,1)S(1)}, bf16[1,8,64,512]{3,2,1,0:T(8,128)(2,1)S(1)}, u32[]{:S(2)}, u32[]{:S(2)}) collective-permute-start(bf16[1,8,64,512]{3,2,1,0:T(8,128)(2,1)S(1)} %get-tuple-element.266), channel_id=1, source_target_pairs={{0,16},{16,0},{1,17},{17,1},{2,18},{18,2},{3,19},{19,3},{4,20},{20... | collective-permute-start | bytes 1572872 | tf_op jit(solution)/shard_map/ppermute | solution.py:41
  278.6 16.0 %collective-permute-start.22 = (bf16[2,1,256,512]{3,2,0,1:T(8,128)(2,1)S(1)}, bf16[2,1,256,512]{3,2,0,1:T(8,128)(2,1)S(1)}, u32[]{:S(2)}, u32[]{:S(2)}) collective-permute-start(bf16[2,1,256,512]{3,2,0,1:T(8,128)(2,1)S(1)} %bitcast.112), channel_id=1, source_target_pairs={{0,4},{1,5},{2,6},{3,7},{4,0},{5,1},{6,2},{7,3},{8,12},{9,13},{10,... | collective-permute-start | bytes 1572872 | tf_op jit(solution)/shard_map/ppermute | solution.py:41
  280.0 14.5 %collective-permute-start.23 = (bf16[1,1,256,384]{3,2,1,0:T(8,128)(2,1)S(1)}, bf16[1,1,256,384]{3,2,1,0:T(8,128)(2,1)S(1)}, u32[]{:S(2)}, u32[]{:S(2)}) collective-permute-start(bf16[1,1,256,384]{3,2,1,0:T(8,128)(2,1)S(1)} %get-tuple-element.273), channel_id=1, source_target_pairs={{0,16},{16,0},{1,17},{17,1},{2,18},{18,2},{3,19},{19,3},{4,20},{20... | collective-permute-start | bytes 589832 | tf_op jit(solution)/shard_map/ppermute | solution.py:41
  292.0 13.7 %collective-permute-start.21 = (bf16[4,1,64,512]{3,2,1,0:T(8,128)(2,1)S(1)}, bf16[4,1,64,512]{3,2,1,0:T(8,128)(2,1)S(1)}, u32[]{:S(2)}, u32[]{:S(2)}) collective-permute-start(bf16[4,1,64,512]{3,2,1,0:T(8,128)(2,1)S(1)} %get-tuple-element.269), channel_id=1, source_target_pairs={{0,2},{1,3},{2,0},{3,1},{4,6},{5,7},{6,4},{7,5},{8,10},{9,11},{10,... | collective-permute-start | bytes 786440 | tf_op jit(solution)/shard_map/ppermute | solution.py:41
  294.7 13.5 %collective-permute-start.24 = (bf16[1,1,256,512]{3,2,1,0:T(8,128)(2,1)S(1)}, bf16[1,1,256,512]{3,2,1,0:T(8,128)(2,1)S(1)}, u32[]{:S(2)}, u32[]{:S(2)}) collective-permute-start(bf16[1,1,256,512]{3,2,1,0:T(8,128)(2,1)S(1)} %get-tuple-element.280), channel_id=1, source_target_pairs={{0,8},{1,9},{2,10},{3,11},{4,12},{5,13},{6,14},{7,15},{8,0},{9,1},... | collective-permute-start | bytes 786440 | tf_op jit(solution)/shard_map/ppermute | solution.py:41
  306.7 26.0 %collective-permute-start.26 = (bf16[2,640,256]{2,1,0:T(8,128)(2,1)}, bf16[2,640,256]{2,1,0:T(8,128)(2,1)}, u32[]{:S(2)}, u32[]{:S(2)}) collective-permute-start(bf16[2,640,256]{2,1,0:T(8,128)(2,1)} %get-tuple-element.299), channel_id=1, source_target_pairs={{0,4},{1,5},{2,6},{3,7},{4,0},{5,1},{6,2},{7,3},{8,12},{9,13},{10,... | collective-permute-start | bytes 1966088 | tf_op jit(solution)/shard_map/ppermute | solution.py:41
  309.0 24.9 %collective-permute-start.25 = (bf16[1,448,512]{2,1,0:T(8,128)(2,1)}, bf16[1,448,512]{2,1,0:T(8,128)(2,1)}, u32[]{:S(2)}, u32[]{:S(2)}) collective-permute-start(bf16[1,448,512]{2,1,0:T(8,128)(2,1)} %pack.1.one_ref), channel_id=1, source_target_pairs={{0,8},{1,9},{2,10},{3,11},{4,12},{5,13},{6,14},{7,15},{8,0},{9,1},... | collective-permute-start | bytes 1376264 | tf_op jit(solution)/shard_map/ppermute | solution.py:41
  335.1 29.2 %collective-permute-start.27 = (bf16[2,448,512]{2,1,0:T(8,128)(2,1)S(1)}, bf16[2,448,512]{2,1,0:T(8,128)(2,1)S(1)}, u32[]{:S(2)}, u32[]{:S(2)}) collective-permute-start(bf16[2,448,512]{2,1,0:T(8,128)(2,1)S(1)} %bitcast.79), channel_id=1, source_target_pairs={{0,4},{1,5},{2,6},{3,7},{4,0},{5,1},{6,2},{7,3},{8,12},{9,13},{10,... | collective-permute-start | bytes 2752520 | tf_op jit(solution)/shard_map/ppermute | solution.py:41
  336.5 27.8 %collective-permute-start.28 = (bf16[1,1,640,256]{3,2,1,0:T(8,128)(2,1)S(1)}, bf16[1,1,640,256]{3,2,1,0:T(8,128)(2,1)S(1)}, u32[]{:S(2)}, u32[]{:S(2)}) collective-permute-start(bf16[1,1,640,256]{3,2,1,0:T(8,128)(2,1)S(1)} %get-tuple-element.305), channel_id=1, source_target_pairs={{0,8},{1,9},{2,10},{3,11},{4,12},{5,13},{6,14},{7,15},{8,0},{9,1},... | collective-permute-start | bytes 983048 | tf_op jit(solution)/shard_map/ppermute | solution.py:41
  338.6 4.3 collective-permute-start.29
  342.8 4.3 collective-permute-start.30
  347.2 17.0 %collective-permute-start.31 = (f32[12,1024]{1,0:T(8,128)S(1)}, f32[12,1024]{1,0:T(8,128)S(1)}, u32[]{:S(2)}, u32[]{:S(2)}) collective-permute-start(f32[12,1024]{1,0:T(8,128)S(1)} %total.6.one_ref), channel_id=1, source_target_pairs={{0,4},{1,5},{2,6},{3,7},{4,0},{5,1},{6,2},{7,3},{8,12},{9,13},{10,... | collective-permute-start | bytes 147464 | tf_op jit(solution)/shard_map/ppermute | solution.py:41
  364.5 40.3 %collective-permute-start.36 = (bf16[4,448,512]{2,1,0:T(8,128)(2,1)S(1)}, bf16[4,448,512]{2,1,0:T(8,128)(2,1)S(1)}, u32[]{:S(2)}, u32[]{:S(2)}) collective-permute-start(bf16[4,448,512]{2,1,0:T(8,128)(2,1)S(1)} %bitcast.72), channel_id=1, source_target_pairs={{0,2},{1,3},{2,0},{3,1},{4,6},{5,7},{6,4},{7,5},{8,10},{9,11},{10,... | collective-permute-start | bytes 5505032 | tf_op jit(solution)/shard_map/ppermute | solution.py:41
  365.7 15.9 %collective-permute-start.32 = (bf16[1,640,256]{2,1,0:T(8,128)(2,1)S(1)}, bf16[1,640,256]{2,1,0:T(8,128)(2,1)S(1)}, u32[]{:S(2)}, u32[]{:S(2)}) collective-permute-start(bf16[1,640,256]{2,1,0:T(8,128)(2,1)S(1)} %add_last.3.one_ref), channel_id=1, source_target_pairs={{0,8},{1,9},{2,10},{3,11},{4,12},{5,13},{6,14},{7,15},{8,0},{9,1},... | collective-permute-start | bytes 983048 | tf_op jit(solution)/shard_map/ppermute | solution.py:41
  381.7 17.7 %collective-permute-start.33 = (bf16[2,640,256]{2,1,0:T(8,128)(2,1)S(1)}, bf16[2,640,256]{2,1,0:T(8,128)(2,1)S(1)}, u32[]{:S(2)}, u32[]{:S(2)}) collective-permute-start(bf16[2,640,256]{2,1,0:T(8,128)(2,1)S(1)} %bitcast.81), channel_id=1, source_target_pairs={{0,4},{1,5},{2,6},{3,7},{4,0},{5,1},{6,2},{7,3},{8,12},{9,13},{10,... | collective-permute-start | bytes 1966088 | tf_op jit(solution)/shard_map/ppermute | solution.py:41
  381.8 15.4 %collective-permute-start.34 = (f32[12,1024]{1,0:T(8,128)S(1)}, f32[12,1024]{1,0:T(8,128)S(1)}, u32[]{:S(2)}, u32[]{:S(2)}) collective-permute-start(f32[12,1024]{1,0:T(8,128)S(1)} %total.7.one_ref), channel_id=1, source_target_pairs={{0,8},{1,9},{2,10},{3,11},{4,12},{5,13},{6,14},{7,15},{8,0},{9,1},... | collective-permute-start | bytes 147464 | tf_op jit(solution)/shard_map/ppermute | solution.py:41
  397.2 1.3 collective-permute-start.35
  407.1 6.8 %collective-permute-start.37 = (bf16[8,448,512]{2,1,0:T(8,128)(2,1)}, bf16[8,448,512]{2,1,0:T(8,128)(2,1)}, u32[]{:S(2)}, u32[]{:S(2)}) collective-permute-start(bf16[8,448,512]{2,1,0:T(8,128)(2,1)} %bitcast.66), channel_id=1, source_target_pairs={{0,1},{1,0},{2,3},{3,2},{4,5},{5,4},{6,7},{7,6},{8,9},{9,8},{10,11... | collective-permute-start | bytes 11010056 | tf_op jit(solution)/shard_map/ppermute | solution.py:41
  407.1 31.2 %collective-permute-start.38 = (bf16[4,640,256]{2,1,0:T(8,128)(2,1)S(1)}, bf16[4,640,256]{2,1,0:T(8,128)(2,1)S(1)}, u32[]{:S(2)}, u32[]{:S(2)}) collective-permute-start(bf16[4,640,256]{2,1,0:T(8,128)(2,1)S(1)} %bitcast.74), channel_id=1, source_target_pairs={{0,2},{1,3},{2,0},{3,1},{4,6},{5,7},{6,4},{7,5},{8,10},{9,11},{10,... | collective-permute-start | bytes 3932168 | tf_op jit(solution)/shard_map/ppermute | solution.py:41
  440.9 5.1 %collective-permute-start.39 = (bf16[8,640,256]{2,1,0:T(8,128)(2,1)S(1)}, bf16[8,640,256]{2,1,0:T(8,128)(2,1)}, u32[]{:S(2)}, u32[]{:S(2)}) collective-permute-start(bf16[8,640,256]{2,1,0:T(8,128)(2,1)S(1)} %bitcast.69), channel_id=1, source_target_pairs={{0,1},{1,0},{2,3},{3,2},{4,5},{5,4},{6,7},{7,6},{8,9},{9,8},{10,11... | collective-permute-start | bytes 7864328 | tf_op jit(solution)/shard_map/ppermute | solution.py:41
  (40 other events, 211.7 us)
Sparse Core Ops, SparseCore 0:
  134.3 83.2 all-gather.1

commit v5 on v4

--- a/solution.py
+++ b/solution.py
@@ -1450,9 +1450,9 @@
     )
     last = flow_i.step(terms_done)
     last = flow_o.step(last)
-    last = flow_s.step(last)
     while len(flow_e.order) >= len(high):
         last = flow_e.step(last)
+    last = flow_s.step(last)
     dqkv = lax.all_to_all(dqkv, "ctx", 0, 0, tiled=True).reshape(pairs, seqs, rows, 3 * LANES)
     last = flow_o.step(last)
     while flow_i.received is not None:

time: 462 us -> 457 us (0.989)
  waiting for transfers between devices: 219 us -> 210 us
    ppermute x40, waiting for transfers between devices: 182 us -> 173 us  [swap_bit(): return lax.ppermute(value, axis, [(i, i ^ 1 << bit) for i in range(size)])]
  transfers between devices with their start and end apart: 45 -> 45, of which waited for: 27 -> 29; matrix products, arithmetic and copies ran while one was open for 4% -> 4% of each run, Pallas kernels for 20% -> 20%
where the time goes in v5:
time: 457 us; the launch traced here: 455 us
  waiting for transfers between devices  210 us (46%)
  Pallas kernels  108 us (24%)
  starting transfers between devices  74.8 us (16%)
  local copies, waits for them, and re-layouts  45.4 us (10%)
  between operations  14.6 us (3%)
    ppermute x40, waiting for transfers between devices, swap_bit(): return lax.ppermute(value, axis, [(i, i ^ 1 << bit) for i in range(size)])  173 us
    ppermute x40, starting transfers between devices, swap_bit(): return lax.ppermute(value, axis, [(i, i ^ 1 << bit) for i in range(size)])  46.3 us
    unnamed x96, local copies, waits for them, and re-layouts  36.4 us
    pallas_call x1, Pallas kernels, feed_forward(): pl.pallas_call(functools.partial(ffn_kernel, len(expand_arrays), len(shri...  21.6 us
    all_to_all x1, waiting for transfers between devices, body(): dmixed = lax.all_to_all(dmixed, 'ctx', 0, 0, tiled=True)  19.8 us
    pallas_call x4, Pallas kernels, finish(): pl.pallas_call(functools.partial(finish_kernel, dim, order[:group]), grid...  13.7 us
    all_to_all x1, waiting for transfers between devices, body(): qkv = lax.all_to_all(qkv, 'ctx', 0, 0, tiled=True)  12.5 us
    pallas_call x8, Pallas kernels, combine(): pl.pallas_call(combine_kernel, grid=(outer, inner // per), in_specs=[bloc...  10.6 us
  transfers between devices with their start and end apart: 45, of which 29 were waited for; matrix products, arithmetic and copies ran while one was open for 4% of the time, Pallas kernels for 20%

profile of v5, /device:TPU:0, one launch (start us, length us, event | category | flops | bytes accessed | tf_op | source)
XLA Modules:
  0.0 455.2 jit_solution(8763300799034604811)
XLA Ops:
  8.5 3.0 collective-permute-start.1
  19.1 2.3 dynamic_slice.18
  22.6 3.1 constant_dynamic-slice_fusion.4
  25.7 2.3 convert_reduce_fusion
  33.8 14.5 %collective-permute-done.2.refs_2_.refs_7_.refs_12_ = bf16[128,3072]{1,0:T(8,128)(2,1)S(1)} collective-permute-done((bf16[128,3072]{1,0:T(8,128)(2,1)S(1)}, bf16[128,3072]{1,0:T(8,128)(2,1)S(1)}, u32[]{:S(2)}, u32[]{:S(2)}) %collective-permute-start.2) | collective-permute-done | bytes 786464 | tf_op jit(solution)/shard_map/ppermute | solution.py:41
  48.8 6.4 %collective-permute-done.3.refs_1_ = bf16[256,2048]{1,0:T(8,128)(2,1)S(1)} collective-permute-done((bf16[256,2048]{1,0:T(8,128)(2,1)}, bf16[256,2048]{1,0:T(8,128)(2,1)S(1)}, u32[]{:S(2)}, u32[]{:S(2)}) %collective-permute-start.3) | collective-permute-done | bytes 1048608 | tf_op jit(solution)/shard_map/ppermute | solution.py:41
  56.2 5.0 %project.1 = (bf16[8,4,64,384]{3,2,1,0:T(8,128)(2,1)S(1)}, f32[8,128]{1,0:T(8,128)S(1)}) custom-call(s32[5]{0:T(128)S(1)} %pad_add_fusion.1.off_ref, bf16[256,1024]{1,0:T(8,128)(2,1)S(1)} %get-tuple-element.243.h_ref, f32[8,1024]{1,0:T(8,128)S(1)} %get-tuple-element.201.v_ref, bf16[512,3072]{1,0:T(8,128)(2,1)} %refs_10_.3, ...), custom_call_target="tpu_custom_call" | custom-call | tf_op jit(solution)/shard_map/project/pallas_call | solution.py:220
  62.4 5.2 %all-to-all-start = ((bf16[16,2,64,384]{3,2,1,0:T(8,128)(2,1)}), bf16[16,2,64,384]{3,2,1,0:T(8,128)(2,1)}, u32[]{:S(2)}, u32[]{:S(2)}) async-start(bf16[16,2,64,384]{3,2,1,0:T(8,128)(2,1)} %bitcast.89), calls=%async_computation | async-start | bytes 3145728 | tf_op jit(solution)/shard_map/all_to_all | solution.py:1387
  69.2 12.8 %collective-permute-done.6.refs_1_ = bf16[1024,256]{1,0:T(8,128)(2,1)S(1)} collective-permute-done((bf16[1024,256]{1,0:T(8,128)(2,1)}, bf16[1024,256]{1,0:T(8,128)(2,1)S(1)}, u32[]{:S(2)}, u32[]{:S(2)}) %collective-permute-start.6) | collective-permute-done | bytes 524320 | tf_op jit(solution)/shard_map/ppermute | solution.py:41
  87.3 12.5 %all-to-all-done.qkv_ref = bf16[16,2,64,384]{3,2,1,0:T(8,128)(2,1)} async-done(((bf16[16,2,64,384]{3,2,1,0:T(8,128)(2,1)}), bf16[16,2,64,384]{3,2,1,0:T(8,128)(2,1)}, u32[]{:S(2)}, u32[]{:S(2)}) %all-to-all-start) | async-done | bytes 1572896 | tf_op jit(solution)/shard_map/all_to_all | solution.py:1387
  99.8 10.0 %attend.1 = (bf16[16,2,64,128]{3,2,1,0:T(8,128)(2,1)S(1)}, f32[2,2,1024]{2,1,0:T(2,128)S(1)}) custom-call(s32[16]{0:T(128)S(1)} %copy-done.37, s32[2]{0:T(128)S(1)} %add_and_fusion.seq_ref, bf16[16,2,64,384]{3,2,1,0:T(8,128)(2,1)} %all-to-all-done.qkv_ref, s32[4,1,1024]{2,1,0:T(1,128)S(1)} %broadcast_in_dim.2.start_ref), custom_call_target="tpu_custom_call" | custom-call | tf_op jit(solution)/shard_map/attend/pallas_call | solution.py:315
  110.5 9.2 %all-to-all-start.1 = ((bf16[16,2,64,128]{3,2,1,0:T(8,128)(2,1)}), bf16[16,2,64,128]{3,2,1,0:T(8,128)(2,1)}, u32[]{:S(2)}, u32[]{:S(2)}) async-start(bf16[16,2,64,128]{3,2,1,0:T(8,128)(2,1)} %copy-done.35), calls=%async_computation.1 | async-start | bytes 1048576 | tf_op jit(solution)/shard_map/all_to_all | solution.py:1393
  119.9 9.5 %collective-permute-done.10.refs_4_ = bf16[2048,512]{1,0:T(8,128)(2,1)} collective-permute-done((bf16[2048,512]{1,0:T(8,128)(2,1)}, bf16[2048,512]{1,0:T(8,128)(2,1)}, u32[]{:S(2)}, u32[]{:S(2)}) %collective-permute-start.10) | collective-permute-done | bytes 2097184 | tf_op jit(solution)/shard_map/ppermute | solution.py:41
  129.4 4.8 %all-to-all-done.1 = bf16[16,2,64,128]{3,2,1,0:T(8,128)(2,1)} async-done(((bf16[16,2,64,128]{3,2,1,0:T(8,128)(2,1)}), bf16[16,2,64,128]{3,2,1,0:T(8,128)(2,1)}, u32[]{:S(2)}, u32[]{:S(2)}) %all-to-all-start.1) | async-done | bytes 524320 | tf_op jit(solution)/shard_map/all_to_all | solution.py:1393
  138.6 2.8 branch.1
  144.3 21.6 %feed_forward.1 = (f32[256,1024]{1,0:T(8,128)S(1)}, f32[256,1024]{1,0:T(8,128)S(1)}, f32[256,1024]{1,0:T(8,128)S(1)}, f32[256,1024]{1,0:T(8,128)}, bf16[1,4,2,25...) custom-call(s32[9]{0:T(128)S(1)} %concatenate.23.sc_ref, ...), custom_call_target="tpu_custom_call" | custom-call | tf_op jit(solution)/shard_map/feed_forward/pallas_call | solution.py:630
  172.4 5.3 %branch_back.1 = (f32[256,1024]{1,0:T(8,128)S(1)}, bf16[8,4,64,128]{3,2,1,0:T(8,128)(2,1)S(1)}, bf16[2,8,64,512]{3,2,1,0:T(8,128)(2,1)S(1)}, bf16[2,8,64,512]{3,2,1,0:T(8,128)(2,1)S(1)}, f32[8,1024]{1,0:T(8,128)S(1)}) custom-call(s32[5]{0:T(128)S(1)} %pad_add_fusion.4.sc_ref, f32[256,1024]{1,0:T(8,128)} %copy-done.24, f32[256,1024]{1,0:T(8,128)} %copy-done.40, ...), custom_call_target="tpu_custom_call" | custom-call | tf_op jit(solution)/shard_map/branch_back/pallas_call | solution.py:722
  181.4 4.5 all-to-all-start.2
  187.6 19.8 %all-to-all-done.2.grad_ref = bf16[16,2,64,128]{3,2,1,0:T(8,128)(2,1)} async-done(((bf16[16,2,64,128]{3,2,1,0:T(8,128)(2,1)}), bf16[16,2,64,128]{3,2,1,0:T(8,128)(2,1)}, u32[]{:S(2)}, u32[]{:S(2)}) %all-to-all-start.2) | async-done | bytes 524320 | tf_op jit(solution)/shard_map/all_to_all | solution.py:1431
  207.4 10.4 %attend_back.1 = (bf16[16,2,64,384]{3,2,1,0:T(8,128)(2,1)S(1)}, f32[8,128]{1,0:T(8,128)S(1)}) custom-call(s32[16]{0:T(128)S(1)} %copy-done.37, s32[2]{0:T(128)S(1)} %add_and_fusion.seq_ref, bf16[16,2,64,384]{3,2,1,0:T(8,128)(2,1)} %all-to-all-done.qkv_ref, bf16[16,2,64,128]{3,2,1,0:T(8,128)(2,1)} %all-to-all-done.2.grad_ref, ...), custom_call_target="tpu_custom_call" | custom-call | tf_op jit(solution)/shard_map/attend_back/pallas_call | solution.py:423
  218.9 9.5 %all-to-all-start.3 = ((bf16[16,2,64,384]{3,2,1,0:T(8,128)(2,1)}), bf16[16,2,64,384]{3,2,1,0:T(8,128)(2,1)}, u32[]{:S(2)}, u32[]{:S(2)}) async-start(bf16[16,2,64,384]{3,2,1,0:T(8,128)(2,1)} %copy-done.3), calls=%async_computation.3 | async-start | bytes 3145728 | tf_op jit(solution)/shard_map/all_to_all | solution.py:1456
  230.4 3.6 combine.8
  238.1 5.5 %input_weight_terms.1 = (bf16[1,2,256,384]{3,2,1,0:T(8,128)(2,1)S(1)}, bf16[1,2,256,384]{3,2,1,0:T(8,128)(2,1)S(1)}, f32[8,128]{1,0:T(8,128)S(1)}) custom-call(s32[3]{0:T(128)S(1)} %get-tuple-element.242.sc_ref, bf16[16,4,64,1024]{3,2,1,0:T(8,128)(2,1)} %all-gather.2.cloned.1.call-done.h_ref, bf16[16,2,64,384]{3,2,1,0:T(8,128)(2,1)S(1)} %copy-done.4), custom_call_target="tpu_custom_call" | custom-call | tf_op jit(solution)/shard_map/input_weight_terms/pallas_call | solution.py:778
  247.0 14.1 %collective-permute-done.13 = bf16[1,4,2,512,256]{4,3,2,1,0:T(8,128)(2,1)} collective-permute-done((bf16[1,4,2,512,256]{4,3,2,1,0:T(8,128)(2,1)}, bf16[1,4,2,512,256]{4,3,2,1,0:T(8,128)(2,1)}, u32[]{:S(2)}, u32[]{:S(2)}) %collective-permute-start.13) | collective-permute-done | bytes 2097184 | tf_op jit(solution)/shard_map/ppermute | solution.py:41
  261.1 2.5 combine.11
  266.1 5.3 %collective-permute-done.20 = bf16[4,1,256,512]{3,2,1,0:T(8,128)(2,1)} collective-permute-done((bf16[4,1,256,512]{3,2,1,0:T(8,128)(2,1)}, bf16[4,1,256,512]{3,2,1,0:T(8,128)(2,1)}, u32[]{:S(2)}, u32[]{:S(2)}) %collective-permute-start.20) | collective-permute-done | bytes 1048608 | tf_op jit(solution)/shard_map/ppermute | solution.py:41
  272.8 2.2 collective-permute-start.22
  281.7 4.3 collective-permute-done.22
  286.1 3.0 collective-permute-start.24
  289.1 9.8 %collective-permute-done.21 = bf16[4,1,64,512]{3,2,1,0:T(8,128)(2,1)S(1)} collective-permute-done((bf16[4,1,64,512]{3,2,1,0:T(8,128)(2,1)S(1)}, bf16[4,1,64,512]{3,2,1,0:T(8,128)(2,1)S(1)}, u32[]{:S(2)}, u32[]{:S(2)}) %collective-permute-start.21) | collective-permute-done | bytes 262176 | tf_op jit(solution)/shard_map/ppermute | solution.py:41
  308.1 7.8 %entry_back.1 = (f32[256,1024]{1,0:T(8,128)}, bf16[256,1024]{1,0:T(8,128)(2,1)}, f32[12,1024]{1,0:T(8,128)S(1)}) custom-call(s32[6]{0:T(128)S(1)} %pad_add_fusion.5.off_ref, bf16[8,4,64,384]{3,2,1,0:T(8,128)(2,1)} %bitcast.15.d_ref, bf16[256,1024]{1,0:T(8,128)(2,1)S(1)} %bitcast.78, f32[256,1024]{1,0:T(8,128)S(1)} %copy-done.31, f32[256,1024]{1,0:T(8,128)S(1)} %copy-done.29, ...), custom_call_target="tpu_custom_call" | custom-call | tf_op jit(solution)/shard_map/entry_back/pallas_call | solution.py:874
  315.9 10.6 %collective-permute-done.26 = bf16[2,640,256]{2,1,0:T(8,128)(2,1)} collective-permute-done((bf16[2,640,256]{2,1,0:T(8,128)(2,1)}, bf16[2,640,256]{2,1,0:T(8,128)(2,1)}, u32[]{:S(2)}, u32[]{:S(2)}) %collective-permute-start.26) | collective-permute-done | bytes 655392 | tf_op jit(solution)/shard_map/ppermute | solution.py:41
  330.7 2.2 collective-permute-start.28
  334.5 2.6 collective-permute-done.29.two_ref
  338.2 3.3 collective-permute-done.30.two_ref
  341.7 17.0 %collective-permute-done.31.two_ref = f32[12,1024]{1,0:T(8,128)S(1)} collective-permute-done((f32[12,1024]{1,0:T(8,128)S(1)}, f32[12,1024]{1,0:T(8,128)S(1)}, u32[]{:S(2)}, u32[]{:S(2)}) %collective-permute-start.31) | collective-permute-done | bytes 49184 | tf_op jit(solution)/shard_map/ppermute | solution.py:41
  362.3 14.8 %collective-permute-done.32.two_ref = bf16[1,640,256]{2,1,0:T(8,128)(2,1)S(1)} collective-permute-done((bf16[1,640,256]{2,1,0:T(8,128)(2,1)S(1)}, bf16[1,640,256]{2,1,0:T(8,128)(2,1)S(1)}, u32[]{:S(2)}, u32[]{:S(2)}) %collective-permute-start.32) | collective-permute-done | bytes 327712 | tf_op jit(solution)/shard_map/ppermute | solution.py:41
  377.2 2.2 collective-permute-start.34
  379.4 13.7 %collective-permute-done.34.two_ref = f32[12,1024]{1,0:T(8,128)S(1)} collective-permute-done((f32[12,1024]{1,0:T(8,128)S(1)}, f32[12,1024]{1,0:T(8,128)S(1)}, u32[]{:S(2)}, u32[]{:S(2)}) %collective-permute-start.34) | collective-permute-done | bytes 49184 | tf_op jit(solution)/shard_map/ppermute | solution.py:41
  395.4 4.7 %collective-permute-done.36.two_ref = bf16[4,448,512]{2,1,0:T(8,128)(2,1)S(1)} collective-permute-done((bf16[4,448,512]{2,1,0:T(8,128)(2,1)S(1)}, bf16[4,448,512]{2,1,0:T(8,128)(2,1)S(1)}, u32[]{:S(2)}, u32[]{:S(2)}) %collective-permute-start.36) | collective-permute-done | bytes 1835040 | tf_op jit(solution)/shard_map/ppermute | solution.py:41
  400.1 2.3 merge.10
  406.2 2.7 finish.4
  409.1 5.0 %finish_extra.1 = (f32[512,3072]{1,0:T(8,128)}, f32[8,128]{1,0:T(8,128)S(1)}) custom-call(s32[2]{0:T(128)S(1)} %get-tuple-element.322.label_ref, bf16[8,448,512]{2,1,0:T(8,128)(2,1)S(1)} %bitcast.68, bf16[8,448,512]{2,1,0:T(8,128)(2,1)} %collective-permute-done.37.far_ref.source), custom_call_target="tpu_custom_call" | custom-call | tf_op jit(solution)/shard_map/finish_extra/pallas_call | solution.py:1223
  414.1 4.2 finish.5
  418.3 15.3 %collective-permute-done.38.two_ref = bf16[4,640,256]{2,1,0:T(8,128)(2,1)S(1)} collective-permute-done((bf16[4,640,256]{2,1,0:T(8,128)(2,1)S(1)}, bf16[4,640,256]{2,1,0:T(8,128)(2,1)S(1)}, u32[]{:S(2)}, u32[]{:S(2)}) %collective-permute-start.38) | collective-permute-done | bytes 1310752 | tf_op jit(solution)/shard_map/ppermute | solution.py:41
  437.0 2.7 finish.6
  441.3 4.0 finish.7
  445.3 3.1 finish_rows.1
  (200 shorter events, 97.8 us)
Async XLA Ops:
  8.5 21.1 %collective-permute-start.1 = (bf16[128,3072]{1,0:T(8,128)(2,1)S(1)}, bf16[128,3072]{1,0:T(8,128)(2,1)S(1)}, u32[]{:S(2)}, u32[]{:S(2)}) collective-permute-start(bf16[128,3072]{1,0:T(8,128)(2,1)S(1)} %constant_dynamic-slice_fusion.3), channel_id=1, source_target_pairs={{0,16},{16,0},{1,17},{17,1},{2,18},{18,2},{3,19},{19,3},{4,20},{20... | collective-permute-start | bytes 2359304 | tf_op jit(solution)/shard_map/ppermute | solution.py:41
  21.4 8.2 %collective-permute-start = (bf16[1,6144]{1,0:T(2,128)(2,1)S(1)}, bf16[1,6144]{1,0:T(2,128)(2,1)S(1)}, u32[]{:S(2)}, u32[]{:S(2)}) collective-permute-start(bf16[1,6144]{1,0:T(2,128)(2,1)S(1)} %reshape.159.refs_0_), channel_id=1, source_target_pairs={{0,16},{16,0},{1,17},{17,1},{2,18},{18,2},{3,19},{19,3},{4,20},{20... | collective-permute-start | bytes 36872 | tf_op jit(solution)/shard_map/ppermute | solution.py:41
  29.6 18.7 %collective-permute-start.2 = (bf16[128,3072]{1,0:T(8,128)(2,1)S(1)}, bf16[128,3072]{1,0:T(8,128)(2,1)S(1)}, u32[]{:S(2)}, u32[]{:S(2)}) collective-permute-start(bf16[128,3072]{1,0:T(8,128)(2,1)S(1)} %collective-permute-done.1.refs_1_.refs_6_.refs_11_), channel_id=1, source_target_pairs={{0,2},{1,3},{2,0},{3,1},{4,6},{5,7},{6,4},{7,5},{8,10},{9,11},{10,... | collective-permute-start | bytes 2359304 | tf_op jit(solution)/shard_map/ppermute | solution.py:41
  31.3 24.0 %collective-permute-start.3 = (bf16[256,2048]{1,0:T(8,128)(2,1)}, bf16[256,2048]{1,0:T(8,128)(2,1)S(1)}, u32[]{:S(2)}, u32[]{:S(2)}) collective-permute-start(bf16[256,2048]{1,0:T(8,128)(2,1)} %dynamic_slice.18), channel_id=1, source_target_pairs={{0,16},{16,0},{1,17},{17,1},{2,18},{18,2},{3,19},{19,3},{4,20},{20... | collective-permute-start | bytes 3145736 | tf_op jit(solution)/shard_map/ppermute | solution.py:41
  48.3 6.9 %collective-permute-start.4 = (bf16[128,3072]{1,0:T(8,128)(2,1)S(1)}, bf16[128,3072]{1,0:T(8,128)(2,1)S(1)}, u32[]{:S(2)}, u32[]{:S(2)}) collective-permute-start(bf16[128,3072]{1,0:T(8,128)(2,1)S(1)} %collective-permute-done.2.refs_2_.refs_7_.refs_12_), channel_id=1, source_target_pairs={{0,1},{1,0},{2,3},{3,2},{4,5},{5,4},{6,7},{7,6},{8,9},{9,8},{10,11... | collective-permute-start | bytes 2359304 | tf_op jit(solution)/shard_map/ppermute | solution.py:41
  48.3 6.9 %collective-permute-start.5 = (bf16[128,3072]{1,0:T(8,128)(2,1)S(1)}, bf16[128,3072]{1,0:T(8,128)(2,1)S(1)}, u32[]{:S(2)}, u32[]{:S(2)}) collective-permute-start(bf16[128,3072]{1,0:T(8,128)(2,1)S(1)} %collective-permute-done.1.refs_1_.refs_6_.refs_11_), channel_id=1, source_target_pairs={{0,1},{1,0},{2,3},{3,2},{4,5},{5,4},{6,7},{7,6},{8,9},{9,8},{10,11... | collective-permute-start | bytes 2359304 | tf_op jit(solution)/shard_map/ppermute | solution.py:41
  62.4 37.4 %copy-start.37 = (s32[16]{0:T(128)S(1)}, s32[16]{0:T(128)}, u32[]{:S(2)}) copy-start(s32[16]{0:T(128)} %table.3) | copy-start | bytes 196
  62.4 37.3 %all-to-all-start = ((bf16[16,2,64,384]{3,2,1,0:T(8,128)(2,1)}), bf16[16,2,64,384]{3,2,1,0:T(8,128)(2,1)}, u32[]{:S(2)}, u32[]{:S(2)}) async-start(bf16[16,2,64,384]{3,2,1,0:T(8,128)(2,1)} %bitcast.89), calls=%async_computation | async-start | bytes 3145728 | tf_op jit(solution)/shard_map/all_to_all | solution.py:1387
  67.6 14.4 %collective-permute-start.6 = (bf16[1024,256]{1,0:T(8,128)(2,1)}, bf16[1024,256]{1,0:T(8,128)(2,1)S(1)}, u32[]{:S(2)}, u32[]{:S(2)}) collective-permute-start(bf16[1024,256]{1,0:T(8,128)(2,1)} %constant_dynamic-slice_fusion.5), channel_id=1, source_target_pairs={{0,16},{16,0},{1,17},{17,1},{2,18},{18,2},{3,19},{19,3},{4,20},{20... | collective-permute-start | bytes 1572872 | tf_op jit(solution)/shard_map/ppermute | solution.py:41
  82.0 47.4 %collective-permute-start.10 = (bf16[2048,512]{1,0:T(8,128)(2,1)}, bf16[2048,512]{1,0:T(8,128)(2,1)}, u32[]{:S(2)}, u32[]{:S(2)}) collective-permute-start(bf16[2048,512]{1,0:T(8,128)(2,1)} %constant_dynamic-slice_fusion.4), channel_id=1, source_target_pairs={{0,16},{16,0},{1,17},{17,1},{2,18},{18,2},{3,19},{19,3},{4,20},{20... | collective-permute-start | bytes 6291464 | tf_op jit(solution)/shard_map/ppermute | solution.py:41
  83.5 3.0 collective-permute-start.7
  84.3 15.4 %collective-permute-start.8 = (bf16[256,1024]{1,0:T(8,128)(2,1)}, bf16[256,1024]{1,0:T(8,128)(2,1)}, u32[]{:S(2)}, u32[]{:S(2)}) collective-permute-start(bf16[256,1024]{1,0:T(8,128)(2,1)} %bitcast.83), channel_id=1, source_target_pairs={{0,1},{1,0},{2,3},{3,2},{4,5},{5,4},{6,7},{7,6},{8,9},{9,8},{10,11... | collective-permute-start | bytes 1572872 | tf_op jit(solution)/shard_map/ppermute | solution.py:41
  84.8 44.6 %collective-permute-start.9 = (bf16[256,2048]{1,0:T(8,128)(2,1)}, bf16[256,2048]{1,0:T(8,128)(2,1)}, u32[]{:S(2)}, u32[]{:S(2)}) collective-permute-start(bf16[256,2048]{1,0:T(8,128)(2,1)} %copy-done.41), channel_id=1, source_target_pairs={{0,2},{1,3},{2,0},{3,1},{4,6},{5,7},{6,4},{7,5},{8,10},{9,11},{10,... | collective-permute-start | bytes 3145736 | tf_op jit(solution)/shard_map/ppermute | solution.py:41
  110.5 23.7 %all-to-all-start.1 = ((bf16[16,2,64,128]{3,2,1,0:T(8,128)(2,1)}), bf16[16,2,64,128]{3,2,1,0:T(8,128)(2,1)}, u32[]{:S(2)}, u32[]{:S(2)}) async-start(bf16[16,2,64,128]{3,2,1,0:T(8,128)(2,1)} %copy-done.35), calls=%async_computation.1 | async-start | bytes 1048576 | tf_op jit(solution)/shard_map/all_to_all | solution.py:1393
  119.7 117.0 %all-gather.2.cloned.1.call-start = ((), (), s32[]{:S(2)}) async-start(), calls=%async_computation.4 | async-start | bytes 8912896 | tf_op jit(solution)/shard_map/all_gather | solution.py:1395
  142.4 1.9 collective-permute-start.11
  144.3 28.1 %copy-start.17 = (bf16[1024,256]{1,0:T(8,128)(2,1)S(1)}, bf16[1024,256]{1,0:T(8,128)(2,1)}, u32[]{:S(2)}) copy-start(bf16[1024,256]{1,0:T(8,128)(2,1)} %copy-done.15) | copy-start | bytes 1572868
  144.3 28.1 %copy-start.20 = (bf16[1024,256]{1,0:T(8,128)(2,1)S(1)}, bf16[1024,256]{1,0:T(8,128)(2,1)}, u32[]{:S(2)}) copy-start(bf16[1024,256]{1,0:T(8,128)(2,1)} %copy-done.18) | copy-start | bytes 1572868
  167.8 3.6 collective-permute-start.12
  168.0 60.8 %collective-permute-start.15 = (bf16[1,4,2,256,512]{4,3,2,1,0:T(8,128)(2,1)}, bf16[1,4,2,256,512]{4,3,2,1,0:T(8,128)(2,1)}, u32[]{:S(2)}, u32[]{:S(2)}) collective-permute-start(bf16[1,4,2,256,512]{4,3,2,1,0:T(8,128)(2,1)} %get-tuple-element.245), channel_id=1, source_target_pairs={{0,16},{16,0},{1,17},{17,1},{2,18},{18,2},{3,19},{19,3},{4,20},{20... | collective-permute-start | bytes 6291464 | tf_op jit(solution)/shard_map/ppermute | solution.py:41
  181.4 26.0 %all-to-all-start.2 = ((bf16[16,2,64,128]{3,2,1,0:T(8,128)(2,1)}), bf16[16,2,64,128]{3,2,1,0:T(8,128)(2,1)}, u32[]{:S(2)}, u32[]{:S(2)}) async-start(bf16[16,2,64,128]{3,2,1,0:T(8,128)(2,1)} %bitcast.100), calls=%async_computation.2 | async-start | bytes 1048576 | tf_op jit(solution)/shard_map/all_to_all | solution.py:1431
  185.8 75.3 %collective-permute-start.13 = (bf16[1,4,2,512,256]{4,3,2,1,0:T(8,128)(2,1)}, bf16[1,4,2,512,256]{4,3,2,1,0:T(8,128)(2,1)}, u32[]{:S(2)}, u32[]{:S(2)}) collective-permute-start(bf16[1,4,2,512,256]{4,3,2,1,0:T(8,128)(2,1)} %get-tuple-element.239), channel_id=1, source_target_pairs={{0,16},{16,0},{1,17},{17,1},{2,18},{18,2},{3,19},{19,3},{4,20},{20... | collective-permute-start | bytes 6291464 | tf_op jit(solution)/shard_map/ppermute | solution.py:41
  187.6 49.1 %collective-permute-start.16 = (f32[256,1024]{1,0:T(8,128)}, f32[256,1024]{1,0:T(8,128)}, u32[]{:S(2)}, u32[]{:S(2)}) collective-permute-start(f32[256,1024]{1,0:T(8,128)} %copy-done.38), channel_id=1, source_target_pairs={{0,1},{1,0},{2,3},{3,2},{4,5},{5,4},{6,7},{7,6},{8,9},{9,8},{10,11... | collective-permute-start | bytes 3145736 | tf_op jit(solution)/shard_map/ppermute | solution.py:41
  218.9 85.7 %all-to-all-start.3 = ((bf16[16,2,64,384]{3,2,1,0:T(8,128)(2,1)}), bf16[16,2,64,384]{3,2,1,0:T(8,128)(2,1)}, u32[]{:S(2)}, u32[]{:S(2)}) async-start(bf16[16,2,64,384]{3,2,1,0:T(8,128)(2,1)} %copy-done.3), calls=%async_computation.3 | async-start | bytes 3145728 | tf_op jit(solution)/shard_map/all_to_all | solution.py:1456
  228.4 17.1 %collective-permute-start.14 = (bf16[2,8,64,512]{3,2,1,0:T(8,128)(2,1)}, bf16[2,8,64,512]{3,2,1,0:T(8,128)(2,1)}, u32[]{:S(2)}, u32[]{:S(2)}) collective-permute-start(bf16[2,8,64,512]{3,2,1,0:T(8,128)(2,1)} %copy-done.39), channel_id=1, source_target_pairs={{0,1},{1,0},{2,3},{3,2},{4,5},{5,4},{6,7},{7,6},{8,9},{9,8},{10,11... | collective-permute-start | bytes 3145736 | tf_op jit(solution)/shard_map/ppermute | solution.py:41
  235.0 36.4 %collective-permute-start.20 = (bf16[4,1,256,512]{3,2,1,0:T(8,128)(2,1)}, bf16[4,1,256,512]{3,2,1,0:T(8,128)(2,1)}, u32[]{:S(2)}, u32[]{:S(2)}) collective-permute-start(bf16[4,1,256,512]{3,2,1,0:T(8,128)(2,1)} %get-tuple-element.264), channel_id=1, source_target_pairs={{0,2},{1,3},{2,0},{3,1},{4,6},{5,7},{6,4},{7,5},{8,10},{9,11},{10,... | collective-permute-start | bytes 3145736 | tf_op jit(solution)/shard_map/ppermute | solution.py:41
  243.6 1.8 collective-permute-start.17
  263.7 35.2 %collective-permute-start.18 = (bf16[4,1,512,256]{3,2,1,0:T(8,128)(2,1)S(1)}, bf16[4,1,512,256]{3,2,1,0:T(8,128)(2,1)S(1)}, u32[]{:S(2)}, u32[]{:S(2)}) collective-permute-start(bf16[4,1,512,256]{3,2,1,0:T(8,128)(2,1)S(1)} %get-tuple-element.260), channel_id=1, source_target_pairs={{0,2},{1,3},{2,0},{3,1},{4,6},{5,7},{6,4},{7,5},{8,10},{9,11},{10,... | collective-permute-start | bytes 3145736 | tf_op jit(solution)/shard_map/ppermute | solution.py:41
  264.6 13.9 %collective-permute-start.19 = (bf16[1,8,64,512]{3,2,1,0:T(8,128)(2,1)S(1)}, bf16[1,8,64,512]{3,2,1,0:T(8,128)(2,1)S(1)}, u32[]{:S(2)}, u32[]{:S(2)}) collective-permute-start(bf16[1,8,64,512]{3,2,1,0:T(8,128)(2,1)S(1)} %get-tuple-element.262), channel_id=1, source_target_pairs={{0,16},{16,0},{1,17},{17,1},{2,18},{18,2},{3,19},{19,3},{4,20},{20... | collective-permute-start | bytes 1572872 | tf_op jit(solution)/shard_map/ppermute | solution.py:41
  272.8 13.2 %collective-permute-start.22 = (bf16[2,1,256,512]{3,2,0,1:T(8,128)(2,1)S(1)}, bf16[2,1,256,512]{3,2,0,1:T(8,128)(2,1)S(1)}, u32[]{:S(2)}, u32[]{:S(2)}) collective-permute-start(bf16[2,1,256,512]{3,2,0,1:T(8,128)(2,1)S(1)} %bitcast.112), channel_id=1, source_target_pairs={{0,4},{1,5},{2,6},{3,7},{4,0},{5,1},{6,2},{7,3},{8,12},{9,13},{10,... | collective-permute-start | bytes 1572872 | tf_op jit(solution)/shard_map/ppermute | solution.py:41
  274.9 6.7 %collective-permute-start.23 = (bf16[1,1,256,384]{3,2,1,0:T(8,128)(2,1)S(1)}, bf16[1,1,256,384]{3,2,1,0:T(8,128)(2,1)S(1)}, u32[]{:S(2)}, u32[]{:S(2)}) collective-permute-start(bf16[1,1,256,384]{3,2,1,0:T(8,128)(2,1)S(1)} %get-tuple-element.273), channel_id=1, source_target_pairs={{0,16},{16,0},{1,17},{17,1},{2,18},{18,2},{3,19},{19,3},{4,20},{20... | collective-permute-start | bytes 589832 | tf_op jit(solution)/shard_map/ppermute | solution.py:41
  278.7 20.2 %collective-permute-start.21 = (bf16[4,1,64,512]{3,2,1,0:T(8,128)(2,1)S(1)}, bf16[4,1,64,512]{3,2,1,0:T(8,128)(2,1)S(1)}, u32[]{:S(2)}, u32[]{:S(2)}) collective-permute-start(bf16[4,1,64,512]{3,2,1,0:T(8,128)(2,1)S(1)} %get-tuple-element.269), channel_id=1, source_target_pairs={{0,2},{1,3},{2,0},{3,1},{4,6},{5,7},{6,4},{7,5},{8,10},{9,11},{10,... | collective-permute-start | bytes 786440 | tf_op jit(solution)/shard_map/ppermute | solution.py:41
  286.1 15.8 %collective-permute-start.24 = (bf16[1,1,256,512]{3,2,1,0:T(8,128)(2,1)S(1)}, bf16[1,1,256,512]{3,2,1,0:T(8,128)(2,1)S(1)}, u32[]{:S(2)}, u32[]{:S(2)}) collective-permute-start(bf16[1,1,256,512]{3,2,1,0:T(8,128)(2,1)S(1)} %get-tuple-element.280), channel_id=1, source_target_pairs={{0,8},{1,9},{2,10},{3,11},{4,12},{5,13},{6,14},{7,15},{8,0},{9,1},... | collective-permute-start | bytes 786440 | tf_op jit(solution)/shard_map/ppermute | solution.py:41
  299.9 26.6 %collective-permute-start.26 = (bf16[2,640,256]{2,1,0:T(8,128)(2,1)}, bf16[2,640,256]{2,1,0:T(8,128)(2,1)}, u32[]{:S(2)}, u32[]{:S(2)}) collective-permute-start(bf16[2,640,256]{2,1,0:T(8,128)(2,1)} %get-tuple-element.299), channel_id=1, source_target_pairs={{0,4},{1,5},{2,6},{3,7},{4,0},{5,1},{6,2},{7,3},{8,12},{9,13},{10,... | collective-permute-start | bytes 1966088 | tf_op jit(solution)/shard_map/ppermute | solution.py:41
  302.8 25.0 %collective-permute-start.25 = (bf16[1,448,512]{2,1,0:T(8,128)(2,1)}, bf16[1,448,512]{2,1,0:T(8,128)(2,1)}, u32[]{:S(2)}, u32[]{:S(2)}) collective-permute-start(bf16[1,448,512]{2,1,0:T(8,128)(2,1)} %pack.1.one_ref), channel_id=1, source_target_pairs={{0,8},{1,9},{2,10},{3,11},{4,12},{5,13},{6,14},{7,15},{8,0},{9,1},... | collective-permute-start | bytes 1376264 | tf_op jit(solution)/shard_map/ppermute | solution.py:41
  329.0 29.8 %collective-permute-start.27 = (bf16[2,448,512]{2,1,0:T(8,128)(2,1)S(1)}, bf16[2,448,512]{2,1,0:T(8,128)(2,1)S(1)}, u32[]{:S(2)}, u32[]{:S(2)}) collective-permute-start(bf16[2,448,512]{2,1,0:T(8,128)(2,1)S(1)} %bitcast.79), channel_id=1, source_target_pairs={{0,4},{1,5},{2,6},{3,7},{4,0},{5,1},{6,2},{7,3},{8,12},{9,13},{10,... | collective-permute-start | bytes 2752520 | tf_op jit(solution)/shard_map/ppermute | solution.py:41
  330.7 28.0 %collective-permute-start.28 = (bf16[1,1,640,256]{3,2,1,0:T(8,128)(2,1)S(1)}, bf16[1,1,640,256]{3,2,1,0:T(8,128)(2,1)S(1)}, u32[]{:S(2)}, u32[]{:S(2)}) collective-permute-start(bf16[1,1,640,256]{3,2,1,0:T(8,128)(2,1)S(1)} %get-tuple-element.305), channel_id=1, source_target_pairs={{0,8},{1,9},{2,10},{3,11},{4,12},{5,13},{6,14},{7,15},{8,0},{9,1},... | collective-permute-start | bytes 983048 | tf_op jit(solution)/shard_map/ppermute | solution.py:41
  332.9 4.3 collective-permute-start.29
  337.2 4.3 collective-permute-start.30
  341.5 17.1 %collective-permute-start.31 = (f32[12,1024]{1,0:T(8,128)S(1)}, f32[12,1024]{1,0:T(8,128)S(1)}, u32[]{:S(2)}, u32[]{:S(2)}) collective-permute-start(f32[12,1024]{1,0:T(8,128)S(1)} %total.6.one_ref), channel_id=1, source_target_pairs={{0,4},{1,5},{2,6},{3,7},{4,0},{5,1},{6,2},{7,3},{8,12},{9,13},{10,... | collective-permute-start | bytes 147464 | tf_op jit(solution)/shard_map/ppermute | solution.py:41
  359.0 41.1 %collective-permute-start.36 = (bf16[4,448,512]{2,1,0:T(8,128)(2,1)S(1)}, bf16[4,448,512]{2,1,0:T(8,128)(2,1)S(1)}, u32[]{:S(2)}, u32[]{:S(2)}) collective-permute-start(bf16[4,448,512]{2,1,0:T(8,128)(2,1)S(1)} %bitcast.72), channel_id=1, source_target_pairs={{0,2},{1,3},{2,0},{3,1},{4,6},{5,7},{6,4},{7,5},{8,10},{9,11},{10,... | collective-permute-start | bytes 5505032 | tf_op jit(solution)/shard_map/ppermute | solution.py:41
  361.0 16.1 %collective-permute-start.32 = (bf16[1,640,256]{2,1,0:T(8,128)(2,1)S(1)}, bf16[1,640,256]{2,1,0:T(8,128)(2,1)S(1)}, u32[]{:S(2)}, u32[]{:S(2)}) collective-permute-start(bf16[1,640,256]{2,1,0:T(8,128)(2,1)S(1)} %add_last.3.one_ref), channel_id=1, source_target_pairs={{0,8},{1,9},{2,10},{3,11},{4,12},{5,13},{6,14},{7,15},{8,0},{9,1},... | collective-permute-start | bytes 983048 | tf_op jit(solution)/shard_map/ppermute | solution.py:41
  377.1 18.1 %collective-permute-start.33 = (bf16[2,640,256]{2,1,0:T(8,128)(2,1)S(1)}, bf16[2,640,256]{2,1,0:T(8,128)(2,1)S(1)}, u32[]{:S(2)}, u32[]{:S(2)}) collective-permute-start(bf16[2,640,256]{2,1,0:T(8,128)(2,1)S(1)} %bitcast.81), channel_id=1, source_target_pairs={{0,4},{1,5},{2,6},{3,7},{4,0},{5,1},{6,2},{7,3},{8,12},{9,13},{10,... | collective-permute-start | bytes 1966088 | tf_op jit(solution)/shard_map/ppermute | solution.py:41
  377.2 15.8 %collective-permute-start.34 = (f32[12,1024]{1,0:T(8,128)S(1)}, f32[12,1024]{1,0:T(8,128)S(1)}, u32[]{:S(2)}, u32[]{:S(2)}) collective-permute-start(f32[12,1024]{1,0:T(8,128)S(1)} %total.7.one_ref), channel_id=1, source_target_pairs={{0,8},{1,9},{2,10},{3,11},{4,12},{5,13},{6,14},{7,15},{8,0},{9,1},... | collective-permute-start | bytes 147464 | tf_op jit(solution)/shard_map/ppermute | solution.py:41
  393.1 1.3 collective-permute-start.35
  402.4 6.8 %collective-permute-start.37 = (bf16[8,448,512]{2,1,0:T(8,128)(2,1)}, bf16[8,448,512]{2,1,0:T(8,128)(2,1)}, u32[]{:S(2)}, u32[]{:S(2)}) collective-permute-start(bf16[8,448,512]{2,1,0:T(8,128)(2,1)} %bitcast.66), channel_id=1, source_target_pairs={{0,1},{1,0},{2,3},{3,2},{4,5},{5,4},{6,7},{7,6},{8,9},{9,8},{10,11... | collective-permute-start | bytes 11010056 | tf_op jit(solution)/shard_map/ppermute | solution.py:41
  402.4 31.2 %collective-permute-start.38 = (bf16[4,640,256]{2,1,0:T(8,128)(2,1)S(1)}, bf16[4,640,256]{2,1,0:T(8,128)(2,1)S(1)}, u32[]{:S(2)}, u32[]{:S(2)}) collective-permute-start(bf16[4,640,256]{2,1,0:T(8,128)(2,1)S(1)} %bitcast.74), channel_id=1, source_target_pairs={{0,2},{1,3},{2,0},{3,1},{4,6},{5,7},{6,4},{7,5},{8,10},{9,11},{10,... | collective-permute-start | bytes 3932168 | tf_op jit(solution)/shard_map/ppermute | solution.py:41
  436.2 5.1 %collective-permute-start.39 = (bf16[8,640,256]{2,1,0:T(8,128)(2,1)S(1)}, bf16[8,640,256]{2,1,0:T(8,128)(2,1)}, u32[]{:S(2)}, u32[]{:S(2)}) collective-permute-start(bf16[8,640,256]{2,1,0:T(8,128)(2,1)S(1)} %bitcast.69), channel_id=1, source_target_pairs={{0,1},{1,0},{2,3},{3,2},{4,5},{5,4},{6,7},{7,6},{8,9},{9,8},{10,11... | collective-permute-start | bytes 7864328 | tf_op jit(solution)/shard_map/ppermute | solution.py:41
  (40 other events, 197.6 us)
Sparse Core Ops, SparseCore 0:
  134.3 83.2 all-gather.1

commit v6 on v5

--- a/solution.py
+++ b/solution.py
@@ -12,7 +12,7 @@
 EPSILON = 1e-05
 MASKED = -1000000000.0
 LANES = 128
-WIDTH = 512
+WIDTH = 256
 MIB = 1024 * 1024
 F32 = jnp.float32
 BF16 = jnp.bfloat16

time: 457 us -> 458 us (level)
  transfers between devices with their start and end apart: 45 -> 45, of which waited for: 29 -> 29; matrix products, arithmetic and copies ran while one was open for 4% -> 4% of each run, Pallas kernels for 20% -> 21%
where the time goes in v6:
time: 458 us; the launch traced here: 457 us
  waiting for transfers between devices  210 us (46%)
  Pallas kernels  112 us (24%)
  starting transfers between devices  71.9 us (16%)
  local copies, waits for them, and re-layouts  45.4 us (10%)
  between operations  14.6 us (3%)
    ppermute x40, waiting for transfers between devices, swap_bit(): return lax.ppermute(value, axis, [(i, i ^ 1 << bit) for i in range(size)])  173 us
    ppermute x40, starting transfers between devices, swap_bit(): return lax.ppermute(value, axis, [(i, i ^ 1 << bit) for i in range(size)])  45.5 us
    unnamed x96, local copies, waits for them, and re-layouts  36.4 us
    pallas_call x1, Pallas kernels, feed_forward(): pl.pallas_call(functools.partial(ffn_kernel, len(expand_arrays), len(shri...  26 us
    all_to_all x1, waiting for transfers between devices, body(): dmixed = lax.all_to_all(dmixed, 'ctx', 0, 0, tiled=True)  19.9 us
    pallas_call x4, Pallas kernels, finish(): pl.pallas_call(functools.partial(finish_kernel, dim, order[:group]), grid...  13.7 us
    all_to_all x1, waiting for transfers between devices, body(): qkv = lax.all_to_all(qkv, 'ctx', 0, 0, tiled=True)  12.5 us
    pallas_call x8, Pallas kernels, combine(): pl.pallas_call(combine_kernel, grid=(outer, inner // per), in_specs=[bloc...  10.6 us
  transfers between devices with their start and end apart: 45, of which 29 were waited for; matrix products, arithmetic and copies ran while one was open for 4% of the time, Pallas kernels for 21%

profile of v6, /device:TPU:0, one launch (start us, length us, event | category | flops | bytes accessed | tf_op | source)
XLA Modules:
  0.0 456.6 jit_solution(11063713237253237511)
XLA Ops:
  8.5 3.0 collective-permute-start.1
  19.1 2.3 dynamic_slice.18
  22.6 3.1 constant_dynamic-slice_fusion.4
  25.7 2.3 convert_reduce_fusion
  33.8 14.5 %collective-permute-done.2.refs_2_.refs_7_.refs_12_ = bf16[128,3072]{1,0:T(8,128)(2,1)S(1)} collective-permute-done((bf16[128,3072]{1,0:T(8,128)(2,1)S(1)}, bf16[128,3072]{1,0:T(8,128)(2,1)S(1)}, u32[]{:S(2)}, u32[]{:S(2)}) %collective-permute-start.2) | collective-permute-done | bytes 786464 | tf_op jit(solution)/shard_map/ppermute | solution.py:41
  48.8 6.4 %collective-permute-done.3.refs_1_ = bf16[256,2048]{1,0:T(8,128)(2,1)S(1)} collective-permute-done((bf16[256,2048]{1,0:T(8,128)(2,1)}, bf16[256,2048]{1,0:T(8,128)(2,1)S(1)}, u32[]{:S(2)}, u32[]{:S(2)}) %collective-permute-start.3) | collective-permute-done | bytes 1048608 | tf_op jit(solution)/shard_map/ppermute | solution.py:41
  56.2 5.0 %project.1 = (bf16[8,4,64,384]{3,2,1,0:T(8,128)(2,1)S(1)}, f32[8,128]{1,0:T(8,128)S(1)}) custom-call(s32[5]{0:T(128)S(1)} %pad_add_fusion.1.off_ref, bf16[256,1024]{1,0:T(8,128)(2,1)S(1)} %get-tuple-element.243.h_ref, f32[8,1024]{1,0:T(8,128)S(1)} %get-tuple-element.201.v_ref, bf16[512,3072]{1,0:T(8,128)(2,1)} %refs_10_.3, ...), custom_call_target="tpu_custom_call" | custom-call | tf_op jit(solution)/shard_map/project/pallas_call | solution.py:220
  62.4 5.2 %all-to-all-start = ((bf16[16,2,64,384]{3,2,1,0:T(8,128)(2,1)}), bf16[16,2,64,384]{3,2,1,0:T(8,128)(2,1)}, u32[]{:S(2)}, u32[]{:S(2)}) async-start(bf16[16,2,64,384]{3,2,1,0:T(8,128)(2,1)} %bitcast.88), calls=%async_computation | async-start | bytes 3145728 | tf_op jit(solution)/shard_map/all_to_all | solution.py:1387
  69.2 12.8 %collective-permute-done.6.refs_1_ = bf16[1024,256]{1,0:T(8,128)(2,1)S(1)} collective-permute-done((bf16[1024,256]{1,0:T(8,128)(2,1)}, bf16[1024,256]{1,0:T(8,128)(2,1)S(1)}, u32[]{:S(2)}, u32[]{:S(2)}) %collective-permute-start.6) | collective-permute-done | bytes 524320 | tf_op jit(solution)/shard_map/ppermute | solution.py:41
  87.3 12.5 %all-to-all-done.qkv_ref = bf16[16,2,64,384]{3,2,1,0:T(8,128)(2,1)} async-done(((bf16[16,2,64,384]{3,2,1,0:T(8,128)(2,1)}), bf16[16,2,64,384]{3,2,1,0:T(8,128)(2,1)}, u32[]{:S(2)}, u32[]{:S(2)}) %all-to-all-start) | async-done | bytes 1572896 | tf_op jit(solution)/shard_map/all_to_all | solution.py:1387
  99.8 10.0 %attend.1 = (bf16[16,2,64,128]{3,2,1,0:T(8,128)(2,1)S(1)}, f32[2,2,1024]{2,1,0:T(2,128)S(1)}) custom-call(s32[16]{0:T(128)S(1)} %copy-done.37, s32[2]{0:T(128)S(1)} %add_and_fusion.seq_ref, bf16[16,2,64,384]{3,2,1,0:T(8,128)(2,1)} %all-to-all-done.qkv_ref, s32[4,1,1024]{2,1,0:T(1,128)S(1)} %broadcast_in_dim.2.start_ref), custom_call_target="tpu_custom_call" | custom-call | tf_op jit(solution)/shard_map/attend/pallas_call | solution.py:315
  110.5 9.2 %all-to-all-start.1 = ((bf16[16,2,64,128]{3,2,1,0:T(8,128)(2,1)}), bf16[16,2,64,128]{3,2,1,0:T(8,128)(2,1)}, u32[]{:S(2)}, u32[]{:S(2)}) async-start(bf16[16,2,64,128]{3,2,1,0:T(8,128)(2,1)} %copy-done.35), calls=%async_computation.1 | async-start | bytes 1048576 | tf_op jit(solution)/shard_map/all_to_all | solution.py:1393
  119.9 9.5 %collective-permute-done.10.refs_4_ = bf16[2048,512]{1,0:T(8,128)(2,1)} collective-permute-done((bf16[2048,512]{1,0:T(8,128)(2,1)}, bf16[2048,512]{1,0:T(8,128)(2,1)}, u32[]{:S(2)}, u32[]{:S(2)}) %collective-permute-start.10) | collective-permute-done | bytes 2097184 | tf_op jit(solution)/shard_map/ppermute | solution.py:41
  129.4 4.8 %all-to-all-done.1 = bf16[16,2,64,128]{3,2,1,0:T(8,128)(2,1)} async-done(((bf16[16,2,64,128]{3,2,1,0:T(8,128)(2,1)}), bf16[16,2,64,128]{3,2,1,0:T(8,128)(2,1)}, u32[]{:S(2)}, u32[]{:S(2)}) %all-to-all-start.1) | async-done | bytes 524320 | tf_op jit(solution)/shard_map/all_to_all | solution.py:1393
  138.6 2.8 branch.1
  144.3 26.0 %feed_forward.1 = (f32[256,1024]{1,0:T(8,128)S(1)}, f32[256,1024]{1,0:T(8,128)S(1)}, f32[256,1024]{1,0:T(8,128)S(1)}, f32[256,1024]{1,0:T(8,128)}, bf16[1,8,1,25...) custom-call(s32[9]{0:T(128)S(1)} %concatenate.23.sc_ref, ...), custom_call_target="tpu_custom_call" | custom-call | tf_op jit(solution)/shard_map/feed_forward/pallas_call | solution.py:630
  175.9 5.3 %branch_back.1 = (f32[256,1024]{1,0:T(8,128)S(1)}, bf16[8,4,64,128]{3,2,1,0:T(8,128)(2,1)S(1)}, bf16[2,8,64,512]{3,2,1,0:T(8,128)(2,1)S(1)}, bf16[2,8,64,512]{3,2,1,0:T(8,128)(2,1)S(1)}, f32[8,1024]{1,0:T(8,128)S(1)}) custom-call(s32[5]{0:T(128)S(1)} %pad_add_fusion.4.sc_ref, f32[256,1024]{1,0:T(8,128)} %copy-done.24, f32[256,1024]{1,0:T(8,128)} %copy-done.40, ...), custom_call_target="tpu_custom_call" | custom-call | tf_op jit(solution)/shard_map/branch_back/pallas_call | solution.py:722
  184.9 4.3 all-to-all-start.2
  190.7 19.9 %all-to-all-done.2.grad_ref = bf16[16,2,64,128]{3,2,1,0:T(8,128)(2,1)} async-done(((bf16[16,2,64,128]{3,2,1,0:T(8,128)(2,1)}), bf16[16,2,64,128]{3,2,1,0:T(8,128)(2,1)}, u32[]{:S(2)}, u32[]{:S(2)}) %all-to-all-start.2) | async-done | bytes 524320 | tf_op jit(solution)/shard_map/all_to_all | solution.py:1431
  210.6 10.4 %attend_back.1 = (bf16[16,2,64,384]{3,2,1,0:T(8,128)(2,1)S(1)}, f32[8,128]{1,0:T(8,128)S(1)}) custom-call(s32[16]{0:T(128)S(1)} %copy-done.37, s32[2]{0:T(128)S(1)} %add_and_fusion.seq_ref, bf16[16,2,64,384]{3,2,1,0:T(8,128)(2,1)} %all-to-all-done.qkv_ref, bf16[16,2,64,128]{3,2,1,0:T(8,128)(2,1)} %all-to-all-done.2.grad_ref, ...), custom_call_target="tpu_custom_call" | custom-call | tf_op jit(solution)/shard_map/attend_back/pallas_call | solution.py:423
  222.1 7.6 %all-to-all-start.3 = ((bf16[16,2,64,384]{3,2,1,0:T(8,128)(2,1)}), bf16[16,2,64,384]{3,2,1,0:T(8,128)(2,1)}, u32[]{:S(2)}, u32[]{:S(2)}) async-start(bf16[16,2,64,384]{3,2,1,0:T(8,128)(2,1)} %copy-done.3), calls=%async_computation.3 | async-start | bytes 3145728 | tf_op jit(solution)/shard_map/all_to_all | solution.py:1456
  231.8 3.6 combine.8
  239.5 5.5 %input_weight_terms.1 = (bf16[1,2,256,384]{3,2,1,0:T(8,128)(2,1)S(1)}, bf16[1,2,256,384]{3,2,1,0:T(8,128)(2,1)S(1)}, f32[8,128]{1,0:T(8,128)S(1)}) custom-call(s32[3]{0:T(128)S(1)} %get-tuple-element.242.sc_ref, bf16[16,4,64,1024]{3,2,1,0:T(8,128)(2,1)} %all-gather.2.cloned.1.call-done.h_ref, bf16[16,2,64,384]{3,2,1,0:T(8,128)(2,1)S(1)} %copy-done.4), custom_call_target="tpu_custom_call" | custom-call | tf_op jit(solution)/shard_map/input_weight_terms/pallas_call | solution.py:778
  248.4 17.1 %collective-permute-done.13 = bf16[1,8,1,512,256]{4,3,2,1,0:T(8,128)(2,1)} collective-permute-done((bf16[1,8,1,512,256]{4,3,2,1,0:T(8,128)(2,1)}, bf16[1,8,1,512,256]{4,3,2,1,0:T(8,128)(2,1)}, u32[]{:S(2)}, u32[]{:S(2)}) %collective-permute-start.13) | collective-permute-done | bytes 2097184 | tf_op jit(solution)/shard_map/ppermute | solution.py:41
  265.5 2.5 combine.11
  270.4 2.3 collective-permute-done.20
  274.1 2.2 collective-permute-start.22
  277.8 6.0 %collective-permute-done.19 = bf16[1,8,64,512]{3,2,1,0:T(8,128)(2,1)S(1)} collective-permute-done((bf16[1,8,64,512]{3,2,1,0:T(8,128)(2,1)S(1)}, bf16[1,8,64,512]{3,2,1,0:T(8,128)(2,1)S(1)}, u32[]{:S(2)}, u32[]{:S(2)}) %collective-permute-start.19) | collective-permute-done | bytes 524320 | tf_op jit(solution)/shard_map/ppermute | solution.py:41
  287.5 3.2 collective-permute-start.24
  290.7 9.5 %collective-permute-done.21 = bf16[4,1,64,512]{3,2,1,0:T(8,128)(2,1)S(1)} collective-permute-done((bf16[4,1,64,512]{3,2,1,0:T(8,128)(2,1)S(1)}, bf16[4,1,64,512]{3,2,1,0:T(8,128)(2,1)S(1)}, u32[]{:S(2)}, u32[]{:S(2)}) %collective-permute-start.21) | collective-permute-done | bytes 262176 | tf_op jit(solution)/shard_map/ppermute | solution.py:41
  301.2 2.1 collective-permute-start.26
  309.4 7.8 %entry_back.1 = (f32[256,1024]{1,0:T(8,128)}, bf16[256,1024]{1,0:T(8,128)(2,1)}, f32[12,1024]{1,0:T(8,128)S(1)}) custom-call(s32[6]{0:T(128)S(1)} %pad_add_fusion.5.off_ref, bf16[8,4,64,384]{3,2,1,0:T(8,128)(2,1)} %bitcast.14.d_ref, bf16[256,1024]{1,0:T(8,128)(2,1)S(1)} %bitcast.77, f32[256,1024]{1,0:T(8,128)S(1)} %copy-done.31, f32[256,1024]{1,0:T(8,128)S(1)} %copy-done.29, ...), custom_call_target="tpu_custom_call" | custom-call | tf_op jit(solution)/shard_map/entry_back/pallas_call | solution.py:874
  317.3 10.6 %collective-permute-done.26 = bf16[2,640,256]{2,1,0:T(8,128)(2,1)} collective-permute-done((bf16[2,640,256]{2,1,0:T(8,128)(2,1)}, bf16[2,640,256]{2,1,0:T(8,128)(2,1)}, u32[]{:S(2)}, u32[]{:S(2)}) %collective-permute-start.26) | collective-permute-done | bytes 655392 | tf_op jit(solution)/shard_map/ppermute | solution.py:41
  335.8 2.8 collective-permute-done.29.two_ref
  339.5 3.4 collective-permute-done.30.two_ref
  343.1 17.2 %collective-permute-done.31.two_ref = f32[12,1024]{1,0:T(8,128)S(1)} collective-permute-done((f32[12,1024]{1,0:T(8,128)S(1)}, f32[12,1024]{1,0:T(8,128)S(1)}, u32[]{:S(2)}, u32[]{:S(2)}) %collective-permute-start.31) | collective-permute-done | bytes 49184 | tf_op jit(solution)/shard_map/ppermute | solution.py:41
  363.5 14.8 %collective-permute-done.32.two_ref = bf16[1,640,256]{2,1,0:T(8,128)(2,1)S(1)} collective-permute-done((bf16[1,640,256]{2,1,0:T(8,128)(2,1)S(1)}, bf16[1,640,256]{2,1,0:T(8,128)(2,1)S(1)}, u32[]{:S(2)}, u32[]{:S(2)}) %collective-permute-start.32) | collective-permute-done | bytes 327712 | tf_op jit(solution)/shard_map/ppermute | solution.py:41
  378.4 2.2 collective-permute-start.34
  380.6 13.7 %collective-permute-done.34.two_ref = f32[12,1024]{1,0:T(8,128)S(1)} collective-permute-done((f32[12,1024]{1,0:T(8,128)S(1)}, f32[12,1024]{1,0:T(8,128)S(1)}, u32[]{:S(2)}, u32[]{:S(2)}) %collective-permute-start.34) | collective-permute-done | bytes 49184 | tf_op jit(solution)/shard_map/ppermute | solution.py:41
  396.6 4.9 %collective-permute-done.36.two_ref = bf16[4,448,512]{2,1,0:T(8,128)(2,1)S(1)} collective-permute-done((bf16[4,448,512]{2,1,0:T(8,128)(2,1)S(1)}, bf16[4,448,512]{2,1,0:T(8,128)(2,1)S(1)}, u32[]{:S(2)}, u32[]{:S(2)}) %collective-permute-start.36) | collective-permute-done | bytes 1835040 | tf_op jit(solution)/shard_map/ppermute | solution.py:41
  401.5 2.3 merge.10
  407.6 2.7 finish.4
  410.5 5.0 %finish_extra.1 = (f32[512,3072]{1,0:T(8,128)}, f32[8,128]{1,0:T(8,128)S(1)}) custom-call(s32[2]{0:T(128)S(1)} %get-tuple-element.322.label_ref, bf16[8,448,512]{2,1,0:T(8,128)(2,1)S(1)} %bitcast.67, bf16[8,448,512]{2,1,0:T(8,128)(2,1)} %collective-permute-done.37.far_ref.source), custom_call_target="tpu_custom_call" | custom-call | tf_op jit(solution)/shard_map/finish_extra/pallas_call | solution.py:1223
  415.5 4.2 finish.5
  419.7 15.3 %collective-permute-done.38.two_ref = bf16[4,640,256]{2,1,0:T(8,128)(2,1)S(1)} collective-permute-done((bf16[4,640,256]{2,1,0:T(8,128)(2,1)S(1)}, bf16[4,640,256]{2,1,0:T(8,128)(2,1)S(1)}, u32[]{:S(2)}, u32[]{:S(2)}) %collective-permute-start.38) | collective-permute-done | bytes 1310752 | tf_op jit(solution)/shard_map/ppermute | solution.py:41
  438.4 2.7 finish.6
  442.7 4.0 finish.7
  446.7 3.1 finish_rows.1
  (200 shorter events, 94.5 us)
Async XLA Ops:
  8.5 21.1 %collective-permute-start.1 = (bf16[128,3072]{1,0:T(8,128)(2,1)S(1)}, bf16[128,3072]{1,0:T(8,128)(2,1)S(1)}, u32[]{:S(2)}, u32[]{:S(2)}) collective-permute-start(bf16[128,3072]{1,0:T(8,128)(2,1)S(1)} %constant_dynamic-slice_fusion.3), channel_id=1, source_target_pairs={{0,16},{16,0},{1,17},{17,1},{2,18},{18,2},{3,19},{19,3},{4,20},{20... | collective-permute-start | bytes 2359304 | tf_op jit(solution)/shard_map/ppermute | solution.py:41
  21.4 8.2 %collective-permute-start = (bf16[1,6144]{1,0:T(2,128)(2,1)S(1)}, bf16[1,6144]{1,0:T(2,128)(2,1)S(1)}, u32[]{:S(2)}, u32[]{:S(2)}) collective-permute-start(bf16[1,6144]{1,0:T(2,128)(2,1)S(1)} %reshape.159.refs_0_), channel_id=1, source_target_pairs={{0,16},{16,0},{1,17},{17,1},{2,18},{18,2},{3,19},{19,3},{4,20},{20... | collective-permute-start | bytes 36872 | tf_op jit(solution)/shard_map/ppermute | solution.py:41
  29.6 18.7 %collective-permute-start.2 = (bf16[128,3072]{1,0:T(8,128)(2,1)S(1)}, bf16[128,3072]{1,0:T(8,128)(2,1)S(1)}, u32[]{:S(2)}, u32[]{:S(2)}) collective-permute-start(bf16[128,3072]{1,0:T(8,128)(2,1)S(1)} %collective-permute-done.1.refs_1_.refs_6_.refs_11_), channel_id=1, source_target_pairs={{0,2},{1,3},{2,0},{3,1},{4,6},{5,7},{6,4},{7,5},{8,10},{9,11},{10,... | collective-permute-start | bytes 2359304 | tf_op jit(solution)/shard_map/ppermute | solution.py:41
  31.3 24.0 %collective-permute-start.3 = (bf16[256,2048]{1,0:T(8,128)(2,1)}, bf16[256,2048]{1,0:T(8,128)(2,1)S(1)}, u32[]{:S(2)}, u32[]{:S(2)}) collective-permute-start(bf16[256,2048]{1,0:T(8,128)(2,1)} %dynamic_slice.18), channel_id=1, source_target_pairs={{0,16},{16,0},{1,17},{17,1},{2,18},{18,2},{3,19},{19,3},{4,20},{20... | collective-permute-start | bytes 3145736 | tf_op jit(solution)/shard_map/ppermute | solution.py:41
  48.3 6.9 %collective-permute-start.4 = (bf16[128,3072]{1,0:T(8,128)(2,1)S(1)}, bf16[128,3072]{1,0:T(8,128)(2,1)S(1)}, u32[]{:S(2)}, u32[]{:S(2)}) collective-permute-start(bf16[128,3072]{1,0:T(8,128)(2,1)S(1)} %collective-permute-done.2.refs_2_.refs_7_.refs_12_), channel_id=1, source_target_pairs={{0,1},{1,0},{2,3},{3,2},{4,5},{5,4},{6,7},{7,6},{8,9},{9,8},{10,11... | collective-permute-start | bytes 2359304 | tf_op jit(solution)/shard_map/ppermute | solution.py:41
  48.3 6.9 %collective-permute-start.5 = (bf16[128,3072]{1,0:T(8,128)(2,1)S(1)}, bf16[128,3072]{1,0:T(8,128)(2,1)S(1)}, u32[]{:S(2)}, u32[]{:S(2)}) collective-permute-start(bf16[128,3072]{1,0:T(8,128)(2,1)S(1)} %collective-permute-done.1.refs_1_.refs_6_.refs_11_), channel_id=1, source_target_pairs={{0,1},{1,0},{2,3},{3,2},{4,5},{5,4},{6,7},{7,6},{8,9},{9,8},{10,11... | collective-permute-start | bytes 2359304 | tf_op jit(solution)/shard_map/ppermute | solution.py:41
  62.4 37.4 %copy-start.37 = (s32[16]{0:T(128)S(1)}, s32[16]{0:T(128)}, u32[]{:S(2)}) copy-start(s32[16]{0:T(128)} %table.3) | copy-start | bytes 196
  62.4 37.3 %all-to-all-start = ((bf16[16,2,64,384]{3,2,1,0:T(8,128)(2,1)}), bf16[16,2,64,384]{3,2,1,0:T(8,128)(2,1)}, u32[]{:S(2)}, u32[]{:S(2)}) async-start(bf16[16,2,64,384]{3,2,1,0:T(8,128)(2,1)} %bitcast.88), calls=%async_computation | async-start | bytes 3145728 | tf_op jit(solution)/shard_map/all_to_all | solution.py:1387
  67.6 14.4 %collective-permute-start.6 = (bf16[1024,256]{1,0:T(8,128)(2,1)}, bf16[1024,256]{1,0:T(8,128)(2,1)S(1)}, u32[]{:S(2)}, u32[]{:S(2)}) collective-permute-start(bf16[1024,256]{1,0:T(8,128)(2,1)} %constant_dynamic-slice_fusion.5), channel_id=1, source_target_pairs={{0,16},{16,0},{1,17},{17,1},{2,18},{18,2},{3,19},{19,3},{4,20},{20... | collective-permute-start | bytes 1572872 | tf_op jit(solution)/shard_map/ppermute | solution.py:41
  82.0 47.4 %collective-permute-start.10 = (bf16[2048,512]{1,0:T(8,128)(2,1)}, bf16[2048,512]{1,0:T(8,128)(2,1)}, u32[]{:S(2)}, u32[]{:S(2)}) collective-permute-start(bf16[2048,512]{1,0:T(8,128)(2,1)} %constant_dynamic-slice_fusion.4), channel_id=1, source_target_pairs={{0,16},{16,0},{1,17},{17,1},{2,18},{18,2},{3,19},{19,3},{4,20},{20... | collective-permute-start | bytes 6291464 | tf_op jit(solution)/shard_map/ppermute | solution.py:41
  83.5 3.0 collective-permute-start.7
  84.3 15.4 %collective-permute-start.8 = (bf16[256,1024]{1,0:T(8,128)(2,1)}, bf16[256,1024]{1,0:T(8,128)(2,1)}, u32[]{:S(2)}, u32[]{:S(2)}) collective-permute-start(bf16[256,1024]{1,0:T(8,128)(2,1)} %bitcast.82), channel_id=1, source_target_pairs={{0,1},{1,0},{2,3},{3,2},{4,5},{5,4},{6,7},{7,6},{8,9},{9,8},{10,11... | collective-permute-start | bytes 1572872 | tf_op jit(solution)/shard_map/ppermute | solution.py:41
  84.8 44.6 %collective-permute-start.9 = (bf16[256,2048]{1,0:T(8,128)(2,1)}, bf16[256,2048]{1,0:T(8,128)(2,1)}, u32[]{:S(2)}, u32[]{:S(2)}) collective-permute-start(bf16[256,2048]{1,0:T(8,128)(2,1)} %copy-done.41), channel_id=1, source_target_pairs={{0,2},{1,3},{2,0},{3,1},{4,6},{5,7},{6,4},{7,5},{8,10},{9,11},{10,... | collective-permute-start | bytes 3145736 | tf_op jit(solution)/shard_map/ppermute | solution.py:41
  110.5 23.7 %all-to-all-start.1 = ((bf16[16,2,64,128]{3,2,1,0:T(8,128)(2,1)}), bf16[16,2,64,128]{3,2,1,0:T(8,128)(2,1)}, u32[]{:S(2)}, u32[]{:S(2)}) async-start(bf16[16,2,64,128]{3,2,1,0:T(8,128)(2,1)} %copy-done.35), calls=%async_computation.1 | async-start | bytes 1048576 | tf_op jit(solution)/shard_map/all_to_all | solution.py:1393
  119.7 118.4 %all-gather.2.cloned.1.call-start = ((), (), s32[]{:S(2)}) async-start(), calls=%async_computation.4 | async-start | bytes 8912896 | tf_op jit(solution)/shard_map/all_gather | solution.py:1395
  142.4 1.9 collective-permute-start.11
  144.3 31.6 %copy-start.17 = (bf16[1024,256]{1,0:T(8,128)(2,1)S(1)}, bf16[1024,256]{1,0:T(8,128)(2,1)}, u32[]{:S(2)}) copy-start(bf16[1024,256]{1,0:T(8,128)(2,1)} %copy-done.15) | copy-start | bytes 1572868
  144.3 31.6 %copy-start.20 = (bf16[1024,256]{1,0:T(8,128)(2,1)S(1)}, bf16[1024,256]{1,0:T(8,128)(2,1)}, u32[]{:S(2)}) copy-start(bf16[1024,256]{1,0:T(8,128)(2,1)} %copy-done.18) | copy-start | bytes 1572868
  172.2 2.7 collective-permute-start.12
  172.4 57.8 %collective-permute-start.15 = (bf16[1,8,1,256,512]{4,3,2,1,0:T(8,128)(2,1)}, bf16[1,8,1,256,512]{4,3,2,1,0:T(8,128)(2,1)}, u32[]{:S(2)}, u32[]{:S(2)}) collective-permute-start(bf16[1,8,1,256,512]{4,3,2,1,0:T(8,128)(2,1)} %get-tuple-element.245), channel_id=1, source_target_pairs={{0,16},{16,0},{1,17},{17,1},{2,18},{18,2},{3,19},{19,3},{4,20},{20... | collective-permute-start | bytes 6291464 | tf_op jit(solution)/shard_map/ppermute | solution.py:41
  184.9 25.7 %all-to-all-start.2 = ((bf16[16,2,64,128]{3,2,1,0:T(8,128)(2,1)}), bf16[16,2,64,128]{3,2,1,0:T(8,128)(2,1)}, u32[]{:S(2)}, u32[]{:S(2)}) async-start(bf16[16,2,64,128]{3,2,1,0:T(8,128)(2,1)} %bitcast.99), calls=%async_computation.2 | async-start | bytes 1048576 | tf_op jit(solution)/shard_map/all_to_all | solution.py:1431
  189.1 76.4 %collective-permute-start.13 = (bf16[1,8,1,512,256]{4,3,2,1,0:T(8,128)(2,1)}, bf16[1,8,1,512,256]{4,3,2,1,0:T(8,128)(2,1)}, u32[]{:S(2)}, u32[]{:S(2)}) collective-permute-start(bf16[1,8,1,512,256]{4,3,2,1,0:T(8,128)(2,1)} %get-tuple-element.239), channel_id=1, source_target_pairs={{0,16},{16,0},{1,17},{17,1},{2,18},{18,2},{3,19},{19,3},{4,20},{20... | collective-permute-start | bytes 6291464 | tf_op jit(solution)/shard_map/ppermute | solution.py:41
  190.7 47.4 %collective-permute-start.16 = (f32[256,1024]{1,0:T(8,128)}, f32[256,1024]{1,0:T(8,128)}, u32[]{:S(2)}, u32[]{:S(2)}) collective-permute-start(f32[256,1024]{1,0:T(8,128)} %copy-done.38), channel_id=1, source_target_pairs={{0,1},{1,0},{2,3},{3,2},{4,5},{5,4},{6,7},{7,6},{8,9},{9,8},{10,11... | collective-permute-start | bytes 3145736 | tf_op jit(solution)/shard_map/ppermute | solution.py:41
  222.1 83.8 %all-to-all-start.3 = ((bf16[16,2,64,384]{3,2,1,0:T(8,128)(2,1)}), bf16[16,2,64,384]{3,2,1,0:T(8,128)(2,1)}, u32[]{:S(2)}, u32[]{:S(2)}) async-start(bf16[16,2,64,384]{3,2,1,0:T(8,128)(2,1)} %copy-done.3), calls=%async_computation.3 | async-start | bytes 3145728 | tf_op jit(solution)/shard_map/all_to_all | solution.py:1456
  229.8 17.1 %collective-permute-start.14 = (bf16[2,8,64,512]{3,2,1,0:T(8,128)(2,1)}, bf16[2,8,64,512]{3,2,1,0:T(8,128)(2,1)}, u32[]{:S(2)}, u32[]{:S(2)}) collective-permute-start(bf16[2,8,64,512]{3,2,1,0:T(8,128)(2,1)} %copy-done.39), channel_id=1, source_target_pairs={{0,1},{1,0},{2,3},{3,2},{4,5},{5,4},{6,7},{7,6},{8,9},{9,8},{10,11... | collective-permute-start | bytes 3145736 | tf_op jit(solution)/shard_map/ppermute | solution.py:41
  236.4 36.3 %collective-permute-start.20 = (bf16[4,1,256,512]{3,2,1,0:T(8,128)(2,1)}, bf16[4,1,256,512]{3,2,1,0:T(8,128)(2,1)}, u32[]{:S(2)}, u32[]{:S(2)}) collective-permute-start(bf16[4,1,256,512]{3,2,1,0:T(8,128)(2,1)} %get-tuple-element.264), channel_id=1, source_target_pairs={{0,2},{1,3},{2,0},{3,1},{4,6},{5,7},{6,4},{7,5},{8,10},{9,11},{10,... | collective-permute-start | bytes 3145736 | tf_op jit(solution)/shard_map/ppermute | solution.py:41
  245.0 1.8 collective-permute-start.17
  268.1 32.2 %collective-permute-start.18 = (bf16[4,1,512,256]{3,2,1,0:T(8,128)(2,1)S(1)}, bf16[4,1,512,256]{3,2,1,0:T(8,128)(2,1)S(1)}, u32[]{:S(2)}, u32[]{:S(2)}) collective-permute-start(bf16[4,1,512,256]{3,2,1,0:T(8,128)(2,1)S(1)} %get-tuple-element.260), channel_id=1, source_target_pairs={{0,2},{1,3},{2,0},{3,1},{4,6},{5,7},{6,4},{7,5},{8,10},{9,11},{10,... | collective-permute-start | bytes 3145736 | tf_op jit(solution)/shard_map/ppermute | solution.py:41
  268.9 14.9 %collective-permute-start.19 = (bf16[1,8,64,512]{3,2,1,0:T(8,128)(2,1)S(1)}, bf16[1,8,64,512]{3,2,1,0:T(8,128)(2,1)S(1)}, u32[]{:S(2)}, u32[]{:S(2)}) collective-permute-start(bf16[1,8,64,512]{3,2,1,0:T(8,128)(2,1)S(1)} %get-tuple-element.262), channel_id=1, source_target_pairs={{0,16},{16,0},{1,17},{17,1},{2,18},{18,2},{3,19},{19,3},{4,20},{20... | collective-permute-start | bytes 1572872 | tf_op jit(solution)/shard_map/ppermute | solution.py:41
  274.1 13.3 %collective-permute-start.22 = (bf16[2,1,256,512]{3,2,0,1:T(8,128)(2,1)S(1)}, bf16[2,1,256,512]{3,2,0,1:T(8,128)(2,1)S(1)}, u32[]{:S(2)}, u32[]{:S(2)}) collective-permute-start(bf16[2,1,256,512]{3,2,0,1:T(8,128)(2,1)S(1)} %bitcast.111), channel_id=1, source_target_pairs={{0,4},{1,5},{2,6},{3,7},{4,0},{5,1},{6,2},{7,3},{8,12},{9,13},{10,... | collective-permute-start | bytes 1572872 | tf_op jit(solution)/shard_map/ppermute | solution.py:41
  276.3 9.7 %collective-permute-start.23 = (bf16[1,1,256,384]{3,2,1,0:T(8,128)(2,1)S(1)}, bf16[1,1,256,384]{3,2,1,0:T(8,128)(2,1)S(1)}, u32[]{:S(2)}, u32[]{:S(2)}) collective-permute-start(bf16[1,1,256,384]{3,2,1,0:T(8,128)(2,1)S(1)} %get-tuple-element.273), channel_id=1, source_target_pairs={{0,16},{16,0},{1,17},{17,1},{2,18},{18,2},{3,19},{19,3},{4,20},{20... | collective-permute-start | bytes 589832 | tf_op jit(solution)/shard_map/ppermute | solution.py:41
  284.0 16.3 %collective-permute-start.21 = (bf16[4,1,64,512]{3,2,1,0:T(8,128)(2,1)S(1)}, bf16[4,1,64,512]{3,2,1,0:T(8,128)(2,1)S(1)}, u32[]{:S(2)}, u32[]{:S(2)}) collective-permute-start(bf16[4,1,64,512]{3,2,1,0:T(8,128)(2,1)S(1)} %get-tuple-element.269), channel_id=1, source_target_pairs={{0,2},{1,3},{2,0},{3,1},{4,6},{5,7},{6,4},{7,5},{8,10},{9,11},{10,... | collective-permute-start | bytes 786440 | tf_op jit(solution)/shard_map/ppermute | solution.py:41
  287.5 15.8 %collective-permute-start.24 = (bf16[1,1,256,512]{3,2,1,0:T(8,128)(2,1)S(1)}, bf16[1,1,256,512]{3,2,1,0:T(8,128)(2,1)S(1)}, u32[]{:S(2)}, u32[]{:S(2)}) collective-permute-start(bf16[1,1,256,512]{3,2,1,0:T(8,128)(2,1)S(1)} %get-tuple-element.280), channel_id=1, source_target_pairs={{0,8},{1,9},{2,10},{3,11},{4,12},{5,13},{6,14},{7,15},{8,0},{9,1},... | collective-permute-start | bytes 786440 | tf_op jit(solution)/shard_map/ppermute | solution.py:41
  301.2 26.7 %collective-permute-start.26 = (bf16[2,640,256]{2,1,0:T(8,128)(2,1)}, bf16[2,640,256]{2,1,0:T(8,128)(2,1)}, u32[]{:S(2)}, u32[]{:S(2)}) collective-permute-start(bf16[2,640,256]{2,1,0:T(8,128)(2,1)} %get-tuple-element.299), channel_id=1, source_target_pairs={{0,4},{1,5},{2,6},{3,7},{4,0},{5,1},{6,2},{7,3},{8,12},{9,13},{10,... | collective-permute-start | bytes 1966088 | tf_op jit(solution)/shard_map/ppermute | solution.py:41
  304.2 25.0 %collective-permute-start.25 = (bf16[1,448,512]{2,1,0:T(8,128)(2,1)}, bf16[1,448,512]{2,1,0:T(8,128)(2,1)}, u32[]{:S(2)}, u32[]{:S(2)}) collective-permute-start(bf16[1,448,512]{2,1,0:T(8,128)(2,1)} %pack.1.one_ref), channel_id=1, source_target_pairs={{0,8},{1,9},{2,10},{3,11},{4,12},{5,13},{6,14},{7,15},{8,0},{9,1},... | collective-permute-start | bytes 1376264 | tf_op jit(solution)/shard_map/ppermute | solution.py:41
  330.4 30.0 %collective-permute-start.27 = (bf16[2,448,512]{2,1,0:T(8,128)(2,1)S(1)}, bf16[2,448,512]{2,1,0:T(8,128)(2,1)S(1)}, u32[]{:S(2)}, u32[]{:S(2)}) collective-permute-start(bf16[2,448,512]{2,1,0:T(8,128)(2,1)S(1)} %bitcast.78), channel_id=1, source_target_pairs={{0,4},{1,5},{2,6},{3,7},{4,0},{5,1},{6,2},{7,3},{8,12},{9,13},{10,... | collective-permute-start | bytes 2752520 | tf_op jit(solution)/shard_map/ppermute | solution.py:41
  332.3 28.0 %collective-permute-start.28 = (bf16[1,1,640,256]{3,2,1,0:T(8,128)(2,1)S(1)}, bf16[1,1,640,256]{3,2,1,0:T(8,128)(2,1)S(1)}, u32[]{:S(2)}, u32[]{:S(2)}) collective-permute-start(bf16[1,1,640,256]{3,2,1,0:T(8,128)(2,1)S(1)} %get-tuple-element.305), channel_id=1, source_target_pairs={{0,8},{1,9},{2,10},{3,11},{4,12},{5,13},{6,14},{7,15},{8,0},{9,1},... | collective-permute-start | bytes 983048 | tf_op jit(solution)/shard_map/ppermute | solution.py:41
  334.3 4.3 collective-permute-start.29
  338.6 4.3 collective-permute-start.30
  342.9 17.3 %collective-permute-start.31 = (f32[12,1024]{1,0:T(8,128)S(1)}, f32[12,1024]{1,0:T(8,128)S(1)}, u32[]{:S(2)}, u32[]{:S(2)}) collective-permute-start(f32[12,1024]{1,0:T(8,128)S(1)} %total.6.one_ref), channel_id=1, source_target_pairs={{0,4},{1,5},{2,6},{3,7},{4,0},{5,1},{6,2},{7,3},{8,12},{9,13},{10,... | collective-permute-start | bytes 147464 | tf_op jit(solution)/shard_map/ppermute | solution.py:41
  360.6 41.0 %collective-permute-start.36 = (bf16[4,448,512]{2,1,0:T(8,128)(2,1)S(1)}, bf16[4,448,512]{2,1,0:T(8,128)(2,1)S(1)}, u32[]{:S(2)}, u32[]{:S(2)}) collective-permute-start(bf16[4,448,512]{2,1,0:T(8,128)(2,1)S(1)} %bitcast.71), channel_id=1, source_target_pairs={{0,2},{1,3},{2,0},{3,1},{4,6},{5,7},{6,4},{7,5},{8,10},{9,11},{10,... | collective-permute-start | bytes 5505032 | tf_op jit(solution)/shard_map/ppermute | solution.py:41
  362.4 15.9 %collective-permute-start.32 = (bf16[1,640,256]{2,1,0:T(8,128)(2,1)S(1)}, bf16[1,640,256]{2,1,0:T(8,128)(2,1)S(1)}, u32[]{:S(2)}, u32[]{:S(2)}) collective-permute-start(bf16[1,640,256]{2,1,0:T(8,128)(2,1)S(1)} %add_last.3.one_ref), channel_id=1, source_target_pairs={{0,8},{1,9},{2,10},{3,11},{4,12},{5,13},{6,14},{7,15},{8,0},{9,1},... | collective-permute-start | bytes 983048 | tf_op jit(solution)/shard_map/ppermute | solution.py:41
  378.4 18.1 %collective-permute-start.33 = (bf16[2,640,256]{2,1,0:T(8,128)(2,1)S(1)}, bf16[2,640,256]{2,1,0:T(8,128)(2,1)S(1)}, u32[]{:S(2)}, u32[]{:S(2)}) collective-permute-start(bf16[2,640,256]{2,1,0:T(8,128)(2,1)S(1)} %bitcast.80), channel_id=1, source_target_pairs={{0,4},{1,5},{2,6},{3,7},{4,0},{5,1},{6,2},{7,3},{8,12},{9,13},{10,... | collective-permute-start | bytes 1966088 | tf_op jit(solution)/shard_map/ppermute | solution.py:41
  378.4 15.8 %collective-permute-start.34 = (f32[12,1024]{1,0:T(8,128)S(1)}, f32[12,1024]{1,0:T(8,128)S(1)}, u32[]{:S(2)}, u32[]{:S(2)}) collective-permute-start(f32[12,1024]{1,0:T(8,128)S(1)} %total.7.one_ref), channel_id=1, source_target_pairs={{0,8},{1,9},{2,10},{3,11},{4,12},{5,13},{6,14},{7,15},{8,0},{9,1},... | collective-permute-start | bytes 147464 | tf_op jit(solution)/shard_map/ppermute | solution.py:41
  394.3 1.3 collective-permute-start.35
  403.8 6.8 %collective-permute-start.37 = (bf16[8,448,512]{2,1,0:T(8,128)(2,1)}, bf16[8,448,512]{2,1,0:T(8,128)(2,1)}, u32[]{:S(2)}, u32[]{:S(2)}) collective-permute-start(bf16[8,448,512]{2,1,0:T(8,128)(2,1)} %bitcast.65), channel_id=1, source_target_pairs={{0,1},{1,0},{2,3},{3,2},{4,5},{5,4},{6,7},{7,6},{8,9},{9,8},{10,11... | collective-permute-start | bytes 11010056 | tf_op jit(solution)/shard_map/ppermute | solution.py:41
  403.8 31.2 %collective-permute-start.38 = (bf16[4,640,256]{2,1,0:T(8,128)(2,1)S(1)}, bf16[4,640,256]{2,1,0:T(8,128)(2,1)S(1)}, u32[]{:S(2)}, u32[]{:S(2)}) collective-permute-start(bf16[4,640,256]{2,1,0:T(8,128)(2,1)S(1)} %bitcast.73), channel_id=1, source_target_pairs={{0,2},{1,3},{2,0},{3,1},{4,6},{5,7},{6,4},{7,5},{8,10},{9,11},{10,... | collective-permute-start | bytes 3932168 | tf_op jit(solution)/shard_map/ppermute | solution.py:41
  437.6 5.1 %collective-permute-start.39 = (bf16[8,640,256]{2,1,0:T(8,128)(2,1)S(1)}, bf16[8,640,256]{2,1,0:T(8,128)(2,1)}, u32[]{:S(2)}, u32[]{:S(2)}) collective-permute-start(bf16[8,640,256]{2,1,0:T(8,128)(2,1)S(1)} %bitcast.68), channel_id=1, source_target_pairs={{0,1},{1,0},{2,3},{3,2},{4,5},{5,4},{6,7},{7,6},{8,9},{9,8},{10,11... | collective-permute-start | bytes 7864328 | tf_op jit(solution)/shard_map/ppermute | solution.py:41
  (40 other events, 200.8 us)
Sparse Core Ops, SparseCore 0:
  134.4 83.1 all-gather.1
